TPU v7x, 256 devices: a whole 4x4x8 slice. The times are simulated.
256 devices in a mesh: expert: 32 (over x, z_hi, core), dp: 8 (over y, z_lo).
Axes of the slice: x: 4, y: 4, z: 8 (z_hi: 4, z_lo: 2; z = z_hi * 2 + z_lo), core: 2. Of those that a mesh axis runs over, the one named last changes fastest.
Arguments:
- tokens: bfloat16 [24576, 2048], P(('expert', 'dp')), may hold values from -6 to 6
- norm_gain: float32 [2048], replicated, may hold values from 0.1 to 1.9
- expert_ids: int32 [24576, 8], P(('expert', 'dp')), may hold values from 0 to 63, all different within a row; in each aligned block of 96 rows (0 to 95, 96 to 191, ...) at most 16 rows name the same one
- route_weights: float32 [24576, 8], P(('expert', 'dp')), may hold values from 0.05 to 1
- gate_weight: bfloat16 [64, 2048, 768], P('expert', 'dp'), may hold values from -0.125 to 0.125
- up_weight: bfloat16 [64, 2048, 768], P('expert', 'dp'), may hold values from -0.125 to 0.125
- down_weight: bfloat16 [64, 768, 2048], P('expert', 'dp'), may hold values from -0.21875 to 0.21875
- pair_list: int32 [32], replicated, may hold values from 0 to 31, as said below
Outputs:
- mixed: bfloat16 [24576, 2048], P(('expert', 'dp'))
- held_gate: bfloat16 [32, 2048, 768], P('expert', 'dp')
- held_up: bfloat16 [32, 2048, 768], P('expert', 'dp')
- held_down: bfloat16 [32, 768, 2048], P('expert', 'dp')
Inputs may be any that keep to these rules, and one draw needn't show every extreme that they name: pair_list[pair_list[e]] = e, and pair_list[e] is e itself or differs from e in exactly one bit. `expert_ids`: each row names 8 different experts; among the rows of one device no expert is named more than 16 times, and in every draw some device's rows name one expert exactly 16 times.
All inputs are finite; a program needn't handle non-finite values.
Results may differ from a plain program's by a relative error of at most 0.0075.
Values may be sent and summed in bfloat16 or wider, within the bound.
No kernel may reach another device: no remote copies, remote signals or barrier semaphores. Data moves between devices by JAX's collectives and lax.ppermute only.
A program may use at most 192 MiB of HBM per device.

v0:
```python
import jax
import jax.numpy as jnp
from jax import lax
from jax.sharding import Mesh
from jax.sharding import PartitionSpec as P

EXPERT = ("expert_0", "expert_1", "expert_2")
DP = ("dp_0", "dp_1")
EXPERT_DP = ("expert_0", "expert_1", "expert_2", "dp_0", "dp_1")


def split_up(value, dim, count):
    dims = value.shape
    pieces = value.reshape(*dims[:dim], count, dims[dim] // count, *dims[dim + 1 :])
    return jnp.moveaxis(pieces, dim, 0)


def in_order(pieces, dim):
    pieces = jnp.moveaxis(pieces, 0, dim)
    dims = pieces.shape
    return pieces.reshape(*dims[:dim], dims[dim] * dims[dim + 1], *dims[dim + 2 :])


def exchange_in_order(pieces, axes, sequence):
    dims = [lax.axis_size(a) for a in axes]
    pieces = pieces.reshape(*dims, *pieces.shape[1:])
    for k in sequence:
        pieces = lax.all_to_all(pieces, axes[k], split_axis=k, concat_axis=k, tiled=True)
    return pieces.reshape(-1, *pieces.shape[len(axes) :])


def two_step_exchange(value, groups, sequence, split_dim, concat_dim):
    count = lax.axis_size(groups[0]) * lax.axis_size(groups[1])
    pieces = split_up(value, split_dim, count)
    return in_order(exchange_in_order(pieces, groups, sequence), concat_dim)


def side_by_side(arrays, axis, dim, along):
    ends, at = ([], 0)
    for a in arrays[:-1]:
        at += a.shape[along]
        ends.append(at)
    both = jnp.concatenate(arrays, axis=along)
    return tuple(jnp.split(lax.all_gather(both, axis, axis=dim, tiled=True), ends, axis=along))


def gathered_by_axis(value, axes, dim):
    for axis in reversed(axes):
        value = lax.all_gather(value, axis, axis=dim, tiled=True)
    return value


def body(
    tokens, norm_gain, expert_ids, route_weights, gate_weight, up_weight, down_weight, pair_list
):
    axis_count = lax.axis_size(EXPERT)
    per_device = gate_weight.shape[0]
    experts_all = axis_count * per_device
    token_rows, top_count = expert_ids.shape
    width = tokens.shape[1]
    capacity = max(2, 4 * token_rows * top_count // (3 * experts_all))
    values = tokens.astype(jnp.float32)
    scale = lax.rsqrt(jnp.mean(values * values, axis=-1, keepdims=True) + 1e-06)
    normed = (values * scale * norm_gain).astype(jnp.bfloat16)
    packed = jnp.concatenate(
        [gate_weight[0].reshape(-1), up_weight[0].reshape(-1), down_weight[0].reshape(-1)]
    )
    pieces = packed.reshape(axis_count, -1)
    spread = lax.all_to_all(pieces, EXPERT, split_axis=0, concat_axis=0, tiled=True)
    picked = jnp.take(spread, pair_list, axis=0)
    holding = two_step_exchange(
        picked, (("expert_0", "expert_1"), "expert_2"), (1, 0), 0, 0
    ).reshape(-1)
    block_size = gate_weight[0].size
    new_gate = holding[:block_size].reshape(gate_weight.shape[1:])
    new_up = holding[block_size : 2 * block_size].reshape(up_weight.shape[1:])
    new_down = holding[2 * block_size :].reshape(down_weight.shape[1:])
    expert_range = jnp.arange(experts_all, dtype=jnp.int32)
    home_device = expert_range // per_device
    flat_ids = expert_ids.reshape(-1)
    onehot = (flat_ids[:, None] == expert_range[None, :]).astype(jnp.int32)
    ranks = jnp.sum(jnp.cumsum(onehot, axis=0) * onehot, axis=1) - 1
    owners = jnp.sum(onehot * home_device[None, :], axis=1)
    slot_index = (owners * per_device + flat_ids % per_device) * capacity + ranks
    total_slots = experts_all * capacity
    slot_range = jnp.arange(total_slots, dtype=jnp.int32)
    matches = slot_index.reshape(token_rows, top_count)[None, :, :] == slot_range[:, None, None]
    placing = jnp.any(matches, axis=2).astype(jnp.bfloat16)
    outgoing = jnp.dot(placing, normed, preferred_element_type=jnp.float32).astype(jnp.bfloat16)
    outgoing = outgoing.reshape(axis_count, per_device * capacity, width)
    received = lax.all_to_all(outgoing, EXPERT, split_axis=0, concat_axis=0, tiled=True)
    received = received.reshape(axis_count, per_device, capacity, width)
    pieces = side_by_side((gate_weight, up_weight), DP, 1, 0)
    columns = received
    gate_part = jnp.einsum("semd,edf->semf", columns, pieces[0], preferred_element_type=jnp.float32)
    up_part = jnp.einsum("semd,edf->semf", columns, pieces[1], preferred_element_type=jnp.float32)
    hidden = (jax.nn.silu(gate_part) * up_part).astype(jnp.bfloat16)
    columns = hidden
    expert_out = jnp.einsum(
        "semf,efd->semd",
        columns,
        gathered_by_axis(down_weight, DP, 1),
        preferred_element_type=jnp.float32,
    ).astype(jnp.bfloat16)
    returned = lax.all_to_all(
        expert_out.reshape(axis_count, per_device * capacity, width),
        EXPERT,
        split_axis=0,
        concat_axis=0,
        tiled=True,
    )
    returned = returned.reshape(total_slots, width)
    route_bf = route_weights.astype(jnp.bfloat16)
    weighting = jnp.sum(
        jnp.where(matches, route_bf[None, :, :], jnp.zeros((), jnp.bfloat16)), axis=2
    )
    mixed = jnp.einsum("sr,sd->rd", weighting, returned, preferred_element_type=jnp.float32).astype(
        jnp.bfloat16
    )
    return (mixed, new_gate[None], new_up[None], new_down[None])


def solution(mesh):
    split = Mesh(
        mesh.devices.reshape(4, 4, 2, 4, 2), ("expert_0", "expert_1", "expert_2", "dp_0", "dp_1")
    )
    placed = (
        P(EXPERT_DP, None),
        P(),
        P(EXPERT_DP, None),
        P(EXPERT_DP, None),
        P(EXPERT, DP, None),
        P(EXPERT, DP, None),
        P(EXPERT, DP, None),
        P(),
    )
    return jax.shard_map(
        body,
        mesh=split,
        in_specs=placed,
        out_specs=(
            P(EXPERT_DP, None),
            P(EXPERT, DP, None),
            P(EXPERT, DP, None),
            P(EXPERT, DP, None),
        ),
        check_vma=False,
    )
```

profile of v0, /device:TPU:22, one launch (start us, length us, event | category | flops | bytes accessed | tf_op | source)
XLA Modules:
  0.0 626.9 jit_solution(9959726804754248452)
XLA Ops:
  8.0 2.8 pad_maximum_fusion
  10.9 0.8 slice-done
  13.6 7.8 %reduce.3 = bf16[32,18432]{1,0:T(8,128)(2,1)S(1)} reduce(bf16[32,1,18432]{2,1,0:T(2,128)(2,1)S(1)} %all_to_all.27, bf16[]{:T(256)} %broadcast.125), dimensions={1}, to_apply=%all_to_all.27.reduce_sub_computation | reduce | bytes 2359298 | tf_op jit(solution)/shard_map/all_to_all | solution.py:69
  21.4 1.7 reshape.137
  23.2 11.6 %all-to-all-start.2 = ((bf16[32,2,9216]{2,1,0:T(2,128)(2,1)}), bf16[32,2,9216]{2,1,0:T(2,128)(2,1)S(1)}, u32[]{:S(2)}, u32[]{:S(2)}) async-start(bf16[32,2,9216]{2,1,0:T(2,128)(2,1)} %reshape.137), calls=%async_computation.2 | async-start | bytes 2359296 | tf_op jit(solution)/shard_map/all_to_all | solution.py:69
  35.1 1.8 reduce-window.6
  38.1 1.0 fusion.10
  39.2 3.4 convolution_convert_fusion
  42.5 31.9 %all-to-all-done.2 = bf16[32,2,9216]{2,1,0:T(2,128)(2,1)S(1)} async-done(((bf16[32,2,9216]{2,1,0:T(2,128)(2,1)}), bf16[32,2,9216]{2,1,0:T(2,128)(2,1)S(1)}, u32[]{:S(2)}, u32[]{:S(2)}) %all-to-all-start.2) | async-done | bytes 1179680 | tf_op jit(solution)/shard_map/all_to_all | solution.py:69
  74.4 1.0 reshape.138
  76.1 1.3 gather_fusion
  77.4 0.8 gather.7
  78.9 4.7 all_to_all.33
  83.6 7.0 %all-to-all-start = ((bf16[32,32,2048]{2,1,0:T(8,128)(2,1)}), bf16[32,32,2048]{2,1,0:T(8,128)(2,1)}, u32[]{:S(2)}, u32[]{:S(2)}) async-start(bf16[32,32,2048]{2,1,0:T(8,128)(2,1)} %bitcast.74), calls=%async_computation | async-start | bytes 8388608 | tf_op jit(solution)/shard_map/all_to_all | solution.py:91
  91.3 2.2 copy.74
  93.6 137.1 %all-to-all-done = bf16[32,32,2048]{2,1,0:T(8,128)(2,1)} async-done(((bf16[32,32,2048]{2,1,0:T(8,128)(2,1)}), bf16[32,32,2048]{2,1,0:T(8,128)(2,1)}, u32[]{:S(2)}, u32[]{:S(2)}) %all-to-all-start) | async-done | bytes 4194336 | tf_op jit(solution)/shard_map/all_to_all | solution.py:91
  230.7 6.0 all-to-all-start.4
  236.7 6.5 %copy.68 = bf16[32,32,2048]{2,0,1:T(8,128)(2,1)} copy(bf16[32,32,2048]{2,1,0:T(8,128)(2,1)} %all-to-all-done) | data formatting | bytes 8388608 | tf_op jit(solution)/shard_map/all_to_all | solution.py:91
  243.3 187.3 %all-gather.4.cloned.1.call-done = bf16[4,2048,768]{2,1,0:T(8,128)(2,1)} async-done(((bf16[4,256,768]{2,1,0:T(8,128)(2,1)}), bf16[4,2048,768]{2,1,0:T(8,128)(2,1)}) %all-gather.4.cloned.1.call-update) | async-done | bytes 12582928 | tf_op jit(solution)/shard_map/all_gather | solution.py:44
  430.6 7.2 %fusion = f32[2,768,32,16]{1,2,3,0:T(8,128)S(1)} fusion(bf16[32,2,16,2048]{3,0,2,1:T(8,128)(2,1)} %bitcast.76, bf16[4,2048,768]{2,1,0:T(8,128)(2,1)} %all-gather.4.cloned.1.call-done), kind=kOutput, calls=%fused_computation.2 | convolution fusion | flops 3221225472 | bytes 13631488 | tf_op jit(solution)/shard_map/semd,edf->semf/dot_general | solution.py:96
  437.8 6.9 %fusion.6 = bf16[32,2,16,768]{3,0,2,1:T(8,128)(2,1)S(1)} fusion(f32[2,768,32,16]{1,2,3,0:T(8,128)S(1)} %fusion, bf16[32,2,16,2048]{3,0,2,1:T(8,128)(2,1)S(1)} %bitcast.77, bf16[4,2048,768]{2,1,0:T(8,128)(2,1)} %all-gather.4.cloned.1.call-done), kind=kOutput, calls=%fused_computation.10 | convolution fusion | flops 3225944064 | bytes 15204352 | tf_op jit(solution)/shard_map/semd,edf->semf/dot_general | solution.py:95
  444.8 56.3 %all-gather.8.cloned.1.call-done = bf16[2,768,2048]{2,1,0:T(8,128)(2,1)} async-done(((bf16[2,192,2048]{2,1,0:T(8,128)(2,1)}), bf16[2,768,2048]{2,1,0:T(8,128)(2,1)}) %all-gather.8.cloned.1.call-update) | async-done | bytes 6291472 | tf_op jit(solution)/shard_map/all_gather | solution.py:49
  501.0 7.6 %convert_bitcast_fusion = bf16[32,2,16,2048]{3,2,0,1:T(8,128)(2,1)S(1)} fusion(bf16[2,768,2048]{2,1,0:T(8,128)(2,1)} %all-gather.8.cloned.1.call-done, bf16[32,2,16,768]{3,0,2,1:T(8,128)(2,1)S(1)} %fusion.6), kind=kOutput, calls=%fused_computation.7 | convolution fusion | flops 3223322624 | bytes 12058624 | tf_op jit(solution)/shard_map/semf,efd->semd/dot_general | solution.py:99
  508.6 2.3 copy.70
  510.9 10.4 %all-to-all-start.1 = ((bf16[32,32,2048]{2,1,0:T(8,128)(2,1)}), bf16[32,32,2048]{2,1,0:T(8,128)(2,1)}, u32[]{:S(2)}, u32[]{:S(2)}) async-start(bf16[32,32,2048]{2,1,0:T(8,128)(2,1)} %bitcast.75), calls=%async_computation.1 | async-start | bytes 8388608 | tf_op jit(solution)/shard_map/all_to_all | solution.py:105
  521.4 1.0 fusion.12
  522.4 0.8 slice.39
  523.2 0.8 slice.46
  524.0 0.8 slice.36
  524.8 0.9 fusion.27
  525.7 90.9 %all-to-all-done.1 = bf16[32,32,2048]{2,1,0:T(8,128)(2,1)} async-done(((bf16[32,32,2048]{2,1,0:T(8,128)(2,1)}), bf16[32,32,2048]{2,1,0:T(8,128)(2,1)}, u32[]{:S(2)}, u32[]{:S(2)}) %all-to-all-start.1) | async-done | bytes 4194336 | tf_op jit(solution)/shard_map/all_to_all | solution.py:105
  616.6 3.7 convolution_convert_fusion.1
  (61 shorter events, 6.5 us)
Async XLA Ops:
  7.2 83.5 %all-gather.6.cloned.1.call-start = ((), (), s32[]{:S(2)}) async-start(), calls=%async_computation.6 | async-start | bytes 2359296 | tf_op jit(solution)/shard_map/all_gather | solution.py:49
  7.9 2.9 copy-start.1
  7.9 422.7 %all-gather.4.cloned.1.call-start = ((), (), s32[]{:S(2)}) async-start(), calls=%async_computation.5 | async-start | bytes 14155776 | tf_op jit(solution)/shard_map/all_gather | solution.py:44
  10.7 1.0 slice-start
  10.7 1.3 slice-start.1
  21.4 13.4 %copy-start.5 = (s32[96,8]{0,1:T(8,128)S(1)}, s32[96,8]{0,1:T(8,128)}, u32[]{:S(2)}) copy-start(s32[96,8]{0,1:T(8,128)} %param.10) | copy-start | bytes 9220
  21.4 16.3 %copy-start.8 = (s32[32]{0:T(128)S(1)}, s32[32]{0:T(128)}, u32[]{:S(2)}) copy-start(s32[32]{0:T(128)} %param.15) | copy-start | bytes 388
  21.4 16.5 %copy-start.2 = (bf16[96,2048]{1,0:T(8,128)(2,1)S(1)}, bf16[96,2048]{1,0:T(8,128)(2,1)}, u32[]{:S(2)}) copy-start(bf16[96,2048]{1,0:T(8,128)(2,1)} %param.8) | copy-start | bytes 1179652
  21.4 17.8 %copy-start.6 = (f32[2048]{0:T(1024)S(1)}, f32[2048]{0:T(1024)}, u32[]{:S(2)}) copy-start(f32[2048]{0:T(1024)} %param.9) | copy-start | bytes 24580
  23.2 51.2 %all-to-all-start.2 = ((bf16[32,2,9216]{2,1,0:T(2,128)(2,1)}), bf16[32,2,9216]{2,1,0:T(2,128)(2,1)S(1)}, u32[]{:S(2)}, u32[]{:S(2)}) async-start(bf16[32,2,9216]{2,1,0:T(2,128)(2,1)} %reshape.137), calls=%async_computation.2 | async-start | bytes 2359296 | tf_op jit(solution)/shard_map/all_to_all | solution.py:69
  38.1 4.4 copy-start.3
  83.6 147.1 %all-to-all-start = ((bf16[32,32,2048]{2,1,0:T(8,128)(2,1)}), bf16[32,32,2048]{2,1,0:T(8,128)(2,1)}, u32[]{:S(2)}, u32[]{:S(2)}) async-start(bf16[32,32,2048]{2,1,0:T(8,128)(2,1)} %bitcast.74), calls=%async_computation | async-start | bytes 8388608 | tf_op jit(solution)/shard_map/all_to_all | solution.py:91
  90.6 410.4 %all-gather.8.cloned.1.call-start = ((), (), s32[]{:S(2)}) async-start(), calls=%async_computation.7 | async-start | bytes 7864320 | tf_op jit(solution)/shard_map/all_gather | solution.py:49
  230.7 280.1 %all-to-all-start.4 = ((bf16[16,2,1,18432]{3,1,2,0:T(2,128)(2,1)}), bf16[16,2,1,18432]{3,1,2,0:T(2,128)(2,1)S(1)}, u32[]{:S(2)}, u32[]{:S(2)}) async-start(bf16[16,2,1,18432]{3,1,2,0:T(2,128)(2,1)} %copy.74), calls=%async_computation.4 | async-start | bytes 2359296 | tf_op jit(solution)/shard_map/all_to_all | solution.py:28
  430.6 7.2 %copy-start = (bf16[32,32,2048]{2,0,1:T(8,128)(2,1)S(1)}, bf16[32,32,2048]{2,0,1:T(8,128)(2,1)}, u32[]{:S(2)}) copy-start(bf16[32,32,2048]{2,0,1:T(8,128)(2,1)} %copy.68) | copy-start | bytes 12582916
  510.9 10.4 %copy-start.7 = (f32[96,8]{0,1:T(8,128)S(1)}, f32[96,8]{0,1:T(8,128)}, u32[]{:S(2)}) copy-start(f32[96,8]{0,1:T(8,128)} %param.11) | copy-start | bytes 9220
  510.9 10.5 %copy-start.4 = (s32[96,8]{1,0:T(8,128)S(1)}, s32[96,8]{1,0:T(8,128)}, u32[]{:S(2)}) copy-start(s32[96,8]{1,0:T(8,128)} %copy-done.3) | copy-start | bytes 9220
  510.9 105.7 %all-to-all-start.1 = ((bf16[32,32,2048]{2,1,0:T(8,128)(2,1)}), bf16[32,32,2048]{2,1,0:T(8,128)(2,1)}, u32[]{:S(2)}, u32[]{:S(2)}) async-start(bf16[32,32,2048]{2,1,0:T(8,128)(2,1)} %bitcast.75), calls=%async_computation.1 | async-start | bytes 8388608 | tf_op jit(solution)/shard_map/all_to_all | solution.py:105
Sparse Core Ops, SparseCore 0:
  9.8 52.4 all-gather.5
  64.1 366.4 all-gather.3
  432.4 68.5 all-gather.7
where the time goes:
time: 631 us; the launch traced here: 627 us
  waiting for transfers between devices  505 us (80%)
  starting transfers between devices  35.1 us (6%)
  matrix products  28.8 us (5%)
  local copies, waits for them, and re-layouts  23.6 us (4%)
  other arithmetic  15.7 us (2%)
  between operations  14.1 us (2%)
    all_gather x1, waiting for transfers between devices, side_by_side(): lax.all_gather(both, axis, axis=dim, tiled=True)  187 us
    all_to_all x1, waiting for transfers between devices, body(): lax.all_to_all(outgoing, EXPERT, split_axis=0, concat_axis=0, tiled=True)  137 us
    all_to_all x1, waiting for transfers between devices, body(): lax.all_to_all(expert_out.reshape(axis_count, per_device * capacity, widt...  90.9 us
    all_gather x2, waiting for transfers between devices, gathered_by_axis(): value = lax.all_gather(value, axis, axis=dim, tiled=True)  56.3 us
    all_to_all x1, waiting for transfers between devices, body(): lax.all_to_all(pieces, EXPERT, split_axis=0, concat_axis=0, tiled=True)  31.9 us
  transfers between devices with their start and end apart: 7, of which 5 were waited for; matrix products, arithmetic and copies ran while one was open for 10% of the time, Pallas kernels for 0%

commit v1 on v0

v1 whole, which is shorter than its diff:
```python
import functools

import jax
import jax.numpy as jnp
from jax import lax
from jax.experimental import pallas as pl
from jax.experimental.pallas import tpu as pltpu
from jax.sharding import Mesh
from jax.sharding import PartitionSpec as P

EXPERT = ("x", "zh", "c")
DP = ("y", "zl")
PLANE = ("x", "c")
Z = ("zh", "zl")
EXPERT_DP = EXPERT + DP
MOST = 16
NX, NZH, NC, NY, NZL = 4, 4, 2, 4, 2
NZ = NZH * NZL
BF = jnp.bfloat16
F32 = jnp.float32
GROUPS = ((0, -1, 1), (-2, 2), (-3, 3, 4))


def shift(value, axes, count, step):
    return lax.ppermute(value, axes, [(i, (i + step) % count) for i in range(count)])


def to_plane(value, dx, dc):
    pairs = []
    for x in range(NX):
        for c in range(NC):
            pairs.append((x * NC + c, ((x + dx) % NX) * NC + (c ^ dc)))
    return lax.ppermute(value, PLANE, pairs)


def from_plane(value, dx, dc):
    return to_plane(value, (-dx) % NX, dc)


REL = tuple((dx, dc) for dx in range(NX) for dc in range(NC))


def flip(value, axis, bit):
    count = {"x": NX, "zh": NZH, "c": NC, "zl": NZL}[axis]
    return lax.ppermute(value, axis, [(i, i ^ bit) for i in range(count)])


def after(value, *others):
    return lax.optimization_barrier((value, *others))[0]


def ffn_kernel(splits, place_ref, *refs):
    n_rows = len(splits)
    weight_refs, refs = refs[:6], refs[6:]
    row_refs, refs = refs[:n_rows], refs[n_rows:]
    out_refs, refs = refs[:n_rows], refs[n_rows:]
    gate_v, up_v, down_v, rows_v, res_v, sem_w, sem_r, sem_o = refs
    zl = place_ref[0]
    copies = []
    starts = []
    at = 0
    for i, n in enumerate(splits):
        starts.append(at)
        cp = pltpu.make_async_copy(row_refs[i], rows_v.at[pl.ds(at, n)], sem_r.at[i])
        cp.start()
        copies.append(cp)
        at += n
    total = at
    loads = []
    for half in range(2):
        zl_from = zl if half == 0 else 1 - zl
        for k, dest in enumerate((gate_v, up_v, down_v)):
            src = weight_refs[half * 3 + k]
            piece = src.shape[1]
            for y in range(NY):
                row = pl.multiple_of((y * NZL + zl_from) * piece, piece)
                cp = pltpu.make_async_copy(
                    src.at[y], dest.at[pl.ds(row, piece)], sem_w.at[(half * 3 + k) * NY + y]
                )
                cp.start()
                loads.append(cp)
    for cp in copies:
        cp.wait()
    for cp in loads:
        cp.wait()

    @pl.loop(0, total // 128)
    def _(step):
        at = pl.multiple_of(step * 128, 128)
        block = rows_v[pl.ds(at, 128), :]
        gate = jnp.dot(block, gate_v[...], preferred_element_type=F32)
        up = jnp.dot(block, up_v[...], preferred_element_type=F32)
        hidden = (gate / (1.0 + jnp.exp(-gate)) * up).astype(BF)
        res_v[pl.ds(at, 128), :] = jnp.dot(
            hidden, down_v[...], preferred_element_type=F32
        ).astype(BF)

    outs = []
    for i, n in enumerate(splits):
        cp = pltpu.make_async_copy(res_v.at[pl.ds(starts[i], n)], out_refs[i], sem_o.at[i])
        cp.start()
        outs.append(cp)
    for cp in outs:
        cp.wait()


def ffn(place, weights, rows):
    splits = tuple(r.shape[0] for r in rows)
    total = sum(splits)
    width = rows[0].shape[1]
    hidden = weights[0].shape[2]
    any_spec = pl.BlockSpec(memory_space=pl.ANY)
    flops = 2 * total * width * hidden * 3
    return pl.pallas_call(
        functools.partial(ffn_kernel, splits),
        out_shape=[jax.ShapeDtypeStruct(r.shape, BF) for r in rows],
        in_specs=[pl.BlockSpec(memory_space=pltpu.SMEM)] + [any_spec] * (6 + len(rows)),
        out_specs=[any_spec] * len(rows),
        scratch_shapes=[
            pltpu.VMEM((width, hidden), BF),
            pltpu.VMEM((width, hidden), BF),
            pltpu.VMEM((hidden, width), BF),
            pltpu.VMEM((total, width), BF),
            pltpu.VMEM((total, width), BF),
            pltpu.SemaphoreType.DMA((6 * NY,)),
            pltpu.SemaphoreType.DMA((len(rows),)),
            pltpu.SemaphoreType.DMA((len(rows),)),
        ],
        compiler_params=pltpu.CompilerParams(vmem_limit_bytes=44 << 20),
        cost_estimate=pl.CostEstimate(
            flops=flops, transcendentals=total * hidden, bytes_accessed=18 << 20
        ),
        name="expert_ffn",
    )(place, *weights, *rows)


def own_weights(weights):
    zl = lax.axis_index("zl")
    own = [jnp.where(zl == 0, w[0], w[1]) for w in weights]
    other = [jnp.where(zl == 0, w[1], w[0]) for w in weights]
    swapped = [flip(w, "zl", 1) for w in other]
    order = [own[0], own[1], swapped[0], swapped[1], own[2], swapped[2]]
    full = [lax.all_gather(w, "y", axis=0, tiled=False) for w in order]
    return [full[0], full[1], full[4], full[2], full[3], full[5]]


def held_blocks(weights, pair_list, gate):
    first = [w[0] for w in weights]
    gated = lax.optimization_barrier((*first, gate))[:3]
    me = lax.axis_index(EXPERT)
    want = jnp.sum(jnp.where(jnp.arange(pair_list.shape[0]) == me, pair_list ^ me, 0))
    outs = []
    for own, value in zip(first, gated):
        best = own
        for axis, bit, code in (("c", 1, 1), ("zh", 1, 2), ("zh", 2, 4), ("x", 1, 8), ("x", 2, 16)):
            best = jnp.where(want == code, flip(value, axis, bit), best)
        outs.append(best)
    return outs


def body(
    tokens, norm_gain, expert_ids, route_weights, gate_weight, up_weight, down_weight, pair_list
):
    width = tokens.shape[1]
    rows, top = expert_ids.shape
    x_me, zh_me, c_me = (lax.axis_index(a) for a in EXPERT)
    zl_me = lax.axis_index("zl")
    weights = own_weights((gate_weight, up_weight, down_weight))

    meta = jnp.concatenate([expert_ids.T.astype(BF), route_weights.T.astype(BF)], axis=0)
    metas = lax.all_gather(meta, Z, axis=0, tiled=False)
    values = tokens.astype(F32)
    scale = lax.rsqrt(jnp.mean(values * values, axis=-1, keepdims=True) + 1e-06)
    normed = (values * scale * norm_gain).astype(BF)
    held = {0: normed}
    up_, down_ = normed, normed
    for d in range(1, NZ // 2 + 1):
        up_ = shift(up_, Z, NZ, 1)
        held[-d if d < NZ // 2 else d] = up_
        if d < NZ // 2:
            down_ = shift(down_, Z, NZ, -1)
            held[d] = down_

    far = jnp.arange(len(REL), dtype=jnp.int32)
    holder = ((x_me + far // NC) & (NX - 1)) * (NZH * NC) + zh_me * NC + (c_me ^ (far & (NC - 1)))
    experts = holder * NZL + zl_me
    z_me = zh_me * NZL + zl_me
    slots = jnp.arange(MOST, dtype=jnp.int32)
    metas = jnp.take(metas, (z_me + jnp.arange(NZ, dtype=jnp.int32)) & (NZ - 1), axis=0)

    def choose(d):
        mine = metas[d % NZ]
        ids = mine[:top].astype(jnp.int32)
        named = ids[None, :, :] == experts[:, None, None]
        chosen = jnp.any(named, axis=1)
        factor = jnp.sum(jnp.where(named, mine[None, top:], jnp.zeros((), BF)), axis=1)
        ranks = jnp.cumsum(chosen.astype(jnp.int32), axis=1) - 1
        taken = (ranks[:, None, :] == slots[None, :, None]) & chosen[:, None, :]
        return taken, factor

    received, takens = [], []
    for group in GROUPS:
        n = len(group)
        parts = [choose(d) for d in group]
        taken = jnp.stack([p[0] for p in parts], axis=1)
        eye = jnp.eye(n, dtype=jnp.bool_)[None, :, None, :, None]
        placing = (taken[:, :, :, None, :] & eye).reshape(len(REL) * n * MOST, n * rows)
        factor = jnp.stack([p[1] for p in parts], axis=1)
        spread = jnp.where(
            taken[:, :, :, None, :] & eye, factor[:, :, None, None, :], jnp.zeros((), BF)
        ).reshape(len(REL) * n * MOST, n * rows)
        takens.append(spread)
        source = jnp.concatenate([held[d] for d in group], axis=0)
        out = jnp.dot(placing.astype(BF), source, preferred_element_type=F32).astype(BF)
        out = out.reshape(len(REL), n * MOST, width)
        got = []
        for r, (dx, dc) in enumerate(REL):
            got.append(out[r] if r == 0 else to_plane(out[r], dx, dc))
        received.append(got)

    new = held_blocks((gate_weight, up_weight, down_weight), pair_list, received[-1][-1])

    place = zl_me.astype(jnp.int32).reshape(1)
    partial = {}
    order = [len(GROUPS) - 1, *range(len(GROUPS) - 1)]
    calls = [[len(GROUPS) - 1], list(range(len(GROUPS) - 2, -1, -1))]
    for call in calls:
        flat = [r for g in call for r in received[g]]
        done = ffn(place, weights, flat)
        for k, g in enumerate(call):
            n = len(GROUPS[g])
            mine = done[k * len(REL) : (k + 1) * len(REL)]
            back = []
            for r, (dx, dc) in enumerate(REL):
                back.append(mine[r] if r == 0 else from_plane(mine[r], dx, dc))
            stack = jnp.concatenate(back, axis=0)
            part = lax.dot_general(
                takens[g], stack, (((0,), (0,)), ((), ())), preferred_element_type=F32
            ).reshape(n, rows, width)
            for i, d in enumerate(GROUPS[g]):
                partial[d] = part[i]

    def joined(got, d):
        return (got.astype(F32) + partial[d]).astype(BF)

    forward = shift(partial[4].astype(BF), Z, NZ, 1)
    for d in (3, 2, 1):
        forward = shift(joined(forward, d), Z, NZ, 1)
    backward = shift(partial[-3].astype(BF), Z, NZ, -1)
    for d in (-2, -1):
        backward = shift(joined(backward, d), Z, NZ, -1)
    mixed = (forward.astype(F32) + backward.astype(F32) + partial[0]).astype(BF)
    return (mixed, *(v[None] for v in new))


def solution(mesh):
    split = Mesh(mesh.devices.reshape(NX, NZH, NC, NY, NZL), EXPERT_DP)
    rows = P(EXPERT_DP, None)
    blocks = P(EXPERT, DP, None)
    return jax.shard_map(
        body,
        mesh=split,
        in_specs=(rows, P(), rows, rows, blocks, blocks, blocks, P()),
        out_specs=(rows, blocks, blocks, blocks),
        check_vma=False,
    )
```

time: 631 us -> 508 us (0.81)
  waiting for transfers between devices: 505 us -> 294 us
  starting transfers between devices: 35.1 us -> 80.5 us
  Pallas kernels: 0 us -> 34.6 us
  blocking collectives: 4.68 us -> 27.3 us
  matrix products: 28.8 us -> 6.71 us
    ppermute x0 -> x74, waiting for transfers between devices: none -> 294 us  [the longest x18 131 us: flip(): return lax.ppermute(value, axis, [(i, i ^ bit) for i in range(count)])]
    all_to_all x4 -> x0, waiting for transfers between devices: 260 us -> none  [the longest x1 137 us: body(): lax.all_to_all(outgoing, EXPERT, split_axis=0, concat_axis=0, tiled=True)]
    all_gather x3 -> x6, waiting for transfers between devices: 244 us -> 0.04 us  [own_weights(): full = [lax.all_gather(w, 'y', axis=0, tiled=False) for w in order]]
    ppermute x0 -> x74, starting transfers between devices: none -> 80.3 us  [the longest x42 35.1 us: to_plane(): return lax.ppermute(value, PLANE, pairs)]
    all_to_all x4 -> x0, starting transfers between devices: 35 us -> none  [the longest x1 11.6 us: body(): lax.all_to_all(pieces, EXPERT, split_axis=0, concat_axis=0, tiled=True)]
    pallas_call x0 -> x2, Pallas kernels: none -> 34.6 us  [ffn(): pl.pallas_call(functools.partial(ffn_kernel, splits), out_shape=[jax.Shap...]
    all_gather x0 -> x1, blocking collectives: none -> 27.3 us  [body(): metas = lax.all_gather(meta, Z, axis=0, tiled=False)]
    dot_general x5 -> x6, matrix products: 28.8 us -> 6.71 us  [the longest x3 4.63 us: body(): jnp.dot(placing.astype(BF), source, preferred_element_type=F32).astype(BF)]
  transfers between devices with their start and end apart: 7 -> 80, of which waited for: 5 -> 40; matrix products, arithmetic and copies ran while one was open for 10% -> 5% of each run, Pallas kernels for 0% -> 7%
where the time goes in v1:
time: 508 us; the launch traced here: 499 us
  waiting for transfers between devices  294 us (58%)
  starting transfers between devices  80.5 us (16%)
  Pallas kernels  34.6 us (7%)
  blocking collectives  27.3 us (5%)
  local copies, waits for them, and re-layouts  24.6 us (5%)
  between operations  18.6 us (4%)
  other arithmetic  12.6 us (2%)
  matrix products  6.71 us (1%)
    ppermute x18, waiting for transfers between devices, flip(): return lax.ppermute(value, axis, [(i, i ^ bit) for i in range(count)])  131 us
    ppermute x42, waiting for transfers between devices, to_plane(): return lax.ppermute(value, PLANE, pairs)  102 us
    ppermute x14, waiting for transfers between devices, shift(): lax.ppermute(value, axes, [(i, (i + step) % count) for i in range(count)])  61.3 us
    ppermute x42, starting transfers between devices, to_plane(): return lax.ppermute(value, PLANE, pairs)  35.1 us
    pallas_call x2, Pallas kernels, ffn(): pl.pallas_call(functools.partial(ffn_kernel, splits), out_shape=[jax.Shap...  34.6 us
    all_gather x1, blocking collectives, body(): metas = lax.all_gather(meta, Z, axis=0, tiled=False)  27.3 us
    ppermute x14, starting transfers between devices, shift(): lax.ppermute(value, axes, [(i, (i + step) % count) for i in range(count)])  23.9 us
    ppermute x18, starting transfers between devices, flip(): return lax.ppermute(value, axis, [(i, i ^ bit) for i in range(count)])  21.3 us
  transfers between devices with their start and end apart: 80, of which 40 were waited for; matrix products, arithmetic and copies ran while one was open for 5% of the time, Pallas kernels for 7%

profile of v1, /device:TPU:22, one launch (start us, length us, event | category | flops | bytes accessed | tf_op | source)
XLA Modules:
  0.0 499.2 jit_solution(9349787626311312911)
XLA Ops:
  18.1 27.3 %all-gather = bf16[128,96]{1,0:T(8,128)(2,1)S(1)} all-gather(bf16[16,96]{1,0:T(8,128)(2,1)S(1)} %pad_maximum_fusion.2), channel_id=2, replica_groups=mesh['x'=4,'zh'=4,'c'=2,'y'=4,'zl'=2] {'zh','zl'}, dimensions={0}, use_global_device_ids=true | all-gather | bytes 27648 | tf_op jit(solution)/shard_map/all_gather | solution.py:171
  51.9 8.6 %collective-permute-done.4 = bf16[96,2048]{1,0:T(8,128)(2,1)S(1)} collective-permute-done((bf16[96,2048]{1,0:T(8,128)(2,1)S(1)}, bf16[96,2048]{1,0:T(8,128)(2,1)S(1)}, u32[]{:S(2)}, u32[]{:S(2)}) %collective-permute-start.4) | collective-permute-done | bytes 393248 | tf_op jit(solution)/shard_map/ppermute | solution.py:25
  64.4 9.1 %collective-permute-done.5 = bf16[96,2048]{1,0:T(8,128)(2,1)} collective-permute-done((bf16[96,2048]{1,0:T(8,128)(2,1)S(1)}, bf16[96,2048]{1,0:T(8,128)(2,1)}, u32[]{:S(2)}, u32[]{:S(2)}) %collective-permute-start.5) | collective-permute-done | bytes 393248 | tf_op jit(solution)/shard_map/ppermute | solution.py:25
  74.9 7.9 %collective-permute-done.9 = bf16[96,2048]{1,0:T(8,128)(2,1)} collective-permute-done((bf16[96,2048]{1,0:T(8,128)(2,1)}, bf16[96,2048]{1,0:T(8,128)(2,1)}, u32[]{:S(2)}, u32[]{:S(2)}) %collective-permute-start.9) | collective-permute-done | bytes 393248 | tf_op jit(solution)/shard_map/ppermute | solution.py:25
  86.1 6.3 %collective-permute-done.16.refs_13_ = bf16[48,2048]{1,0:T(8,128)(2,1)S(1)} collective-permute-done((bf16[48,2048]{1,0:T(8,128)(2,1)S(1)}, bf16[48,2048]{1,0:T(8,128)(2,1)S(1)}, u32[]{:S(2)}, u32[]{:S(2)}) %collective-permute-start.16) | collective-permute-done | bytes 196640 | tf_op jit(solution)/shard_map/ppermute | solution.py:33
  106.1 6.4 %collective-permute-done.60 = bf16[256,768]{1,0:T(8,128)(2,1)} collective-permute-done((bf16[256,768]{1,0:T(8,128)(2,1)}, bf16[256,768]{1,0:T(8,128)(2,1)}, u32[]{:S(2)}, u32[]{:S(2)}) %collective-permute-start.60) | collective-permute-done | bytes 393248 | tf_op jit(solution)/shard_map/ppermute | solution.py:45
  117.5 14.5 %collective-permute-done.62 = bf16[256,768]{1,0:T(8,128)(2,1)} collective-permute-done((bf16[256,768]{1,0:T(8,128)(2,1)}, bf16[256,768]{1,0:T(8,128)(2,1)}, u32[]{:S(2)}, u32[]{:S(2)}) %collective-permute-start.62) | collective-permute-done | bytes 393248 | tf_op jit(solution)/shard_map/ppermute | solution.py:45
  133.4 10.6 %collective-permute-done = bf16[256,768]{1,0:T(8,128)(2,1)S(1)} collective-permute-done((bf16[256,768]{1,0:T(8,128)(2,1)S(1)}, bf16[256,768]{1,0:T(8,128)(2,1)S(1)}, u32[]{:S(2)}, u32[]{:S(2)}) %collective-permute-start) | collective-permute-done | bytes 393248 | tf_op jit(solution)/shard_map/ppermute | solution.py:45
  158.7 7.3 %collective-permute-done.65 = bf16[256,768]{1,0:T(8,128)(2,1)S(1)} collective-permute-done((bf16[256,768]{1,0:T(8,128)(2,1)}, bf16[256,768]{1,0:T(8,128)(2,1)S(1)}, u32[]{:S(2)}, u32[]{:S(2)}) %collective-permute-start.65) | collective-permute-done | bytes 393248 | tf_op jit(solution)/shard_map/ppermute | solution.py:45
  166.0 7.3 %collective-permute-done.66 = bf16[256,768]{1,0:T(8,128)(2,1)S(1)} collective-permute-done((bf16[256,768]{1,0:T(8,128)(2,1)}, bf16[256,768]{1,0:T(8,128)(2,1)S(1)}, u32[]{:S(2)}, u32[]{:S(2)}) %collective-permute-start.66) | collective-permute-done | bytes 393248 | tf_op jit(solution)/shard_map/ppermute | solution.py:45
  173.3 15.4 %collective-permute-done.67 = bf16[256,768]{1,0:T(8,128)(2,1)S(1)} collective-permute-done((bf16[256,768]{1,0:T(8,128)(2,1)}, bf16[256,768]{1,0:T(8,128)(2,1)S(1)}, u32[]{:S(2)}, u32[]{:S(2)}) %collective-permute-start.67) | collective-permute-done | bytes 393248 | tf_op jit(solution)/shard_map/ppermute | solution.py:45
  189.7 11.0 %collective-permute-done.1 = bf16[256,768]{1,0:T(8,128)(2,1)S(1)} collective-permute-done((bf16[256,768]{1,0:T(8,128)(2,1)S(1)}, bf16[256,768]{1,0:T(8,128)(2,1)S(1)}, u32[]{:S(2)}, u32[]{:S(2)}) %collective-permute-start.1) | collective-permute-done | bytes 393248 | tf_op jit(solution)/shard_map/ppermute | solution.py:45
  206.5 8.8 %collective-permute-done.69 = bf16[96,2048]{1,0:T(8,128)(2,1)S(1)} collective-permute-done((bf16[96,2048]{1,0:T(8,128)(2,1)S(1)}, bf16[96,2048]{1,0:T(8,128)(2,1)S(1)}, u32[]{:S(2)}, u32[]{:S(2)}) %collective-permute-start.69) | collective-permute-done | bytes 393248 | tf_op jit(solution)/shard_map/ppermute | solution.py:45
  220.3 6.2 %collective-permute-done.71 = bf16[96,2048]{1,0:T(8,128)(2,1)S(1)} collective-permute-done((bf16[96,2048]{1,0:T(8,128)(2,1)S(1)}, bf16[96,2048]{1,0:T(8,128)(2,1)S(1)}, u32[]{:S(2)}, u32[]{:S(2)}) %collective-permute-start.71) | collective-permute-done | bytes 393248 | tf_op jit(solution)/shard_map/ppermute | solution.py:45
  226.5 14.4 %collective-permute-done.72 = bf16[96,2048]{1,0:T(8,128)(2,1)S(1)} collective-permute-done((bf16[96,2048]{1,0:T(8,128)(2,1)S(1)}, bf16[96,2048]{1,0:T(8,128)(2,1)S(1)}, u32[]{:S(2)}, u32[]{:S(2)}) %collective-permute-start.72) | collective-permute-done | bytes 393248 | tf_op jit(solution)/shard_map/ppermute | solution.py:45
  241.9 11.0 %collective-permute-done.2 = bf16[96,2048]{1,0:T(8,128)(2,1)S(1)} collective-permute-done((bf16[96,2048]{1,0:T(8,128)(2,1)S(1)}, bf16[96,2048]{1,0:T(8,128)(2,1)S(1)}, u32[]{:S(2)}, u32[]{:S(2)}) %collective-permute-start.2) | collective-permute-done | bytes 393248 | tf_op jit(solution)/shard_map/ppermute | solution.py:45
  266.4 10.8 %collective-permute-done.35.refs_17_ = bf16[48,2048]{1,0:T(8,128)(2,1)S(1)} collective-permute-done((bf16[48,2048]{1,0:T(8,128)(2,1)S(1)}, bf16[48,2048]{1,0:T(8,128)(2,1)S(1)}, u32[]{:S(2)}, u32[]{:S(2)}) %collective-permute-start.35) | collective-permute-done | bytes 196640 | tf_op jit(solution)/shard_map/ppermute | solution.py:33
  310.8 20.3 %expert_ffn.3 = (bf16[32,2048]{1,0:T(8,128)(2,1)S(1)}, bf16[32,2048]{1,0:T(8,128)(2,1)S(1)}, bf16[32,2048]{1,0:T(8,128)(2,1)S(1)}, bf16[32,2048]{1,0:T(8,128)(2,...) custom-call(s32[1]{0:T(128)} %bitcast.13.place_ref, ...), custom_call_target="tpu_custom_call" | custom-call | flops 6039797760 | bytes 18874368 | tf_op jit(solution)/shard_map/expert_ffn/pallas_call | solution.py:114
  340.1 14.3 %expert_ffn.2 = (bf16[48,2048]{1,0:T(8,128)(2,1)S(1)}, bf16[48,2048]{1,0:T(8,128)(2,1)S(1)}, bf16[48,2048]{1,0:T(8,128)(2,1)S(1)}, bf16[48,2048]{1,0:T(8,128)(2,...) custom-call(s32[1]{0:T(128)} %bitcast.13.place_ref, ...), custom_call_target="tpu_custom_call" | custom-call | flops 3623878656 | bytes 18874368 | tf_op jit(solution)/shard_map/expert_ffn/pallas_call | solution.py:114
  354.6 7.1 %collective-permute-done.41 = bf16[32,2048]{1,0:T(8,128)(2,1)S(1)} collective-permute-done((bf16[32,2048]{1,0:T(8,128)(2,1)S(1)}, bf16[32,2048]{1,0:T(8,128)(2,1)S(1)}, u32[]{:S(2)}, u32[]{:S(2)}) %collective-permute-start.41) | collective-permute-done | bytes 131104 | tf_op jit(solution)/shard_map/ppermute | solution.py:33
  361.7 6.9 %collective-permute-done.42 = bf16[32,2048]{1,0:T(8,128)(2,1)S(1)} collective-permute-done((bf16[32,2048]{1,0:T(8,128)(2,1)S(1)}, bf16[32,2048]{1,0:T(8,128)(2,1)S(1)}, u32[]{:S(2)}, u32[]{:S(2)}) %collective-permute-start.42) | collective-permute-done | bytes 131104 | tf_op jit(solution)/shard_map/ppermute | solution.py:33
  368.6 6.9 %collective-permute-done.43 = bf16[32,2048]{1,0:T(8,128)(2,1)S(1)} collective-permute-done((bf16[32,2048]{1,0:T(8,128)(2,1)S(1)}, bf16[32,2048]{1,0:T(8,128)(2,1)S(1)}, u32[]{:S(2)}, u32[]{:S(2)}) %collective-permute-start.43) | collective-permute-done | bytes 131104 | tf_op jit(solution)/shard_map/ppermute | solution.py:33
  375.5 6.6 %collective-permute-done.44 = bf16[32,2048]{1,0:T(8,128)(2,1)S(1)} collective-permute-done((bf16[32,2048]{1,0:T(8,128)(2,1)S(1)}, bf16[32,2048]{1,0:T(8,128)(2,1)S(1)}, u32[]{:S(2)}, u32[]{:S(2)}) %collective-permute-start.44) | collective-permute-done | bytes 131104 | tf_op jit(solution)/shard_map/ppermute | solution.py:33
  394.2 7.5 %collective-permute-done.18 = bf16[48,2048]{1,0:T(8,128)(2,1)S(1)} collective-permute-done((bf16[48,2048]{1,0:T(8,128)(2,1)S(1)}, bf16[48,2048]{1,0:T(8,128)(2,1)S(1)}, u32[]{:S(2)}, u32[]{:S(2)}) %collective-permute-start.18) | collective-permute-done | bytes 196640 | tf_op jit(solution)/shard_map/ppermute | solution.py:33
  401.8 8.2 %collective-permute-done.19 = bf16[48,2048]{1,0:T(8,128)(2,1)S(1)} collective-permute-done((bf16[48,2048]{1,0:T(8,128)(2,1)S(1)}, bf16[48,2048]{1,0:T(8,128)(2,1)S(1)}, u32[]{:S(2)}, u32[]{:S(2)}) %collective-permute-start.19) | collective-permute-done | bytes 196640 | tf_op jit(solution)/shard_map/ppermute | solution.py:33
  409.9 8.2 %collective-permute-done.20 = bf16[48,2048]{1,0:T(8,128)(2,1)S(1)} collective-permute-done((bf16[48,2048]{1,0:T(8,128)(2,1)S(1)}, bf16[48,2048]{1,0:T(8,128)(2,1)S(1)}, u32[]{:S(2)}, u32[]{:S(2)}) %collective-permute-start.20) | collective-permute-done | bytes 196640 | tf_op jit(solution)/shard_map/ppermute | solution.py:33
  418.1 7.9 %collective-permute-done.21 = bf16[48,2048]{1,0:T(8,128)(2,1)S(1)} collective-permute-done((bf16[48,2048]{1,0:T(8,128)(2,1)S(1)}, bf16[48,2048]{1,0:T(8,128)(2,1)S(1)}, u32[]{:S(2)}, u32[]{:S(2)}) %collective-permute-start.21) | collective-permute-done | bytes 196640 | tf_op jit(solution)/shard_map/ppermute | solution.py:33
  426.0 6.1 %collective-permute-done.22 = bf16[48,2048]{1,0:T(8,128)(2,1)S(1)} collective-permute-done((bf16[48,2048]{1,0:T(8,128)(2,1)S(1)}, bf16[48,2048]{1,0:T(8,128)(2,1)S(1)}, u32[]{:S(2)}, u32[]{:S(2)}) %collective-permute-start.22) | collective-permute-done | bytes 196640 | tf_op jit(solution)/shard_map/ppermute | solution.py:33
  432.1 5.8 %collective-permute-done.23 = bf16[48,2048]{1,0:T(8,128)(2,1)S(1)} collective-permute-done((bf16[48,2048]{1,0:T(8,128)(2,1)S(1)}, bf16[48,2048]{1,0:T(8,128)(2,1)S(1)}, u32[]{:S(2)}, u32[]{:S(2)}) %collective-permute-start.23) | collective-permute-done | bytes 196640 | tf_op jit(solution)/shard_map/ppermute | solution.py:33
  447.5 9.0 %collective-permute-done.24 = bf16[96,2048]{1,0:T(8,128)(2,1)S(1)} collective-permute-done((bf16[96,2048]{1,0:T(8,128)(2,1)S(1)}, bf16[96,2048]{1,0:T(8,128)(2,1)S(1)}, u32[]{:S(2)}, u32[]{:S(2)}) %collective-permute-start.24) | collective-permute-done | bytes 393248 | tf_op jit(solution)/shard_map/ppermute | solution.py:25
  456.7 11.4 %collective-permute-done.25 = bf16[96,2048]{1,0:T(8,128)(2,1)S(1)} collective-permute-done((bf16[96,2048]{1,0:T(8,128)(2,1)S(1)}, bf16[96,2048]{1,0:T(8,128)(2,1)S(1)}, u32[]{:S(2)}, u32[]{:S(2)}) %collective-permute-start.25) | collective-permute-done | bytes 393248 | tf_op jit(solution)/shard_map/ppermute | solution.py:25
  472.6 6.3 %collective-permute-done.47 = bf16[96,2048]{1,0:T(8,128)(2,1)S(1)} collective-permute-done((bf16[96,2048]{1,0:T(8,128)(2,1)S(1)}, bf16[96,2048]{1,0:T(8,128)(2,1)S(1)}, u32[]{:S(2)}, u32[]{:S(2)}) %collective-permute-start.47) | collective-permute-done | bytes 393248 | tf_op jit(solution)/shard_map/ppermute | solution.py:25
  (329 shorter events, 165.4 us)
Async XLA Ops:
  7.2 295.7 %all-gather.11.cloned.1.call-start = ((), (), s32[]{:S(2)}) async-start(), calls=%async_computation | async-start | bytes 1966080 | tf_op jit(solution)/shard_map/all_gather | solution.py:143
  9.4 293.5 %all-gather.13.cloned.1.call-start = ((), (), s32[]{:S(2)}) async-start(), calls=%async_computation.1 | async-start | bytes 1966080 | tf_op jit(solution)/shard_map/all_gather | solution.py:143
  10.5 292.4 %all-gather.15.cloned.1.call-start = ((), (), s32[]{:S(2)}) async-start(), calls=%async_computation.2 | async-start | bytes 1966080 | tf_op jit(solution)/shard_map/all_gather | solution.py:143
  10.9 37.5 %collective-permute-start.3 = (bf16[96,2048]{1,0:T(8,128)(2,1)S(1)}, bf16[96,2048]{1,0:T(8,128)(2,1)S(1)}, u32[]{:S(2)}, u32[]{:S(2)}) collective-permute-start(bf16[96,2048]{1,0:T(8,128)(2,1)S(1)} %fusion.12), channel_id=1, source_target_pairs={{0,1},{1,16},{16,17},{17,32},{32,33},{33,48},{48,49},{49,0},{2,3},... | collective-permute-start | bytes 1179656 | tf_op jit(solution)/shard_map/ppermute | solution.py:25
  12.9 37.9 %collective-permute-start.6 = (bf16[96,2048]{1,0:T(8,128)(2,1)S(1)}, bf16[96,2048]{1,0:T(8,128)(2,1)}, u32[]{:S(2)}, u32[]{:S(2)}) collective-permute-start(bf16[96,2048]{1,0:T(8,128)(2,1)S(1)} %fusion.12), channel_id=1, source_target_pairs={{0,49},{1,0},{16,1},{17,16},{32,17},{33,32},{48,33},{49,48},{2,51}... | collective-permute-start | bytes 1179656 | tf_op jit(solution)/shard_map/ppermute | solution.py:25
  17.9 285.0 %all-gather.17.cloned.1.call-start = ((), (), s32[]{:S(2)}) async-start(), calls=%async_computation.3 | async-start | bytes 1966080 | tf_op jit(solution)/shard_map/all_gather | solution.py:143
  94.6 17.9 %collective-permute-start.60 = (bf16[256,768]{1,0:T(8,128)(2,1)}, bf16[256,768]{1,0:T(8,128)(2,1)}, u32[]{:S(2)}, u32[]{:S(2)}) collective-permute-start(bf16[256,768]{1,0:T(8,128)(2,1)} %get-tuple-element.55), channel_id=1, source_target_pairs={{0,64},{64,0},{128,192},{192,128},{1,65},{65,1},{129,193},{193,129... | collective-permute-start | bytes 1179656 | tf_op jit(solution)/shard_map/ppermute | solution.py:45
  94.6 22.9 %collective-permute-start.61 = (bf16[256,768]{1,0:T(8,128)(2,1)}, bf16[256,768]{1,0:T(8,128)(2,1)}, u32[]{:S(2)}, u32[]{:S(2)}) collective-permute-start(bf16[256,768]{1,0:T(8,128)(2,1)} %get-tuple-element.55), channel_id=1, source_target_pairs={{0,32},{16,48},{32,0},{48,16},{1,33},{17,49},{33,1},{49,17},{2,34}... | collective-permute-start | bytes 1179656 | tf_op jit(solution)/shard_map/ppermute | solution.py:45
  99.3 32.8 %collective-permute-start.62 = (bf16[256,768]{1,0:T(8,128)(2,1)}, bf16[256,768]{1,0:T(8,128)(2,1)}, u32[]{:S(2)}, u32[]{:S(2)}) collective-permute-start(bf16[256,768]{1,0:T(8,128)(2,1)} %get-tuple-element.55), channel_id=1, source_target_pairs={{0,16},{16,0},{32,48},{48,32},{1,17},{17,1},{33,49},{49,33},{2,18}... | collective-permute-start | bytes 1179656 | tf_op jit(solution)/shard_map/ppermute | solution.py:45
  99.7 32.3 %collective-permute-start.63 = (bf16[256,768]{1,0:T(8,128)(2,1)}, bf16[256,768]{1,0:T(8,128)(2,1)}, u32[]{:S(2)}, u32[]{:S(2)}) collective-permute-start(bf16[256,768]{1,0:T(8,128)(2,1)} %get-tuple-element.55), channel_id=1, source_target_pairs={{0,8},{8,0},{1,9},{9,1},{2,10},{10,2},{3,11},{11,3},{4,12},{12,4},... | collective-permute-start | bytes 1179656 | tf_op jit(solution)/shard_map/ppermute | solution.py:45
  144.8 158.1 %all-gather.19.cloned.1.call-start = ((), (), s32[]{:S(2)}) async-start(), calls=%async_computation.4 | async-start | bytes 1966080 | tf_op jit(solution)/shard_map/all_gather | solution.py:143
  148.6 17.4 %collective-permute-start.65 = (bf16[256,768]{1,0:T(8,128)(2,1)}, bf16[256,768]{1,0:T(8,128)(2,1)S(1)}, u32[]{:S(2)}, u32[]{:S(2)}) collective-permute-start(bf16[256,768]{1,0:T(8,128)(2,1)} %get-tuple-element.56), channel_id=1, source_target_pairs={{0,64},{64,0},{128,192},{192,128},{1,65},{65,1},{129,193},{193,129... | collective-permute-start | bytes 1179656 | tf_op jit(solution)/shard_map/ppermute | solution.py:45
  148.6 24.7 %collective-permute-start.66 = (bf16[256,768]{1,0:T(8,128)(2,1)}, bf16[256,768]{1,0:T(8,128)(2,1)S(1)}, u32[]{:S(2)}, u32[]{:S(2)}) collective-permute-start(bf16[256,768]{1,0:T(8,128)(2,1)} %get-tuple-element.56), channel_id=1, source_target_pairs={{0,32},{16,48},{32,0},{48,16},{1,33},{17,49},{33,1},{49,17},{2,34}... | collective-permute-start | bytes 1179656 | tf_op jit(solution)/shard_map/ppermute | solution.py:45
  153.3 35.4 %collective-permute-start.67 = (bf16[256,768]{1,0:T(8,128)(2,1)}, bf16[256,768]{1,0:T(8,128)(2,1)S(1)}, u32[]{:S(2)}, u32[]{:S(2)}) collective-permute-start(bf16[256,768]{1,0:T(8,128)(2,1)} %get-tuple-element.56), channel_id=1, source_target_pairs={{0,16},{16,0},{32,48},{48,32},{1,17},{17,1},{33,49},{49,33},{2,18}... | collective-permute-start | bytes 1179656 | tf_op jit(solution)/shard_map/ppermute | solution.py:45
  153.3 35.4 %collective-permute-start.68 = (bf16[256,768]{1,0:T(8,128)(2,1)}, bf16[256,768]{1,0:T(8,128)(2,1)S(1)}, u32[]{:S(2)}, u32[]{:S(2)}) collective-permute-start(bf16[256,768]{1,0:T(8,128)(2,1)} %get-tuple-element.56), channel_id=1, source_target_pairs={{0,8},{8,0},{1,9},{9,1},{2,10},{10,2},{3,11},{11,3},{4,12},{12,4},... | collective-permute-start | bytes 1179656 | tf_op jit(solution)/shard_map/ppermute | solution.py:45
  201.6 101.4 %all-gather.21.cloned.1.call-start = ((), (), s32[]{:S(2)}) async-start(), calls=%async_computation.5 | async-start | bytes 1966080 | tf_op jit(solution)/shard_map/all_gather | solution.py:143
  203.7 22.8 %collective-permute-start.71 = (bf16[96,2048]{1,0:T(8,128)(2,1)S(1)}, bf16[96,2048]{1,0:T(8,128)(2,1)S(1)}, u32[]{:S(2)}, u32[]{:S(2)}) collective-permute-start(bf16[96,2048]{1,0:T(8,128)(2,1)S(1)} %copy-done.29), channel_id=1, source_target_pairs={{0,32},{16,48},{32,0},{48,16},{1,33},{17,49},{33,1},{49,17},{2,34}... | collective-permute-start | bytes 1179656 | tf_op jit(solution)/shard_map/ppermute | solution.py:45
  206.0 34.9 %collective-permute-start.72 = (bf16[96,2048]{1,0:T(8,128)(2,1)S(1)}, bf16[96,2048]{1,0:T(8,128)(2,1)S(1)}, u32[]{:S(2)}, u32[]{:S(2)}) collective-permute-start(bf16[96,2048]{1,0:T(8,128)(2,1)S(1)} %copy-done.29), channel_id=1, source_target_pairs={{0,16},{16,0},{32,48},{48,32},{1,17},{17,1},{33,49},{49,33},{2,18}... | collective-permute-start | bytes 1179656 | tf_op jit(solution)/shard_map/ppermute | solution.py:45
  206.5 34.4 %collective-permute-start.73 = (bf16[96,2048]{1,0:T(8,128)(2,1)S(1)}, bf16[96,2048]{1,0:T(8,128)(2,1)S(1)}, u32[]{:S(2)}, u32[]{:S(2)}) collective-permute-start(bf16[96,2048]{1,0:T(8,128)(2,1)S(1)} %copy-done.29), channel_id=1, source_target_pairs={{0,8},{8,0},{1,9},{9,1},{2,10},{10,2},{3,11},{11,3},{4,12},{12,4},... | collective-permute-start | bytes 1179656 | tf_op jit(solution)/shard_map/ppermute | solution.py:45
  259.8 17.4 %collective-permute-start.35 = (bf16[48,2048]{1,0:T(8,128)(2,1)S(1)}, bf16[48,2048]{1,0:T(8,128)(2,1)S(1)}, u32[]{:S(2)}, u32[]{:S(2)}) collective-permute-start(bf16[48,2048]{1,0:T(8,128)(2,1)S(1)} %get-tuple-element.90), channel_id=1, source_target_pairs={{0,72},{8,64},{64,136},{72,128},{128,200},{136,192},{192,8},{200,0... | collective-permute-start | bytes 589832 | tf_op jit(solution)/shard_map/ppermute | solution.py:33
  261.5 19.4 %collective-permute-start.37 = (bf16[48,2048]{1,0:T(8,128)(2,1)S(1)}, bf16[48,2048]{1,0:T(8,128)(2,1)S(1)}, u32[]{:S(2)}, u32[]{:S(2)}) collective-permute-start(bf16[48,2048]{1,0:T(8,128)(2,1)S(1)} %get-tuple-element.88), channel_id=1, source_target_pairs={{0,136},{8,128},{64,200},{72,192},{128,8},{136,0},{192,72},{200,64... | collective-permute-start | bytes 589832 | tf_op jit(solution)/shard_map/ppermute | solution.py:33
  292.7 38.4 %collective-permute-start.10 = (bf16[48,2048]{1,0:T(8,128)(2,1)}, bf16[48,2048]{1,0:T(8,128)(2,1)S(1)}, u32[]{:S(2)}, u32[]{:S(2)}) collective-permute-start(bf16[48,2048]{1,0:T(8,128)(2,1)} %get-tuple-element.84), channel_id=1, source_target_pairs={{0,8},{8,0},{64,72},{72,64},{128,136},{136,128},{192,200},{200,192... | collective-permute-start | bytes 589832 | tf_op jit(solution)/shard_map/ppermute | solution.py:33
  293.5 39.3 %collective-permute-start.11 = (bf16[48,2048]{1,0:T(8,128)(2,1)}, bf16[48,2048]{1,0:T(8,128)(2,1)S(1)}, u32[]{:S(2)}, u32[]{:S(2)}) collective-permute-start(bf16[48,2048]{1,0:T(8,128)(2,1)} %get-tuple-element.83), channel_id=1, source_target_pairs={{0,64},{8,72},{64,128},{72,136},{128,192},{136,200},{192,0},{200,8... | collective-permute-start | bytes 589832 | tf_op jit(solution)/shard_map/ppermute | solution.py:33
  297.4 35.5 %collective-permute-start.12 = (bf16[48,2048]{1,0:T(8,128)(2,1)}, bf16[48,2048]{1,0:T(8,128)(2,1)S(1)}, u32[]{:S(2)}, u32[]{:S(2)}) collective-permute-start(bf16[48,2048]{1,0:T(8,128)(2,1)} %get-tuple-element.82), channel_id=1, source_target_pairs={{0,72},{8,64},{64,136},{72,128},{128,200},{136,192},{192,8},{200,0... | collective-permute-start | bytes 589832 | tf_op jit(solution)/shard_map/ppermute | solution.py:33
  298.4 34.5 %collective-permute-start.13 = (bf16[48,2048]{1,0:T(8,128)(2,1)}, bf16[48,2048]{1,0:T(8,128)(2,1)S(1)}, u32[]{:S(2)}, u32[]{:S(2)}) collective-permute-start(bf16[48,2048]{1,0:T(8,128)(2,1)} %get-tuple-element.81), channel_id=1, source_target_pairs={{0,128},{8,136},{64,192},{72,200},{128,0},{136,8},{192,64},{200,72... | collective-permute-start | bytes 589832 | tf_op jit(solution)/shard_map/ppermute | solution.py:33
  299.2 34.3 %collective-permute-start.14 = (bf16[48,2048]{1,0:T(8,128)(2,1)}, bf16[48,2048]{1,0:T(8,128)(2,1)S(1)}, u32[]{:S(2)}, u32[]{:S(2)}) collective-permute-start(bf16[48,2048]{1,0:T(8,128)(2,1)} %get-tuple-element.80), channel_id=1, source_target_pairs={{0,136},{8,128},{64,200},{72,192},{128,8},{136,0},{192,72},{200,64... | collective-permute-start | bytes 589832 | tf_op jit(solution)/shard_map/ppermute | solution.py:33
  332.8 108.6 %collective-permute-start.48 = (bf16[48,2048]{1,0:T(8,128)(2,1)S(1)}, bf16[48,2048]{1,0:T(8,128)(2,1)S(1)}, u32[]{:S(2)}, u32[]{:S(2)}) collective-permute-start(bf16[48,2048]{1,0:T(8,128)(2,1)S(1)} %get-tuple-element.48), channel_id=1, source_target_pairs={{0,8},{8,0},{64,72},{72,64},{128,136},{136,128},{192,200},{200,192... | collective-permute-start | bytes 589832 | tf_op jit(solution)/shard_map/ppermute | solution.py:33
  332.8 109.9 %collective-permute-start.49 = (bf16[48,2048]{1,0:T(8,128)(2,1)S(1)}, bf16[48,2048]{1,0:T(8,128)(2,1)S(1)}, u32[]{:S(2)}, u32[]{:S(2)}) collective-permute-start(bf16[48,2048]{1,0:T(8,128)(2,1)S(1)} %get-tuple-element.49), channel_id=1, source_target_pairs={{0,192},{8,200},{64,0},{72,8},{128,64},{136,72},{192,128},{200,136... | collective-permute-start | bytes 589832 | tf_op jit(solution)/shard_map/ppermute | solution.py:33
  332.9 111.1 %collective-permute-start.50 = (bf16[48,2048]{1,0:T(8,128)(2,1)S(1)}, bf16[48,2048]{1,0:T(8,128)(2,1)S(1)}, u32[]{:S(2)}, u32[]{:S(2)}) collective-permute-start(bf16[48,2048]{1,0:T(8,128)(2,1)S(1)} %get-tuple-element.50), channel_id=1, source_target_pairs={{0,200},{8,192},{64,8},{72,0},{128,72},{136,64},{192,136},{200,128... | collective-permute-start | bytes 589832 | tf_op jit(solution)/shard_map/ppermute | solution.py:33
  333.5 110.9 %collective-permute-start.51 = (bf16[48,2048]{1,0:T(8,128)(2,1)S(1)}, bf16[48,2048]{1,0:T(8,128)(2,1)S(1)}, u32[]{:S(2)}, u32[]{:S(2)}) collective-permute-start(bf16[48,2048]{1,0:T(8,128)(2,1)S(1)} %get-tuple-element.51), channel_id=1, source_target_pairs={{0,128},{8,136},{64,192},{72,200},{128,0},{136,8},{192,64},{200,72... | collective-permute-start | bytes 589832 | tf_op jit(solution)/shard_map/ppermute | solution.py:33
  437.9 18.7 %collective-permute-start.52 = (bf16[48,2048]{1,0:T(8,128)(2,1)S(1)}, bf16[48,2048]{1,0:T(8,128)(2,1)S(1)}, u32[]{:S(2)}, u32[]{:S(2)}) collective-permute-start(bf16[48,2048]{1,0:T(8,128)(2,1)S(1)} %get-tuple-element.52), channel_id=1, source_target_pairs={{0,136},{8,128},{64,200},{72,192},{128,8},{136,0},{192,72},{200,64... | collective-permute-start | bytes 589832 | tf_op jit(solution)/shard_map/ppermute | solution.py:33
  442.8 29.0 %collective-permute-start.54 = (bf16[48,2048]{1,0:T(8,128)(2,1)S(1)}, bf16[48,2048]{1,0:T(8,128)(2,1)S(1)}, u32[]{:S(2)}, u32[]{:S(2)}) collective-permute-start(bf16[48,2048]{1,0:T(8,128)(2,1)S(1)} %get-tuple-element.54), channel_id=1, source_target_pairs={{0,72},{8,64},{64,136},{72,128},{128,200},{136,192},{192,8},{200,0... | collective-permute-start | bytes 589832 | tf_op jit(solution)/shard_map/ppermute | solution.py:33
  (89 other events, 1127.0 us)
Sparse Core Ops, SparseCore 0:
  9.8 30.5 all-gather.10
  42.3 29.1 all-gather.12
  73.3 29.1 all-gather.14
  144.9 29.0 all-gather.16
  201.7 26.8 all-gather.18
  253.9 27.8 all-gather.20

commit v2 on v0

v2 whole, which is shorter than its diff:
```python
import functools

import jax
import jax.numpy as jnp
from jax import lax
from jax.experimental import pallas as pl
from jax.experimental.pallas import tpu as pltpu
from jax.sharding import Mesh
from jax.sharding import PartitionSpec as P

EXPERT = ("x", "zh", "c")
DP = ("y", "zl")
Z = ("zh", "zl")
EXPERT_DP = EXPERT + DP
MOST = 16
NX, NZH, NC, NY, NZL = 4, 4, 2, 4, 2
NZ = NZH * NZL
PLACES = NX * NC
ROWS, TOP, WIDTH, HIDDEN = 96, 8, 2048, 768
META = 8
SHARD, DSHARD = 256, 96
PACK = 384
HALF = PACK // 2
SIDE = 2 * HIDDEN
BF = jnp.bfloat16
F32 = jnp.float32
GROUPS = ((0, -1, 1), (-2, 2), (-3, 3, 4))
VMEM = pl.BlockSpec(memory_space=pltpu.VMEM)
SMEM = pl.BlockSpec(memory_space=pltpu.SMEM)
ANY = pl.BlockSpec(memory_space=pl.ANY)
LIMIT = 48 << 20


def shift(value, axes, count, step):
    return lax.ppermute(value, axes, [(i, (i + step) % count) for i in range(count)])


def along_z(value, step):
    return shift(value, Z, NZ, step)


def along_y(value, step):
    return shift(value, "y", NY, step)


def flip(value, axis):
    return lax.ppermute(value, axis, [(0, 1), (1, 0)])


def across(value, axis):
    return lax.all_to_all(value, axis, split_axis=0, concat_axis=0, tiled=True)


def fence(*values):
    return lax.optimization_barrier(values)


def call(kernel, outs, in_specs, out_specs, name, scratch=(), cost=None):
    return pl.pallas_call(
        kernel,
        out_shape=outs,
        in_specs=in_specs,
        out_specs=out_specs,
        scratch_shapes=scratch,
        compiler_params=pltpu.CompilerParams(vmem_limit_bytes=LIMIT),
        cost_estimate=cost,
        name=name,
    )


def shape(*dims, dtype=BF):
    return jax.ShapeDtypeStruct(dims, dtype)


def prep_kernel(tokens_ref, gain_ref, ids_ref, weights_ref, out_ref):
    values = tokens_ref[...].astype(F32)
    scale = lax.rsqrt(jnp.mean(values * values, axis=-1, keepdims=True) + 1e-06)
    out_ref[pl.ds(0, ROWS), :] = (values * scale * gain_ref[...]).astype(BF)
    out_ref[pl.ds(ROWS, META), 0:128] = ids_ref[...].astype(F32).astype(BF)
    out_ref[pl.ds(ROWS, META), 128:256] = weights_ref[...].astype(BF)
    out_ref[pl.ds(ROWS, META), 256:WIDTH] = jnp.zeros((META, WIDTH - 256), BF)


def pack_kernel(place_ref, gate_ref, up_ref, down_ref, own_ref, other_ref, first_ref):
    zl = place_ref[3]
    for out_ref, e in ((own_ref, zl), (other_ref, 1 - zl), (first_ref, 0)):
        out_ref[0:SHARD, 0:HIDDEN] = gate_ref[e]
        out_ref[0:SHARD, HIDDEN:SIDE] = up_ref[e]
        out_ref[SHARD : SHARD + DSHARD, :] = down_ref[e, :, 0:SIDE]
        for j in range(3):
            out_ref[SHARD + DSHARD : PACK, 512 * j : 512 * (j + 1)] = down_ref[
                e, 32 * j : 32 * (j + 1), SIDE:WIDTH
            ]


def unpack_kernel(kind_ref, z_ref, x_ref, c_ref, gate_ref, up_ref, down_ref):
    for kind, ref in enumerate((z_ref, x_ref, c_ref)):

        @pl.when(kind_ref[0] == kind)
        def _(ref=ref):
            gate_ref[...] = ref[0:SHARD, 0:HIDDEN]
            up_ref[...] = ref[0:SHARD, HIDDEN:SIDE]
            down_ref[:, 0:SIDE] = ref[SHARD : SHARD + DSHARD, :]
            for j in range(3):
                down_ref[32 * j : 32 * (j + 1), SIDE:WIDTH] = ref[
                    SHARD + DSHARD : PACK, 512 * j : 512 * (j + 1)
                ]


def dispatch_kernel(n, place_ref, *refs):
    sources, (same_ref, other_ref, weight_ref) = refs[:n], refs[n:]
    x_me, zh, c, zl = (place_ref[k] for k in range(4))
    before = lax.broadcasted_iota(jnp.int32, (128, 128), 0)
    after = lax.broadcasted_iota(jnp.int32, (128, 128), 1)
    upto = (before <= after).astype(F32).astype(BF)
    slot = (before & (MOST - 1)).astype(F32)
    for i, ref in enumerate(sources):
        ids = ref[ROWS : ROWS + META, 0:128].astype(F32)
        route = ref[ROWS : ROWS + META, 128:256].astype(F32)
        chosen, factor = [], []
        for dc in range(NC):
            for x in range(NX):
                expert = ((x * NZH + zh) * NC + (c ^ dc)) * NZL + zl
                named = jnp.where(ids == expert.astype(F32), 1.0, 0.0)
                chosen.append(jnp.sum(named, axis=0, keepdims=True))
                factor.append(jnp.sum(named * route, axis=0, keepdims=True))
        chosen = jnp.concatenate(chosen, axis=0)
        factor = jnp.concatenate(factor, axis=0)
        ranks = jnp.dot(chosen.astype(BF), upto, preferred_element_type=F32) - 1.0
        ranks = jnp.where(chosen > 0.0, ranks, -1.0)

        def spread(v):
            return jnp.broadcast_to(v[:, None, :], (PLACES, MOST, 128)).reshape(128, 128)

        taken = spread(ranks) == slot
        placing = jnp.where(taken, 1.0, 0.0).astype(BF)
        rows = jnp.dot(placing[:, 0:ROWS], ref[0:ROWS, :], preferred_element_type=F32).astype(BF)
        for x in range(NX):
            at = x * n * MOST + i * MOST
            same_ref[at : at + MOST, :] = rows[x * MOST : (x + 1) * MOST]
            far = (NX + x) * MOST
            other_ref[at : at + MOST, :] = rows[far : far + MOST]
        weight_ref[i] = jnp.where(taken, spread(factor), 0.0).T.astype(BF)


def dispatch(place, sources):
    n = len(sources)
    rows = NX * n * MOST
    return call(
        functools.partial(dispatch_kernel, n),
        [shape(rows, WIDTH), shape(rows, WIDTH), shape(n, 128, 128)],
        [SMEM] + [VMEM] * n,
        [VMEM] * 3,
        "dispatch",
    )(place, *sources)


def ffn_kernel(splits, block, place_ref, *refs):
    pieces, refs = refs[:10], refs[10:]
    n = len(splits)
    row_refs, out_refs = refs[:n], refs[n : 2 * n]
    side_v, down_v, rows_v, res_v, sem_w, sem_r, sem_o = refs[2 * n :]
    zl, y_me = place_ref[3], place_ref[4]
    loads, starts, at = [], [], 0

    def load(src, dst):
        cp = pltpu.make_async_copy(src, dst, sem_w.at[len(loads)])
        cp.start()
        loads.append(cp)

    def down_parts(src, at, base):
        load(src.at[pl.ds(at, DSHARD)], down_v.at[pl.ds(base, DSHARD), 0:SIDE])
        for j in range(3):
            load(
                src.at[pl.ds(at + DSHARD, 32), 512 * j : 512 * (j + 1)],
                down_v.at[pl.ds(base + 32 * j, 32), SIDE:WIDTH],
            )

    gets = []
    for i, rows in enumerate(splits):
        starts.append(at)
        cp = pltpu.make_async_copy(row_refs[i], rows_v.at[pl.ds(at, rows)], sem_r.at[i])
        cp.start()
        gets.append(cp)
        at += rows
    total = at
    for half in range(2):
        from_zl = zl if half == 0 else 1 - zl
        full, (top, low) = pieces[5 * half : 5 * half + 3], pieces[5 * half + 3 : 5 * half + 5]
        for step, src in zip((0, NY - 1, 1), full):
            holder = ((y_me + step) & (NY - 1)) * NZL + from_zl
            base = pl.multiple_of(holder * SHARD, SHARD)
            load(src.at[pl.ds(0, SHARD)], side_v.at[pl.ds(base, SHARD)])
            down_parts(src, SHARD, pl.multiple_of(holder * DSHARD, DSHARD))
        holder = ((y_me + 2) & (NY - 1)) * NZL + from_zl
        base = pl.multiple_of(holder * SHARD, SHARD)
        load(top, side_v.at[pl.ds(base, HALF)])
        load(low.at[pl.ds(0, SHARD - HALF)], side_v.at[pl.ds(base + HALF, SHARD - HALF)])
        down_parts(low, SHARD - HALF, pl.multiple_of(holder * DSHARD, DSHARD))
    for cp in gets:
        cp.wait()
    for cp in loads:
        cp.wait()

    @pl.loop(0, total // block)
    def _(step):
        at = pl.multiple_of(step * block, block)
        both = jnp.dot(rows_v[pl.ds(at, block), :], side_v[...], preferred_element_type=F32)
        gate, up = both[:, 0:HIDDEN], both[:, HIDDEN:SIDE]
        hidden = (gate / (1.0 + jnp.exp(-gate)) * up).astype(BF)
        res_v[pl.ds(at, block), :] = jnp.dot(
            hidden, down_v[...], preferred_element_type=F32
        ).astype(BF)

    puts = []
    for i, rows in enumerate(splits):
        cp = pltpu.make_async_copy(res_v.at[pl.ds(starts[i], rows)], out_refs[i], sem_o.at[i])
        cp.start()
        puts.append(cp)
    for cp in puts:
        cp.wait()


def ffn(place, pieces, rows, block):
    splits = tuple(r.shape[0] for r in rows)
    total = sum(splits)
    return call(
        functools.partial(ffn_kernel, splits, block),
        [shape(s, WIDTH) for s in splits],
        [SMEM] + [ANY] * (10 + len(rows)),
        [ANY] * len(rows),
        "expert_ffn",
        scratch=[
            pltpu.VMEM((WIDTH, SIDE), BF),
            pltpu.VMEM((HIDDEN, WIDTH), BF),
            pltpu.VMEM((total, WIDTH), BF),
            pltpu.VMEM((total, WIDTH), BF),
            pltpu.SemaphoreType.DMA((2 * (3 * 5 + 2 + 4),)),
            pltpu.SemaphoreType.DMA((len(rows),)),
            pltpu.SemaphoreType.DMA((len(rows),)),
        ],
        cost=pl.CostEstimate(
            flops=6 * total * WIDTH * HIDDEN,
            transcendentals=total * HIDDEN,
            bytes_accessed=10 * WIDTH * HIDDEN,
        ),
    )(place, *pieces, *rows)


def combine_kernel(n, weight_ref, same_ref, other_ref, *outs):
    for i, out_ref in enumerate(outs):
        rows = []
        for ref in (same_ref, other_ref):
            for x in range(NX):
                at = x * n * MOST + i * MOST
                rows.append(ref[at : at + MOST, :])
        stack = jnp.concatenate(rows, axis=0)
        out_ref[...] = jnp.dot(
            weight_ref[i, 0:ROWS, :], stack, preferred_element_type=F32
        ).astype(out_ref.dtype)


def combine(weight, same, other, dtypes):
    n = len(dtypes)
    return call(
        functools.partial(combine_kernel, n),
        [shape(ROWS, WIDTH, dtype=t) for t in dtypes],
        [VMEM] * 3,
        [VMEM] * n,
        "combine",
    )(weight, same, other)


def spread_pieces(value):
    return value.reshape(NX, PACK // NX, SIDE)


def body(
    tokens, norm_gain, expert_ids, route_weights, gate_weight, up_weight, down_weight, pair_list
):
    x_me, zh_me, c_me = (lax.axis_index(a) for a in EXPERT)
    zl_me, y_me = lax.axis_index("zl"), lax.axis_index("y")
    place = jnp.stack([x_me, zh_me, c_me, zl_me, y_me]).astype(jnp.int32)

    ids = jnp.pad(expert_ids.T, ((0, 0), (0, 128 - ROWS)), constant_values=-1)
    route = jnp.pad(route_weights.T, ((0, 0), (0, 128 - ROWS)))
    near = call(prep_kernel, shape(ROWS + META, WIDTH), [VMEM] * 4, VMEM, "prep")(
        tokens, norm_gain[None, :], ids, route
    )
    own, other, first = call(
        pack_kernel, [shape(PACK, SIDE)] * 3, [SMEM] + [VMEM] * 3, [VMEM] * 3, "pack"
    )(place, gate_weight, up_weight, down_weight)

    p1, m1 = along_z(near, 1), along_z(near, -1)
    yp, ym = along_y(own, 1), along_y(own, -1)
    swapped = flip(other, "zl")
    s0, o0, w0 = dispatch(place, (near, p1, m1))
    p2, m2 = along_z(p1, 1), along_z(m1, -1)
    o0, s0 = across(o0.reshape(NX, -1, WIDTH), "x"), across(s0.reshape(NX, -1, WIDTH), "x")
    yt, yl = along_y(yp[:HALF], 1), along_y(ym[HALF:], -1)
    hx = across(spread_pieces(first), "x")
    p2, m2, yp, ym, yt, yl, swapped, o0, s0, hx, first = fence(
        p2, m2, yp, ym, yt, yl, swapped, o0, s0, hx, first
    )

    p3, m3 = along_z(p2, 1), along_z(m2, -1)
    vp, vm = along_y(swapped, 1), along_y(swapped, -1)
    o0 = flip(o0, "c")
    s1, o1, w1 = dispatch(place, (p2, m2))
    far = along_z(p3, 1)
    o1, s1 = across(o1.reshape(NX, -1, WIDTH), "x"), across(s1.reshape(NX, -1, WIDTH), "x")
    vt, vl = along_y(vp[:HALF], 1), along_y(vm[HALF:], -1)
    s2, o2, w2 = dispatch(place, (p3, m3, far))
    o2, s2, o1, s1 = fence(o2, s2, o1, s1)
    o2, s2 = across(o2.reshape(NX, -1, WIDTH), "x"), across(s2.reshape(NX, -1, WIDTH), "x")
    o1 = flip(o1, "c")
    o2 = flip(o2, "c")
    o0, s0, o1, s1, o2, s2, vp, vm, vt, vl, hx, first = fence(
        o0, s0, o1, s1, o2, s2, vp, vm, vt, vl, hx, first
    )

    holders = jnp.arange(NX, dtype=jnp.int32)
    x_from = pair_list[(holders * NZH + zh_me) * NC + c_me] >> 3
    z_from = (pair_list[(x_me * NZH + holders) * NC + c_me] >> 1) & (NZH - 1)
    me = (x_me * NZH + zh_me) * NC + c_me
    bits = jnp.sum(jnp.where(jnp.arange(pair_list.shape[0]) == me, pair_list ^ me, 0))
    kind = jnp.where(bits == 1, 2, jnp.where(bits >= 8, 1, 0)).astype(jnp.int32).reshape(1)
    hc = flip(first, "c")
    hz = across(spread_pieces(first), "zh")
    hx = across(jnp.take(hx, x_from, axis=0, mode="clip"), "x").reshape(PACK, SIDE)
    hz = across(jnp.take(hz, z_from, axis=0, mode="clip"), "zh").reshape(PACK, SIDE)
    new = call(
        unpack_kernel,
        [shape(SHARD, HIDDEN), shape(SHARD, HIDDEN), shape(DSHARD, WIDTH)],
        [SMEM] + [VMEM] * 3,
        [VMEM] * 3,
        "unpack",
    )(kind, hz, hx, hc)

    pieces = (own, yp, ym, yt, yl, swapped, vp, vm, vt, vl)

    def flat(v):
        return v.reshape(-1, WIDTH)

    def blocks(v):
        return v.reshape(NX, -1, WIDTH)

    s2, o2 = ffn(place, pieces, (flat(s2), flat(o2)), 384)
    o2, s2, o1, s1, o0, s0 = fence(o2, s2, o1, s1, o0, s0)
    s1, o1, s0, o0 = ffn(place, pieces, (flat(s1), flat(o1), flat(s0), flat(o0)), 320)
    o2 = across(blocks(flip(o2, "c")), "x")
    s2 = across(blocks(s2), "x")
    o1, o0 = flip(o1, "c"), flip(o0, "c")
    o2, s2, o1, s1 = fence(o2, s2, o1, s1)
    c_m3, c_p3, c_4 = combine(w2, flat(s2), flat(o2), (F32, BF, BF))
    o1, s1 = across(blocks(o1), "x"), across(blocks(s1), "x")
    o1, s1, o0, s0 = fence(o1, s1, o0, s0)
    c_m2, c_p2 = combine(w1, flat(s1), flat(o1), (F32, F32))
    o0, s0 = across(blocks(o0), "x"), across(blocks(s0), "x")
    c_0, c_m1, c_p1 = combine(w0, flat(s0), flat(o0), (F32, F32, F32))

    def joined(got, mine):
        return (got.astype(F32) + mine).astype(BF)

    down = along_z(c_4, -1)
    down = along_z(joined(down, c_m3), -1)
    rise = along_z(c_p3, 1)
    down = along_z(joined(down, c_m2), -1)
    rise = along_z(joined(rise, c_p2), 1)
    down = along_z(joined(down, c_m1), -1)
    rise = along_z(joined(rise, c_p1), 1)
    mixed = (down.astype(F32) + rise.astype(F32) + c_0).astype(BF)
    return (mixed, *(v[None] for v in new))


def solution(mesh):
    split = Mesh(mesh.devices.reshape(NX, NZH, NC, NY, NZL), EXPERT_DP)
    rows = P(EXPERT_DP, None)
    blocks = P(EXPERT, DP, None)
    return jax.shard_map(
        body,
        mesh=split,
        in_specs=(rows, P(), rows, rows, blocks, blocks, blocks, P()),
        out_specs=(rows, blocks, blocks, blocks),
        check_vma=False,
    )
```

time: 631 us -> 343 us (0.54)
  waiting for transfers between devices: 505 us -> 109 us
  starting transfers between devices: 35.1 us -> 109 us
  blocking collectives: 4.68 us -> 39.7 us
  Pallas kernels: 0 us -> 33.9 us
  matrix products: 28.8 us -> 0 us
  between operations: 14.1 us -> 2.21 us
    all_gather x3 -> x0, waiting for transfers between devices: 244 us -> none  [the longest x1 187 us: side_by_side(): lax.all_gather(both, axis, axis=dim, tiled=True)]
    all_to_all x4 -> x13, waiting for transfers between devices: 260 us -> 38.5 us  [across(): return lax.all_to_all(value, axis, split_axis=0, concat_axis=0, tiled=True)]
    ppermute x0 -> x30, waiting for transfers between devices: none -> 70.8 us  [the longest x22 64.4 us: shift(): lax.ppermute(value, axes, [(i, (i + step) % count) for i in range(count)])]
    ppermute x0 -> x30, starting transfers between devices: none -> 40.2 us  [the longest x22 40.1 us: shift(): lax.ppermute(value, axes, [(i, (i + step) % count) for i in range(count)])]
    all_to_all x1 -> x3, blocking collectives: 4.68 us -> 39.7 us  [across(): return lax.all_to_all(value, axis, split_axis=0, concat_axis=0, tiled=True)]
    all_to_all x4 -> x13, starting transfers between devices: 35 us -> 69.1 us  [across(): return lax.all_to_all(value, axis, split_axis=0, concat_axis=0, tiled=True)]
    pallas_call x0 -> x11, Pallas kernels: none -> 33.9 us  [the longest x2 20 us: ffn(): call(functools.partial(ffn_kernel, splits, block), [shape(s, WIDTH) for s...]
    dot_general x5 -> x0, matrix products: 28.8 us -> none  [the longest x1 7.59 us: body(): jnp.einsum('semf,efd->semd', columns, gathered_by_axis(down_weight, DP, 1...]
  transfers between devices with their start and end apart: 7 -> 43, of which waited for: 5 -> 18; matrix products, arithmetic and copies ran while one was open for 10% -> 8% of each run, Pallas kernels for 0% -> 6%
where the time goes in v2:
time: 343 us; the launch traced here: 337 us
  starting transfers between devices  109 us (32%)
  waiting for transfers between devices  109 us (32%)
  blocking collectives  39.7 us (12%)
  Pallas kernels  33.9 us (10%)
  local copies, waits for them, and re-layouts  29.7 us (9%)
  other arithmetic  12.4 us (4%)
    all_to_all x13, starting transfers between devices, across(): return lax.all_to_all(value, axis, split_axis=0, concat_axis=0, tiled=True)  69.1 us
    ppermute x22, waiting for transfers between devices, shift(): lax.ppermute(value, axes, [(i, (i + step) % count) for i in range(count)])  64.4 us
    ppermute x22, starting transfers between devices, shift(): lax.ppermute(value, axes, [(i, (i + step) % count) for i in range(count)])  40.1 us
    all_to_all x3, blocking collectives, across(): return lax.all_to_all(value, axis, split_axis=0, concat_axis=0, tiled=True)  39.7 us
    all_to_all x13, waiting for transfers between devices, across(): return lax.all_to_all(value, axis, split_axis=0, concat_axis=0, tiled=True)  38.5 us
    pallas_call x2, Pallas kernels, ffn(): call(functools.partial(ffn_kernel, splits, block), [shape(s, WIDTH) for s...  20 us
    unnamed x68, local copies, waits for them, and re-layouts  15.6 us
    convert_element_type x5, other arithmetic, joined(): return (got.astype(F32) + mine).astype(BF)  9.78 us
  transfers between devices with their start and end apart: 43, of which 18 were waited for; matrix products, arithmetic and copies ran while one was open for 8% of the time, Pallas kernels for 6%

profile of v2, /device:TPU:22, one launch (start us, length us, event | category | flops | bytes accessed | tf_op | source)
XLA Modules:
  0.0 336.6 jit_solution(9488069983089143796)
XLA Ops:
  6.9 4.9 %all-to-all-start.2 = ((bf16[4,96,1536]{2,1,0:T(8,128)(2,1)}), bf16[4,96,1536]{2,1,0:T(8,128)(2,1)}, u32[]{:S(2)}, u32[]{:S(2)}) async-start(bf16[4,96,1536]{2,1,0:T(8,128)(2,1)} %bitcast.10), calls=%async_computation.2 | async-start | bytes 2359296 | tf_op jit(solution)/shard_map/all_to_all | solution.py:51
  16.1 4.0 %collective-permute-start.2 = (bf16[104,2048]{1,0:T(8,128)(2,1)S(1)}, bf16[104,2048]{1,0:T(8,128)(2,1)S(1)}, u32[]{:S(2)}, u32[]{:S(2)}) collective-permute-start(bf16[104,2048]{1,0:T(8,128)(2,1)S(1)} %prep.1.refs_0_), channel_id=1, source_target_pairs={{0,49},{1,0},{16,1},{17,16},{32,17},{33,32},{48,33},{49,48},{2,51}... | collective-permute-start | bytes 1277960 | tf_op jit(solution)/shard_map/ppermute | solution.py:35
  20.1 8.8 %collective-permute-done.refs_1_ = bf16[104,2048]{1,0:T(8,128)(2,1)S(1)} collective-permute-done((bf16[104,2048]{1,0:T(8,128)(2,1)S(1)}, bf16[104,2048]{1,0:T(8,128)(2,1)S(1)}, u32[]{:S(2)}, u32[]{:S(2)}) %collective-permute-start) | collective-permute-done | bytes 426016 | tf_op jit(solution)/shard_map/ppermute | solution.py:35
  31.6 4.8 %all-to-all-start = ((bf16[4,48,2048]{2,1,0:T(8,128)(2,1)}), bf16[4,48,2048]{2,1,0:T(8,128)(2,1)}, u32[]{:S(2)}, u32[]{:S(2)}) async-start(bf16[4,48,2048]{2,1,0:T(8,128)(2,1)} %bitcast.8), calls=%async_computation | async-start | bytes 1572864 | tf_op jit(solution)/shard_map/all_to_all | solution.py:51
  42.6 3.1 all-to-all-done
  45.7 6.2 %all-to-all-start.1 = ((bf16[4,48,2048]{2,1,0:T(8,128)(2,1)}), bf16[4,48,2048]{2,1,0:T(8,128)(2,1)}, u32[]{:S(2)}, u32[]{:S(2)}) async-start(bf16[4,48,2048]{2,1,0:T(8,128)(2,1)} %bitcast.9), calls=%async_computation.1 | async-start | bytes 1572864 | tf_op jit(solution)/shard_map/all_to_all | solution.py:51
  53.6 3.2 collective-permute-start.3
  56.8 12.9 %collective-permute-done.1.refs_0_ = bf16[104,2048]{1,0:T(8,128)(2,1)S(1)} collective-permute-done((bf16[104,2048]{1,0:T(8,128)(2,1)S(1)}, bf16[104,2048]{1,0:T(8,128)(2,1)S(1)}, u32[]{:S(2)}, u32[]{:S(2)}) %collective-permute-start.1) | collective-permute-done | bytes 426016 | tf_op jit(solution)/shard_map/ppermute | solution.py:35
  74.5 4.8 %all-to-all-start.3 = ((bf16[4,32,2048]{2,1,0:T(8,128)(2,1)}), bf16[4,32,2048]{2,1,0:T(8,128)(2,1)}, u32[]{:S(2)}, u32[]{:S(2)}) async-start(bf16[4,32,2048]{2,1,0:T(8,128)(2,1)} %bitcast.11), calls=%async_computation.3 | async-start | bytes 1048576 | tf_op jit(solution)/shard_map/all_to_all | solution.py:51
  79.3 2.9 collective-permute-start.10
  82.4 3.0 all-to-all-done.3
  85.4 5.5 %all-to-all-start.4 = ((bf16[4,32,2048]{2,1,0:T(8,128)(2,1)}), bf16[4,32,2048]{2,1,0:T(8,128)(2,1)S(1)}, u32[]{:S(2)}, u32[]{:S(2)}) async-start(bf16[4,32,2048]{2,1,0:T(8,128)(2,1)} %bitcast.12), calls=%async_computation.4 | async-start | bytes 1048576 | tf_op jit(solution)/shard_map/all_to_all | solution.py:51
  96.9 6.2 %all-to-all-start.5 = ((bf16[4,48,2048]{2,1,0:T(8,128)(2,1)}), bf16[4,48,2048]{2,1,0:T(8,128)(2,1)}, u32[]{:S(2)}, u32[]{:S(2)}) async-start(bf16[4,48,2048]{2,1,0:T(8,128)(2,1)} %bitcast.13), calls=%async_computation.5 | async-start | bytes 1572864 | tf_op jit(solution)/shard_map/all_to_all | solution.py:51
  103.2 7.5 %all-to-all-done.5 = bf16[4,48,2048]{2,1,0:T(8,128)(2,1)} async-done(((bf16[4,48,2048]{2,1,0:T(8,128)(2,1)}), bf16[4,48,2048]{2,1,0:T(8,128)(2,1)}, u32[]{:S(2)}, u32[]{:S(2)}) %all-to-all-start.5) | async-done | bytes 786464 | tf_op jit(solution)/shard_map/all_to_all | solution.py:51
  110.7 5.5 %all-to-all-start.6 = ((bf16[4,48,2048]{2,1,0:T(8,128)(2,1)}), bf16[4,48,2048]{2,1,0:T(8,128)(2,1)S(1)}, u32[]{:S(2)}, u32[]{:S(2)}) async-start(bf16[4,48,2048]{2,1,0:T(8,128)(2,1)} %bitcast.14), calls=%async_computation.6 | async-start | bytes 1572864 | tf_op jit(solution)/shard_map/all_to_all | solution.py:51
  127.4 6.4 %collective-permute-done.17.refs_8_ = bf16[192,1536]{1,0:T(8,128)(2,1)S(1)} collective-permute-done((bf16[192,1536]{1,0:T(8,128)(2,1)}, bf16[192,1536]{1,0:T(8,128)(2,1)S(1)}, u32[]{:S(2)}, u32[]{:S(2)}) %collective-permute-start.17) | collective-permute-done | bytes 589856 | tf_op jit(solution)/shard_map/ppermute | solution.py:35
  133.8 3.0 collective-permute-done.18.refs_9_
  136.9 8.4 %expert_ffn.2 = (bf16[192,2048]{1,0:T(8,128)(2,1)S(1)}, bf16[192,2048]{1,0:T(8,128)(2,1)S(1)}) custom-call(s32[5]{0:T(128)S(1)} %stack.23.place_ref, bf16[384,1536]{1,0:T(8,128)(2,1)} %copy-done.20, bf16[384,1536]{1,0:T(8,128)(2,1)} %collective-permute-done.4.refs_1_, bf16[384,1536]{1,0:T(8,128)(2,1)} %collective-permute-done.5.refs_2_, ...), custom_call_target="tpu_custom_call" | custom-call | flops 3623878656 | bytes 15728640 | tf_op jit(solution)/shard_map/expert_ffn/pallas_call | solution.py:227
  145.4 15.5 %all_to_all.80 = bf16[4,48,2048]{2,1,0:T(8,128)(2,1)S(1)} all-to-all(bf16[4,48,2048]{2,1,0:T(8,128)(2,1)S(1)} %bitcast.54), channel_id=1, replica_groups=mesh['x'=4,'zh'=4,'c'=2,'y'=4,'zl'=2] {'x'}, dimensions={0} | all-to-all | bytes 1572864 | tf_op jit(solution)/shard_map/all_to_all | solution.py:51
  161.8 5.5 %all-to-all-start.7 = ((bf16[4,48,2048]{2,1,0:T(8,128)(2,1)}), bf16[4,48,2048]{2,1,0:T(8,128)(2,1)S(1)}, u32[]{:S(2)}, u32[]{:S(2)}) async-start(bf16[4,48,2048]{2,1,0:T(8,128)(2,1)} %bitcast.60), calls=%async_computation.7 | async-start | bytes 1572864 | tf_op jit(solution)/shard_map/all_to_all | solution.py:51
  169.5 11.6 %expert_ffn.3 = (bf16[128,2048]{1,0:T(8,128)(2,1)S(1)}, bf16[128,2048]{1,0:T(8,128)(2,1)S(1)}, bf16[192,2048]{1,0:T(8,128)(2,1)S(1)}, bf16[192,2048]{1,0:T(8,128)(2,1)S(1)}) custom-call(s32[5]{0:T(128)S(1)} %stack.23.place_ref, bf16[384,1536]{1,0:T(8,128)(2,1)} %copy-done.20, bf16[384,1536]{1,0:T(8,128)(2,1)} %collective-permute-done.4.refs_1_, ...), custom_call_target="tpu_custom_call" | custom-call | flops 6039797760 | bytes 15728640 | tf_op jit(solution)/shard_map/expert_ffn/pallas_call | solution.py:227
  184.8 12.3 %all_to_all.81 = bf16[4,32,2048]{2,1,0:T(8,128)(2,1)S(1)} all-to-all(bf16[4,32,2048]{2,1,0:T(8,128)(2,1)S(1)} %bitcast.56), channel_id=1, replica_groups=mesh['x'=4,'zh'=4,'c'=2,'y'=4,'zl'=2] {'x'}, dimensions={0} | all-to-all | bytes 1048576 | tf_op jit(solution)/shard_map/all_to_all | solution.py:51
  197.1 11.9 %all_to_all.82 = bf16[4,32,2048]{2,1,0:T(8,128)(2,1)} all-to-all(bf16[4,32,2048]{2,1,0:T(8,128)(2,1)S(1)} %bitcast.61), channel_id=1, replica_groups=mesh['x'=4,'zh'=4,'c'=2,'y'=4,'zl'=2] {'x'}, dimensions={0} | all-to-all | bytes 1048576 | tf_op jit(solution)/shard_map/all_to_all | solution.py:51
  209.0 6.1 %all-to-all-start.13 = ((bf16[4,96,1536]{2,1,0:T(8,128)(2,1)}), bf16[4,96,1536]{2,1,0:T(8,128)(2,1)}, u32[]{:S(2)}, u32[]{:S(2)}) async-start(bf16[4,96,1536]{2,1,0:T(8,128)(2,1)} %bitcast.34), calls=%async_computation.13 | async-start | bytes 2359296 | tf_op jit(solution)/shard_map/all_to_all | solution.py:51
  217.6 20.3 %all-to-all-done.13 = bf16[4,96,1536]{2,1,0:T(8,128)(2,1)} async-done(((bf16[4,96,1536]{2,1,0:T(8,128)(2,1)}), bf16[4,96,1536]{2,1,0:T(8,128)(2,1)}, u32[]{:S(2)}, u32[]{:S(2)}) %all-to-all-start.13) | async-done | bytes 1179680 | tf_op jit(solution)/shard_map/all_to_all | solution.py:51
  237.9 5.7 %all-to-all-start.11 = ((bf16[4,48,2048]{2,1,0:T(8,128)(2,1)}), bf16[4,48,2048]{2,1,0:T(8,128)(2,1)S(1)}, u32[]{:S(2)}, u32[]{:S(2)}) async-start(bf16[4,48,2048]{2,1,0:T(8,128)(2,1)} %bitcast.52), calls=%async_computation.11 | async-start | bytes 1572864 | tf_op jit(solution)/shard_map/all_to_all | solution.py:51
  247.0 5.1 %collective-permute-start.21 = (bf16[96,2048]{1,0:T(8,128)(2,1)}, bf16[96,2048]{1,0:T(8,128)(2,1)S(1)}, u32[]{:S(2)}, u32[]{:S(2)}) collective-permute-start(bf16[96,2048]{1,0:T(8,128)(2,1)} %get-tuple-element.121), channel_id=1, source_target_pairs={{0,49},{1,0},{16,1},{17,16},{32,17},{33,32},{48,33},{49,48},{2,51}... | collective-permute-start | bytes 1179656 | tf_op jit(solution)/shard_map/ppermute | solution.py:35
  252.2 4.8 %all-to-all-start.12 = ((bf16[4,48,2048]{2,1,0:T(8,128)(2,1)}), bf16[4,48,2048]{2,1,0:T(8,128)(2,1)S(1)}, u32[]{:S(2)}, u32[]{:S(2)}) async-start(bf16[4,48,2048]{2,1,0:T(8,128)(2,1)} %bitcast.31), calls=%async_computation.12 | async-start | bytes 1572864 | tf_op jit(solution)/shard_map/all_to_all | solution.py:51
  259.9 7.2 %collective-permute-start.26 = (bf16[96,2048]{1,0:T(8,128)(2,1)}, bf16[96,2048]{1,0:T(8,128)(2,1)}, u32[]{:S(2)}, u32[]{:S(2)}) collective-permute-start(bf16[96,2048]{1,0:T(8,128)(2,1)} %get-tuple-element.135), channel_id=1, source_target_pairs={{0,1},{1,16},{16,17},{17,32},{32,33},{33,48},{48,49},{49,0},{2,3},... | collective-permute-start | bytes 1179656 | tf_op jit(solution)/shard_map/ppermute | solution.py:35
  271.2 4.8 %all-to-all-start.15 = ((bf16[4,96,1536]{2,1,0:T(8,128)(2,1)}), bf16[4,96,1536]{2,1,0:T(8,128)(2,1)S(1)}, u32[]{:S(2)}, u32[]{:S(2)}) async-start(bf16[4,96,1536]{2,1,0:T(8,128)(2,1)} %gather_fusion.3), calls=%async_computation.15 | async-start | bytes 2359296 | tf_op jit(solution)/shard_map/all_to_all | solution.py:51
  290.8 4.1 %all-to-all-start.14 = ((bf16[4,96,1536]{2,1,0:T(8,128)(2,1)}), bf16[4,96,1536]{2,1,0:T(8,128)(2,1)S(1)}, u32[]{:S(2)}, u32[]{:S(2)}) async-start(bf16[4,96,1536]{2,1,0:T(8,128)(2,1)} %gather_fusion.1), calls=%async_computation.14 | async-start | bytes 2359296 | tf_op jit(solution)/shard_map/all_to_all | solution.py:51
  304.6 27.6 %collective-permute-done.28 = bf16[96,2048]{1,0:T(8,128)(2,1)} collective-permute-done((bf16[96,2048]{1,0:T(8,128)(2,1)}, bf16[96,2048]{1,0:T(8,128)(2,1)}, u32[]{:S(2)}, u32[]{:S(2)}) %collective-permute-start.28) | collective-permute-done | bytes 393248 | tf_op jit(solution)/shard_map/ppermute | solution.py:35
  (161 shorter events, 90.3 us)
Async XLA Ops:
  6.9 24.7 %all-to-all-start.2 = ((bf16[4,96,1536]{2,1,0:T(8,128)(2,1)}), bf16[4,96,1536]{2,1,0:T(8,128)(2,1)}, u32[]{:S(2)}, u32[]{:S(2)}) async-start(bf16[4,96,1536]{2,1,0:T(8,128)(2,1)} %bitcast.10), calls=%async_computation.2 | async-start | bytes 2359296 | tf_op jit(solution)/shard_map/all_to_all | solution.py:51
  11.9 27.5 %collective-permute-start.4 = (bf16[384,1536]{1,0:T(8,128)(2,1)S(1)}, bf16[384,1536]{1,0:T(8,128)(2,1)}, u32[]{:S(2)}, u32[]{:S(2)}) collective-permute-start(bf16[384,1536]{1,0:T(8,128)(2,1)S(1)} %get-tuple-element.74.refs_0_), channel_id=1, source_target_pairs={{0,2},{2,4},{4,6},{6,0},{1,3},{3,5},{5,7},{7,1},{8,10},{10,12},{12... | collective-permute-start | bytes 3538952 | tf_op jit(solution)/shard_map/ppermute | solution.py:35
  13.1 38.8 %collective-permute-start.5 = (bf16[384,1536]{1,0:T(8,128)(2,1)S(1)}, bf16[384,1536]{1,0:T(8,128)(2,1)}, u32[]{:S(2)}, u32[]{:S(2)}) collective-permute-start(bf16[384,1536]{1,0:T(8,128)(2,1)S(1)} %get-tuple-element.74.refs_0_), channel_id=1, source_target_pairs={{0,6},{2,0},{4,2},{6,4},{1,7},{3,1},{5,3},{7,5},{8,14},{10,8},{12,... | collective-permute-start | bytes 3538952 | tf_op jit(solution)/shard_map/ppermute | solution.py:35
  14.1 14.9 %collective-permute-start = (bf16[104,2048]{1,0:T(8,128)(2,1)S(1)}, bf16[104,2048]{1,0:T(8,128)(2,1)S(1)}, u32[]{:S(2)}, u32[]{:S(2)}) collective-permute-start(bf16[104,2048]{1,0:T(8,128)(2,1)S(1)} %prep.1.refs_0_), channel_id=1, source_target_pairs={{0,1},{1,16},{16,17},{17,32},{32,33},{33,48},{48,49},{49,0},{2,3},... | collective-permute-start | bytes 1277960 | tf_op jit(solution)/shard_map/ppermute | solution.py:35
  31.6 14.1 %all-to-all-start = ((bf16[4,48,2048]{2,1,0:T(8,128)(2,1)}), bf16[4,48,2048]{2,1,0:T(8,128)(2,1)}, u32[]{:S(2)}, u32[]{:S(2)}) async-start(bf16[4,48,2048]{2,1,0:T(8,128)(2,1)} %bitcast.8), calls=%async_computation | async-start | bytes 1572864 | tf_op jit(solution)/shard_map/all_to_all | solution.py:51
  36.4 35.4 %collective-permute-start.8 = (bf16[384,1536]{1,0:T(8,128)(2,1)}, bf16[384,1536]{1,0:T(8,128)(2,1)}, u32[]{:S(2)}, u32[]{:S(2)}) collective-permute-start(bf16[384,1536]{1,0:T(8,128)(2,1)} %copy-done.21), channel_id=1, source_target_pairs={{0,1},{1,0},{2,3},{3,2},{4,5},{5,4},{6,7},{7,6},{8,9},{9,8},{10,11... | collective-permute-start | bytes 3538952 | tf_op jit(solution)/shard_map/ppermute | solution.py:47
  41.3 30.6 %collective-permute-start.6 = (bf16[192,1536]{1,0:T(8,128)(2,1)}, bf16[192,1536]{1,0:T(8,128)(2,1)}, u32[]{:S(2)}, u32[]{:S(2)}) collective-permute-start(bf16[192,1536]{1,0:T(8,128)(2,1)} %slice.24), channel_id=1, source_target_pairs={{0,2},{2,4},{4,6},{6,0},{1,3},{3,5},{5,7},{7,1},{8,10},{10,12},{12... | collective-permute-start | bytes 1769480 | tf_op jit(solution)/shard_map/ppermute | solution.py:35
  45.7 26.2 %all-to-all-start.1 = ((bf16[4,48,2048]{2,1,0:T(8,128)(2,1)}), bf16[4,48,2048]{2,1,0:T(8,128)(2,1)}, u32[]{:S(2)}, u32[]{:S(2)}) async-start(bf16[4,48,2048]{2,1,0:T(8,128)(2,1)} %bitcast.9), calls=%async_computation.1 | async-start | bytes 1572864 | tf_op jit(solution)/shard_map/all_to_all | solution.py:51
  53.0 18.8 %collective-permute-start.7 = (bf16[192,1536]{1,0:T(8,128)(2,1)S(1)}, bf16[192,1536]{1,0:T(8,128)(2,1)S(1)}, u32[]{:S(2)}, u32[]{:S(2)}) collective-permute-start(bf16[192,1536]{1,0:T(8,128)(2,1)S(1)} %slice.25), channel_id=1, source_target_pairs={{0,6},{2,0},{4,2},{6,4},{1,7},{3,1},{5,3},{7,5},{8,14},{10,8},{12,... | collective-permute-start | bytes 1769480 | tf_op jit(solution)/shard_map/ppermute | solution.py:35
  53.6 16.1 %collective-permute-start.1 = (bf16[104,2048]{1,0:T(8,128)(2,1)S(1)}, bf16[104,2048]{1,0:T(8,128)(2,1)S(1)}, u32[]{:S(2)}, u32[]{:S(2)}) collective-permute-start(bf16[104,2048]{1,0:T(8,128)(2,1)S(1)} %collective-permute-done.refs_1_), channel_id=1, source_target_pairs={{0,1},{1,16},{16,17},{17,32},{32,33},{33,48},{48,49},{49,0},{2,3},... | collective-permute-start | bytes 1277960 | tf_op jit(solution)/shard_map/ppermute | solution.py:35
  53.6 18.3 %collective-permute-start.3 = (bf16[104,2048]{1,0:T(8,128)(2,1)S(1)}, bf16[104,2048]{1,0:T(8,128)(2,1)S(1)}, u32[]{:S(2)}, u32[]{:S(2)}) collective-permute-start(bf16[104,2048]{1,0:T(8,128)(2,1)S(1)} %collective-permute-done.2.refs_2_), channel_id=1, source_target_pairs={{0,49},{1,0},{16,1},{17,16},{32,17},{33,32},{48,33},{49,48},{2,51}... | collective-permute-start | bytes 1277960 | tf_op jit(solution)/shard_map/ppermute | solution.py:35
  90.9 25.3 %collective-permute-start.15 = (bf16[384,1536]{1,0:T(8,128)(2,1)}, bf16[384,1536]{1,0:T(8,128)(2,1)}, u32[]{:S(2)}, u32[]{:S(2)}) collective-permute-start(bf16[384,1536]{1,0:T(8,128)(2,1)} %collective-permute-done.8.refs_5_), channel_id=1, source_target_pairs={{0,2},{2,4},{4,6},{6,0},{1,3},{3,5},{5,7},{7,1},{8,10},{10,12},{12... | collective-permute-start | bytes 3538952 | tf_op jit(solution)/shard_map/ppermute | solution.py:35
  92.2 27.2 %collective-permute-start.16 = (bf16[384,1536]{1,0:T(8,128)(2,1)}, bf16[384,1536]{1,0:T(8,128)(2,1)}, u32[]{:S(2)}, u32[]{:S(2)}) collective-permute-start(bf16[384,1536]{1,0:T(8,128)(2,1)} %collective-permute-done.8.refs_5_), channel_id=1, source_target_pairs={{0,6},{2,0},{4,2},{6,4},{1,7},{3,1},{5,3},{7,5},{8,14},{10,8},{12,... | collective-permute-start | bytes 3538952 | tf_op jit(solution)/shard_map/ppermute | solution.py:35
  103.1 19.0 %collective-permute-start.12 = (bf16[4,48,2048]{2,1,0:T(8,128)(2,1)}, bf16[4,48,2048]{2,1,0:T(8,128)(2,1)}, u32[]{:S(2)}, u32[]{:S(2)}) collective-permute-start(bf16[4,48,2048]{2,1,0:T(8,128)(2,1)} %all-to-all-done), channel_id=1, source_target_pairs={{0,8},{8,0},{1,9},{9,1},{2,10},{10,2},{3,11},{11,3},{4,12},{12,4},... | collective-permute-start | bytes 2359304 | tf_op jit(solution)/shard_map/ppermute | solution.py:47
  110.7 26.2 %collective-permute-start.14 = (bf16[4,48,2048]{2,1,0:T(8,128)(2,1)}, bf16[4,48,2048]{2,1,0:T(8,128)(2,1)S(1)}, u32[]{:S(2)}, u32[]{:S(2)}) collective-permute-start(bf16[4,48,2048]{2,1,0:T(8,128)(2,1)} %all-to-all-done.5), channel_id=1, source_target_pairs={{0,8},{8,0},{1,9},{9,1},{2,10},{10,2},{3,11},{11,3},{4,12},{12,4},... | collective-permute-start | bytes 2359304 | tf_op jit(solution)/shard_map/ppermute | solution.py:47
  110.7 16.7 %all-to-all-start.6 = ((bf16[4,48,2048]{2,1,0:T(8,128)(2,1)}), bf16[4,48,2048]{2,1,0:T(8,128)(2,1)S(1)}, u32[]{:S(2)}, u32[]{:S(2)}) async-start(bf16[4,48,2048]{2,1,0:T(8,128)(2,1)} %bitcast.14), calls=%async_computation.6 | async-start | bytes 1572864 | tf_op jit(solution)/shard_map/all_to_all | solution.py:51
  118.2 15.7 %collective-permute-start.17 = (bf16[192,1536]{1,0:T(8,128)(2,1)}, bf16[192,1536]{1,0:T(8,128)(2,1)S(1)}, u32[]{:S(2)}, u32[]{:S(2)}) collective-permute-start(bf16[192,1536]{1,0:T(8,128)(2,1)} %slice.26), channel_id=1, source_target_pairs={{0,2},{2,4},{4,6},{6,0},{1,3},{3,5},{5,7},{7,1},{8,10},{10,12},{12... | collective-permute-start | bytes 1769480 | tf_op jit(solution)/shard_map/ppermute | solution.py:35
  121.4 15.5 %collective-permute-start.18 = (bf16[192,1536]{1,0:T(8,128)(2,1)}, bf16[192,1536]{1,0:T(8,128)(2,1)}, u32[]{:S(2)}, u32[]{:S(2)}) collective-permute-start(bf16[192,1536]{1,0:T(8,128)(2,1)} %slice.27), channel_id=1, source_target_pairs={{0,6},{2,0},{4,2},{6,4},{1,7},{3,1},{5,3},{7,5},{8,14},{10,8},{12,... | collective-permute-start | bytes 1769480 | tf_op jit(solution)/shard_map/ppermute | solution.py:35
  145.3 15.6 %collective-permute-start.19 = (bf16[192,2048]{1,0:T(8,128)(2,1)S(1)}, bf16[192,2048]{1,0:T(8,128)(2,1)S(1)}, u32[]{:S(2)}, u32[]{:S(2)}) collective-permute-start(bf16[192,2048]{1,0:T(8,128)(2,1)S(1)} %get-tuple-element.111), channel_id=1, source_target_pairs={{0,8},{8,0},{1,9},{9,1},{2,10},{10,2},{3,11},{11,3},{4,12},{12,4},... | collective-permute-start | bytes 2359304 | tf_op jit(solution)/shard_map/ppermute | solution.py:47
  161.8 22.9 %all-to-all-start.7 = ((bf16[4,48,2048]{2,1,0:T(8,128)(2,1)}), bf16[4,48,2048]{2,1,0:T(8,128)(2,1)S(1)}, u32[]{:S(2)}, u32[]{:S(2)}) async-start(bf16[4,48,2048]{2,1,0:T(8,128)(2,1)} %bitcast.60), calls=%async_computation.7 | async-start | bytes 1572864 | tf_op jit(solution)/shard_map/all_to_all | solution.py:51
  209.0 28.9 %all-to-all-start.13 = ((bf16[4,96,1536]{2,1,0:T(8,128)(2,1)}), bf16[4,96,1536]{2,1,0:T(8,128)(2,1)}, u32[]{:S(2)}, u32[]{:S(2)}) async-start(bf16[4,96,1536]{2,1,0:T(8,128)(2,1)} %bitcast.34), calls=%async_computation.13 | async-start | bytes 2359296 | tf_op jit(solution)/shard_map/all_to_all | solution.py:51
  237.9 14.3 %all-to-all-start.11 = ((bf16[4,48,2048]{2,1,0:T(8,128)(2,1)}), bf16[4,48,2048]{2,1,0:T(8,128)(2,1)S(1)}, u32[]{:S(2)}, u32[]{:S(2)}) async-start(bf16[4,48,2048]{2,1,0:T(8,128)(2,1)} %bitcast.52), calls=%async_computation.11 | async-start | bytes 1572864 | tf_op jit(solution)/shard_map/all_to_all | solution.py:51
  247.0 20.1 %collective-permute-start.21 = (bf16[96,2048]{1,0:T(8,128)(2,1)}, bf16[96,2048]{1,0:T(8,128)(2,1)S(1)}, u32[]{:S(2)}, u32[]{:S(2)}) collective-permute-start(bf16[96,2048]{1,0:T(8,128)(2,1)} %get-tuple-element.121), channel_id=1, source_target_pairs={{0,49},{1,0},{16,1},{17,16},{32,17},{33,32},{48,33},{49,48},{2,51}... | collective-permute-start | bytes 1179656 | tf_op jit(solution)/shard_map/ppermute | solution.py:35
  252.2 19.0 %all-to-all-start.12 = ((bf16[4,48,2048]{2,1,0:T(8,128)(2,1)}), bf16[4,48,2048]{2,1,0:T(8,128)(2,1)S(1)}, u32[]{:S(2)}, u32[]{:S(2)}) async-start(bf16[4,48,2048]{2,1,0:T(8,128)(2,1)} %bitcast.31), calls=%async_computation.12 | async-start | bytes 1572864 | tf_op jit(solution)/shard_map/all_to_all | solution.py:51
  257.0 77.2 %collective-permute-start.29 = (bf16[384,1536]{1,0:T(8,128)(2,1)}, bf16[384,1536]{1,0:T(8,128)(2,1)}, u32[]{:S(2)}, u32[]{:S(2)}) collective-permute-start(bf16[384,1536]{1,0:T(8,128)(2,1)} %get-tuple-element.139), channel_id=1, source_target_pairs={{0,8},{8,0},{1,9},{9,1},{2,10},{10,2},{3,11},{11,3},{4,12},{12,4},... | collective-permute-start | bytes 3538952 | tf_op jit(solution)/shard_map/ppermute | solution.py:47
  259.9 16.5 %collective-permute-start.26 = (bf16[96,2048]{1,0:T(8,128)(2,1)}, bf16[96,2048]{1,0:T(8,128)(2,1)}, u32[]{:S(2)}, u32[]{:S(2)}) collective-permute-start(bf16[96,2048]{1,0:T(8,128)(2,1)} %get-tuple-element.135), channel_id=1, source_target_pairs={{0,1},{1,16},{16,17},{17,32},{32,33},{33,48},{48,49},{49,0},{2,3},... | collective-permute-start | bytes 1179656 | tf_op jit(solution)/shard_map/ppermute | solution.py:35
  269.1 14.8 %collective-permute-start.22 = (bf16[96,2048]{1,0:T(8,128)(2,1)}, bf16[96,2048]{1,0:T(8,128)(2,1)}, u32[]{:S(2)}, u32[]{:S(2)}) collective-permute-start(bf16[96,2048]{1,0:T(8,128)(2,1)} %add_convert_fusion.5), channel_id=1, source_target_pairs={{0,49},{1,0},{16,1},{17,16},{32,17},{33,32},{48,33},{49,48},{2,51}... | collective-permute-start | bytes 1179656 | tf_op jit(solution)/shard_map/ppermute | solution.py:35
  271.2 19.6 %all-to-all-start.15 = ((bf16[4,96,1536]{2,1,0:T(8,128)(2,1)}), bf16[4,96,1536]{2,1,0:T(8,128)(2,1)S(1)}, u32[]{:S(2)}, u32[]{:S(2)}) async-start(bf16[4,96,1536]{2,1,0:T(8,128)(2,1)} %gather_fusion.3), calls=%async_computation.15 | async-start | bytes 2359296 | tf_op jit(solution)/shard_map/all_to_all | solution.py:51
  278.5 16.5 %collective-permute-start.27 = (bf16[96,2048]{1,0:T(8,128)(2,1)}, bf16[96,2048]{1,0:T(8,128)(2,1)}, u32[]{:S(2)}, u32[]{:S(2)}) collective-permute-start(bf16[96,2048]{1,0:T(8,128)(2,1)} %add_convert_fusion.2), channel_id=1, source_target_pairs={{0,1},{1,16},{16,17},{17,32},{32,33},{33,48},{48,49},{49,0},{2,3},... | collective-permute-start | bytes 1179656 | tf_op jit(solution)/shard_map/ppermute | solution.py:35
  290.8 43.4 %all-to-all-start.14 = ((bf16[4,96,1536]{2,1,0:T(8,128)(2,1)}), bf16[4,96,1536]{2,1,0:T(8,128)(2,1)S(1)}, u32[]{:S(2)}, u32[]{:S(2)}) async-start(bf16[4,96,1536]{2,1,0:T(8,128)(2,1)} %gather_fusion.1), calls=%async_computation.14 | async-start | bytes 2359296 | tf_op jit(solution)/shard_map/all_to_all | solution.py:51
  296.9 35.4 %collective-permute-start.28 = (bf16[96,2048]{1,0:T(8,128)(2,1)}, bf16[96,2048]{1,0:T(8,128)(2,1)}, u32[]{:S(2)}, u32[]{:S(2)}) collective-permute-start(bf16[96,2048]{1,0:T(8,128)(2,1)} %add_convert_fusion.1), channel_id=1, source_target_pairs={{0,1},{1,16},{16,17},{17,32},{32,33},{33,48},{48,49},{49,0},{2,3},... | collective-permute-start | bytes 1179656 | tf_op jit(solution)/shard_map/ppermute | solution.py:35
  300.0 32.2 %collective-permute-start.25 = (bf16[96,2048]{1,0:T(8,128)(2,1)}, bf16[96,2048]{1,0:T(8,128)(2,1)}, u32[]{:S(2)}, u32[]{:S(2)}) collective-permute-start(bf16[96,2048]{1,0:T(8,128)(2,1)} %add_convert_fusion.3), channel_id=1, source_target_pairs={{0,49},{1,0},{16,1},{17,16},{32,17},{33,32},{48,33},{49,48},{2,51}... | collective-permute-start | bytes 1179656 | tf_op jit(solution)/shard_map/ppermute | solution.py:35
  (45 other events, 363.6 us)

commit v3 on v2

v3 whole, which is shorter than its diff:
```python
import functools

import jax
import jax.numpy as jnp
from jax import lax
from jax.experimental import pallas as pl
from jax.experimental.pallas import tpu as pltpu
from jax.sharding import Mesh
from jax.sharding import PartitionSpec as P

EXPERT = ("x", "zh", "c")
DP = ("y", "zl")
Z = ("zh", "zl")
EXPERT_DP = EXPERT + DP
MOST = 16
NX, NZH, NC, NY, NZL = 4, 4, 2, 4, 2
NZ = NZH * NZL
PLACES = NX * NC
ROWS, TOP, WIDTH, HIDDEN = 96, 8, 2048, 768
META = 8
SHARD, DSHARD = 256, 96
PACK = 384
HALF = PACK // 2
SIDE = 2 * HIDDEN
BF = jnp.bfloat16
F32 = jnp.float32
GROUPS = ((0, -1, 1), (-2, 2), (-3, 3, 4))
VMEM = pl.BlockSpec(memory_space=pltpu.VMEM)
SMEM = pl.BlockSpec(memory_space=pltpu.SMEM)
ANY = pl.BlockSpec(memory_space=pl.ANY)
LIMIT = 48 << 20


def shift(value, axes, count, step):
    return lax.ppermute(value, axes, [(i, (i + step) % count) for i in range(count)])


def along_z(value, step):
    return shift(value, Z, NZ, step)


def along_y(value, step):
    return shift(value, "y", NY, step)


def flip(value, axis):
    return lax.ppermute(value, axis, [(0, 1), (1, 0)])


def across(value, axis):
    return lax.all_to_all(value, axis, split_axis=0, concat_axis=0, tiled=True)


def fence(*values):
    return lax.optimization_barrier(values)


def call(kernel, outs, in_specs, out_specs, name, scratch=(), cost=None):
    return pl.pallas_call(
        kernel,
        out_shape=outs,
        in_specs=in_specs,
        out_specs=out_specs,
        scratch_shapes=scratch,
        compiler_params=pltpu.CompilerParams(vmem_limit_bytes=LIMIT),
        cost_estimate=cost,
        name=name,
    )


def shape(*dims, dtype=BF):
    return jax.ShapeDtypeStruct(dims, dtype)


def prep_kernel(tokens_ref, gain_ref, ids_ref, weights_ref, out_ref):
    values = tokens_ref[...].astype(F32)
    scale = lax.rsqrt(jnp.mean(values * values, axis=-1, keepdims=True) + 1e-06)
    out_ref[pl.ds(0, ROWS), :] = (values * scale * gain_ref[...]).astype(BF)
    out_ref[pl.ds(ROWS, META), :] = jnp.full((META, WIDTH), -1.0, BF)
    out_ref[pl.ds(ROWS, META), 0:ROWS] = ids_ref[...].astype(F32).astype(BF)
    out_ref[pl.ds(ROWS, META), 128 : 128 + ROWS] = weights_ref[...].astype(BF)


def pack_kernel(place_ref, gate_ref, up_ref, down_ref, own_ref, other_ref, first_ref):
    zl = place_ref[3]
    for out_ref, e in ((own_ref, zl), (other_ref, 1 - zl), (first_ref, 0)):
        out_ref[0:SHARD, 0:HIDDEN] = gate_ref[e]
        out_ref[0:SHARD, HIDDEN:SIDE] = up_ref[e]
        out_ref[SHARD : SHARD + DSHARD, :] = down_ref[e, :, 0:SIDE]
        for j in range(3):
            out_ref[SHARD + DSHARD : PACK, 512 * j : 512 * (j + 1)] = down_ref[
                e, 32 * j : 32 * (j + 1), SIDE:WIDTH
            ]


def unpack_kernel(kind_ref, *refs):
    gate_ref, up_ref, down_ref = refs[-3:]
    for kind, ref in zip((0, 1, 2, 4, 8, 16), refs):

        @pl.when(kind_ref[0] == kind)
        def _(ref=ref):
            gate_ref[...] = ref[0:SHARD, 0:HIDDEN]
            up_ref[...] = ref[0:SHARD, HIDDEN:SIDE]
            down_ref[:, 0:SIDE] = ref[SHARD : SHARD + DSHARD, :]
            for j in range(3):
                down_ref[32 * j : 32 * (j + 1), SIDE:WIDTH] = ref[
                    SHARD + DSHARD : PACK, 512 * j : 512 * (j + 1)
                ]


def dispatch_kernel(n, place_ref, *refs):
    sources, (out_ref, weight_ref) = refs[:n], refs[n:]
    zh, zl = place_ref[1], place_ref[3]
    before = lax.broadcasted_iota(jnp.int32, (128, 128), 0)
    after = lax.broadcasted_iota(jnp.int32, (128, 128), 1)
    upto = (before <= after).astype(F32).astype(BF)
    slot = (before & (MOST - 1)).astype(F32)
    for i, ref in enumerate(sources):
        ids = ref[ROWS : ROWS + META, 0:128].astype(F32)
        route = ref[ROWS : ROWS + META, 128:256].astype(F32)
        chosen, factor = [], []
        for p in range(PLACES):
            expert = ((p // NC * NZH + zh) * NC + p % NC) * NZL + zl
            named = jnp.where(ids == expert.astype(F32), 1.0, 0.0)
            chosen.append(jnp.sum(named, axis=0, keepdims=True))
            factor.append(jnp.sum(named * route, axis=0, keepdims=True))
        chosen = jnp.concatenate(chosen, axis=0)
        factor = jnp.concatenate(factor, axis=0)
        ranks = jnp.dot(chosen.astype(BF), upto, preferred_element_type=F32) - 1.0
        ranks = jnp.where(chosen > 0.0, ranks, -1.0)

        def spread(v):
            return jnp.broadcast_to(v[:, None, :], (PLACES, MOST, 128)).reshape(128, 128)

        taken = spread(ranks) == slot
        placing = jnp.where(taken, 1.0, 0.0).astype(BF)
        rows = jnp.dot(placing[:, 0:ROWS], ref[0:ROWS, :], preferred_element_type=F32).astype(BF)
        for p in range(PLACES):
            at = (p * n + i) * MOST
            out_ref[at : at + MOST, :] = rows[p * MOST : (p + 1) * MOST]
        weight_ref[i] = jnp.where(taken, spread(factor), 0.0).T.astype(BF)


def dispatch(place, sources):
    n = len(sources)
    return call(
        functools.partial(dispatch_kernel, n),
        [shape(PLACES * n * MOST, WIDTH), shape(n, 128, 128)],
        [SMEM] + [VMEM] * n,
        [VMEM] * 2,
        "dispatch",
        cost=pl.CostEstimate(flops=0, transcendentals=0, bytes_accessed=80 << 20),
    )(place, *sources)


def ffn_kernel(splits, block, place_ref, own_ref, swap_ref, *refs):
    n = len(splits)
    row_refs, out_refs = refs[:n], refs[n : 2 * n]
    side_v, down_v, rows_v, res_v, sem_w, sem_r, sem_o = refs[2 * n :]
    zl = place_ref[3]
    loads, gets, puts, starts, at = [], [], [], [], 0

    def load(src, dst):
        cp = pltpu.make_async_copy(src, dst, sem_w.at[len(loads)])
        cp.start()
        loads.append(cp)

    for i, rows in enumerate(splits):
        starts.append(at)
        cp = pltpu.make_async_copy(row_refs[i], rows_v.at[pl.ds(at, rows)], sem_r.at[i])
        cp.start()
        gets.append(cp)
        at += rows
    total = at
    for src, from_zl in ((own_ref, zl), (swap_ref, 1 - zl)):
        for y in range(NY):
            holder = y * NZL + from_zl
            base = pl.multiple_of(holder * SHARD, SHARD)
            load(src.at[y, pl.ds(0, SHARD)], side_v.at[pl.ds(base, SHARD)])
            base = pl.multiple_of(holder * DSHARD, DSHARD)
            load(src.at[y, pl.ds(SHARD, DSHARD)], down_v.at[pl.ds(base, DSHARD), 0:SIDE])
            for j in range(3):
                load(
                    src.at[y, pl.ds(SHARD + DSHARD, 32), 512 * j : 512 * (j + 1)],
                    down_v.at[pl.ds(base + 32 * j, 32), SIDE:WIDTH],
                )
    for cp in gets:
        cp.wait()
    for cp in loads:
        cp.wait()

    @pl.loop(0, total // block)
    def _(step):
        at = pl.multiple_of(step * block, block)
        both = jnp.dot(rows_v[pl.ds(at, block), :], side_v[...], preferred_element_type=F32)
        gate, up = both[:, 0:HIDDEN], both[:, HIDDEN:SIDE]
        hidden = (gate / (1.0 + jnp.exp(-gate)) * up).astype(BF)
        res_v[pl.ds(at, block), :] = jnp.dot(
            hidden, down_v[...], preferred_element_type=F32
        ).astype(BF)

    for i, rows in enumerate(splits):
        cp = pltpu.make_async_copy(res_v.at[pl.ds(starts[i], rows)], out_refs[i], sem_o.at[i])
        cp.start()
        puts.append(cp)
    for cp in puts:
        cp.wait()


def ffn(place, own, swapped, groups, block):
    splits = tuple(g.shape[0] for g in groups)
    total = sum(splits)
    return call(
        functools.partial(ffn_kernel, splits, block),
        [shape(r, WIDTH) for r in splits],
        [SMEM] + [ANY] * (2 + len(groups)),
        [ANY] * len(groups),
        "expert_ffn",
        scratch=[
            pltpu.VMEM((WIDTH, SIDE), BF),
            pltpu.VMEM((HIDDEN, WIDTH), BF),
            pltpu.VMEM((total, WIDTH), BF),
            pltpu.VMEM((total, WIDTH), BF),
            pltpu.SemaphoreType.DMA((2 * NY * 5,)),
            pltpu.SemaphoreType.DMA((len(groups),)),
            pltpu.SemaphoreType.DMA((len(groups),)),
        ],
        cost=pl.CostEstimate(
            flops=6 * total * WIDTH * HIDDEN,
            transcendentals=total * HIDDEN,
            bytes_accessed=10 * WIDTH * HIDDEN,
        ),
    )(place, own, swapped, *groups)


def combine_kernel(n, weight_ref, back_ref, *outs):
    for i, out_ref in enumerate(outs):
        stack = jnp.concatenate(
            [back_ref[(p * n + i) * MOST : (p * n + i + 1) * MOST, :] for p in range(PLACES)],
            axis=0,
        )
        out_ref[...] = jnp.dot(
            weight_ref[i, 0:ROWS, :], stack, preferred_element_type=F32
        ).astype(out_ref.dtype)


def combine(weight, back, dtypes):
    n = len(dtypes)
    return call(
        functools.partial(combine_kernel, n),
        [shape(ROWS, WIDTH, dtype=t) for t in dtypes],
        [VMEM] * 2,
        [VMEM] * n,
        "combine",
    )(weight, back)


PLANE = ("x", "c")


def in_plane(rows):
    blocks = rows.reshape(PLACES, -1, WIDTH)
    return across(blocks, PLANE).reshape(-1, WIDTH)


def partner(value, axis, bit):
    count = {"x": NX, "zh": NZH, "c": NC, "zl": NZL}[axis]
    return lax.ppermute(value, axis, [(i, i ^ bit) for i in range(count)])


def joined(got, mine):
    return (got.astype(F32) + mine).astype(BF)


def body(
    tokens, norm_gain, expert_ids, route_weights, gate_weight, up_weight, down_weight, pair_list
):
    x_me, zh_me, c_me = (lax.axis_index(a) for a in EXPERT)
    zl_me = lax.axis_index("zl")
    place = jnp.stack([x_me, zh_me, c_me, zl_me]).astype(jnp.int32)

    near = call(prep_kernel, shape(ROWS + META, WIDTH), [VMEM] * 4, VMEM, "prep")(
        tokens, norm_gain[None, :], expert_ids.T, route_weights.T
    )
    near, place = fence(near, place)
    own, other, first = call(
        pack_kernel, [shape(PACK, SIDE)] * 3, [SMEM] + [VMEM] * 3, [VMEM] * 3, "pack"
    )(place, gate_weight, up_weight, down_weight)

    own_full = lax.all_gather(own, "y", axis=0, tiled=False)
    swapped = partner(other, "zl", 1)

    p1, m1 = along_z(near, 1), along_z(near, -1)
    p2, m2 = along_z(p1, 1), along_z(m1, -1)
    d0, w0 = dispatch(place, (near, p1, m1))
    r0 = in_plane(d0)
    hx1 = partner(first, "x", 1)
    p3, m3 = along_z(p2, 1), along_z(m2, -1)
    far = along_z(p3, 1)
    d1, w1 = dispatch(place, (p2, m2))
    d1, r0, hx1, p3, m3, first, swapped = fence(d1, r0, hx1, p3, m3, first, swapped)
    swap_full = lax.all_gather(swapped, "y", axis=0, tiled=False)
    r1 = in_plane(d1)
    d2, w2 = dispatch(place, (p3, m3, far))
    d2, r1, first = fence(d2, r1, first)
    r2 = in_plane(d2)
    hz1 = partner(first, "zh", 1)
    r0, r1, r2, first = fence(r0, r1, r2, first)
    hx2 = partner(first, "x", 2)
    r0, r1, r2, first, hz1, hx2, own_full, swap_full = fence(
        r0, r1, r2, first, hz1, hx2, own_full, swap_full
    )

    (s2,) = ffn(place, own_full, swap_full, (r2,), 384)
    hz2 = partner(first, "zh", 2)
    s2, r1, r0 = fence(s2, r1, r0)
    b2 = in_plane(s2)
    s1, s0 = ffn(place, own_full, swap_full, (r1, r0), 320)
    b2, s1, s0 = fence(b2, s1, s0)

    c_m3, c_p3, c_4 = combine(w2, b2, (F32, BF, BF))
    down, rise = along_z(c_4, -1), along_z(c_p3, 1)
    b1 = in_plane(s1)
    down = along_z(joined(down, c_m3), -1)
    b1, s0, rise, hz2, hx1, hz1, hx2, first = fence(b1, s0, rise, hz2, hx1, hz1, hx2, first)
    b0 = in_plane(s0)
    c_m2, c_p2 = combine(w1, b1, (F32, F32))
    down = along_z(joined(down, c_m2), -1)
    rise = along_z(joined(rise, c_p2), 1)

    hc = partner(first, "c", 1)
    me = (x_me * NZH + zh_me) * NC + c_me
    bits = jnp.sum(jnp.where(jnp.arange(pair_list.shape[0]) == me, pair_list ^ me, 0))
    new = call(
        unpack_kernel,
        [shape(SHARD, HIDDEN), shape(SHARD, HIDDEN), shape(DSHARD, WIDTH)],
        [SMEM] + [VMEM] * 6,
        [VMEM] * 3,
        "unpack",
    )(bits.astype(jnp.int32).reshape(1), first, hc, hz1, hz2, hx1, hx2)

    c_0, c_m1, c_p1 = combine(w0, b0, (F32, F32, F32))
    down = along_z(joined(down, c_m1), -1)
    rise = along_z(joined(rise, c_p1), 1)
    mixed = (down.astype(F32) + rise.astype(F32) + c_0).astype(BF)
    return (mixed, *(v[None] for v in new))


def solution(mesh):
    split = Mesh(mesh.devices.reshape(NX, NZH, NC, NY, NZL), EXPERT_DP)
    rows = P(EXPERT_DP, None)
    blocks = P(EXPERT, DP, None)
    return jax.shard_map(
        body,
        mesh=split,
        in_specs=(rows, P(), rows, rows, blocks, blocks, blocks, P()),
        out_specs=(rows, blocks, blocks, blocks),
        check_vma=False,
    )
```

time: 343 us -> 301 us (0.88); the launches traced: 337 us -> 299 us
  waiting for transfers between devices: 109 us -> 172 us
  starting transfers between devices: 109 us -> 55.9 us
  blocking collectives: 39.7 us -> 0 us
  local copies, waits for them, and re-layouts: 29.7 us -> 14.3 us
  between operations: 2.21 us -> 14.2 us
  other arithmetic: 12.4 us -> 6.82 us
    ppermute x8 -> x6, waiting for transfers between devices: 6.41 us -> 59.6 us  [partner(): return lax.ppermute(value, axis, [(i, i ^ bit) for i in range(count)])]
    all_to_all x3 -> x0, blocking collectives: 39.7 us -> none  [across(): return lax.all_to_all(value, axis, split_axis=0, concat_axis=0, tiled=True)]
    all_to_all x13 -> x6, starting transfers between devices: 69.1 us -> 29.6 us  [across(): return lax.all_to_all(value, axis, split_axis=0, concat_axis=0, tiled=True)]
    ppermute x22 -> x14, waiting for transfers between devices: 64.4 us -> 84.1 us  [shift(): lax.ppermute(value, axes, [(i, (i + step) % count) for i in range(count)])]
    ppermute x22 -> x14, starting transfers between devices: 40.1 us -> 21.6 us  [shift(): lax.ppermute(value, axes, [(i, (i + step) % count) for i in range(count)])]
    all_to_all x13 -> x6, waiting for transfers between devices: 38.5 us -> 28.1 us  [across(): return lax.all_to_all(value, axis, split_axis=0, concat_axis=0, tiled=True)]
    gather x4 -> x0, local copies, waits for them, and re-layouts: 7.11 us -> none  [the longest x1 2.93 us: body(): jnp.take(hx, x_from, axis=0, mode='clip')]
    slice x4 -> x0, local copies, waits for them, and re-layouts: 6.9 us -> none  [the longest x2 3.85 us: body(): vt, vl = (along_y(vp[:HALF], 1), along_y(vm[HALF:], -1))]
  transfers between devices with their start and end apart: 43 -> 28, of which waited for: 18 -> 17; matrix products, arithmetic and copies ran while one was open for 8% -> 2% of each run, Pallas kernels for 6% -> 8%
where the time goes in v3:
time: 301 us; the launch traced here: 299 us
  waiting for transfers between devices  172 us (57%)
  starting transfers between devices  55.9 us (19%)
  Pallas kernels  35.9 us (12%)
  local copies, waits for them, and re-layouts  14.3 us (5%)
  between operations  14.2 us (5%)
  other arithmetic  6.82 us (2%)
    ppermute x14, waiting for transfers between devices, shift(): lax.ppermute(value, axes, [(i, (i + step) % count) for i in range(count)])  84.1 us
    ppermute x6, waiting for transfers between devices, partner(): return lax.ppermute(value, axis, [(i, i ^ bit) for i in range(count)])  59.6 us
    all_to_all x6, starting transfers between devices, across(): return lax.all_to_all(value, axis, split_axis=0, concat_axis=0, tiled=True)  29.6 us
    all_to_all x6, waiting for transfers between devices, across(): return lax.all_to_all(value, axis, split_axis=0, concat_axis=0, tiled=True)  28.1 us
    ppermute x14, starting transfers between devices, shift(): lax.ppermute(value, axes, [(i, (i + step) % count) for i in range(count)])  21.6 us
    pallas_call x2, Pallas kernels, ffn(): call(functools.partial(ffn_kernel, splits, block), [shape(r, WIDTH) for r...  20.2 us
    unnamed x48, local copies, waits for them, and re-layouts  14.3 us
    pallas_call x3, Pallas kernels, dispatch(): call(functools.partial(dispatch_kernel, n), [shape(PLACES * n * MOST, WID...  6.55 us
  transfers between devices with their start and end apart: 28, of which 17 were waited for; matrix products, arithmetic and copies ran while one was open for 2% of the time, Pallas kernels for 8%

profile of v3, /device:TPU:22, one launch (start us, length us, event | category | flops | bytes accessed | tf_op | source)
XLA Modules:
  0.0 299.0 jit_solution(17098816816214716472)
XLA Ops:
  14.0 2.5 pack.1
  16.5 5.9 %collective-permute-start.2 = (bf16[104,2048]{1,0:T(8,128)(2,1)S(1)}, bf16[104,2048]{1,0:T(8,128)(2,1)S(1)}, u32[]{:S(2)}, u32[]{:S(2)}) collective-permute-start(bf16[104,2048]{1,0:T(8,128)(2,1)S(1)} %prep.1.refs_0_), channel_id=1, source_target_pairs={{0,49},{1,0},{16,1},{17,16},{32,17},{33,32},{48,33},{49,48},{2,51}... | collective-permute-start | bytes 1277960 | tf_op jit(solution)/shard_map/ppermute | solution.py:35
  22.5 9.1 %collective-permute-done.2.refs_2_ = bf16[104,2048]{1,0:T(8,128)(2,1)S(1)} collective-permute-done((bf16[104,2048]{1,0:T(8,128)(2,1)S(1)}, bf16[104,2048]{1,0:T(8,128)(2,1)S(1)}, u32[]{:S(2)}, u32[]{:S(2)}) %collective-permute-start.2) | collective-permute-done | bytes 426016 | tf_op jit(solution)/shard_map/ppermute | solution.py:35
  31.5 3.4 %collective-permute-done.refs_1_ = bf16[104,2048]{1,0:T(8,128)(2,1)S(1)} collective-permute-done((bf16[104,2048]{1,0:T(8,128)(2,1)S(1)}, bf16[104,2048]{1,0:T(8,128)(2,1)S(1)}, u32[]{:S(2)}, u32[]{:S(2)}) %collective-permute-start) | collective-permute-done | bytes 426016 | tf_op jit(solution)/shard_map/ppermute | solution.py:35
  35.0 2.7 dispatch.4
  37.7 4.8 %all-to-all-start = ((bf16[8,48,2048]{2,1,0:T(8,128)(2,1)}), bf16[8,48,2048]{2,1,0:T(8,128)(2,1)S(1)}, u32[]{:S(2)}, u32[]{:S(2)}) async-start(bf16[8,48,2048]{2,1,0:T(8,128)(2,1)} %bitcast.7), calls=%async_computation | async-start | bytes 3145728 | tf_op jit(solution)/shard_map/all_to_all | solution.py:51
  45.4 34.4 %collective-permute-done.3.refs_1_ = bf16[104,2048]{1,0:T(8,128)(2,1)S(1)} collective-permute-done((bf16[104,2048]{1,0:T(8,128)(2,1)}, bf16[104,2048]{1,0:T(8,128)(2,1)S(1)}, u32[]{:S(2)}, u32[]{:S(2)}) %collective-permute-start.3) | collective-permute-done | bytes 426016 | tf_op jit(solution)/shard_map/ppermute | solution.py:35
  79.8 2.0 collective-permute-start.5
  84.6 2.1 collective-permute-done.4.refs_4_
  86.6 4.3 %collective-permute-done.6.refs_1_ = bf16[104,2048]{1,0:T(8,128)(2,1)} collective-permute-done((bf16[104,2048]{1,0:T(8,128)(2,1)S(1)}, bf16[104,2048]{1,0:T(8,128)(2,1)}, u32[]{:S(2)}, u32[]{:S(2)}) %collective-permute-start.6) | collective-permute-done | bytes 426016 | tf_op jit(solution)/shard_map/ppermute | solution.py:35
  92.4 4.8 %all-to-all-start.1 = ((bf16[8,32,2048]{2,1,0:T(8,128)(2,1)}), bf16[8,32,2048]{2,1,0:T(8,128)(2,1)}, u32[]{:S(2)}, u32[]{:S(2)}) async-start(bf16[8,32,2048]{2,1,0:T(8,128)(2,1)} %bitcast.33), calls=%async_computation.1 | async-start | bytes 2097152 | tf_op jit(solution)/shard_map/all_to_all | solution.py:51
  97.8 12.8 %collective-permute-done.8.refs_2_ = bf16[104,2048]{1,0:T(8,128)(2,1)S(1)} collective-permute-done((bf16[104,2048]{1,0:T(8,128)(2,1)}, bf16[104,2048]{1,0:T(8,128)(2,1)S(1)}, u32[]{:S(2)}, u32[]{:S(2)}) %collective-permute-start.8) | collective-permute-done | bytes 426016 | tf_op jit(solution)/shard_map/ppermute | solution.py:35
  110.5 2.1 dispatch.5
  113.8 4.8 %all-to-all-start.2 = ((bf16[8,48,2048]{2,1,0:T(8,128)(2,1)}), bf16[8,48,2048]{2,1,0:T(8,128)(2,1)S(1)}, u32[]{:S(2)}, u32[]{:S(2)}) async-start(bf16[8,48,2048]{2,1,0:T(8,128)(2,1)} %bitcast.31), calls=%async_computation.2 | async-start | bytes 3145728 | tf_op jit(solution)/shard_map/all_to_all | solution.py:51
  118.6 19.5 %all-to-all-done.2 = bf16[8,48,2048]{2,1,0:T(8,128)(2,1)S(1)} async-done(((bf16[8,48,2048]{2,1,0:T(8,128)(2,1)}), bf16[8,48,2048]{2,1,0:T(8,128)(2,1)S(1)}, u32[]{:S(2)}, u32[]{:S(2)}) %all-to-all-start.2) | async-done | bytes 1572896 | tf_op jit(solution)/shard_map/all_to_all | solution.py:51
  138.2 2.1 collective-permute-start.10
  140.2 31.7 %collective-permute-done.9.refs_2_ = bf16[384,1536]{1,0:T(8,128)(2,1)} collective-permute-done((bf16[384,1536]{1,0:T(8,128)(2,1)}, bf16[384,1536]{1,0:T(8,128)(2,1)}, u32[]{:S(2)}, u32[]{:S(2)}) %collective-permute-start.9) | collective-permute-done | bytes 1179680 | tf_op jit(solution)/shard_map/ppermute | solution.py:268
  171.9 8.6 %expert_ffn.2 = bf16[384,2048]{1,0:T(8,128)(2,1)S(1)} custom-call(s32[4]{0:T(128)S(1)} %pad_add_fusion.place_ref, bf16[4,384,1536]{2,1,0:T(8,128)(2,1)} %bitcast.38, bf16[4,384,1536]{2,1,0:T(8,128)(2,1)} %bitcast.40, bf16[384,2048]{1,0:T(8,128)(2,1)S(1)} %bitcast.30), custom_call_target="tpu_custom_call" | custom-call | flops 3623878656 | bytes 15728640 | tf_op jit(solution)/shard_map/expert_ffn/pallas_call | solution.py:213
  181.7 4.8 %all-to-all-start.3 = ((bf16[8,48,2048]{2,1,0:T(8,128)(2,1)}), bf16[8,48,2048]{2,1,0:T(8,128)(2,1)S(1)}, u32[]{:S(2)}, u32[]{:S(2)}) async-start(bf16[8,48,2048]{2,1,0:T(8,128)(2,1)} %bitcast.32), calls=%async_computation.3 | async-start | bytes 3145728 | tf_op jit(solution)/shard_map/all_to_all | solution.py:51
  188.2 11.5 %expert_ffn.3 = (bf16[256,2048]{1,0:T(8,128)(2,1)S(1)}, bf16[384,2048]{1,0:T(8,128)(2,1)S(1)}) custom-call(s32[4]{0:T(128)S(1)} %pad_add_fusion.place_ref, bf16[4,384,1536]{2,1,0:T(8,128)(2,1)} %bitcast.39, bf16[4,384,1536]{2,1,0:T(8,128)(2,1)} %bitcast.41, bf16[256,2048]{1,0:T(8,128)(2,1)} %bitcast.10.refs_0_, bf16[384,2048]{1,0:T(8,128)(2,1)S(1)} %bitcast.28), custom_call_target="tpu_custom_call" | custom-call | flops 6039797760 | bytes 15728640 | tf_op jit(solution)/shard_map/expert_ffn/pallas_call | solution.py:213
  201.9 4.1 %all-to-all-done.3 = bf16[8,48,2048]{2,1,0:T(8,128)(2,1)S(1)} async-done(((bf16[8,48,2048]{2,1,0:T(8,128)(2,1)}), bf16[8,48,2048]{2,1,0:T(8,128)(2,1)S(1)}, u32[]{:S(2)}, u32[]{:S(2)}) %all-to-all-start.3) | async-done | bytes 1572896 | tf_op jit(solution)/shard_map/all_to_all | solution.py:51
  206.0 5.6 %all-to-all-start.4 = ((bf16[8,32,2048]{2,1,0:T(8,128)(2,1)}), bf16[8,32,2048]{2,1,0:T(8,128)(2,1)S(1)}, u32[]{:S(2)}, u32[]{:S(2)}) async-start(bf16[8,32,2048]{2,1,0:T(8,128)(2,1)} %bitcast.34), calls=%async_computation.4 | async-start | bytes 2097152 | tf_op jit(solution)/shard_map/all_to_all | solution.py:51
  213.7 3.2 %collective-permute-start.11 = (bf16[96,2048]{1,0:T(8,128)(2,1)}, bf16[96,2048]{1,0:T(8,128)(2,1)}, u32[]{:S(2)}, u32[]{:S(2)}) collective-permute-start(bf16[96,2048]{1,0:T(8,128)(2,1)} %get-tuple-element.97), channel_id=1, source_target_pairs={{0,49},{1,0},{16,1},{17,16},{32,17},{33,32},{48,33},{49,48},{2,51}... | collective-permute-start | bytes 1179656 | tf_op jit(solution)/shard_map/ppermute | solution.py:35
  216.9 25.8 %collective-permute-done.14.refs_3_ = bf16[384,1536]{1,0:T(8,128)(2,1)} collective-permute-done((bf16[384,1536]{1,0:T(8,128)(2,1)}, bf16[384,1536]{1,0:T(8,128)(2,1)}, u32[]{:S(2)}, u32[]{:S(2)}) %collective-permute-start.14) | collective-permute-done | bytes 1179680 | tf_op jit(solution)/shard_map/ppermute | solution.py:268
  242.7 7.0 %collective-permute-done.13 = bf16[96,2048]{1,0:T(8,128)(2,1)S(1)} collective-permute-done((bf16[96,2048]{1,0:T(8,128)(2,1)S(1)}, bf16[96,2048]{1,0:T(8,128)(2,1)S(1)}, u32[]{:S(2)}, u32[]{:S(2)}) %collective-permute-start.13) | collective-permute-done | bytes 393248 | tf_op jit(solution)/shard_map/ppermute | solution.py:35
  250.5 4.8 %all-to-all-start.5 = ((bf16[8,48,2048]{2,1,0:T(8,128)(2,1)}), bf16[8,48,2048]{2,1,0:T(8,128)(2,1)S(1)}, u32[]{:S(2)}, u32[]{:S(2)}) async-start(bf16[8,48,2048]{2,1,0:T(8,128)(2,1)} %bitcast.29), calls=%async_computation.5 | async-start | bytes 3145728 | tf_op jit(solution)/shard_map/all_to_all | solution.py:51
  259.1 8.6 %collective-permute-done.12 = bf16[96,2048]{1,0:T(8,128)(2,1)S(1)} collective-permute-done((bf16[96,2048]{1,0:T(8,128)(2,1)S(1)}, bf16[96,2048]{1,0:T(8,128)(2,1)S(1)}, u32[]{:S(2)}, u32[]{:S(2)}) %collective-permute-start.12) | collective-permute-done | bytes 393248 | tf_op jit(solution)/shard_map/ppermute | solution.py:35
  268.5 1.8 collective-permute-start.15
  270.3 4.5 %all-to-all-done.5 = bf16[8,48,2048]{2,1,0:T(8,128)(2,1)S(1)} async-done(((bf16[8,48,2048]{2,1,0:T(8,128)(2,1)}), bf16[8,48,2048]{2,1,0:T(8,128)(2,1)S(1)}, u32[]{:S(2)}, u32[]{:S(2)}) %all-to-all-start.5) | async-done | bytes 1572896 | tf_op jit(solution)/shard_map/all_to_all | solution.py:51
  280.3 3.1 %collective-permute-start.16 = (bf16[96,2048]{1,0:T(8,128)(2,1)S(1)}, bf16[96,2048]{1,0:T(8,128)(2,1)}, u32[]{:S(2)}, u32[]{:S(2)}) collective-permute-start(bf16[96,2048]{1,0:T(8,128)(2,1)S(1)} %add_convert_fusion.3), channel_id=1, source_target_pairs={{0,49},{1,0},{16,1},{17,16},{32,17},{33,32},{48,33},{49,48},{2,51}... | collective-permute-start | bytes 1179656 | tf_op jit(solution)/shard_map/ppermute | solution.py:35
  284.0 4.4 %unpack.1 = (bf16[256,768]{1,0:T(8,128)(2,1)}, bf16[256,768]{1,0:T(8,128)(2,1)}, bf16[96,2048]{1,0:T(8,128)(2,1)}) custom-call(s32[1]{0:T(128)} %bitcast.21.kind_ref, bf16[384,1536]{1,0:T(8,128)(2,1)} %get-tuple-element.116.refs_0_, bf16[384,1536]{1,0:T(8,128)(2,1)} %collective-permute-done.19.refs_1_, bf16[384,1536]{1,0:T(8,128)(2,1)} %collective-permute-done.9.refs_2_, ...), custom_call_target="tpu_custom_call" | custom-call | tf_op jit(solution)/shard_map/unpack/pallas_call | solution.py:334
  290.3 1.9 add_convert_fusion
  (93 shorter events, 35.9 us)
Async XLA Ops:
  7.2 164.7 %all-gather.5.cloned.1.call-start = ((), (), s32[]{:S(2)}) async-start(), calls=%async_computation.6 | async-start | bytes 5898240 | tf_op jit(solution)/shard_map/all_gather | solution.py:290
  16.5 15.0 %collective-permute-start.2 = (bf16[104,2048]{1,0:T(8,128)(2,1)S(1)}, bf16[104,2048]{1,0:T(8,128)(2,1)S(1)}, u32[]{:S(2)}, u32[]{:S(2)}) collective-permute-start(bf16[104,2048]{1,0:T(8,128)(2,1)S(1)} %prep.1.refs_0_), channel_id=1, source_target_pairs={{0,49},{1,0},{16,1},{17,16},{32,17},{33,32},{48,33},{49,48},{2,51}... | collective-permute-start | bytes 1277960 | tf_op jit(solution)/shard_map/ppermute | solution.py:35
  22.5 12.5 %collective-permute-start = (bf16[104,2048]{1,0:T(8,128)(2,1)S(1)}, bf16[104,2048]{1,0:T(8,128)(2,1)S(1)}, u32[]{:S(2)}, u32[]{:S(2)}) collective-permute-start(bf16[104,2048]{1,0:T(8,128)(2,1)S(1)} %prep.1.refs_0_), channel_id=1, source_target_pairs={{0,1},{1,16},{16,17},{17,32},{32,33},{33,48},{48,49},{49,0},{2,3},... | collective-permute-start | bytes 1277960 | tf_op jit(solution)/shard_map/ppermute | solution.py:35
  31.5 6.1 %copy-start.13 = (bf16[104,2048]{1,0:T(8,128)(2,1)}, bf16[104,2048]{1,0:T(8,128)(2,1)S(1)}, u32[]{:S(2)}) copy-start(bf16[104,2048]{1,0:T(8,128)(2,1)S(1)} %collective-permute-done.2.refs_2_) | copy-start | bytes 1277956
  37.7 54.7 %all-to-all-start = ((bf16[8,48,2048]{2,1,0:T(8,128)(2,1)}), bf16[8,48,2048]{2,1,0:T(8,128)(2,1)S(1)}, u32[]{:S(2)}, u32[]{:S(2)}) async-start(bf16[8,48,2048]{2,1,0:T(8,128)(2,1)} %bitcast.7), calls=%async_computation | async-start | bytes 3145728 | tf_op jit(solution)/shard_map/all_to_all | solution.py:51
  42.4 129.5 %all-gather.7.cloned.1.call-start = ((), (), s32[]{:S(2)}) async-start(), calls=%async_computation.7 | async-start | bytes 5898240 | tf_op jit(solution)/shard_map/all_gather | solution.py:302
  42.4 42.1 %collective-permute-start.7 = (bf16[384,1536]{1,0:T(8,128)(2,1)}, bf16[384,1536]{1,0:T(8,128)(2,1)}, u32[]{:S(2)}, u32[]{:S(2)}) collective-permute-start(bf16[384,1536]{1,0:T(8,128)(2,1)} %get-tuple-element.69), channel_id=1, source_target_pairs={{0,1},{1,0},{2,3},{3,2},{4,5},{5,4},{6,7},{7,6},{8,9},{9,8},{10,11... | collective-permute-start | bytes 3538952 | tf_op jit(solution)/shard_map/ppermute | solution.py:268
  42.5 44.2 %collective-permute-start.4 = (bf16[384,1536]{1,0:T(8,128)(2,1)}, bf16[384,1536]{1,0:T(8,128)(2,1)S(1)}, u32[]{:S(2)}, u32[]{:S(2)}) collective-permute-start(bf16[384,1536]{1,0:T(8,128)(2,1)} %get-tuple-element.116.refs_0_), channel_id=1, source_target_pairs={{0,64},{64,0},{128,192},{192,128},{1,65},{65,1},{129,193},{193,129... | collective-permute-start | bytes 3538952 | tf_op jit(solution)/shard_map/ppermute | solution.py:268
  43.4 36.4 %collective-permute-start.3 = (bf16[104,2048]{1,0:T(8,128)(2,1)}, bf16[104,2048]{1,0:T(8,128)(2,1)S(1)}, u32[]{:S(2)}, u32[]{:S(2)}) collective-permute-start(bf16[104,2048]{1,0:T(8,128)(2,1)} %copy-done.13), channel_id=1, source_target_pairs={{0,49},{1,0},{16,1},{17,16},{32,17},{33,32},{48,33},{49,48},{2,51}... | collective-permute-start | bytes 1277960 | tf_op jit(solution)/shard_map/ppermute | solution.py:35
  44.1 35.7 %collective-permute-start.1 = (bf16[104,2048]{1,0:T(8,128)(2,1)}, bf16[104,2048]{1,0:T(8,128)(2,1)}, u32[]{:S(2)}, u32[]{:S(2)}) collective-permute-start(bf16[104,2048]{1,0:T(8,128)(2,1)} %copy-done.12), channel_id=1, source_target_pairs={{0,1},{1,16},{16,17},{17,32},{32,33},{33,48},{48,49},{49,0},{2,3},... | collective-permute-start | bytes 1277960 | tf_op jit(solution)/shard_map/ppermute | solution.py:35
  79.8 11.1 %collective-permute-start.6 = (bf16[104,2048]{1,0:T(8,128)(2,1)S(1)}, bf16[104,2048]{1,0:T(8,128)(2,1)}, u32[]{:S(2)}, u32[]{:S(2)}) collective-permute-start(bf16[104,2048]{1,0:T(8,128)(2,1)S(1)} %collective-permute-done.3.refs_1_), channel_id=1, source_target_pairs={{0,49},{1,0},{16,1},{17,16},{32,17},{33,32},{48,33},{49,48},{2,51}... | collective-permute-start | bytes 1277960 | tf_op jit(solution)/shard_map/ppermute | solution.py:35
  79.8 12.6 %collective-permute-start.5 = (bf16[104,2048]{1,0:T(8,128)(2,1)}, bf16[104,2048]{1,0:T(8,128)(2,1)}, u32[]{:S(2)}, u32[]{:S(2)}) collective-permute-start(bf16[104,2048]{1,0:T(8,128)(2,1)} %collective-permute-done.1.refs_0_), channel_id=1, source_target_pairs={{0,1},{1,16},{16,17},{17,32},{32,33},{33,48},{48,49},{49,0},{2,3},... | collective-permute-start | bytes 1277960 | tf_op jit(solution)/shard_map/ppermute | solution.py:35
  84.6 7.9 %copy-start.15 = (bf16[2,128,128]{2,1,0:T(8,128)(2,1)}, bf16[2,128,128]{2,1,0:T(8,128)(2,1)S(1)}, u32[]{:S(2)}) copy-start(bf16[2,128,128]{2,1,0:T(8,128)(2,1)S(1)} %get-tuple-element.99.weight_ref) | copy-start | bytes 196612
  92.4 21.4 %all-to-all-start.1 = ((bf16[8,32,2048]{2,1,0:T(8,128)(2,1)}), bf16[8,32,2048]{2,1,0:T(8,128)(2,1)}, u32[]{:S(2)}, u32[]{:S(2)}) async-start(bf16[8,32,2048]{2,1,0:T(8,128)(2,1)} %bitcast.33), calls=%async_computation.1 | async-start | bytes 2097152 | tf_op jit(solution)/shard_map/all_to_all | solution.py:51
  97.2 13.3 %collective-permute-start.8 = (bf16[104,2048]{1,0:T(8,128)(2,1)}, bf16[104,2048]{1,0:T(8,128)(2,1)S(1)}, u32[]{:S(2)}, u32[]{:S(2)}) collective-permute-start(bf16[104,2048]{1,0:T(8,128)(2,1)} %collective-permute-done.5.refs_0_), channel_id=1, source_target_pairs={{0,1},{1,16},{16,17},{17,32},{32,33},{33,48},{48,49},{49,0},{2,3},... | collective-permute-start | bytes 1277960 | tf_op jit(solution)/shard_map/ppermute | solution.py:35
  113.8 24.3 %all-to-all-start.2 = ((bf16[8,48,2048]{2,1,0:T(8,128)(2,1)}), bf16[8,48,2048]{2,1,0:T(8,128)(2,1)S(1)}, u32[]{:S(2)}, u32[]{:S(2)}) async-start(bf16[8,48,2048]{2,1,0:T(8,128)(2,1)} %bitcast.31), calls=%async_computation.2 | async-start | bytes 3145728 | tf_op jit(solution)/shard_map/all_to_all | solution.py:51
  118.6 53.3 %collective-permute-start.9 = (bf16[384,1536]{1,0:T(8,128)(2,1)}, bf16[384,1536]{1,0:T(8,128)(2,1)}, u32[]{:S(2)}, u32[]{:S(2)}) collective-permute-start(bf16[384,1536]{1,0:T(8,128)(2,1)} %get-tuple-element.116.refs_0_), channel_id=1, source_target_pairs={{0,16},{16,0},{32,48},{48,32},{1,17},{17,1},{33,49},{49,33},{2,18}... | collective-permute-start | bytes 3538952 | tf_op jit(solution)/shard_map/ppermute | solution.py:268
  138.2 33.8 %collective-permute-start.10 = (bf16[384,1536]{1,0:T(8,128)(2,1)}, bf16[384,1536]{1,0:T(8,128)(2,1)}, u32[]{:S(2)}, u32[]{:S(2)}) collective-permute-start(bf16[384,1536]{1,0:T(8,128)(2,1)} %get-tuple-element.116.refs_0_), channel_id=1, source_target_pairs={{0,128},{64,192},{128,0},{192,64},{1,129},{65,193},{129,1},{193,65... | collective-permute-start | bytes 3538952 | tf_op jit(solution)/shard_map/ppermute | solution.py:268
  181.7 24.3 %all-to-all-start.3 = ((bf16[8,48,2048]{2,1,0:T(8,128)(2,1)}), bf16[8,48,2048]{2,1,0:T(8,128)(2,1)S(1)}, u32[]{:S(2)}, u32[]{:S(2)}) async-start(bf16[8,48,2048]{2,1,0:T(8,128)(2,1)} %bitcast.32), calls=%async_computation.3 | async-start | bytes 3145728 | tf_op jit(solution)/shard_map/all_to_all | solution.py:51
  186.5 56.2 %collective-permute-start.14 = (bf16[384,1536]{1,0:T(8,128)(2,1)}, bf16[384,1536]{1,0:T(8,128)(2,1)}, u32[]{:S(2)}, u32[]{:S(2)}) collective-permute-start(bf16[384,1536]{1,0:T(8,128)(2,1)} %get-tuple-element.116.refs_0_), channel_id=1, source_target_pairs={{0,32},{16,48},{32,0},{48,16},{1,33},{17,49},{33,1},{49,17},{2,34}... | collective-permute-start | bytes 3538952 | tf_op jit(solution)/shard_map/ppermute | solution.py:268
  206.0 43.7 %all-to-all-start.4 = ((bf16[8,32,2048]{2,1,0:T(8,128)(2,1)}), bf16[8,32,2048]{2,1,0:T(8,128)(2,1)S(1)}, u32[]{:S(2)}, u32[]{:S(2)}) async-start(bf16[8,32,2048]{2,1,0:T(8,128)(2,1)} %bitcast.34), calls=%async_computation.4 | async-start | bytes 2097152 | tf_op jit(solution)/shard_map/all_to_all | solution.py:51
  213.7 36.1 %collective-permute-start.13 = (bf16[96,2048]{1,0:T(8,128)(2,1)S(1)}, bf16[96,2048]{1,0:T(8,128)(2,1)S(1)}, u32[]{:S(2)}, u32[]{:S(2)}) collective-permute-start(bf16[96,2048]{1,0:T(8,128)(2,1)S(1)} %get-tuple-element.102), channel_id=1, source_target_pairs={{0,1},{1,16},{16,17},{17,32},{32,33},{33,48},{48,49},{49,0},{2,3},... | collective-permute-start | bytes 1179656 | tf_op jit(solution)/shard_map/ppermute | solution.py:35
  213.7 41.6 %collective-permute-start.11 = (bf16[96,2048]{1,0:T(8,128)(2,1)}, bf16[96,2048]{1,0:T(8,128)(2,1)}, u32[]{:S(2)}, u32[]{:S(2)}) collective-permute-start(bf16[96,2048]{1,0:T(8,128)(2,1)} %get-tuple-element.97), channel_id=1, source_target_pairs={{0,49},{1,0},{16,1},{17,16},{32,17},{33,32},{48,33},{49,48},{2,51}... | collective-permute-start | bytes 1179656 | tf_op jit(solution)/shard_map/ppermute | solution.py:35
  250.5 24.3 %all-to-all-start.5 = ((bf16[8,48,2048]{2,1,0:T(8,128)(2,1)}), bf16[8,48,2048]{2,1,0:T(8,128)(2,1)S(1)}, u32[]{:S(2)}, u32[]{:S(2)}) async-start(bf16[8,48,2048]{2,1,0:T(8,128)(2,1)} %bitcast.29), calls=%async_computation.5 | async-start | bytes 3145728 | tf_op jit(solution)/shard_map/all_to_all | solution.py:51
  256.5 11.2 %collective-permute-start.12 = (bf16[96,2048]{1,0:T(8,128)(2,1)S(1)}, bf16[96,2048]{1,0:T(8,128)(2,1)S(1)}, u32[]{:S(2)}, u32[]{:S(2)}) collective-permute-start(bf16[96,2048]{1,0:T(8,128)(2,1)S(1)} %add_convert_fusion.5), channel_id=1, source_target_pairs={{0,49},{1,0},{16,1},{17,16},{32,17},{33,32},{48,33},{49,48},{2,51}... | collective-permute-start | bytes 1179656 | tf_op jit(solution)/shard_map/ppermute | solution.py:35
  257.6 17.7 %collective-permute-start.17 = (bf16[96,2048]{1,0:T(8,128)(2,1)S(1)}, bf16[96,2048]{1,0:T(8,128)(2,1)S(1)}, u32[]{:S(2)}, u32[]{:S(2)}) collective-permute-start(bf16[96,2048]{1,0:T(8,128)(2,1)S(1)} %add_convert_fusion.2), channel_id=1, source_target_pairs={{0,1},{1,16},{16,17},{17,32},{32,33},{33,48},{48,49},{49,0},{2,3},... | collective-permute-start | bytes 1179656 | tf_op jit(solution)/shard_map/ppermute | solution.py:35
  268.5 10.7 %collective-permute-start.15 = (bf16[96,2048]{1,0:T(8,128)(2,1)}, bf16[96,2048]{1,0:T(8,128)(2,1)}, u32[]{:S(2)}, u32[]{:S(2)}) collective-permute-start(bf16[96,2048]{1,0:T(8,128)(2,1)} %add_convert_fusion.4), channel_id=1, source_target_pairs={{0,49},{1,0},{16,1},{17,16},{32,17},{33,32},{48,33},{49,48},{2,51}... | collective-permute-start | bytes 1179656 | tf_op jit(solution)/shard_map/ppermute | solution.py:35
  270.3 13.7 %collective-permute-start.19 = (bf16[384,1536]{1,0:T(8,128)(2,1)}, bf16[384,1536]{1,0:T(8,128)(2,1)}, u32[]{:S(2)}, u32[]{:S(2)}) collective-permute-start(bf16[384,1536]{1,0:T(8,128)(2,1)} %get-tuple-element.116.refs_0_), channel_id=1, source_target_pairs={{0,8},{8,0},{1,9},{9,1},{2,10},{10,2},{3,11},{11,3},{4,12},{12,4},... | collective-permute-start | bytes 3538952 | tf_op jit(solution)/shard_map/ppermute | solution.py:268
  276.1 7.3 %copy-start.23 = (s32[32]{0:T(128)S(1)}, s32[32]{0:T(128)}, u32[]{:S(2)}) copy-start(s32[32]{0:T(128)} %param.15) | copy-start | bytes 388
  276.1 8.0 %copy-start.4 = (bf16[384,1536]{1,0:T(8,128)(2,1)S(1)}, bf16[384,1536]{1,0:T(8,128)(2,1)}, u32[]{:S(2)}) copy-start(bf16[384,1536]{1,0:T(8,128)(2,1)} %copy-done.3) | copy-start | bytes 3538948
  277.2 11.9 %collective-permute-start.18 = (bf16[96,2048]{1,0:T(8,128)(2,1)S(1)}, bf16[96,2048]{1,0:T(8,128)(2,1)S(1)}, u32[]{:S(2)}, u32[]{:S(2)}) collective-permute-start(bf16[96,2048]{1,0:T(8,128)(2,1)S(1)} %add_convert_fusion.1), channel_id=1, source_target_pairs={{0,1},{1,16},{16,17},{17,32},{32,33},{33,48},{48,49},{49,0},{2,3},... | collective-permute-start | bytes 1179656 | tf_op jit(solution)/shard_map/ppermute | solution.py:35
  280.3 10.0 %collective-permute-start.16 = (bf16[96,2048]{1,0:T(8,128)(2,1)S(1)}, bf16[96,2048]{1,0:T(8,128)(2,1)}, u32[]{:S(2)}, u32[]{:S(2)}) collective-permute-start(bf16[96,2048]{1,0:T(8,128)(2,1)S(1)} %add_convert_fusion.3), channel_id=1, source_target_pairs={{0,49},{1,0},{16,1},{17,16},{32,17},{33,32},{48,33},{49,48},{2,51}... | collective-permute-start | bytes 1179656 | tf_op jit(solution)/shard_map/ppermute | solution.py:35
  (20 other events, 32.4 us)
Sparse Core Ops, SparseCore 0:
  16.7 57.0 all-gather.4
  92.5 51.5 all-gather.6

commit v4 on v3

--- a/solution.py
+++ b/solution.py
@@ -22,12 +22,13 @@
 PACK = 384
 HALF = PACK // 2
 SIDE = 2 * HIDDEN
+PIECE = PACK // NZH
 BF = jnp.bfloat16
 F32 = jnp.float32
 GROUPS = ((0, -1, 1), (-2, 2), (-3, 3, 4))
 VMEM = pl.BlockSpec(memory_space=pltpu.VMEM)
 SMEM = pl.BlockSpec(memory_space=pltpu.SMEM)
-ANY = pl.BlockSpec(memory_space=pl.ANY)
+HBM = pl.BlockSpec(memory_space=pltpu.HBM)
 LIMIT = 48 << 20
 
 
@@ -72,40 +73,99 @@
     return jax.ShapeDtypeStruct(dims, dtype)
 
 
-def prep_kernel(tokens_ref, gain_ref, ids_ref, weights_ref, out_ref):
-    values = tokens_ref[...].astype(F32)
+def prep_kernel(
+    place_ref, tokens_ref, gain_ref, ids_ref, route_ref, gate_ref, up_ref, down_ref,
+    out_ref, own_ref, other_ref, first_ref, tokens_v, gain_v, ids_v, route_v, sem_a, sem_b,
+):
+    zl = place_ref[3]
+    reads, moves = [], []
+    for src, dst in (
+        (tokens_ref, tokens_v), (gain_ref, gain_v), (ids_ref, ids_v), (route_ref, route_v),
+    ):
+        cp = pltpu.make_async_copy(src, dst, sem_a.at[len(reads)])
+        cp.start()
+        reads.append(cp)
+
+    def move(src, dst):
+        cp = pltpu.make_async_copy(src, dst, sem_b.at[len(moves)])
+        cp.start()
+        moves.append(cp)
+
+    for pack_ref, e in ((own_ref, zl), (other_ref, 1 - zl), (first_ref, 0)):
+        move(gate_ref.at[e], pack_ref.at[pl.ds(0, SHARD), 0:HIDDEN])
+        move(up_ref.at[e], pack_ref.at[pl.ds(0, SHARD), HIDDEN:SIDE])
+        move(down_ref.at[e, :, 0:SIDE], pack_ref.at[pl.ds(SHARD, DSHARD), :])
+        for j in range(3):
+            move(
+                down_ref.at[e, pl.ds(32 * j, 32), SIDE:WIDTH],
+                pack_ref.at[pl.ds(SHARD + DSHARD, 32), 512 * j : 512 * (j + 1)],
+            )
+    for cp in reads:
+        cp.wait()
+    values = tokens_v[...].astype(F32)
     scale = lax.rsqrt(jnp.mean(values * values, axis=-1, keepdims=True) + 1e-06)
-    out_ref[pl.ds(0, ROWS), :] = (values * scale * gain_ref[...]).astype(BF)
+    out_ref[pl.ds(0, ROWS), :] = (values * scale * gain_v[...]).astype(BF)
     out_ref[pl.ds(ROWS, META), :] = jnp.full((META, WIDTH), -1.0, BF)
-    out_ref[pl.ds(ROWS, META), 0:ROWS] = ids_ref[...].astype(F32).astype(BF)
-    out_ref[pl.ds(ROWS, META), 128 : 128 + ROWS] = weights_ref[...].astype(BF)
-
-
-def pack_kernel(place_ref, gate_ref, up_ref, down_ref, own_ref, other_ref, first_ref):
-    zl = place_ref[3]
-    for out_ref, e in ((own_ref, zl), (other_ref, 1 - zl), (first_ref, 0)):
-        out_ref[0:SHARD, 0:HIDDEN] = gate_ref[e]
-        out_ref[0:SHARD, HIDDEN:SIDE] = up_ref[e]
-        out_ref[SHARD : SHARD + DSHARD, :] = down_ref[e, :, 0:SIDE]
-        for j in range(3):
-            out_ref[SHARD + DSHARD : PACK, 512 * j : 512 * (j + 1)] = down_ref[
-                e, 32 * j : 32 * (j + 1), SIDE:WIDTH
-            ]
-
-
-def unpack_kernel(kind_ref, *refs):
-    gate_ref, up_ref, down_ref = refs[-3:]
-    for kind, ref in zip((0, 1, 2, 4, 8, 16), refs):
-
-        @pl.when(kind_ref[0] == kind)
+    out_ref[pl.ds(ROWS, META), 0:ROWS] = ids_v[...].astype(F32).astype(BF)
+    out_ref[pl.ds(ROWS, META), 128 : 128 + ROWS] = route_v[...].astype(BF)
+    for cp in moves:
+        cp.wait()
+
+
+def cut_kernel(place_ref, first_ref, *refs):
+    outs, sem = refs[:-1], refs[-1]
+    copies = []
+    for k, out_ref in enumerate(outs):
+        at = pl.multiple_of(((place_ref[1] + k) & (NZH - 1)) * PIECE, PIECE)
+        cp = pltpu.make_async_copy(first_ref.at[pl.ds(at, PIECE)], out_ref, sem.at[k])
+        cp.start()
+        copies.append(cp)
+    for cp in copies:
+        cp.wait()
+
+
+def pick_kernel(chosen_ref, *refs):
+    pieces, outs, sem = refs[:NZH], refs[NZH : 2 * NZH], refs[-1]
+    for k, out_ref in enumerate(outs):
+        for j, piece in enumerate(pieces):
+
+            @pl.when(chosen_ref[k] == j)
+            def _(piece=piece, out_ref=out_ref, k=k):
+                pltpu.make_async_copy(piece, out_ref, sem.at[k]).start()
+
+    for k, out_ref in enumerate(outs):
+        pltpu.make_async_copy(pieces[0], out_ref, sem.at[k]).wait()
+
+
+def unpack_kernel(kind_ref, place_ref, *refs):
+    whole, pieces, refs = refs[:4], refs[4 : 4 + NZH], refs[4 + NZH :]
+    gate_ref, up_ref, down_ref, block, sem = refs
+    for kinds, ref in zip(((0,), (1,), (8,), (16,)), whole):
+
+        @pl.when(kind_ref[0] == kinds[0])
         def _(ref=ref):
-            gate_ref[...] = ref[0:SHARD, 0:HIDDEN]
-            up_ref[...] = ref[0:SHARD, HIDDEN:SIDE]
-            down_ref[:, 0:SIDE] = ref[SHARD : SHARD + DSHARD, :]
-            for j in range(3):
-                down_ref[32 * j : 32 * (j + 1), SIDE:WIDTH] = ref[
-                    SHARD + DSHARD : PACK, 512 * j : 512 * (j + 1)
-                ]
+            cp = pltpu.make_async_copy(ref, block, sem.at[NZH])
+            cp.start()
+            cp.wait()
+
+    @pl.when((kind_ref[0] == 2) | (kind_ref[0] == 4))
+    def _():
+        copies = []
+        for k, ref in enumerate(pieces):
+            at = pl.multiple_of(((place_ref[1] - k) & (NZH - 1)) * PIECE, PIECE)
+            cp = pltpu.make_async_copy(ref, block.at[pl.ds(at, PIECE)], sem.at[k])
+            cp.start()
+            copies.append(cp)
+        for cp in copies:
+            cp.wait()
+
+    gate_ref[...] = block[0:SHARD, 0:HIDDEN]
+    up_ref[...] = block[0:SHARD, HIDDEN:SIDE]
+    down_ref[:, 0:SIDE] = block[SHARD : SHARD + DSHARD, :]
+    for j in range(3):
+        down_ref[32 * j : 32 * (j + 1), SIDE:WIDTH] = block[
+            SHARD + DSHARD : PACK, 512 * j : 512 * (j + 1)
+        ]
 
 
 def dispatch_kernel(n, place_ref, *refs):
@@ -213,8 +273,8 @@
     return call(
         functools.partial(ffn_kernel, splits, block),
         [shape(r, WIDTH) for r in splits],
-        [SMEM] + [ANY] * (2 + len(groups)),
-        [ANY] * len(groups),
+        [SMEM] + [HBM] * (2 + len(groups)),
+        [HBM] * len(groups),
         "expert_ffn",
         scratch=[
             pltpu.VMEM((WIDTH, SIDE), BF),
@@ -279,13 +339,24 @@
     zl_me = lax.axis_index("zl")
     place = jnp.stack([x_me, zh_me, c_me, zl_me]).astype(jnp.int32)
 
-    near = call(prep_kernel, shape(ROWS + META, WIDTH), [VMEM] * 4, VMEM, "prep")(
-        tokens, norm_gain[None, :], expert_ids.T, route_weights.T
+    near, own, other, first = call(
+        prep_kernel,
+        [shape(ROWS + META, WIDTH)] + [shape(PACK, SIDE)] * 3,
+        [SMEM] + [HBM] * 7,
+        [VMEM] + [HBM] * 3,
+        "prep",
+        scratch=[
+            pltpu.VMEM((ROWS, WIDTH), BF),
+            pltpu.VMEM((1, WIDTH), F32),
+            pltpu.VMEM((TOP, ROWS), jnp.int32),
+            pltpu.VMEM((TOP, ROWS), F32),
+            pltpu.SemaphoreType.DMA((4,)),
+            pltpu.SemaphoreType.DMA((18,)),
+        ],
+    )(
+        place, tokens, norm_gain[None, :], expert_ids.T, route_weights.T,
+        gate_weight, up_weight, down_weight,
     )
-    near, place = fence(near, place)
-    own, other, first = call(
-        pack_kernel, [shape(PACK, SIDE)] * 3, [SMEM] + [VMEM] * 3, [VMEM] * 3, "pack"
-    )(place, gate_weight, up_weight, down_weight)
 
     own_full = lax.all_gather(own, "y", axis=0, tiled=False)
     swapped = partner(other, "zl", 1)
@@ -293,51 +364,63 @@
     p1, m1 = along_z(near, 1), along_z(near, -1)
     p2, m2 = along_z(p1, 1), along_z(m1, -1)
     d0, w0 = dispatch(place, (near, p1, m1))
+    hx1 = partner(first, "x", 1)
+    d0, hx1, swapped = fence(d0, hx1, swapped)
+    swap_full = lax.all_gather(swapped, "y", axis=0, tiled=False)
     r0 = in_plane(d0)
-    hx1 = partner(first, "x", 1)
     p3, m3 = along_z(p2, 1), along_z(m2, -1)
+    d1, w1 = dispatch(place, (p2, m2))
+    d1, r0, p3, m3 = fence(d1, r0, p3, m3)
+    r1 = in_plane(d1)
     far = along_z(p3, 1)
-    d1, w1 = dispatch(place, (p2, m2))
-    d1, r0, hx1, p3, m3, first, swapped = fence(d1, r0, hx1, p3, m3, first, swapped)
-    swap_full = lax.all_gather(swapped, "y", axis=0, tiled=False)
-    r1 = in_plane(d1)
+    far, first = fence(far, first)
+    cut = call(
+        cut_kernel, [shape(PIECE, SIDE)] * NZH, [SMEM, HBM], [HBM] * NZH, "cut",
+        scratch=[pltpu.SemaphoreType.DMA((NZH,))],
+    )(place, first)
+    held = [cut[0]] + [shift(cut[k], "zh", NZH, k) for k in range(1, NZH)]
     d2, w2 = dispatch(place, (p3, m3, far))
-    d2, r1, first = fence(d2, r1, first)
+    d2, r1 = fence(d2, r1)
     r2 = in_plane(d2)
-    hz1 = partner(first, "zh", 1)
-    r0, r1, r2, first = fence(r0, r1, r2, first)
-    hx2 = partner(first, "x", 2)
-    r0, r1, r2, first, hz1, hx2, own_full, swap_full = fence(
-        r0, r1, r2, first, hz1, hx2, own_full, swap_full
-    )
+    r0, r1, r2, first, *held = fence(r0, r1, r2, first, *held)
 
     (s2,) = ffn(place, own_full, swap_full, (r2,), 384)
-    hz2 = partner(first, "zh", 2)
-    s2, r1, r0 = fence(s2, r1, r0)
+    s2, r1, r0, *held = fence(s2, r1, r0, *held)
     b2 = in_plane(s2)
     s1, s0 = ffn(place, own_full, swap_full, (r1, r0), 320)
-    b2, s1, s0 = fence(b2, s1, s0)
+    turn = (zh_me + jnp.arange(NZH, dtype=jnp.int32)) & (NZH - 1)
+    matched = jnp.take(pair_list, (x_me * NZH + turn) * NC + c_me, mode="clip")
+    chosen = (zh_me - (matched >> 1)) & (NZH - 1)
+    picked = call(
+        pick_kernel, [shape(PIECE, SIDE)] * NZH, [SMEM] + [HBM] * NZH, [HBM] * NZH, "pick",
+        scratch=[pltpu.SemaphoreType.DMA((NZH,))],
+    )(chosen.astype(jnp.int32), *held)
+    held = [picked[0]] + [shift(picked[k], "zh", NZH, k) for k in range(1, NZH)]
+    b2, s1, s0, *held = fence(b2, s1, s0, *held)
 
     c_m3, c_p3, c_4 = combine(w2, b2, (F32, BF, BF))
     down, rise = along_z(c_4, -1), along_z(c_p3, 1)
     b1 = in_plane(s1)
     down = along_z(joined(down, c_m3), -1)
-    b1, s0, rise, hz2, hx1, hz1, hx2, first = fence(b1, s0, rise, hz2, hx1, hz1, hx2, first)
+    b1, s0, rise = fence(b1, s0, rise)
     b0 = in_plane(s0)
     c_m2, c_p2 = combine(w1, b1, (F32, F32))
     down = along_z(joined(down, c_m2), -1)
     rise = along_z(joined(rise, c_p2), 1)
-
+    b0, first, hx1, *held = fence(b0, first, hx1, *held)
+
+    hx2 = partner(first, "x", 2)
     hc = partner(first, "c", 1)
     me = (x_me * NZH + zh_me) * NC + c_me
     bits = jnp.sum(jnp.where(jnp.arange(pair_list.shape[0]) == me, pair_list ^ me, 0))
     new = call(
         unpack_kernel,
         [shape(SHARD, HIDDEN), shape(SHARD, HIDDEN), shape(DSHARD, WIDTH)],
-        [SMEM] + [VMEM] * 6,
+        [SMEM] * 2 + [HBM] * 8,
         [VMEM] * 3,
         "unpack",
-    )(bits.astype(jnp.int32).reshape(1), first, hc, hz1, hz2, hx1, hx2)
+        scratch=[pltpu.VMEM((PACK, SIDE), BF), pltpu.SemaphoreType.DMA((NZH + 1,))],
+    )(bits.astype(jnp.int32).reshape(1), place, first, hc, hx1, hx2, *held)
 
     c_0, c_m1, c_p1 = combine(w0, b0, (F32, F32, F32))
     down = along_z(joined(down, c_m1), -1)

time: 301 us -> 285 us (0.947)
  waiting for transfers between devices: 172 us -> 124 us
  starting transfers between devices: 55.9 us -> 70.5 us
  local copies, waits for them, and re-layouts: 14.3 us -> 27.9 us
    ppermute x6 -> x4, waiting for transfers between devices: 59.6 us -> 7.62 us  [partner(): return lax.ppermute(value, axis, [(i, i ^ bit) for i in range(count)])]
    ppermute x14 -> x20, waiting for transfers between devices: 84.1 us -> 112 us  [shift(): lax.ppermute(value, axes, [(i, (i + step) % count) for i in range(count)])]
    all_to_all x6, waiting for transfers between devices: 28.1 us -> 4.82 us  [across(): return lax.all_to_all(value, axis, split_axis=0, concat_axis=0, tiled=True)]
    ppermute x14 -> x20, starting transfers between devices: 21.6 us -> 36.5 us  [shift(): lax.ppermute(value, axes, [(i, (i + step) % count) for i in range(count)])]
    unnamed x48 -> x80, local copies, waits for them, and re-layouts: 14.3 us -> 27.3 us
  transfers between devices with their start and end apart: 28 -> 32, of which waited for: 17 -> 16; matrix products, arithmetic and copies ran while one was open for 2% -> 3% of each run, Pallas kernels for 8% -> 8%
where the time goes in v4:
time: 285 us; the launch traced here: 282 us
  waiting for transfers between devices  124 us (44%)
  starting transfers between devices  70.5 us (25%)
  Pallas kernels  35.8 us (13%)
  local copies, waits for them, and re-layouts  27.9 us (10%)
  between operations  14.3 us (5%)
  other arithmetic  9.29 us (3%)
    ppermute x20, waiting for transfers between devices, shift(): lax.ppermute(value, axes, [(i, (i + step) % count) for i in range(count)])  112 us
    ppermute x20, starting transfers between devices, shift(): lax.ppermute(value, axes, [(i, (i + step) % count) for i in range(count)])  36.5 us
    all_to_all x6, starting transfers between devices, across(): return lax.all_to_all(value, axis, split_axis=0, concat_axis=0, tiled=True)  29.1 us
    unnamed x80, local copies, waits for them, and re-layouts  27.3 us
    pallas_call x2, Pallas kernels, ffn(): call(functools.partial(ffn_kernel, splits, block), [shape(r, WIDTH) for r...  20.1 us
    ppermute x4, waiting for transfers between devices, partner(): return lax.ppermute(value, axis, [(i, i ^ bit) for i in range(count)])  7.62 us
    convert_element_type x5, other arithmetic, joined(): return (got.astype(F32) + mine).astype(BF)  6.52 us
  transfers between devices with their start and end apart: 32, of which 16 were waited for; matrix products, arithmetic and copies ran while one was open for 3% of the time, Pallas kernels for 8%

profile of v4, /device:TPU:22, one launch (start us, length us, event | category | flops | bytes accessed | tf_op | source)
XLA Modules:
  0.0 282.1 jit_solution(12966379476586451813)
XLA Ops:
  13.8 2.8 prep.1
  19.5 4.9 %collective-permute-start.2 = (bf16[104,2048]{1,0:T(8,128)(2,1)S(1)}, bf16[104,2048]{1,0:T(8,128)(2,1)S(1)}, u32[]{:S(2)}, u32[]{:S(2)}) collective-permute-start(bf16[104,2048]{1,0:T(8,128)(2,1)S(1)} %get-tuple-element.78.refs_0_), channel_id=1, source_target_pairs={{0,49},{1,0},{16,1},{17,16},{32,17},{33,32},{48,33},{49,48},{2,51}... | collective-permute-start | bytes 1277960 | tf_op jit(solution)/shard_map/ppermute | solution.py:36
  24.5 29.5 %collective-permute-done.2.refs_2_ = bf16[104,2048]{1,0:T(8,128)(2,1)S(1)} collective-permute-done((bf16[104,2048]{1,0:T(8,128)(2,1)S(1)}, bf16[104,2048]{1,0:T(8,128)(2,1)S(1)}, u32[]{:S(2)}, u32[]{:S(2)}) %collective-permute-start.2) | collective-permute-done | bytes 426016 | tf_op jit(solution)/shard_map/ppermute | solution.py:36
  54.0 2.6 dispatch.4
  58.3 4.8 %all-to-all-start = ((bf16[8,48,2048]{2,1,0:T(8,128)(2,1)}), bf16[8,48,2048]{2,1,0:T(8,128)(2,1)S(1)}, u32[]{:S(2)}, u32[]{:S(2)}) async-start(bf16[8,48,2048]{2,1,0:T(8,128)(2,1)} %bitcast.7), calls=%async_computation | async-start | bytes 3145728 | tf_op jit(solution)/shard_map/all_to_all | solution.py:52
  63.1 5.7 %collective-permute-start.3 = (bf16[104,2048]{1,0:T(8,128)(2,1)S(1)}, bf16[104,2048]{1,0:T(8,128)(2,1)S(1)}, u32[]{:S(2)}, u32[]{:S(2)}) collective-permute-start(bf16[104,2048]{1,0:T(8,128)(2,1)S(1)} %collective-permute-done.2.refs_2_), channel_id=1, source_target_pairs={{0,49},{1,0},{16,1},{17,16},{32,17},{33,32},{48,33},{49,48},{2,51}... | collective-permute-start | bytes 1277960 | tf_op jit(solution)/shard_map/ppermute | solution.py:36
  68.7 9.4 %collective-permute-done.3.refs_1_ = bf16[104,2048]{1,0:T(8,128)(2,1)S(1)} collective-permute-done((bf16[104,2048]{1,0:T(8,128)(2,1)S(1)}, bf16[104,2048]{1,0:T(8,128)(2,1)S(1)}, u32[]{:S(2)}, u32[]{:S(2)}) %collective-permute-start.3) | collective-permute-done | bytes 426016 | tf_op jit(solution)/shard_map/ppermute | solution.py:36
  78.1 3.7 %collective-permute-start.7 = (bf16[104,2048]{1,0:T(8,128)(2,1)S(1)}, bf16[104,2048]{1,0:T(8,128)(2,1)S(1)}, u32[]{:S(2)}, u32[]{:S(2)}) collective-permute-start(bf16[104,2048]{1,0:T(8,128)(2,1)S(1)} %collective-permute-done.3.refs_1_), channel_id=1, source_target_pairs={{0,49},{1,0},{16,1},{17,16},{32,17},{33,32},{48,33},{49,48},{2,51}... | collective-permute-start | bytes 1277960 | tf_op jit(solution)/shard_map/ppermute | solution.py:36
  84.7 5.7 %collective-permute-done.7.refs_1_ = bf16[104,2048]{1,0:T(8,128)(2,1)S(1)} collective-permute-done((bf16[104,2048]{1,0:T(8,128)(2,1)S(1)}, bf16[104,2048]{1,0:T(8,128)(2,1)S(1)}, u32[]{:S(2)}, u32[]{:S(2)}) %collective-permute-start.7) | collective-permute-done | bytes 426016 | tf_op jit(solution)/shard_map/ppermute | solution.py:36
  90.4 3.4 %collective-permute-done.6.refs_0_ = bf16[104,2048]{1,0:T(8,128)(2,1)S(1)} collective-permute-done((bf16[104,2048]{1,0:T(8,128)(2,1)S(1)}, bf16[104,2048]{1,0:T(8,128)(2,1)S(1)}, u32[]{:S(2)}, u32[]{:S(2)}) %collective-permute-start.6) | collective-permute-done | bytes 426016 | tf_op jit(solution)/shard_map/ppermute | solution.py:36
  93.8 4.8 %all-to-all-start.1 = ((bf16[8,32,2048]{2,1,0:T(8,128)(2,1)}), bf16[8,32,2048]{2,1,0:T(8,128)(2,1)S(1)}, u32[]{:S(2)}, u32[]{:S(2)}) async-start(bf16[8,32,2048]{2,1,0:T(8,128)(2,1)} %bitcast.36), calls=%async_computation.1 | async-start | bytes 2097152 | tf_op jit(solution)/shard_map/all_to_all | solution.py:52
  98.6 13.1 %collective-permute-done.8.refs_2_ = bf16[104,2048]{1,0:T(8,128)(2,1)S(1)} collective-permute-done((bf16[104,2048]{1,0:T(8,128)(2,1)S(1)}, bf16[104,2048]{1,0:T(8,128)(2,1)S(1)}, u32[]{:S(2)}, u32[]{:S(2)}) %collective-permute-start.8) | collective-permute-done | bytes 426016 | tf_op jit(solution)/shard_map/ppermute | solution.py:36
  116.1 4.9 %all-to-all-start.2 = ((bf16[8,48,2048]{2,1,0:T(8,128)(2,1)}), bf16[8,48,2048]{2,1,0:T(8,128)(2,1)S(1)}, u32[]{:S(2)}, u32[]{:S(2)}) async-start(bf16[8,48,2048]{2,1,0:T(8,128)(2,1)} %bitcast.33), calls=%async_computation.2 | async-start | bytes 3145728 | tf_op jit(solution)/shard_map/all_to_all | solution.py:52
  123.9 4.0 %collective-permute-start.11 = (bf16[96,1536]{1,0:T(8,128)(2,1)S(1)}, bf16[96,1536]{1,0:T(8,128)(2,1)S(1)}, u32[]{:S(2)}, u32[]{:S(2)}) collective-permute-start(bf16[96,1536]{1,0:T(8,128)(2,1)S(1)} %get-tuple-element.99), channel_id=1, source_target_pairs={{0,48},{16,0},{32,16},{48,32},{1,49},{17,1},{33,17},{49,33},{2,50}... | collective-permute-start | bytes 884744 | tf_op jit(solution)/shard_map/ppermute | solution.py:36
  127.9 11.7 %collective-permute-done.9.refs_1_ = bf16[96,1536]{1,0:T(8,128)(2,1)S(1)} collective-permute-done((bf16[96,1536]{1,0:T(8,128)(2,1)S(1)}, bf16[96,1536]{1,0:T(8,128)(2,1)S(1)}, u32[]{:S(2)}, u32[]{:S(2)}) %collective-permute-start.9) | collective-permute-done | bytes 294944 | tf_op jit(solution)/shard_map/ppermute | solution.py:36
  139.6 8.3 %collective-permute-done.10.refs_2_ = bf16[96,1536]{1,0:T(8,128)(2,1)S(1)} collective-permute-done((bf16[96,1536]{1,0:T(8,128)(2,1)S(1)}, bf16[96,1536]{1,0:T(8,128)(2,1)S(1)}, u32[]{:S(2)}, u32[]{:S(2)}) %collective-permute-start.10) | collective-permute-done | bytes 294944 | tf_op jit(solution)/shard_map/ppermute | solution.py:36
  148.6 4.0 %collective-permute-done.11.refs_3_ = bf16[96,1536]{1,0:T(8,128)(2,1)S(1)} collective-permute-done((bf16[96,1536]{1,0:T(8,128)(2,1)S(1)}, bf16[96,1536]{1,0:T(8,128)(2,1)S(1)}, u32[]{:S(2)}, u32[]{:S(2)}) %collective-permute-start.11) | collective-permute-done | bytes 294944 | tf_op jit(solution)/shard_map/ppermute | solution.py:36
  153.3 8.7 %expert_ffn.2 = bf16[384,2048]{1,0:T(8,128)(2,1)S(1)} custom-call(s32[4]{0:T(128)S(1)} %pad_add_fusion.place_ref, bf16[4,384,1536]{2,1,0:T(8,128)(2,1)} %bitcast.40, bf16[4,384,1536]{2,1,0:T(8,128)(2,1)} %bitcast.42, bf16[384,2048]{1,0:T(8,128)(2,1)S(1)} %bitcast.32), custom_call_target="tpu_custom_call" | custom-call | flops 3623878656 | bytes 15728640 | tf_op jit(solution)/shard_map/expert_ffn/pallas_call | solution.py:273
  163.2 4.9 %all-to-all-start.3 = ((bf16[8,48,2048]{2,1,0:T(8,128)(2,1)}), bf16[8,48,2048]{2,1,0:T(8,128)(2,1)S(1)}, u32[]{:S(2)}, u32[]{:S(2)}) async-start(bf16[8,48,2048]{2,1,0:T(8,128)(2,1)} %bitcast.31), calls=%async_computation.3 | async-start | bytes 3145728 | tf_op jit(solution)/shard_map/all_to_all | solution.py:52
  173.8 3.0 %collective-permute-start.13 = (bf16[96,1536]{1,0:T(8,128)(2,1)S(1)}, bf16[96,1536]{1,0:T(8,128)(2,1)S(1)}, u32[]{:S(2)}, u32[]{:S(2)}) collective-permute-start(bf16[96,1536]{1,0:T(8,128)(2,1)S(1)} %get-tuple-element.118), channel_id=1, source_target_pairs={{0,32},{16,48},{32,0},{48,16},{1,33},{17,49},{33,1},{49,17},{2,34}... | collective-permute-start | bytes 884744 | tf_op jit(solution)/shard_map/ppermute | solution.py:36
  181.2 11.4 %expert_ffn.3 = (bf16[256,2048]{1,0:T(8,128)(2,1)S(1)}, bf16[384,2048]{1,0:T(8,128)(2,1)S(1)}) custom-call(s32[4]{0:T(128)S(1)} %pad_add_fusion.place_ref, bf16[4,384,1536]{2,1,0:T(8,128)(2,1)} %bitcast.41, bf16[4,384,1536]{2,1,0:T(8,128)(2,1)} %bitcast.43, bf16[256,2048]{1,0:T(8,128)(2,1)S(1)} %bitcast.34, bf16[384,2048]{1,0:T(8,128)(2,1)S(1)} %bitcast.29), custom_call_target="tpu_custom_call" | custom-call | flops 6039797760 | bytes 15728640 | tf_op jit(solution)/shard_map/expert_ffn/pallas_call | solution.py:273
  199.2 4.8 %all-to-all-start.4 = ((bf16[8,32,2048]{2,1,0:T(8,128)(2,1)}), bf16[8,32,2048]{2,1,0:T(8,128)(2,1)}, u32[]{:S(2)}, u32[]{:S(2)}) async-start(bf16[8,32,2048]{2,1,0:T(8,128)(2,1)} %bitcast.35), calls=%async_computation.4 | async-start | bytes 2097152 | tf_op jit(solution)/shard_map/all_to_all | solution.py:52
  206.1 3.2 %collective-permute-start.15 = (bf16[96,2048]{1,0:T(8,128)(2,1)}, bf16[96,2048]{1,0:T(8,128)(2,1)}, u32[]{:S(2)}, u32[]{:S(2)}) collective-permute-start(bf16[96,2048]{1,0:T(8,128)(2,1)} %get-tuple-element.121), channel_id=1, source_target_pairs={{0,49},{1,0},{16,1},{17,16},{32,17},{33,32},{48,33},{49,48},{2,51}... | collective-permute-start | bytes 1179656 | tf_op jit(solution)/shard_map/ppermute | solution.py:36
  209.4 9.1 %collective-permute-done.17 = bf16[96,2048]{1,0:T(8,128)(2,1)S(1)} collective-permute-done((bf16[96,2048]{1,0:T(8,128)(2,1)S(1)}, bf16[96,2048]{1,0:T(8,128)(2,1)S(1)}, u32[]{:S(2)}, u32[]{:S(2)}) %collective-permute-start.17) | collective-permute-done | bytes 393248 | tf_op jit(solution)/shard_map/ppermute | solution.py:36
  219.3 4.8 %all-to-all-start.5 = ((bf16[8,48,2048]{2,1,0:T(8,128)(2,1)}), bf16[8,48,2048]{2,1,0:T(8,128)(2,1)S(1)}, u32[]{:S(2)}, u32[]{:S(2)}) async-start(bf16[8,48,2048]{2,1,0:T(8,128)(2,1)} %bitcast.30), calls=%async_computation.5 | async-start | bytes 3145728 | tf_op jit(solution)/shard_map/all_to_all | solution.py:52
  229.7 6.7 %collective-permute-done.16 = bf16[96,2048]{1,0:T(8,128)(2,1)S(1)} collective-permute-done((bf16[96,2048]{1,0:T(8,128)(2,1)S(1)}, bf16[96,2048]{1,0:T(8,128)(2,1)S(1)}, u32[]{:S(2)}, u32[]{:S(2)}) %collective-permute-start.16) | collective-permute-done | bytes 393248 | tf_op jit(solution)/shard_map/ppermute | solution.py:36
  238.8 4.8 %all-to-all-done.5 = bf16[8,48,2048]{2,1,0:T(8,128)(2,1)S(1)} async-done(((bf16[8,48,2048]{2,1,0:T(8,128)(2,1)}), bf16[8,48,2048]{2,1,0:T(8,128)(2,1)S(1)}, u32[]{:S(2)}, u32[]{:S(2)}) %all-to-all-start.5) | async-done | bytes 1572896 | tf_op jit(solution)/shard_map/all_to_all | solution.py:52
  243.6 2.1 collective-permute-start.23
  250.8 3.2 %collective-permute-start.19 = (bf16[96,2048]{1,0:T(8,128)(2,1)}, bf16[96,2048]{1,0:T(8,128)(2,1)}, u32[]{:S(2)}, u32[]{:S(2)}) collective-permute-start(bf16[96,2048]{1,0:T(8,128)(2,1)} %add_convert_fusion.3), channel_id=1, source_target_pairs={{0,49},{1,0},{16,1},{17,16},{32,17},{33,32},{48,33},{49,48},{2,51}... | collective-permute-start | bytes 1179656 | tf_op jit(solution)/shard_map/ppermute | solution.py:36
  254.7 7.2 %collective-permute-done.21 = bf16[96,2048]{1,0:T(8,128)(2,1)} collective-permute-done((bf16[96,2048]{1,0:T(8,128)(2,1)}, bf16[96,2048]{1,0:T(8,128)(2,1)}, u32[]{:S(2)}, u32[]{:S(2)}) %collective-permute-start.21) | collective-permute-done | bytes 393248 | tf_op jit(solution)/shard_map/ppermute | solution.py:36
  265.1 7.6 %collective-permute-done.23.refs_3_ = bf16[384,1536]{1,0:T(8,128)(2,1)} collective-permute-done((bf16[384,1536]{1,0:T(8,128)(2,1)S(1)}, bf16[384,1536]{1,0:T(8,128)(2,1)}, u32[]{:S(2)}, u32[]{:S(2)}) %collective-permute-start.23) | collective-permute-done | bytes 1179680 | tf_op jit(solution)/shard_map/ppermute | solution.py:328
  272.8 2.5 unpack.1
  (138 shorter events, 60.3 us)
Async XLA Ops:
  7.2 146.1 %all-gather.5.cloned.1.call-start = ((), (), s32[]{:S(2)}) async-start(), calls=%async_computation.6 | async-start | bytes 5898240 | tf_op jit(solution)/shard_map/all_gather | solution.py:361
  16.6 136.7 %all-gather.7.cloned.1.call-start = ((), (), s32[]{:S(2)}) async-start(), calls=%async_computation.7 | async-start | bytes 5898240 | tf_op jit(solution)/shard_map/all_gather | solution.py:369
  16.7 40.6 %collective-permute-start.5 = (bf16[384,1536]{1,0:T(8,128)(2,1)}, bf16[384,1536]{1,0:T(8,128)(2,1)}, u32[]{:S(2)}, u32[]{:S(2)}) collective-permute-start(bf16[384,1536]{1,0:T(8,128)(2,1)} %get-tuple-element.82), channel_id=1, source_target_pairs={{0,1},{1,0},{2,3},{3,2},{4,5},{5,4},{6,7},{7,6},{8,9},{9,8},{10,11... | collective-permute-start | bytes 3538952 | tf_op jit(solution)/shard_map/ppermute | solution.py:328
  18.7 38.6 %collective-permute-start.4 = (bf16[384,1536]{1,0:T(8,128)(2,1)}, bf16[384,1536]{1,0:T(8,128)(2,1)S(1)}, u32[]{:S(2)}, u32[]{:S(2)}) collective-permute-start(bf16[384,1536]{1,0:T(8,128)(2,1)} %get-tuple-element.143.first_ref.refs_0_), channel_id=1, source_target_pairs={{0,64},{64,0},{128,192},{192,128},{1,65},{65,1},{129,193},{193,129... | collective-permute-start | bytes 3538952 | tf_op jit(solution)/shard_map/ppermute | solution.py:328
  19.5 34.5 %collective-permute-start.2 = (bf16[104,2048]{1,0:T(8,128)(2,1)S(1)}, bf16[104,2048]{1,0:T(8,128)(2,1)S(1)}, u32[]{:S(2)}, u32[]{:S(2)}) collective-permute-start(bf16[104,2048]{1,0:T(8,128)(2,1)S(1)} %get-tuple-element.78.refs_0_), channel_id=1, source_target_pairs={{0,49},{1,0},{16,1},{17,16},{32,17},{33,32},{48,33},{49,48},{2,51}... | collective-permute-start | bytes 1277960 | tf_op jit(solution)/shard_map/ppermute | solution.py:36
  24.4 29.5 %collective-permute-start = (bf16[104,2048]{1,0:T(8,128)(2,1)S(1)}, bf16[104,2048]{1,0:T(8,128)(2,1)S(1)}, u32[]{:S(2)}, u32[]{:S(2)}) collective-permute-start(bf16[104,2048]{1,0:T(8,128)(2,1)S(1)} %get-tuple-element.78.refs_0_), channel_id=1, source_target_pairs={{0,1},{1,16},{16,17},{17,32},{32,33},{33,48},{48,49},{49,0},{2,3},... | collective-permute-start | bytes 1277960 | tf_op jit(solution)/shard_map/ppermute | solution.py:36
  58.3 35.5 %all-to-all-start = ((bf16[8,48,2048]{2,1,0:T(8,128)(2,1)}), bf16[8,48,2048]{2,1,0:T(8,128)(2,1)S(1)}, u32[]{:S(2)}, u32[]{:S(2)}) async-start(bf16[8,48,2048]{2,1,0:T(8,128)(2,1)} %bitcast.7), calls=%async_computation | async-start | bytes 3145728 | tf_op jit(solution)/shard_map/all_to_all | solution.py:52
  63.1 15.1 %collective-permute-start.3 = (bf16[104,2048]{1,0:T(8,128)(2,1)S(1)}, bf16[104,2048]{1,0:T(8,128)(2,1)S(1)}, u32[]{:S(2)}, u32[]{:S(2)}) collective-permute-start(bf16[104,2048]{1,0:T(8,128)(2,1)S(1)} %collective-permute-done.2.refs_2_), channel_id=1, source_target_pairs={{0,49},{1,0},{16,1},{17,16},{32,17},{33,32},{48,33},{49,48},{2,51}... | collective-permute-start | bytes 1277960 | tf_op jit(solution)/shard_map/ppermute | solution.py:36
  68.7 13.1 %collective-permute-start.1 = (bf16[104,2048]{1,0:T(8,128)(2,1)S(1)}, bf16[104,2048]{1,0:T(8,128)(2,1)S(1)}, u32[]{:S(2)}, u32[]{:S(2)}) collective-permute-start(bf16[104,2048]{1,0:T(8,128)(2,1)S(1)} %collective-permute-done.refs_1_), channel_id=1, source_target_pairs={{0,1},{1,16},{16,17},{17,32},{32,33},{33,48},{48,49},{49,0},{2,3},... | collective-permute-start | bytes 1277960 | tf_op jit(solution)/shard_map/ppermute | solution.py:36
  78.1 12.3 %collective-permute-start.7 = (bf16[104,2048]{1,0:T(8,128)(2,1)S(1)}, bf16[104,2048]{1,0:T(8,128)(2,1)S(1)}, u32[]{:S(2)}, u32[]{:S(2)}) collective-permute-start(bf16[104,2048]{1,0:T(8,128)(2,1)S(1)} %collective-permute-done.3.refs_1_), channel_id=1, source_target_pairs={{0,49},{1,0},{16,1},{17,16},{32,17},{33,32},{48,33},{49,48},{2,51}... | collective-permute-start | bytes 1277960 | tf_op jit(solution)/shard_map/ppermute | solution.py:36
  81.8 12.0 %collective-permute-start.6 = (bf16[104,2048]{1,0:T(8,128)(2,1)S(1)}, bf16[104,2048]{1,0:T(8,128)(2,1)S(1)}, u32[]{:S(2)}, u32[]{:S(2)}) collective-permute-start(bf16[104,2048]{1,0:T(8,128)(2,1)S(1)} %collective-permute-done.1.refs_0_), channel_id=1, source_target_pairs={{0,1},{1,16},{16,17},{17,32},{32,33},{33,48},{48,49},{49,0},{2,3},... | collective-permute-start | bytes 1277960 | tf_op jit(solution)/shard_map/ppermute | solution.py:36
  93.8 21.3 %all-to-all-start.1 = ((bf16[8,32,2048]{2,1,0:T(8,128)(2,1)}), bf16[8,32,2048]{2,1,0:T(8,128)(2,1)S(1)}, u32[]{:S(2)}, u32[]{:S(2)}) async-start(bf16[8,32,2048]{2,1,0:T(8,128)(2,1)} %bitcast.36), calls=%async_computation.1 | async-start | bytes 2097152 | tf_op jit(solution)/shard_map/all_to_all | solution.py:52
  98.6 13.1 %collective-permute-start.8 = (bf16[104,2048]{1,0:T(8,128)(2,1)S(1)}, bf16[104,2048]{1,0:T(8,128)(2,1)S(1)}, u32[]{:S(2)}, u32[]{:S(2)}) collective-permute-start(bf16[104,2048]{1,0:T(8,128)(2,1)S(1)} %collective-permute-done.6.refs_0_), channel_id=1, source_target_pairs={{0,1},{1,16},{16,17},{17,32},{32,33},{33,48},{48,49},{49,0},{2,3},... | collective-permute-start | bytes 1277960 | tf_op jit(solution)/shard_map/ppermute | solution.py:36
  116.1 37.2 %all-to-all-start.2 = ((bf16[8,48,2048]{2,1,0:T(8,128)(2,1)}), bf16[8,48,2048]{2,1,0:T(8,128)(2,1)S(1)}, u32[]{:S(2)}, u32[]{:S(2)}) async-start(bf16[8,48,2048]{2,1,0:T(8,128)(2,1)} %bitcast.33), calls=%async_computation.2 | async-start | bytes 3145728 | tf_op jit(solution)/shard_map/all_to_all | solution.py:52
  121.9 17.7 %collective-permute-start.9 = (bf16[96,1536]{1,0:T(8,128)(2,1)S(1)}, bf16[96,1536]{1,0:T(8,128)(2,1)S(1)}, u32[]{:S(2)}, u32[]{:S(2)}) collective-permute-start(bf16[96,1536]{1,0:T(8,128)(2,1)S(1)} %get-tuple-element.97), channel_id=1, source_target_pairs={{0,16},{16,32},{32,48},{48,0},{1,17},{17,33},{33,49},{49,1},{2,18}... | collective-permute-start | bytes 884744 | tf_op jit(solution)/shard_map/ppermute | solution.py:36
  122.0 25.9 %collective-permute-start.10 = (bf16[96,1536]{1,0:T(8,128)(2,1)S(1)}, bf16[96,1536]{1,0:T(8,128)(2,1)S(1)}, u32[]{:S(2)}, u32[]{:S(2)}) collective-permute-start(bf16[96,1536]{1,0:T(8,128)(2,1)S(1)} %get-tuple-element.98), channel_id=1, source_target_pairs={{0,32},{16,48},{32,0},{48,16},{1,33},{17,49},{33,1},{49,17},{2,34}... | collective-permute-start | bytes 884744 | tf_op jit(solution)/shard_map/ppermute | solution.py:36
  123.9 28.7 %collective-permute-start.11 = (bf16[96,1536]{1,0:T(8,128)(2,1)S(1)}, bf16[96,1536]{1,0:T(8,128)(2,1)S(1)}, u32[]{:S(2)}, u32[]{:S(2)}) collective-permute-start(bf16[96,1536]{1,0:T(8,128)(2,1)S(1)} %get-tuple-element.99), channel_id=1, source_target_pairs={{0,48},{16,0},{32,16},{48,32},{1,49},{17,1},{33,17},{49,33},{2,50}... | collective-permute-start | bytes 884744 | tf_op jit(solution)/shard_map/ppermute | solution.py:36
  163.2 36.0 %all-to-all-start.3 = ((bf16[8,48,2048]{2,1,0:T(8,128)(2,1)}), bf16[8,48,2048]{2,1,0:T(8,128)(2,1)S(1)}, u32[]{:S(2)}, u32[]{:S(2)}) async-start(bf16[8,48,2048]{2,1,0:T(8,128)(2,1)} %bitcast.31), calls=%async_computation.3 | async-start | bytes 3145728 | tf_op jit(solution)/shard_map/all_to_all | solution.py:52
  172.4 22.3 %collective-permute-start.12 = (bf16[96,1536]{1,0:T(8,128)(2,1)S(1)}, bf16[96,1536]{1,0:T(8,128)(2,1)S(1)}, u32[]{:S(2)}, u32[]{:S(2)}) collective-permute-start(bf16[96,1536]{1,0:T(8,128)(2,1)S(1)} %get-tuple-element.117), channel_id=1, source_target_pairs={{0,16},{16,32},{32,48},{48,0},{1,17},{17,33},{33,49},{49,1},{2,18}... | collective-permute-start | bytes 884744 | tf_op jit(solution)/shard_map/ppermute | solution.py:36
  173.8 23.1 %collective-permute-start.13 = (bf16[96,1536]{1,0:T(8,128)(2,1)S(1)}, bf16[96,1536]{1,0:T(8,128)(2,1)S(1)}, u32[]{:S(2)}, u32[]{:S(2)}) collective-permute-start(bf16[96,1536]{1,0:T(8,128)(2,1)S(1)} %get-tuple-element.118), channel_id=1, source_target_pairs={{0,32},{16,48},{32,0},{48,16},{1,33},{17,49},{33,1},{49,17},{2,34}... | collective-permute-start | bytes 884744 | tf_op jit(solution)/shard_map/ppermute | solution.py:36
  176.8 21.7 %collective-permute-start.14 = (bf16[96,1536]{1,0:T(8,128)(2,1)S(1)}, bf16[96,1536]{1,0:T(8,128)(2,1)S(1)}, u32[]{:S(2)}, u32[]{:S(2)}) collective-permute-start(bf16[96,1536]{1,0:T(8,128)(2,1)S(1)} %get-tuple-element.119), channel_id=1, source_target_pairs={{0,48},{16,0},{32,16},{48,32},{1,49},{17,1},{33,17},{49,33},{2,50}... | collective-permute-start | bytes 884744 | tf_op jit(solution)/shard_map/ppermute | solution.py:36
  199.2 19.3 %all-to-all-start.4 = ((bf16[8,32,2048]{2,1,0:T(8,128)(2,1)}), bf16[8,32,2048]{2,1,0:T(8,128)(2,1)}, u32[]{:S(2)}, u32[]{:S(2)}) async-start(bf16[8,32,2048]{2,1,0:T(8,128)(2,1)} %bitcast.35), calls=%async_computation.4 | async-start | bytes 2097152 | tf_op jit(solution)/shard_map/all_to_all | solution.py:52
  206.1 12.4 %collective-permute-start.17 = (bf16[96,2048]{1,0:T(8,128)(2,1)S(1)}, bf16[96,2048]{1,0:T(8,128)(2,1)S(1)}, u32[]{:S(2)}, u32[]{:S(2)}) collective-permute-start(bf16[96,2048]{1,0:T(8,128)(2,1)S(1)} %get-tuple-element.126), channel_id=1, source_target_pairs={{0,1},{1,16},{16,17},{17,32},{32,33},{33,48},{48,49},{49,0},{2,3},... | collective-permute-start | bytes 1179656 | tf_op jit(solution)/shard_map/ppermute | solution.py:36
  206.1 17.9 %collective-permute-start.15 = (bf16[96,2048]{1,0:T(8,128)(2,1)}, bf16[96,2048]{1,0:T(8,128)(2,1)}, u32[]{:S(2)}, u32[]{:S(2)}) collective-permute-start(bf16[96,2048]{1,0:T(8,128)(2,1)} %get-tuple-element.121), channel_id=1, source_target_pairs={{0,49},{1,0},{16,1},{17,16},{32,17},{33,32},{48,33},{49,48},{2,51}... | collective-permute-start | bytes 1179656 | tf_op jit(solution)/shard_map/ppermute | solution.py:36
  219.3 24.3 %all-to-all-start.5 = ((bf16[8,48,2048]{2,1,0:T(8,128)(2,1)}), bf16[8,48,2048]{2,1,0:T(8,128)(2,1)S(1)}, u32[]{:S(2)}, u32[]{:S(2)}) async-start(bf16[8,48,2048]{2,1,0:T(8,128)(2,1)} %bitcast.30), calls=%async_computation.5 | async-start | bytes 3145728 | tf_op jit(solution)/shard_map/all_to_all | solution.py:52
  225.2 11.2 %collective-permute-start.16 = (bf16[96,2048]{1,0:T(8,128)(2,1)S(1)}, bf16[96,2048]{1,0:T(8,128)(2,1)S(1)}, u32[]{:S(2)}, u32[]{:S(2)}) collective-permute-start(bf16[96,2048]{1,0:T(8,128)(2,1)S(1)} %add_convert_fusion.5), channel_id=1, source_target_pairs={{0,49},{1,0},{16,1},{17,16},{32,17},{33,32},{48,33},{49,48},{2,51}... | collective-permute-start | bytes 1179656 | tf_op jit(solution)/shard_map/ppermute | solution.py:36
  227.7 19.3 %collective-permute-start.20 = (bf16[96,2048]{1,0:T(8,128)(2,1)}, bf16[96,2048]{1,0:T(8,128)(2,1)}, u32[]{:S(2)}, u32[]{:S(2)}) collective-permute-start(bf16[96,2048]{1,0:T(8,128)(2,1)} %add_convert_fusion.2), channel_id=1, source_target_pairs={{0,1},{1,16},{16,17},{17,32},{32,33},{33,48},{48,49},{49,0},{2,3},... | collective-permute-start | bytes 1179656 | tf_op jit(solution)/shard_map/ppermute | solution.py:36
  237.3 11.6 %collective-permute-start.18 = (bf16[96,2048]{1,0:T(8,128)(2,1)}, bf16[96,2048]{1,0:T(8,128)(2,1)}, u32[]{:S(2)}, u32[]{:S(2)}) collective-permute-start(bf16[96,2048]{1,0:T(8,128)(2,1)} %add_convert_fusion.4), channel_id=1, source_target_pairs={{0,49},{1,0},{16,1},{17,16},{32,17},{33,32},{48,33},{49,48},{2,51}... | collective-permute-start | bytes 1179656 | tf_op jit(solution)/shard_map/ppermute | solution.py:36
  243.6 29.1 %collective-permute-start.23 = (bf16[384,1536]{1,0:T(8,128)(2,1)S(1)}, bf16[384,1536]{1,0:T(8,128)(2,1)}, u32[]{:S(2)}, u32[]{:S(2)}) collective-permute-start(bf16[384,1536]{1,0:T(8,128)(2,1)S(1)} %copy-done), channel_id=1, source_target_pairs={{0,128},{64,192},{128,0},{192,64},{1,129},{65,193},{129,1},{193,65... | collective-permute-start | bytes 3538952 | tf_op jit(solution)/shard_map/ppermute | solution.py:328
  245.7 27.1 %collective-permute-start.22 = (bf16[384,1536]{1,0:T(8,128)(2,1)S(1)}, bf16[384,1536]{1,0:T(8,128)(2,1)}, u32[]{:S(2)}, u32[]{:S(2)}) collective-permute-start(bf16[384,1536]{1,0:T(8,128)(2,1)S(1)} %copy-done), channel_id=1, source_target_pairs={{0,8},{8,0},{1,9},{9,1},{2,10},{10,2},{3,11},{11,3},{4,12},{12,4},... | collective-permute-start | bytes 3538952 | tf_op jit(solution)/shard_map/ppermute | solution.py:328
  248.9 13.1 %collective-permute-start.21 = (bf16[96,2048]{1,0:T(8,128)(2,1)}, bf16[96,2048]{1,0:T(8,128)(2,1)}, u32[]{:S(2)}, u32[]{:S(2)}) collective-permute-start(bf16[96,2048]{1,0:T(8,128)(2,1)} %add_convert_fusion.1), channel_id=1, source_target_pairs={{0,1},{1,16},{16,17},{17,32},{32,33},{33,48},{48,49},{49,0},{2,3},... | collective-permute-start | bytes 1179656 | tf_op jit(solution)/shard_map/ppermute | solution.py:36
  250.8 12.3 %collective-permute-start.19 = (bf16[96,2048]{1,0:T(8,128)(2,1)}, bf16[96,2048]{1,0:T(8,128)(2,1)}, u32[]{:S(2)}, u32[]{:S(2)}) collective-permute-start(bf16[96,2048]{1,0:T(8,128)(2,1)} %add_convert_fusion.3), channel_id=1, source_target_pairs={{0,49},{1,0},{16,1},{17,16},{32,17},{33,32},{48,33},{49,48},{2,51}... | collective-permute-start | bytes 1179656 | tf_op jit(solution)/shard_map/ppermute | solution.py:36
  (40 other events, 164.5 us)
Sparse Core Ops, SparseCore 0:
  16.7 57.0 all-gather.4
  75.6 55.6 all-gather.6

commit v5 on v4

--- a/solution.py
+++ b/solution.py
@@ -272,7 +272,7 @@
     total = sum(splits)
     return call(
         functools.partial(ffn_kernel, splits, block),
-        [shape(r, WIDTH) for r in splits],
+        [pltpu.HBM((r, WIDTH), BF) for r in splits],
         [SMEM] + [HBM] * (2 + len(groups)),
         [HBM] * len(groups),
         "expert_ffn",
@@ -354,23 +354,30 @@
             pltpu.SemaphoreType.DMA((18,)),
         ],
     )(
-        place, tokens, norm_gain[None, :], expert_ids.T, route_weights.T,
-        gate_weight, up_weight, down_weight,
+        place, *(
+            pltpu.with_memory_space_constraint(v, pltpu.HBM)
+            for v in (
+                tokens, norm_gain[None, :], expert_ids.T, route_weights.T,
+                gate_weight, up_weight, down_weight,
+            )
+        )
     )
 
     own_full = lax.all_gather(own, "y", axis=0, tiled=False)
+
+    p1, m1 = along_z(near, 1), along_z(near, -1)
+    p1, m1, other = fence(p1, m1, other)
     swapped = partner(other, "zl", 1)
-
-    p1, m1 = along_z(near, 1), along_z(near, -1)
     p2, m2 = along_z(p1, 1), along_z(m1, -1)
     d0, w0 = dispatch(place, (near, p1, m1))
     hx1 = partner(first, "x", 1)
-    d0, hx1, swapped = fence(d0, hx1, swapped)
-    swap_full = lax.all_gather(swapped, "y", axis=0, tiled=False)
+    d0, hx1 = fence(d0, hx1)
     r0 = in_plane(d0)
+    p2, m2, swapped = fence(p2, m2, swapped)
     p3, m3 = along_z(p2, 1), along_z(m2, -1)
     d1, w1 = dispatch(place, (p2, m2))
-    d1, r0, p3, m3 = fence(d1, r0, p3, m3)
+    d1, r0, p3, m3, swapped = fence(d1, r0, p3, m3, swapped)
+    swap_full = lax.all_gather(swapped, "y", axis=0, tiled=False)
     r1 = in_plane(d1)
     far = along_z(p3, 1)
     far, first = fence(far, first)
@@ -384,10 +391,12 @@
     r2 = in_plane(d2)
     r0, r1, r2, first, *held = fence(r0, r1, r2, first, *held)
 
+    hx2 = partner(first, "x", 2)
     (s2,) = ffn(place, own_full, swap_full, (r2,), 384)
-    s2, r1, r0, *held = fence(s2, r1, r0, *held)
+    s2, r1, r0, hx2, *held = fence(s2, r1, r0, hx2, *held)
     b2 = in_plane(s2)
     s1, s0 = ffn(place, own_full, swap_full, (r1, r0), 320)
+    b2, s1, s0, *held = fence(b2, s1, s0, *held)
     turn = (zh_me + jnp.arange(NZH, dtype=jnp.int32)) & (NZH - 1)
     matched = jnp.take(pair_list, (x_me * NZH + turn) * NC + c_me, mode="clip")
     chosen = (zh_me - (matched >> 1)) & (NZH - 1)
@@ -396,7 +405,6 @@
         scratch=[pltpu.SemaphoreType.DMA((NZH,))],
     )(chosen.astype(jnp.int32), *held)
     held = [picked[0]] + [shift(picked[k], "zh", NZH, k) for k in range(1, NZH)]
-    b2, s1, s0, *held = fence(b2, s1, s0, *held)
 
     c_m3, c_p3, c_4 = combine(w2, b2, (F32, BF, BF))
     down, rise = along_z(c_4, -1), along_z(c_p3, 1)
@@ -409,7 +417,6 @@
     rise = along_z(joined(rise, c_p2), 1)
     b0, first, hx1, *held = fence(b0, first, hx1, *held)
 
-    hx2 = partner(first, "x", 2)
     hc = partner(first, "c", 1)
     me = (x_me * NZH + zh_me) * NC + c_me
     bits = jnp.sum(jnp.where(jnp.arange(pair_list.shape[0]) == me, pair_list ^ me, 0))

time: 285 us -> 359 us (1.26)
  Pallas kernels: 35.8 us -> 109 us
  waiting for transfers between devices: 124 us -> 132 us
  local copies, waits for them, and re-layouts: 27.9 us -> 21.1 us
    pallas_call x1, Pallas kernels: 2.82 us -> 73.3 us  [body(): call(prep_kernel, [shape(ROWS + META, WIDTH)] + [shape(PACK, SIDE)] * 3,...]
    ppermute x4, waiting for transfers between devices: 7.62 us -> 23.8 us  [partner(): return lax.ppermute(value, axis, [(i, i ^ bit) for i in range(count)])]
    ppermute x20, waiting for transfers between devices: 112 us -> 103 us  [shift(): lax.ppermute(value, axes, [(i, (i + step) % count) for i in range(count)])]
    unnamed x80 -> x66, local copies, waits for them, and re-layouts: 27.3 us -> 20.5 us
  transfers between devices with their start and end apart: 32 -> 32, of which waited for: 16 -> 15; matrix products, arithmetic and copies ran while one was open for 3% -> 3% of each run, Pallas kernels for 8% -> 9%
where the time goes in v5:
time: 359 us; the launch traced here: 358 us
  waiting for transfers between devices  132 us (37%)
  Pallas kernels  109 us (30%)
  starting transfers between devices  72.2 us (20%)
  local copies, waits for them, and re-layouts  21.1 us (6%)
  between operations  14.3 us (4%)
  other arithmetic  9.04 us (3%)
    ppermute x20, waiting for transfers between devices, shift(): lax.ppermute(value, axes, [(i, (i + step) % count) for i in range(count)])  103 us
    pallas_call x1, Pallas kernels, body(): call(prep_kernel, [shape(ROWS + META, WIDTH)] + [shape(PACK, SIDE)] * 3,...  73.3 us
    ppermute x20, starting transfers between devices, shift(): lax.ppermute(value, axes, [(i, (i + step) % count) for i in range(count)])  39 us
    all_to_all x6, starting transfers between devices, across(): return lax.all_to_all(value, axis, split_axis=0, concat_axis=0, tiled=True)  30.8 us
    ppermute x4, waiting for transfers between devices, partner(): return lax.ppermute(value, axis, [(i, i ^ bit) for i in range(count)])  23.8 us
    pallas_call x2, Pallas kernels, ffn(): call(functools.partial(ffn_kernel, splits, block), [pltpu.HBM((r, WIDTH),...  22.6 us
    unnamed x66, local copies, waits for them, and re-layouts  20.5 us
  transfers between devices with their start and end apart: 32, of which 15 were waited for; matrix products, arithmetic and copies ran while one was open for 3% of the time, Pallas kernels for 9%

profile of v5, /device:TPU:22, one launch (start us, length us, event | category | flops | bytes accessed | tf_op | source)
XLA Modules:
  0.0 357.8 jit_solution(4124587768018560204)
XLA Ops:
  7.3 73.3 %prep.1 = (bf16[104,2048]{1,0:T(8,128)(2,1)S(1)}, bf16[384,1536]{1,0:T(8,128)(2,1)}, bf16[384,1536]{1,0:T(8,128)(2,1)}, bf16[384,1536]{1,0:T(8,128)(2,1)S(1)}) custom-call(s32[4]{0:T(128)S(1)} %pad_add_fusion.place_ref, bf16[96,2048]{1,0:T(8,128)(2,1)} %tokens_ref.1, f32[1,2048]{1,0:T(1,128)} %bitcast.37, s32[8,96]{1,0:T(8,128)} %bitcast.38, ...), custom_call_target="tpu_custom_call" | custom-call | tf_op jit(solution)/shard_map/prep/pallas_call | solution.py:342
  81.6 5.9 %collective-permute-start.1 = (bf16[104,2048]{1,0:T(8,128)(2,1)S(1)}, bf16[104,2048]{1,0:T(8,128)(2,1)S(1)}, u32[]{:S(2)}, u32[]{:S(2)}) collective-permute-start(bf16[104,2048]{1,0:T(8,128)(2,1)S(1)} %get-tuple-element.85.refs_0_), channel_id=1, source_target_pairs={{0,49},{1,0},{16,1},{17,16},{32,17},{33,32},{48,33},{49,48},{2,51}... | collective-permute-start | bytes 1277960 | tf_op jit(solution)/shard_map/ppermute | solution.py:36
  87.4 8.8 %collective-permute-done.1.refs_2_ = bf16[104,2048]{1,0:T(8,128)(2,1)S(1)} collective-permute-done((bf16[104,2048]{1,0:T(8,128)(2,1)S(1)}, bf16[104,2048]{1,0:T(8,128)(2,1)S(1)}, u32[]{:S(2)}, u32[]{:S(2)}) %collective-permute-start.1) | collective-permute-done | bytes 426016 | tf_op jit(solution)/shard_map/ppermute | solution.py:36
  96.2 3.4 collective-permute-done.refs_1_
  103.0 5.5 %collective-permute-done.5.refs_2_ = bf16[384,1536]{1,0:T(8,128)(2,1)S(1)} collective-permute-done((bf16[384,1536]{1,0:T(8,128)(2,1)S(1)}, bf16[384,1536]{1,0:T(8,128)(2,1)S(1)}, u32[]{:S(2)}, u32[]{:S(2)}) %collective-permute-start.5) | collective-permute-done | bytes 1179680 | tf_op jit(solution)/shard_map/ppermute | solution.py:328
  109.5 4.8 %all-to-all-start = ((bf16[8,48,2048]{2,1,0:T(8,128)(2,1)}), bf16[8,48,2048]{2,1,0:T(8,128)(2,1)S(1)}, u32[]{:S(2)}, u32[]{:S(2)}) async-start(bf16[8,48,2048]{2,1,0:T(8,128)(2,1)} %bitcast.30), calls=%async_computation | async-start | bytes 3145728 | tf_op jit(solution)/shard_map/all_to_all | solution.py:52
  116.2 4.0 %collective-permute-start.3 = (bf16[104,2048]{1,0:T(8,128)(2,1)}, bf16[104,2048]{1,0:T(8,128)(2,1)}, u32[]{:S(2)}, u32[]{:S(2)}) collective-permute-start(bf16[104,2048]{1,0:T(8,128)(2,1)} %copy-done.8), channel_id=1, source_target_pairs={{0,49},{1,0},{16,1},{17,16},{32,17},{33,32},{48,33},{49,48},{2,51}... | collective-permute-start | bytes 1277960 | tf_op jit(solution)/shard_map/ppermute | solution.py:36
  120.2 12.9 %collective-permute-done.2.refs_0_ = bf16[104,2048]{1,0:T(8,128)(2,1)S(1)} collective-permute-done((bf16[104,2048]{1,0:T(8,128)(2,1)}, bf16[104,2048]{1,0:T(8,128)(2,1)S(1)}, u32[]{:S(2)}, u32[]{:S(2)}) %collective-permute-start.2) | collective-permute-done | bytes 426016 | tf_op jit(solution)/shard_map/ppermute | solution.py:36
  135.5 3.1 collective-permute-start.7
  141.9 3.7 %collective-permute-done.6.refs_0_ = bf16[104,2048]{1,0:T(8,128)(2,1)S(1)} collective-permute-done((bf16[104,2048]{1,0:T(8,128)(2,1)S(1)}, bf16[104,2048]{1,0:T(8,128)(2,1)S(1)}, u32[]{:S(2)}, u32[]{:S(2)}) %collective-permute-start.6) | collective-permute-done | bytes 426016 | tf_op jit(solution)/shard_map/ppermute | solution.py:36
  148.4 5.3 %all-to-all-start.1 = ((bf16[8,32,2048]{2,1,0:T(8,128)(2,1)}), bf16[8,32,2048]{2,1,0:T(8,128)(2,1)}, u32[]{:S(2)}, u32[]{:S(2)}) async-start(bf16[8,32,2048]{2,1,0:T(8,128)(2,1)} %bitcast.33), calls=%async_computation.1 | async-start | bytes 2097152 | tf_op jit(solution)/shard_map/all_to_all | solution.py:52
  153.7 13.1 %collective-permute-done.8.refs_2_ = bf16[104,2048]{1,0:T(8,128)(2,1)S(1)} collective-permute-done((bf16[104,2048]{1,0:T(8,128)(2,1)S(1)}, bf16[104,2048]{1,0:T(8,128)(2,1)S(1)}, u32[]{:S(2)}, u32[]{:S(2)}) %collective-permute-start.8) | collective-permute-done | bytes 426016 | tf_op jit(solution)/shard_map/ppermute | solution.py:36
  171.1 4.8 %all-to-all-start.2 = ((bf16[8,48,2048]{2,1,0:T(8,128)(2,1)}), bf16[8,48,2048]{2,1,0:T(8,128)(2,1)S(1)}, u32[]{:S(2)}, u32[]{:S(2)}) async-start(bf16[8,48,2048]{2,1,0:T(8,128)(2,1)} %bitcast.32), calls=%async_computation.2 | async-start | bytes 3145728 | tf_op jit(solution)/shard_map/all_to_all | solution.py:52
  177.5 2.5 collective-permute-start.10
  180.1 3.6 collective-permute-start.11
  183.6 13.5 %collective-permute-done.9.refs_1_ = bf16[96,1536]{1,0:T(8,128)(2,1)S(1)} collective-permute-done((bf16[96,1536]{1,0:T(8,128)(2,1)S(1)}, bf16[96,1536]{1,0:T(8,128)(2,1)S(1)}, u32[]{:S(2)}, u32[]{:S(2)}) %collective-permute-start.9) | collective-permute-done | bytes 294944 | tf_op jit(solution)/shard_map/ppermute | solution.py:36
  197.8 2.9 collective-permute-done.10.refs_2_
  201.4 6.8 %collective-permute-done.11.refs_3_ = bf16[96,1536]{1,0:T(8,128)(2,1)S(1)} collective-permute-done((bf16[96,1536]{1,0:T(8,128)(2,1)S(1)}, bf16[96,1536]{1,0:T(8,128)(2,1)S(1)}, u32[]{:S(2)}, u32[]{:S(2)}) %collective-permute-start.11) | collective-permute-done | bytes 294944 | tf_op jit(solution)/shard_map/ppermute | solution.py:36
  210.4 9.8 %expert_ffn.2 = bf16[384,2048]{1,0:T(8,128)(2,1)} custom-call(s32[4]{0:T(128)S(1)} %pad_add_fusion.place_ref, bf16[4,384,1536]{2,1,0:T(8,128)(2,1)} %bitcast.40, bf16[4,384,1536]{2,1,0:T(8,128)(2,1)} %bitcast.42, bf16[384,2048]{1,0:T(8,128)(2,1)S(1)} %bitcast.31), custom_call_target="tpu_custom_call" | custom-call | flops 3623878656 | bytes 15728640 | tf_op jit(solution)/shard_map/expert_ffn/pallas_call | solution.py:273
  220.2 18.3 %collective-permute-done.12.refs_3_ = bf16[384,1536]{1,0:T(8,128)(2,1)} collective-permute-done((bf16[384,1536]{1,0:T(8,128)(2,1)S(1)}, bf16[384,1536]{1,0:T(8,128)(2,1)}, u32[]{:S(2)}, u32[]{:S(2)}) %collective-permute-start.12) | collective-permute-done | bytes 1179680 | tf_op jit(solution)/shard_map/ppermute | solution.py:328
  238.5 4.8 %all-to-all-start.3 = ((bf16[8,48,2048]{2,1,0:T(8,128)(2,1)}), bf16[8,48,2048]{2,1,0:T(8,128)(2,1)S(1)}, u32[]{:S(2)}, u32[]{:S(2)}) async-start(bf16[8,48,2048]{2,1,0:T(8,128)(2,1)} %bitcast.35), calls=%async_computation.3 | async-start | bytes 3145728 | tf_op jit(solution)/shard_map/all_to_all | solution.py:52
  244.7 12.9 %expert_ffn.3 = (bf16[256,2048]{1,0:T(8,128)(2,1)}, bf16[384,2048]{1,0:T(8,128)(2,1)}) custom-call(s32[4]{0:T(128)S(1)} %pad_add_fusion.place_ref, bf16[4,384,1536]{2,1,0:T(8,128)(2,1)} %bitcast.41, bf16[4,384,1536]{2,1,0:T(8,128)(2,1)} %bitcast.43, bf16[256,2048]{1,0:T(8,128)(2,1)} %bitcast.12.refs_0_, bf16[384,2048]{1,0:T(8,128)(2,1)S(1)} %bitcast.29), custom_call_target="tpu_custom_call" | custom-call | flops 6039797760 | bytes 15728640 | tf_op jit(solution)/shard_map/expert_ffn/pallas_call | solution.py:273
  257.6 5.2 %all-to-all-done.3 = bf16[8,48,2048]{2,1,0:T(8,128)(2,1)S(1)} async-done(((bf16[8,48,2048]{2,1,0:T(8,128)(2,1)}), bf16[8,48,2048]{2,1,0:T(8,128)(2,1)S(1)}, u32[]{:S(2)}, u32[]{:S(2)}) %all-to-all-start.3) | async-done | bytes 1572896 | tf_op jit(solution)/shard_map/all_to_all | solution.py:52
  262.8 6.4 %all-to-all-start.4 = ((bf16[8,32,2048]{2,1,0:T(8,128)(2,1)}), bf16[8,32,2048]{2,1,0:T(8,128)(2,1)}, u32[]{:S(2)}, u32[]{:S(2)}) async-start(bf16[8,32,2048]{2,1,0:T(8,128)(2,1)} %bitcast.36), calls=%async_computation.4 | async-start | bytes 2097152 | tf_op jit(solution)/shard_map/all_to_all | solution.py:52
  282.2 3.9 %collective-permute-start.18 = (bf16[96,1536]{1,0:T(8,128)(2,1)}, bf16[96,1536]{1,0:T(8,128)(2,1)}, u32[]{:S(2)}, u32[]{:S(2)}) collective-permute-start(bf16[96,1536]{1,0:T(8,128)(2,1)} %get-tuple-element.148), channel_id=1, source_target_pairs={{0,32},{16,48},{32,0},{48,16},{1,33},{17,49},{33,1},{49,17},{2,34}... | collective-permute-start | bytes 884744 | tf_op jit(solution)/shard_map/ppermute | solution.py:36
  287.0 4.8 %all-to-all-start.5 = ((bf16[8,48,2048]{2,1,0:T(8,128)(2,1)}), bf16[8,48,2048]{2,1,0:T(8,128)(2,1)S(1)}, u32[]{:S(2)}, u32[]{:S(2)}) async-start(bf16[8,48,2048]{2,1,0:T(8,128)(2,1)} %bitcast.34), calls=%async_computation.5 | async-start | bytes 3145728 | tf_op jit(solution)/shard_map/all_to_all | solution.py:52
  292.9 3.2 collective-permute-start.14
  298.0 22.2 %collective-permute-done.14 = bf16[96,2048]{1,0:T(8,128)(2,1)S(1)} collective-permute-done((bf16[96,2048]{1,0:T(8,128)(2,1)S(1)}, bf16[96,2048]{1,0:T(8,128)(2,1)S(1)}, u32[]{:S(2)}, u32[]{:S(2)}) %collective-permute-start.14) | collective-permute-done | bytes 393248 | tf_op jit(solution)/shard_map/ppermute | solution.py:36
  321.0 2.7 collective-permute-start.16
  326.3 6.2 %collective-permute-done.16 = bf16[96,2048]{1,0:T(8,128)(2,1)} collective-permute-done((bf16[96,2048]{1,0:T(8,128)(2,1)}, bf16[96,2048]{1,0:T(8,128)(2,1)}, u32[]{:S(2)}, u32[]{:S(2)}) %collective-permute-start.16) | collective-permute-done | bytes 393248 | tf_op jit(solution)/shard_map/ppermute | solution.py:36
  334.5 3.7 %collective-permute-start.20 = (bf16[96,2048]{1,0:T(8,128)(2,1)}, bf16[96,2048]{1,0:T(8,128)(2,1)}, u32[]{:S(2)}, u32[]{:S(2)}) collective-permute-start(bf16[96,2048]{1,0:T(8,128)(2,1)} %add_convert_fusion.3), channel_id=1, source_target_pairs={{0,49},{1,0},{16,1},{17,16},{32,17},{33,32},{48,33},{49,48},{2,51}... | collective-permute-start | bytes 1179656 | tf_op jit(solution)/shard_map/ppermute | solution.py:36
  338.8 7.3 %collective-permute-done.20 = bf16[96,2048]{1,0:T(8,128)(2,1)} collective-permute-done((bf16[96,2048]{1,0:T(8,128)(2,1)}, bf16[96,2048]{1,0:T(8,128)(2,1)}, u32[]{:S(2)}, u32[]{:S(2)}) %collective-permute-start.20) | collective-permute-done | bytes 393248 | tf_op jit(solution)/shard_map/ppermute | solution.py:36
  (124 shorter events, 54.3 us)
Async XLA Ops:
  7.2 203.3 %all-gather.5.cloned.1.call-start = ((), (), s32[]{:S(2)}) async-start(), calls=%async_computation.6 | async-start | bytes 5898240 | tf_op jit(solution)/shard_map/all_gather | solution.py:366
  80.7 27.8 %collective-permute-start.5 = (bf16[384,1536]{1,0:T(8,128)(2,1)S(1)}, bf16[384,1536]{1,0:T(8,128)(2,1)S(1)}, u32[]{:S(2)}, u32[]{:S(2)}) collective-permute-start(bf16[384,1536]{1,0:T(8,128)(2,1)S(1)} %get-tuple-element.156.first_ref.refs_0_), channel_id=1, source_target_pairs={{0,64},{64,0},{128,192},{192,128},{1,65},{65,1},{129,193},{193,129... | collective-permute-start | bytes 3538952 | tf_op jit(solution)/shard_map/ppermute | solution.py:328
  81.6 14.7 %collective-permute-start.1 = (bf16[104,2048]{1,0:T(8,128)(2,1)S(1)}, bf16[104,2048]{1,0:T(8,128)(2,1)S(1)}, u32[]{:S(2)}, u32[]{:S(2)}) collective-permute-start(bf16[104,2048]{1,0:T(8,128)(2,1)S(1)} %get-tuple-element.85.refs_0_), channel_id=1, source_target_pairs={{0,49},{1,0},{16,1},{17,16},{32,17},{33,32},{48,33},{49,48},{2,51}... | collective-permute-start | bytes 1277960 | tf_op jit(solution)/shard_map/ppermute | solution.py:36
  87.4 12.2 %collective-permute-start = (bf16[104,2048]{1,0:T(8,128)(2,1)S(1)}, bf16[104,2048]{1,0:T(8,128)(2,1)S(1)}, u32[]{:S(2)}, u32[]{:S(2)}) collective-permute-start(bf16[104,2048]{1,0:T(8,128)(2,1)S(1)} %get-tuple-element.85.refs_0_), channel_id=1, source_target_pairs={{0,1},{1,16},{16,17},{17,32},{32,33},{33,48},{48,49},{49,0},{2,3},... | collective-permute-start | bytes 1277960 | tf_op jit(solution)/shard_map/ppermute | solution.py:36
  99.6 35.7 %collective-permute-start.4 = (bf16[384,1536]{1,0:T(8,128)(2,1)}, bf16[384,1536]{1,0:T(8,128)(2,1)}, u32[]{:S(2)}, u32[]{:S(2)}) collective-permute-start(bf16[384,1536]{1,0:T(8,128)(2,1)} %get-tuple-element.89), channel_id=1, source_target_pairs={{0,1},{1,0},{2,3},{3,2},{4,5},{5,4},{6,7},{7,6},{8,9},{9,8},{10,11... | collective-permute-start | bytes 3538952 | tf_op jit(solution)/shard_map/ppermute | solution.py:328
  109.5 37.8 %all-to-all-start = ((bf16[8,48,2048]{2,1,0:T(8,128)(2,1)}), bf16[8,48,2048]{2,1,0:T(8,128)(2,1)S(1)}, u32[]{:S(2)}, u32[]{:S(2)}) async-start(bf16[8,48,2048]{2,1,0:T(8,128)(2,1)} %bitcast.30), calls=%async_computation | async-start | bytes 3145728 | tf_op jit(solution)/shard_map/all_to_all | solution.py:52
  114.2 96.2 %all-gather.7.cloned.1.call-start = ((), (), s32[]{:S(2)}) async-start(), calls=%async_computation.7 | async-start | bytes 5898240 | tf_op jit(solution)/shard_map/all_gather | solution.py:380
  114.2 18.9 %collective-permute-start.2 = (bf16[104,2048]{1,0:T(8,128)(2,1)}, bf16[104,2048]{1,0:T(8,128)(2,1)S(1)}, u32[]{:S(2)}, u32[]{:S(2)}) collective-permute-start(bf16[104,2048]{1,0:T(8,128)(2,1)} %copy-done.13), channel_id=1, source_target_pairs={{0,1},{1,16},{16,17},{17,32},{32,33},{33,48},{48,49},{49,0},{2,3},... | collective-permute-start | bytes 1277960 | tf_op jit(solution)/shard_map/ppermute | solution.py:36
  116.2 19.1 %collective-permute-start.3 = (bf16[104,2048]{1,0:T(8,128)(2,1)}, bf16[104,2048]{1,0:T(8,128)(2,1)}, u32[]{:S(2)}, u32[]{:S(2)}) collective-permute-start(bf16[104,2048]{1,0:T(8,128)(2,1)} %copy-done.8), channel_id=1, source_target_pairs={{0,49},{1,0},{16,1},{17,16},{32,17},{33,32},{48,33},{49,48},{2,51}... | collective-permute-start | bytes 1277960 | tf_op jit(solution)/shard_map/ppermute | solution.py:36
  135.3 10.4 %collective-permute-start.6 = (bf16[104,2048]{1,0:T(8,128)(2,1)S(1)}, bf16[104,2048]{1,0:T(8,128)(2,1)S(1)}, u32[]{:S(2)}, u32[]{:S(2)}) collective-permute-start(bf16[104,2048]{1,0:T(8,128)(2,1)S(1)} %collective-permute-done.2.refs_0_), channel_id=1, source_target_pairs={{0,1},{1,16},{16,17},{17,32},{32,33},{33,48},{48,49},{49,0},{2,3},... | collective-permute-start | bytes 1277960 | tf_op jit(solution)/shard_map/ppermute | solution.py:36
  135.5 10.9 %collective-permute-start.7 = (bf16[104,2048]{1,0:T(8,128)(2,1)}, bf16[104,2048]{1,0:T(8,128)(2,1)S(1)}, u32[]{:S(2)}, u32[]{:S(2)}) collective-permute-start(bf16[104,2048]{1,0:T(8,128)(2,1)} %collective-permute-done.3.refs_1_), channel_id=1, source_target_pairs={{0,49},{1,0},{16,1},{17,16},{32,17},{33,32},{48,33},{49,48},{2,51}... | collective-permute-start | bytes 1277960 | tf_op jit(solution)/shard_map/ppermute | solution.py:36
  148.4 22.8 %all-to-all-start.1 = ((bf16[8,32,2048]{2,1,0:T(8,128)(2,1)}), bf16[8,32,2048]{2,1,0:T(8,128)(2,1)}, u32[]{:S(2)}, u32[]{:S(2)}) async-start(bf16[8,32,2048]{2,1,0:T(8,128)(2,1)} %bitcast.33), calls=%async_computation.1 | async-start | bytes 2097152 | tf_op jit(solution)/shard_map/all_to_all | solution.py:52
  153.7 13.1 %collective-permute-start.8 = (bf16[104,2048]{1,0:T(8,128)(2,1)S(1)}, bf16[104,2048]{1,0:T(8,128)(2,1)S(1)}, u32[]{:S(2)}, u32[]{:S(2)}) collective-permute-start(bf16[104,2048]{1,0:T(8,128)(2,1)S(1)} %copy-done.10), channel_id=1, source_target_pairs={{0,1},{1,16},{16,17},{17,32},{32,33},{33,48},{48,49},{49,0},{2,3},... | collective-permute-start | bytes 1277960 | tf_op jit(solution)/shard_map/ppermute | solution.py:36
  171.1 37.8 %all-to-all-start.2 = ((bf16[8,48,2048]{2,1,0:T(8,128)(2,1)}), bf16[8,48,2048]{2,1,0:T(8,128)(2,1)S(1)}, u32[]{:S(2)}, u32[]{:S(2)}) async-start(bf16[8,48,2048]{2,1,0:T(8,128)(2,1)} %bitcast.32), calls=%async_computation.2 | async-start | bytes 3145728 | tf_op jit(solution)/shard_map/all_to_all | solution.py:52
  177.5 19.6 %collective-permute-start.9 = (bf16[96,1536]{1,0:T(8,128)(2,1)S(1)}, bf16[96,1536]{1,0:T(8,128)(2,1)S(1)}, u32[]{:S(2)}, u32[]{:S(2)}) collective-permute-start(bf16[96,1536]{1,0:T(8,128)(2,1)S(1)} %get-tuple-element.110), channel_id=1, source_target_pairs={{0,16},{16,32},{32,48},{48,0},{1,17},{17,33},{33,49},{49,1},{2,18}... | collective-permute-start | bytes 884744 | tf_op jit(solution)/shard_map/ppermute | solution.py:36
  177.5 23.2 %collective-permute-start.10 = (bf16[96,1536]{1,0:T(8,128)(2,1)S(1)}, bf16[96,1536]{1,0:T(8,128)(2,1)S(1)}, u32[]{:S(2)}, u32[]{:S(2)}) collective-permute-start(bf16[96,1536]{1,0:T(8,128)(2,1)S(1)} %get-tuple-element.111), channel_id=1, source_target_pairs={{0,32},{16,48},{32,0},{48,16},{1,33},{17,49},{33,1},{49,17},{2,34}... | collective-permute-start | bytes 884744 | tf_op jit(solution)/shard_map/ppermute | solution.py:36
  180.1 28.2 %collective-permute-start.11 = (bf16[96,1536]{1,0:T(8,128)(2,1)S(1)}, bf16[96,1536]{1,0:T(8,128)(2,1)S(1)}, u32[]{:S(2)}, u32[]{:S(2)}) collective-permute-start(bf16[96,1536]{1,0:T(8,128)(2,1)S(1)} %get-tuple-element.112), channel_id=1, source_target_pairs={{0,48},{16,0},{32,16},{48,32},{1,49},{17,1},{33,17},{49,33},{2,50}... | collective-permute-start | bytes 884744 | tf_op jit(solution)/shard_map/ppermute | solution.py:36
  209.0 29.5 %collective-permute-start.12 = (bf16[384,1536]{1,0:T(8,128)(2,1)S(1)}, bf16[384,1536]{1,0:T(8,128)(2,1)}, u32[]{:S(2)}, u32[]{:S(2)}) collective-permute-start(bf16[384,1536]{1,0:T(8,128)(2,1)S(1)} %get-tuple-element.156.first_ref.refs_0_), channel_id=1, source_target_pairs={{0,128},{64,192},{128,0},{192,64},{1,129},{65,193},{129,1},{193,65... | collective-permute-start | bytes 3538952 | tf_op jit(solution)/shard_map/ppermute | solution.py:328
  238.5 24.3 %all-to-all-start.3 = ((bf16[8,48,2048]{2,1,0:T(8,128)(2,1)}), bf16[8,48,2048]{2,1,0:T(8,128)(2,1)S(1)}, u32[]{:S(2)}, u32[]{:S(2)}) async-start(bf16[8,48,2048]{2,1,0:T(8,128)(2,1)} %bitcast.35), calls=%async_computation.3 | async-start | bytes 3145728 | tf_op jit(solution)/shard_map/all_to_all | solution.py:52
  262.8 23.5 %all-to-all-start.4 = ((bf16[8,32,2048]{2,1,0:T(8,128)(2,1)}), bf16[8,32,2048]{2,1,0:T(8,128)(2,1)}, u32[]{:S(2)}, u32[]{:S(2)}) async-start(bf16[8,32,2048]{2,1,0:T(8,128)(2,1)} %bitcast.36), calls=%async_computation.4 | async-start | bytes 2097152 | tf_op jit(solution)/shard_map/all_to_all | solution.py:52
  271.3 20.6 %collective-permute-start.13 = (bf16[96,2048]{1,0:T(8,128)(2,1)}, bf16[96,2048]{1,0:T(8,128)(2,1)}, u32[]{:S(2)}, u32[]{:S(2)}) collective-permute-start(bf16[96,2048]{1,0:T(8,128)(2,1)} %get-tuple-element.131), channel_id=1, source_target_pairs={{0,49},{1,0},{16,1},{17,16},{32,17},{33,32},{48,33},{49,48},{2,51}... | collective-permute-start | bytes 1179656 | tf_op jit(solution)/shard_map/ppermute | solution.py:36
  271.3 15.0 %collective-permute-start.15 = (bf16[96,2048]{1,0:T(8,128)(2,1)}, bf16[96,2048]{1,0:T(8,128)(2,1)S(1)}, u32[]{:S(2)}, u32[]{:S(2)}) collective-permute-start(bf16[96,2048]{1,0:T(8,128)(2,1)} %get-tuple-element.136), channel_id=1, source_target_pairs={{0,1},{1,16},{16,17},{17,32},{32,33},{33,48},{48,49},{49,0},{2,3},... | collective-permute-start | bytes 1179656 | tf_op jit(solution)/shard_map/ppermute | solution.py:36
  280.1 43.5 %collective-permute-start.17 = (bf16[96,1536]{1,0:T(8,128)(2,1)}, bf16[96,1536]{1,0:T(8,128)(2,1)}, u32[]{:S(2)}, u32[]{:S(2)}) collective-permute-start(bf16[96,1536]{1,0:T(8,128)(2,1)} %get-tuple-element.147), channel_id=1, source_target_pairs={{0,16},{16,32},{32,48},{48,0},{1,17},{17,33},{33,49},{49,1},{2,18}... | collective-permute-start | bytes 884744 | tf_op jit(solution)/shard_map/ppermute | solution.py:36
  282.2 41.5 %collective-permute-start.18 = (bf16[96,1536]{1,0:T(8,128)(2,1)}, bf16[96,1536]{1,0:T(8,128)(2,1)}, u32[]{:S(2)}, u32[]{:S(2)}) collective-permute-start(bf16[96,1536]{1,0:T(8,128)(2,1)} %get-tuple-element.148), channel_id=1, source_target_pairs={{0,32},{16,48},{32,0},{48,16},{1,33},{17,49},{33,1},{49,17},{2,34}... | collective-permute-start | bytes 884744 | tf_op jit(solution)/shard_map/ppermute | solution.py:36
  286.1 37.6 %collective-permute-start.19 = (bf16[96,1536]{1,0:T(8,128)(2,1)}, bf16[96,1536]{1,0:T(8,128)(2,1)}, u32[]{:S(2)}, u32[]{:S(2)}) collective-permute-start(bf16[96,1536]{1,0:T(8,128)(2,1)} %get-tuple-element.149), channel_id=1, source_target_pairs={{0,48},{16,0},{32,16},{48,32},{1,49},{17,1},{33,17},{49,33},{2,50}... | collective-permute-start | bytes 884744 | tf_op jit(solution)/shard_map/ppermute | solution.py:36
  287.0 36.7 %all-to-all-start.5 = ((bf16[8,48,2048]{2,1,0:T(8,128)(2,1)}), bf16[8,48,2048]{2,1,0:T(8,128)(2,1)S(1)}, u32[]{:S(2)}, u32[]{:S(2)}) async-start(bf16[8,48,2048]{2,1,0:T(8,128)(2,1)} %bitcast.34), calls=%async_computation.5 | async-start | bytes 3145728 | tf_op jit(solution)/shard_map/all_to_all | solution.py:52
  292.9 27.2 %collective-permute-start.14 = (bf16[96,2048]{1,0:T(8,128)(2,1)S(1)}, bf16[96,2048]{1,0:T(8,128)(2,1)S(1)}, u32[]{:S(2)}, u32[]{:S(2)}) collective-permute-start(bf16[96,2048]{1,0:T(8,128)(2,1)S(1)} %add_convert_fusion.5), channel_id=1, source_target_pairs={{0,49},{1,0},{16,1},{17,16},{32,17},{33,32},{48,33},{49,48},{2,51}... | collective-permute-start | bytes 1179656 | tf_op jit(solution)/shard_map/ppermute | solution.py:36
  297.9 26.3 %collective-permute-start.21 = (bf16[96,2048]{1,0:T(8,128)(2,1)S(1)}, bf16[96,2048]{1,0:T(8,128)(2,1)}, u32[]{:S(2)}, u32[]{:S(2)}) collective-permute-start(bf16[96,2048]{1,0:T(8,128)(2,1)S(1)} %add_convert_fusion.2), channel_id=1, source_target_pairs={{0,1},{1,16},{16,17},{17,32},{32,33},{33,48},{48,49},{49,0},{2,3},... | collective-permute-start | bytes 1179656 | tf_op jit(solution)/shard_map/ppermute | solution.py:36
  321.0 11.5 %collective-permute-start.16 = (bf16[96,2048]{1,0:T(8,128)(2,1)}, bf16[96,2048]{1,0:T(8,128)(2,1)}, u32[]{:S(2)}, u32[]{:S(2)}) collective-permute-start(bf16[96,2048]{1,0:T(8,128)(2,1)} %add_convert_fusion.4), channel_id=1, source_target_pairs={{0,49},{1,0},{16,1},{17,16},{32,17},{33,32},{48,33},{49,48},{2,51}... | collective-permute-start | bytes 1179656 | tf_op jit(solution)/shard_map/ppermute | solution.py:36
  326.3 12.5 %collective-permute-start.22 = (bf16[96,2048]{1,0:T(8,128)(2,1)}, bf16[96,2048]{1,0:T(8,128)(2,1)}, u32[]{:S(2)}, u32[]{:S(2)}) collective-permute-start(bf16[96,2048]{1,0:T(8,128)(2,1)} %add_convert_fusion.1), channel_id=1, source_target_pairs={{0,1},{1,16},{16,17},{17,32},{32,33},{33,48},{48,49},{49,0},{2,3},... | collective-permute-start | bytes 1179656 | tf_op jit(solution)/shard_map/ppermute | solution.py:36
  326.3 22.1 %collective-permute-start.23 = (bf16[384,1536]{1,0:T(8,128)(2,1)S(1)}, bf16[384,1536]{1,0:T(8,128)(2,1)S(1)}, u32[]{:S(2)}, u32[]{:S(2)}) collective-permute-start(bf16[384,1536]{1,0:T(8,128)(2,1)S(1)} %get-tuple-element.156.first_ref.refs_0_), channel_id=1, source_target_pairs={{0,8},{8,0},{1,9},{9,1},{2,10},{10,2},{3,11},{11,3},{4,12},{12,4},... | collective-permute-start | bytes 3538952 | tf_op jit(solution)/shard_map/ppermute | solution.py:328
  334.5 11.7 %collective-permute-start.20 = (bf16[96,2048]{1,0:T(8,128)(2,1)}, bf16[96,2048]{1,0:T(8,128)(2,1)}, u32[]{:S(2)}, u32[]{:S(2)}) collective-permute-start(bf16[96,2048]{1,0:T(8,128)(2,1)} %add_convert_fusion.3), channel_id=1, source_target_pairs={{0,49},{1,0},{16,1},{17,16},{32,17},{33,32},{48,33},{49,48},{2,51}... | collective-permute-start | bytes 1179656 | tf_op jit(solution)/shard_map/ppermute | solution.py:36
  (33 other events, 132.2 us)
Sparse Core Ops, SparseCore 0:
  80.8 57.0 all-gather.4
  147.4 52.6 all-gather.6

commit v6 on v5

--- a/solution.py
+++ b/solution.py
@@ -138,17 +138,18 @@
 
 
 def unpack_kernel(kind_ref, place_ref, *refs):
-    whole, pieces, refs = refs[:4], refs[4 : 4 + NZH], refs[4 + NZH :]
+    whole, pieces, refs = refs[:3], refs[3 : 3 + NZH], refs[3 + NZH :]
     gate_ref, up_ref, down_ref, block, sem = refs
-    for kinds, ref in zip(((0,), (1,), (8,), (16,)), whole):
-
-        @pl.when(kind_ref[0] == kinds[0])
+    kind = kind_ref[0]
+    for chosen, ref in zip((kind == 0, kind == 1, kind >= 8), whole):
+
+        @pl.when(chosen)
         def _(ref=ref):
             cp = pltpu.make_async_copy(ref, block, sem.at[NZH])
             cp.start()
             cp.wait()
 
-    @pl.when((kind_ref[0] == 2) | (kind_ref[0] == 4))
+    @pl.when((kind == 2) | (kind == 4))
     def _():
         copies = []
         for k, ref in enumerate(pieces):
@@ -343,7 +344,7 @@
         prep_kernel,
         [shape(ROWS + META, WIDTH)] + [shape(PACK, SIDE)] * 3,
         [SMEM] + [HBM] * 7,
-        [VMEM] + [HBM] * 3,
+        [VMEM] * 4,
         "prep",
         scratch=[
             pltpu.VMEM((ROWS, WIDTH), BF),
@@ -370,8 +371,9 @@
     swapped = partner(other, "zl", 1)
     p2, m2 = along_z(p1, 1), along_z(m1, -1)
     d0, w0 = dispatch(place, (near, p1, m1))
-    hx1 = partner(first, "x", 1)
-    d0, hx1 = fence(d0, hx1)
+    hx = across(first.reshape(NX, PACK // NX, SIDE), "x")
+    hc = partner(first, "c", 1)
+    d0, hx, hc = fence(d0, hx, hc)
     r0 = in_plane(d0)
     p2, m2, swapped = fence(p2, m2, swapped)
     p3, m3 = along_z(p2, 1), along_z(m2, -1)
@@ -389,14 +391,11 @@
     d2, w2 = dispatch(place, (p3, m3, far))
     d2, r1 = fence(d2, r1)
     r2 = in_plane(d2)
-    r0, r1, r2, first, *held = fence(r0, r1, r2, first, *held)
-
-    hx2 = partner(first, "x", 2)
-    (s2,) = ffn(place, own_full, swap_full, (r2,), 384)
-    s2, r1, r0, hx2, *held = fence(s2, r1, r0, hx2, *held)
-    b2 = in_plane(s2)
-    s1, s0 = ffn(place, own_full, swap_full, (r1, r0), 320)
-    b2, s1, s0, *held = fence(b2, s1, s0, *held)
+    r0, r1, r2, first, hx, *held = fence(r0, r1, r2, first, hx, *held)
+    x_turn = jnp.arange(NX, dtype=jnp.int32)
+    x_from = jnp.take(pair_list, (x_turn * NZH + zh_me) * NC + c_me, mode="clip") >> 3
+    hx = across(jnp.take(hx, x_from, axis=0, mode="clip"), "x").reshape(PACK, SIDE)
+
     turn = (zh_me + jnp.arange(NZH, dtype=jnp.int32)) & (NZH - 1)
     matched = jnp.take(pair_list, (x_me * NZH + turn) * NC + c_me, mode="clip")
     chosen = (zh_me - (matched >> 1)) & (NZH - 1)
@@ -406,28 +405,31 @@
     )(chosen.astype(jnp.int32), *held)
     held = [picked[0]] + [shift(picked[k], "zh", NZH, k) for k in range(1, NZH)]
 
+    (s2,) = ffn(place, own_full, swap_full, (r2,), 384)
+    s2, r1, r0, hx, *held = fence(s2, r1, r0, hx, *held)
+    b2 = in_plane(s2)
+    s1, s0 = ffn(place, own_full, swap_full, (r1, r0), 320)
+    b2, s1, s0 = fence(b2, s1, s0)
     c_m3, c_p3, c_4 = combine(w2, b2, (F32, BF, BF))
     down, rise = along_z(c_4, -1), along_z(c_p3, 1)
     b1 = in_plane(s1)
     down = along_z(joined(down, c_m3), -1)
-    b1, s0, rise = fence(b1, s0, rise)
+    b1, s0, rise, *held = fence(b1, s0, rise, *held)
     b0 = in_plane(s0)
     c_m2, c_p2 = combine(w1, b1, (F32, F32))
     down = along_z(joined(down, c_m2), -1)
     rise = along_z(joined(rise, c_p2), 1)
-    b0, first, hx1, *held = fence(b0, first, hx1, *held)
-
-    hc = partner(first, "c", 1)
+
     me = (x_me * NZH + zh_me) * NC + c_me
     bits = jnp.sum(jnp.where(jnp.arange(pair_list.shape[0]) == me, pair_list ^ me, 0))
     new = call(
         unpack_kernel,
         [shape(SHARD, HIDDEN), shape(SHARD, HIDDEN), shape(DSHARD, WIDTH)],
-        [SMEM] * 2 + [HBM] * 8,
+        [SMEM] * 2 + [HBM] * 7,
         [VMEM] * 3,
         "unpack",
         scratch=[pltpu.VMEM((PACK, SIDE), BF), pltpu.SemaphoreType.DMA((NZH + 1,))],
-    )(bits.astype(jnp.int32).reshape(1), place, first, hc, hx1, hx2, *held)
+    )(bits.astype(jnp.int32).reshape(1), place, first, hc, hx, *held)
 
     c_0, c_m1, c_p1 = combine(w0, b0, (F32, F32, F32))
     down = along_z(joined(down, c_m1), -1)

time: 359 us -> 282 us (0.79)
  Pallas kernels: 109 us -> 42.7 us
  waiting for transfers between devices: 132 us -> 117 us
  starting transfers between devices: 72.2 us -> 76.3 us
    pallas_call x1, Pallas kernels: 73.3 us -> 4.33 us  [body(): call(prep_kernel, [shape(ROWS + META, WIDTH)] + [shape(PACK, SIDE)] * 3,...]
    ppermute x4 -> x2, waiting for transfers between devices: 23.8 us -> 0.01 us  [partner(): return lax.ppermute(value, axis, [(i, i ^ bit) for i in range(count)])]
    all_to_all x6 -> x8, starting transfers between devices: 30.8 us -> 40 us  [across(): return lax.all_to_all(value, axis, split_axis=0, concat_axis=0, tiled=True)]
    unnamed x66 -> x50, local copies, waits for them, and re-layouts: 20.5 us -> 14.5 us
    ppermute x20, waiting for transfers between devices: 103 us -> 109 us  [shift(): lax.ppermute(value, axes, [(i, (i + step) % count) for i in range(count)])]
    gather x0 -> x2, local copies, waits for them, and re-layouts: none -> 3.66 us  [the longest x1 3.02 us: body(): jnp.take(hx, x_from, axis=0, mode='clip')]
    all_to_all x6 -> x8, waiting for transfers between devices: 5.23 us -> 8.33 us  [across(): return lax.all_to_all(value, axis, split_axis=0, concat_axis=0, tiled=True)]
  transfers between devices with their start and end apart: 32 -> 32, of which waited for: 15 -> 17; matrix products, arithmetic and copies ran while one was open for 3% -> 4% of each run, Pallas kernels for 9% -> 14%
where the time goes in v6:
time: 282 us; the launch traced here: 279 us
  waiting for transfers between devices  117 us (41%)
  starting transfers between devices  76.3 us (27%)
  Pallas kernels  42.7 us (15%)
  local copies, waits for them, and re-layouts  18.8 us (7%)
  between operations  14.3 us (5%)
  other arithmetic  10.1 us (4%)
    ppermute x20, waiting for transfers between devices, shift(): lax.ppermute(value, axes, [(i, (i + step) % count) for i in range(count)])  109 us
    all_to_all x8, starting transfers between devices, across(): return lax.all_to_all(value, axis, split_axis=0, concat_axis=0, tiled=True)  40 us
    ppermute x20, starting transfers between devices, shift(): lax.ppermute(value, axes, [(i, (i + step) % count) for i in range(count)])  36.2 us
    pallas_call x2, Pallas kernels, ffn(): call(functools.partial(ffn_kernel, splits, block), [pltpu.HBM((r, WIDTH),...  22.5 us
    unnamed x50, local copies, waits for them, and re-layouts  14.5 us
    all_to_all x8, waiting for transfers between devices, across(): return lax.all_to_all(value, axis, split_axis=0, concat_axis=0, tiled=True)  8.33 us
    convert_element_type x5, other arithmetic, joined(): return (got.astype(F32) + mine).astype(BF)  7.41 us
    pallas_call x3, Pallas kernels, dispatch(): call(functools.partial(dispatch_kernel, n), [shape(PLACES * n * MOST, WID...  6.68 us
  transfers between devices with their start and end apart: 32, of which 17 were waited for; matrix products, arithmetic and copies ran while one was open for 4% of the time, Pallas kernels for 14%

profile of v6, /device:TPU:22, one launch (start us, length us, event | category | flops | bytes accessed | tf_op | source)
XLA Modules:
  0.0 279.2 jit_solution(852946485745463350)
XLA Ops:
  7.3 4.3 %prep.1 = (bf16[104,2048]{1,0:T(8,128)(2,1)S(1)}, bf16[384,1536]{1,0:T(8,128)(2,1)}, bf16[384,1536]{1,0:T(8,128)(2,1)S(1)}, bf16[384,1536]{1,0:T(8,128)(2,1)}) custom-call(s32[4]{0:T(128)S(1)} %pad_add_fusion.place_ref, bf16[96,2048]{1,0:T(8,128)(2,1)} %tokens_ref.1, f32[1,2048]{1,0:T(1,128)} %bitcast.41, s32[8,96]{1,0:T(8,128)} %bitcast.42, ...), custom_call_target="tpu_custom_call" | custom-call | tf_op jit(solution)/shard_map/prep/pallas_call | solution.py:343
  12.8 4.8 %all-to-all-start = ((bf16[4,96,1536]{2,1,0:T(8,128)(2,1)}), bf16[4,96,1536]{2,1,0:T(8,128)(2,1)}, u32[]{:S(2)}, u32[]{:S(2)}) async-start(bf16[4,96,1536]{2,1,0:T(8,128)(2,1)} %bitcast.7), calls=%async_computation | async-start | bytes 2359296 | tf_op jit(solution)/shard_map/all_to_all | solution.py:52
  17.6 5.9 %collective-permute-start.1 = (bf16[104,2048]{1,0:T(8,128)(2,1)S(1)}, bf16[104,2048]{1,0:T(8,128)(2,1)S(1)}, u32[]{:S(2)}, u32[]{:S(2)}) collective-permute-start(bf16[104,2048]{1,0:T(8,128)(2,1)S(1)} %get-tuple-element.80.refs_0_), channel_id=1, source_target_pairs={{0,49},{1,0},{16,1},{17,16},{32,17},{33,32},{48,33},{49,48},{2,51}... | collective-permute-start | bytes 1277960 | tf_op jit(solution)/shard_map/ppermute | solution.py:36
  23.5 9.4 %collective-permute-done.1.refs_2_ = bf16[104,2048]{1,0:T(8,128)(2,1)S(1)} collective-permute-done((bf16[104,2048]{1,0:T(8,128)(2,1)S(1)}, bf16[104,2048]{1,0:T(8,128)(2,1)S(1)}, u32[]{:S(2)}, u32[]{:S(2)}) %collective-permute-start.1) | collective-permute-done | bytes 426016 | tf_op jit(solution)/shard_map/ppermute | solution.py:36
  32.9 3.4 %collective-permute-done.refs_1_ = bf16[104,2048]{1,0:T(8,128)(2,1)S(1)} collective-permute-done((bf16[104,2048]{1,0:T(8,128)(2,1)S(1)}, bf16[104,2048]{1,0:T(8,128)(2,1)S(1)}, u32[]{:S(2)}, u32[]{:S(2)}) %collective-permute-start) | collective-permute-done | bytes 426016 | tf_op jit(solution)/shard_map/ppermute | solution.py:36
  40.7 4.8 %all-to-all-start.1 = ((bf16[8,48,2048]{2,1,0:T(8,128)(2,1)}), bf16[8,48,2048]{2,1,0:T(8,128)(2,1)S(1)}, u32[]{:S(2)}, u32[]{:S(2)}) async-start(bf16[8,48,2048]{2,1,0:T(8,128)(2,1)} %bitcast.8), calls=%async_computation.1 | async-start | bytes 3145728 | tf_op jit(solution)/shard_map/all_to_all | solution.py:52
  48.8 21.6 %collective-permute-done.2.refs_0_ = bf16[104,2048]{1,0:T(8,128)(2,1)S(1)} collective-permute-done((bf16[104,2048]{1,0:T(8,128)(2,1)S(1)}, bf16[104,2048]{1,0:T(8,128)(2,1)S(1)}, u32[]{:S(2)}, u32[]{:S(2)}) %collective-permute-start.2) | collective-permute-done | bytes 426016 | tf_op jit(solution)/shard_map/ppermute | solution.py:36
  72.9 3.0 %collective-permute-start.7 = (bf16[104,2048]{1,0:T(8,128)(2,1)S(1)}, bf16[104,2048]{1,0:T(8,128)(2,1)S(1)}, u32[]{:S(2)}, u32[]{:S(2)}) collective-permute-start(bf16[104,2048]{1,0:T(8,128)(2,1)S(1)} %collective-permute-done.3.refs_1_), channel_id=1, source_target_pairs={{0,49},{1,0},{16,1},{17,16},{32,17},{33,32},{48,33},{49,48},{2,51}... | collective-permute-start | bytes 1277960 | tf_op jit(solution)/shard_map/ppermute | solution.py:36
  77.1 6.5 %collective-permute-done.6.refs_0_ = bf16[104,2048]{1,0:T(8,128)(2,1)S(1)} collective-permute-done((bf16[104,2048]{1,0:T(8,128)(2,1)S(1)}, bf16[104,2048]{1,0:T(8,128)(2,1)S(1)}, u32[]{:S(2)}, u32[]{:S(2)}) %collective-permute-start.6) | collective-permute-done | bytes 426016 | tf_op jit(solution)/shard_map/ppermute | solution.py:36
  84.8 4.8 %all-to-all-start.2 = ((bf16[8,32,2048]{2,1,0:T(8,128)(2,1)}), bf16[8,32,2048]{2,1,0:T(8,128)(2,1)S(1)}, u32[]{:S(2)}, u32[]{:S(2)}) async-start(bf16[8,32,2048]{2,1,0:T(8,128)(2,1)} %bitcast.37), calls=%async_computation.2 | async-start | bytes 2097152 | tf_op jit(solution)/shard_map/all_to_all | solution.py:52
  89.6 13.1 %collective-permute-done.8.refs_2_ = bf16[104,2048]{1,0:T(8,128)(2,1)S(1)} collective-permute-done((bf16[104,2048]{1,0:T(8,128)(2,1)S(1)}, bf16[104,2048]{1,0:T(8,128)(2,1)S(1)}, u32[]{:S(2)}, u32[]{:S(2)}) %collective-permute-start.8) | collective-permute-done | bytes 426016 | tf_op jit(solution)/shard_map/ppermute | solution.py:36
  107.1 4.8 %all-to-all-start.3 = ((bf16[8,48,2048]{2,1,0:T(8,128)(2,1)}), bf16[8,48,2048]{2,1,0:T(8,128)(2,1)S(1)}, u32[]{:S(2)}, u32[]{:S(2)}) async-start(bf16[8,48,2048]{2,1,0:T(8,128)(2,1)} %bitcast.14), calls=%async_computation.3 | async-start | bytes 3145728 | tf_op jit(solution)/shard_map/all_to_all | solution.py:52
  114.4 3.1 %collective-permute-start.10 = (bf16[96,1536]{1,0:T(8,128)(2,1)S(1)}, bf16[96,1536]{1,0:T(8,128)(2,1)S(1)}, u32[]{:S(2)}, u32[]{:S(2)}) collective-permute-start(bf16[96,1536]{1,0:T(8,128)(2,1)S(1)} %get-tuple-element.107), channel_id=1, source_target_pairs={{0,32},{16,48},{32,0},{48,16},{1,33},{17,49},{33,1},{49,17},{2,34}... | collective-permute-start | bytes 884744 | tf_op jit(solution)/shard_map/ppermute | solution.py:36
  117.5 3.4 %collective-permute-start.11 = (bf16[96,1536]{1,0:T(8,128)(2,1)S(1)}, bf16[96,1536]{1,0:T(8,128)(2,1)S(1)}, u32[]{:S(2)}, u32[]{:S(2)}) collective-permute-start(bf16[96,1536]{1,0:T(8,128)(2,1)S(1)} %get-tuple-element.108), channel_id=1, source_target_pairs={{0,48},{16,0},{32,16},{48,32},{1,49},{17,1},{33,17},{49,33},{2,50}... | collective-permute-start | bytes 884744 | tf_op jit(solution)/shard_map/ppermute | solution.py:36
  120.9 17.4 %collective-permute-done.9.refs_1_ = bf16[96,1536]{1,0:T(8,128)(2,1)S(1)} collective-permute-done((bf16[96,1536]{1,0:T(8,128)(2,1)S(1)}, bf16[96,1536]{1,0:T(8,128)(2,1)S(1)}, u32[]{:S(2)}, u32[]{:S(2)}) %collective-permute-start.9) | collective-permute-done | bytes 294944 | tf_op jit(solution)/shard_map/ppermute | solution.py:36
  138.3 7.3 %collective-permute-done.11.refs_3_ = bf16[96,1536]{1,0:T(8,128)(2,1)S(1)} collective-permute-done((bf16[96,1536]{1,0:T(8,128)(2,1)S(1)}, bf16[96,1536]{1,0:T(8,128)(2,1)S(1)}, u32[]{:S(2)}, u32[]{:S(2)}) %collective-permute-start.11) | collective-permute-done | bytes 294944 | tf_op jit(solution)/shard_map/ppermute | solution.py:36
  145.6 3.0 %gather_fusion.1 = bf16[4,96,1536]{2,1,0:T(8,128)(2,1)} fusion(bf16[4,96,1536]{2,1,0:T(8,128)(2,1)} %all-to-all-done, s32[1024]{0:T(1024)S(1)} %pad_clamp_fusion.1), kind=kCustom, calls=%fused_computation.1 | custom fusion | bytes 2359312 | tf_op jit(solution)/shard_map/jit(_take)/gather | solution.py:397
  148.6 4.8 %all-to-all-start.4 = ((bf16[4,96,1536]{2,1,0:T(8,128)(2,1)}), bf16[4,96,1536]{2,1,0:T(8,128)(2,1)S(1)}, u32[]{:S(2)}, u32[]{:S(2)}) async-start(bf16[4,96,1536]{2,1,0:T(8,128)(2,1)} %gather_fusion.1), calls=%async_computation.4 | async-start | bytes 2359296 | tf_op jit(solution)/shard_map/all_to_all | solution.py:52
  160.9 3.5 %collective-permute-start.13 = (bf16[96,1536]{1,0:T(8,128)(2,1)}, bf16[96,1536]{1,0:T(8,128)(2,1)S(1)}, u32[]{:S(2)}, u32[]{:S(2)}) collective-permute-start(bf16[96,1536]{1,0:T(8,128)(2,1)} %get-tuple-element.119), channel_id=1, source_target_pairs={{0,32},{16,48},{32,0},{48,16},{1,33},{17,49},{33,1},{49,17},{2,34}... | collective-permute-start | bytes 884744 | tf_op jit(solution)/shard_map/ppermute | solution.py:36
  165.0 9.8 %expert_ffn.2 = bf16[384,2048]{1,0:T(8,128)(2,1)} custom-call(s32[4]{0:T(128)S(1)} %pad_add_fusion.place_ref, bf16[4,384,1536]{2,1,0:T(8,128)(2,1)} %bitcast.44, bf16[4,384,1536]{2,1,0:T(8,128)(2,1)} %bitcast.46, bf16[384,2048]{1,0:T(8,128)(2,1)S(1)} %bitcast.35), custom_call_target="tpu_custom_call" | custom-call | flops 3623878656 | bytes 15728640 | tf_op jit(solution)/shard_map/expert_ffn/pallas_call | solution.py:274
  174.7 5.3 %collective-permute-done.13.refs_5_ = bf16[96,1536]{1,0:T(8,128)(2,1)S(1)} collective-permute-done((bf16[96,1536]{1,0:T(8,128)(2,1)}, bf16[96,1536]{1,0:T(8,128)(2,1)S(1)}, u32[]{:S(2)}, u32[]{:S(2)}) %collective-permute-start.13) | collective-permute-done | bytes 294944 | tf_op jit(solution)/shard_map/ppermute | solution.py:36
  180.0 3.8 %collective-permute-done.14.refs_6_ = bf16[96,1536]{1,0:T(8,128)(2,1)} collective-permute-done((bf16[96,1536]{1,0:T(8,128)(2,1)}, bf16[96,1536]{1,0:T(8,128)(2,1)}, u32[]{:S(2)}, u32[]{:S(2)}) %collective-permute-start.14) | collective-permute-done | bytes 294944 | tf_op jit(solution)/shard_map/ppermute | solution.py:36
  183.9 4.8 %all-to-all-start.5 = ((bf16[8,48,2048]{2,1,0:T(8,128)(2,1)}), bf16[8,48,2048]{2,1,0:T(8,128)(2,1)S(1)}, u32[]{:S(2)}, u32[]{:S(2)}) async-start(bf16[8,48,2048]{2,1,0:T(8,128)(2,1)} %bitcast.39), calls=%async_computation.5 | async-start | bytes 3145728 | tf_op jit(solution)/shard_map/all_to_all | solution.py:52
  191.3 12.7 %expert_ffn.3 = (bf16[256,2048]{1,0:T(8,128)(2,1)}, bf16[384,2048]{1,0:T(8,128)(2,1)}) custom-call(s32[4]{0:T(128)S(1)} %pad_add_fusion.place_ref, bf16[4,384,1536]{2,1,0:T(8,128)(2,1)} %bitcast.45, bf16[4,384,1536]{2,1,0:T(8,128)(2,1)} %bitcast.47, bf16[256,2048]{1,0:T(8,128)(2,1)S(1)} %bitcast.36, bf16[384,2048]{1,0:T(8,128)(2,1)S(1)} %bitcast.34), custom_call_target="tpu_custom_call" | custom-call | flops 6039797760 | bytes 15728640 | tf_op jit(solution)/shard_map/expert_ffn/pallas_call | solution.py:274
  204.0 4.2 %all-to-all-done.5 = bf16[8,48,2048]{2,1,0:T(8,128)(2,1)S(1)} async-done(((bf16[8,48,2048]{2,1,0:T(8,128)(2,1)}), bf16[8,48,2048]{2,1,0:T(8,128)(2,1)S(1)}, u32[]{:S(2)}, u32[]{:S(2)}) %all-to-all-start.5) | async-done | bytes 1572896 | tf_op jit(solution)/shard_map/all_to_all | solution.py:52
  208.2 6.2 %all-to-all-start.6 = ((bf16[8,32,2048]{2,1,0:T(8,128)(2,1)}), bf16[8,32,2048]{2,1,0:T(8,128)(2,1)}, u32[]{:S(2)}, u32[]{:S(2)}) async-start(bf16[8,32,2048]{2,1,0:T(8,128)(2,1)} %bitcast.40), calls=%async_computation.6 | async-start | bytes 2097152 | tf_op jit(solution)/shard_map/all_to_all | solution.py:52
  216.5 3.2 %collective-permute-start.15 = (bf16[96,2048]{1,0:T(8,128)(2,1)}, bf16[96,2048]{1,0:T(8,128)(2,1)}, u32[]{:S(2)}, u32[]{:S(2)}) collective-permute-start(bf16[96,2048]{1,0:T(8,128)(2,1)} %get-tuple-element.127), channel_id=1, source_target_pairs={{0,49},{1,0},{16,1},{17,16},{32,17},{33,32},{48,33},{49,48},{2,51}... | collective-permute-start | bytes 1179656 | tf_op jit(solution)/shard_map/ppermute | solution.py:36
  219.8 9.2 %collective-permute-done.17 = bf16[96,2048]{1,0:T(8,128)(2,1)} collective-permute-done((bf16[96,2048]{1,0:T(8,128)(2,1)S(1)}, bf16[96,2048]{1,0:T(8,128)(2,1)}, u32[]{:S(2)}, u32[]{:S(2)}) %collective-permute-start.17) | collective-permute-done | bytes 393248 | tf_op jit(solution)/shard_map/ppermute | solution.py:36
  229.0 5.0 %all-to-all-start.7 = ((bf16[8,48,2048]{2,1,0:T(8,128)(2,1)}), bf16[8,48,2048]{2,1,0:T(8,128)(2,1)S(1)}, u32[]{:S(2)}, u32[]{:S(2)}) async-start(bf16[8,48,2048]{2,1,0:T(8,128)(2,1)} %bitcast.38), calls=%async_computation.7 | async-start | bytes 3145728 | tf_op jit(solution)/shard_map/all_to_all | solution.py:52
  240.6 5.7 %collective-permute-done.16 = bf16[96,2048]{1,0:T(8,128)(2,1)S(1)} collective-permute-done((bf16[96,2048]{1,0:T(8,128)(2,1)S(1)}, bf16[96,2048]{1,0:T(8,128)(2,1)S(1)}, u32[]{:S(2)}, u32[]{:S(2)}) %collective-permute-start.16) | collective-permute-done | bytes 393248 | tf_op jit(solution)/shard_map/ppermute | solution.py:36
  249.4 4.1 %all-to-all-done.7 = bf16[8,48,2048]{2,1,0:T(8,128)(2,1)S(1)} async-done(((bf16[8,48,2048]{2,1,0:T(8,128)(2,1)}), bf16[8,48,2048]{2,1,0:T(8,128)(2,1)S(1)}, u32[]{:S(2)}, u32[]{:S(2)}) %all-to-all-start.7) | async-done | bytes 1572896 | tf_op jit(solution)/shard_map/all_to_all | solution.py:52
  259.8 3.3 %collective-permute-start.19 = (bf16[96,2048]{1,0:T(8,128)(2,1)}, bf16[96,2048]{1,0:T(8,128)(2,1)}, u32[]{:S(2)}, u32[]{:S(2)}) collective-permute-start(bf16[96,2048]{1,0:T(8,128)(2,1)} %add_convert_fusion.3), channel_id=1, source_target_pairs={{0,49},{1,0},{16,1},{17,16},{32,17},{33,32},{48,33},{49,48},{2,51}... | collective-permute-start | bytes 1179656 | tf_op jit(solution)/shard_map/ppermute | solution.py:36
  (113 shorter events, 58.7 us)
Async XLA Ops:
  7.2 157.8 %all-gather.5.cloned.1.call-start = ((), (), s32[]{:S(2)}) async-start(), calls=%async_computation.8 | async-start | bytes 5898240 | tf_op jit(solution)/shard_map/all_gather | solution.py:367
  12.7 26.9 %collective-permute-start.5 = (bf16[384,1536]{1,0:T(8,128)(2,1)}, bf16[384,1536]{1,0:T(8,128)(2,1)S(1)}, u32[]{:S(2)}, u32[]{:S(2)}) collective-permute-start(bf16[384,1536]{1,0:T(8,128)(2,1)} %get-tuple-element.146.first_ref.refs_0_), channel_id=1, source_target_pairs={{0,8},{8,0},{1,9},{9,1},{2,10},{10,2},{3,11},{11,3},{4,12},{12,4},... | collective-permute-start | bytes 3538952 | tf_op jit(solution)/shard_map/ppermute | solution.py:329
  12.8 26.8 %all-to-all-start = ((bf16[4,96,1536]{2,1,0:T(8,128)(2,1)}), bf16[4,96,1536]{2,1,0:T(8,128)(2,1)}, u32[]{:S(2)}, u32[]{:S(2)}) async-start(bf16[4,96,1536]{2,1,0:T(8,128)(2,1)} %bitcast.7), calls=%async_computation | async-start | bytes 2359296 | tf_op jit(solution)/shard_map/all_to_all | solution.py:52
  17.6 15.3 %collective-permute-start.1 = (bf16[104,2048]{1,0:T(8,128)(2,1)S(1)}, bf16[104,2048]{1,0:T(8,128)(2,1)S(1)}, u32[]{:S(2)}, u32[]{:S(2)}) collective-permute-start(bf16[104,2048]{1,0:T(8,128)(2,1)S(1)} %get-tuple-element.80.refs_0_), channel_id=1, source_target_pairs={{0,49},{1,0},{16,1},{17,16},{32,17},{33,32},{48,33},{49,48},{2,51}... | collective-permute-start | bytes 1277960 | tf_op jit(solution)/shard_map/ppermute | solution.py:36
  23.5 12.8 %collective-permute-start = (bf16[104,2048]{1,0:T(8,128)(2,1)S(1)}, bf16[104,2048]{1,0:T(8,128)(2,1)S(1)}, u32[]{:S(2)}, u32[]{:S(2)}) collective-permute-start(bf16[104,2048]{1,0:T(8,128)(2,1)S(1)} %get-tuple-element.80.refs_0_), channel_id=1, source_target_pairs={{0,1},{1,16},{16,17},{17,32},{32,33},{33,48},{48,49},{49,0},{2,3},... | collective-permute-start | bytes 1277960 | tf_op jit(solution)/shard_map/ppermute | solution.py:36
  36.4 36.2 %collective-permute-start.4 = (bf16[384,1536]{1,0:T(8,128)(2,1)}, bf16[384,1536]{1,0:T(8,128)(2,1)}, u32[]{:S(2)}, u32[]{:S(2)}) collective-permute-start(bf16[384,1536]{1,0:T(8,128)(2,1)} %copy-done.23), channel_id=1, source_target_pairs={{0,1},{1,0},{2,3},{3,2},{4,5},{5,4},{6,7},{7,6},{8,9},{9,8},{10,11... | collective-permute-start | bytes 3538952 | tf_op jit(solution)/shard_map/ppermute | solution.py:329
  40.7 42.9 %all-to-all-start.1 = ((bf16[8,48,2048]{2,1,0:T(8,128)(2,1)}), bf16[8,48,2048]{2,1,0:T(8,128)(2,1)S(1)}, u32[]{:S(2)}, u32[]{:S(2)}) async-start(bf16[8,48,2048]{2,1,0:T(8,128)(2,1)} %bitcast.8), calls=%async_computation.1 | async-start | bytes 3145728 | tf_op jit(solution)/shard_map/all_to_all | solution.py:52
  45.5 119.4 %all-gather.7.cloned.1.call-start = ((), (), s32[]{:S(2)}) async-start(), calls=%async_computation.9 | async-start | bytes 5898240 | tf_op jit(solution)/shard_map/all_gather | solution.py:382
  45.5 24.8 %collective-permute-start.2 = (bf16[104,2048]{1,0:T(8,128)(2,1)S(1)}, bf16[104,2048]{1,0:T(8,128)(2,1)S(1)}, u32[]{:S(2)}, u32[]{:S(2)}) collective-permute-start(bf16[104,2048]{1,0:T(8,128)(2,1)S(1)} %collective-permute-done.refs_1_), channel_id=1, source_target_pairs={{0,1},{1,16},{16,17},{17,32},{32,33},{33,48},{48,49},{49,0},{2,3},... | collective-permute-start | bytes 1277960 | tf_op jit(solution)/shard_map/ppermute | solution.py:36
  47.6 25.0 %collective-permute-start.3 = (bf16[104,2048]{1,0:T(8,128)(2,1)S(1)}, bf16[104,2048]{1,0:T(8,128)(2,1)S(1)}, u32[]{:S(2)}, u32[]{:S(2)}) collective-permute-start(bf16[104,2048]{1,0:T(8,128)(2,1)S(1)} %collective-permute-done.1.refs_2_), channel_id=1, source_target_pairs={{0,49},{1,0},{16,1},{17,16},{32,17},{33,32},{48,33},{49,48},{2,51}... | collective-permute-start | bytes 1277960 | tf_op jit(solution)/shard_map/ppermute | solution.py:36
  72.6 11.0 %collective-permute-start.6 = (bf16[104,2048]{1,0:T(8,128)(2,1)S(1)}, bf16[104,2048]{1,0:T(8,128)(2,1)S(1)}, u32[]{:S(2)}, u32[]{:S(2)}) collective-permute-start(bf16[104,2048]{1,0:T(8,128)(2,1)S(1)} %collective-permute-done.2.refs_0_), channel_id=1, source_target_pairs={{0,1},{1,16},{16,17},{17,32},{32,33},{33,48},{48,49},{49,0},{2,3},... | collective-permute-start | bytes 1277960 | tf_op jit(solution)/shard_map/ppermute | solution.py:36
  72.9 10.7 %collective-permute-start.7 = (bf16[104,2048]{1,0:T(8,128)(2,1)S(1)}, bf16[104,2048]{1,0:T(8,128)(2,1)S(1)}, u32[]{:S(2)}, u32[]{:S(2)}) collective-permute-start(bf16[104,2048]{1,0:T(8,128)(2,1)S(1)} %collective-permute-done.3.refs_1_), channel_id=1, source_target_pairs={{0,49},{1,0},{16,1},{17,16},{32,17},{33,32},{48,33},{49,48},{2,51}... | collective-permute-start | bytes 1277960 | tf_op jit(solution)/shard_map/ppermute | solution.py:36
  84.8 21.3 %all-to-all-start.2 = ((bf16[8,32,2048]{2,1,0:T(8,128)(2,1)}), bf16[8,32,2048]{2,1,0:T(8,128)(2,1)S(1)}, u32[]{:S(2)}, u32[]{:S(2)}) async-start(bf16[8,32,2048]{2,1,0:T(8,128)(2,1)} %bitcast.37), calls=%async_computation.2 | async-start | bytes 2097152 | tf_op jit(solution)/shard_map/all_to_all | solution.py:52
  89.6 13.1 %collective-permute-start.8 = (bf16[104,2048]{1,0:T(8,128)(2,1)S(1)}, bf16[104,2048]{1,0:T(8,128)(2,1)S(1)}, u32[]{:S(2)}, u32[]{:S(2)}) collective-permute-start(bf16[104,2048]{1,0:T(8,128)(2,1)S(1)} %collective-permute-done.6.refs_0_), channel_id=1, source_target_pairs={{0,1},{1,16},{16,17},{17,32},{32,33},{33,48},{48,49},{49,0},{2,3},... | collective-permute-start | bytes 1277960 | tf_op jit(solution)/shard_map/ppermute | solution.py:36
  107.1 38.5 %all-to-all-start.3 = ((bf16[8,48,2048]{2,1,0:T(8,128)(2,1)}), bf16[8,48,2048]{2,1,0:T(8,128)(2,1)S(1)}, u32[]{:S(2)}, u32[]{:S(2)}) async-start(bf16[8,48,2048]{2,1,0:T(8,128)(2,1)} %bitcast.14), calls=%async_computation.3 | async-start | bytes 3145728 | tf_op jit(solution)/shard_map/all_to_all | solution.py:52
  114.4 23.9 %collective-permute-start.9 = (bf16[96,1536]{1,0:T(8,128)(2,1)S(1)}, bf16[96,1536]{1,0:T(8,128)(2,1)S(1)}, u32[]{:S(2)}, u32[]{:S(2)}) collective-permute-start(bf16[96,1536]{1,0:T(8,128)(2,1)S(1)} %get-tuple-element.106), channel_id=1, source_target_pairs={{0,16},{16,32},{32,48},{48,0},{1,17},{17,33},{33,49},{49,1},{2,18}... | collective-permute-start | bytes 884744 | tf_op jit(solution)/shard_map/ppermute | solution.py:36
  114.4 23.9 %collective-permute-start.10 = (bf16[96,1536]{1,0:T(8,128)(2,1)S(1)}, bf16[96,1536]{1,0:T(8,128)(2,1)S(1)}, u32[]{:S(2)}, u32[]{:S(2)}) collective-permute-start(bf16[96,1536]{1,0:T(8,128)(2,1)S(1)} %get-tuple-element.107), channel_id=1, source_target_pairs={{0,32},{16,48},{32,0},{48,16},{1,33},{17,49},{33,1},{49,17},{2,34}... | collective-permute-start | bytes 884744 | tf_op jit(solution)/shard_map/ppermute | solution.py:36
  117.5 28.1 %collective-permute-start.11 = (bf16[96,1536]{1,0:T(8,128)(2,1)S(1)}, bf16[96,1536]{1,0:T(8,128)(2,1)S(1)}, u32[]{:S(2)}, u32[]{:S(2)}) collective-permute-start(bf16[96,1536]{1,0:T(8,128)(2,1)S(1)} %get-tuple-element.108), channel_id=1, source_target_pairs={{0,48},{16,0},{32,16},{48,32},{1,49},{17,1},{33,17},{49,33},{2,50}... | collective-permute-start | bytes 884744 | tf_op jit(solution)/shard_map/ppermute | solution.py:36
  148.6 35.3 %all-to-all-start.4 = ((bf16[4,96,1536]{2,1,0:T(8,128)(2,1)}), bf16[4,96,1536]{2,1,0:T(8,128)(2,1)S(1)}, u32[]{:S(2)}, u32[]{:S(2)}) async-start(bf16[4,96,1536]{2,1,0:T(8,128)(2,1)} %gather_fusion.1), calls=%async_computation.4 | async-start | bytes 2359296 | tf_op jit(solution)/shard_map/all_to_all | solution.py:52
  158.5 16.2 %collective-permute-start.12 = (bf16[96,1536]{1,0:T(8,128)(2,1)}, bf16[96,1536]{1,0:T(8,128)(2,1)S(1)}, u32[]{:S(2)}, u32[]{:S(2)}) collective-permute-start(bf16[96,1536]{1,0:T(8,128)(2,1)} %get-tuple-element.118), channel_id=1, source_target_pairs={{0,16},{16,32},{32,48},{48,0},{1,17},{17,33},{33,49},{49,1},{2,18}... | collective-permute-start | bytes 884744 | tf_op jit(solution)/shard_map/ppermute | solution.py:36
  160.9 19.1 %collective-permute-start.13 = (bf16[96,1536]{1,0:T(8,128)(2,1)}, bf16[96,1536]{1,0:T(8,128)(2,1)S(1)}, u32[]{:S(2)}, u32[]{:S(2)}) collective-permute-start(bf16[96,1536]{1,0:T(8,128)(2,1)} %get-tuple-element.119), channel_id=1, source_target_pairs={{0,32},{16,48},{32,0},{48,16},{1,33},{17,49},{33,1},{49,17},{2,34}... | collective-permute-start | bytes 884744 | tf_op jit(solution)/shard_map/ppermute | solution.py:36
  164.4 19.5 %collective-permute-start.14 = (bf16[96,1536]{1,0:T(8,128)(2,1)}, bf16[96,1536]{1,0:T(8,128)(2,1)}, u32[]{:S(2)}, u32[]{:S(2)}) collective-permute-start(bf16[96,1536]{1,0:T(8,128)(2,1)} %get-tuple-element.120), channel_id=1, source_target_pairs={{0,48},{16,0},{32,16},{48,32},{1,49},{17,1},{33,17},{49,33},{2,50}... | collective-permute-start | bytes 884744 | tf_op jit(solution)/shard_map/ppermute | solution.py:36
  183.9 24.3 %all-to-all-start.5 = ((bf16[8,48,2048]{2,1,0:T(8,128)(2,1)}), bf16[8,48,2048]{2,1,0:T(8,128)(2,1)S(1)}, u32[]{:S(2)}, u32[]{:S(2)}) async-start(bf16[8,48,2048]{2,1,0:T(8,128)(2,1)} %bitcast.39), calls=%async_computation.5 | async-start | bytes 3145728 | tf_op jit(solution)/shard_map/all_to_all | solution.py:52
  208.2 20.8 %all-to-all-start.6 = ((bf16[8,32,2048]{2,1,0:T(8,128)(2,1)}), bf16[8,32,2048]{2,1,0:T(8,128)(2,1)}, u32[]{:S(2)}, u32[]{:S(2)}) async-start(bf16[8,32,2048]{2,1,0:T(8,128)(2,1)} %bitcast.40), calls=%async_computation.6 | async-start | bytes 2097152 | tf_op jit(solution)/shard_map/all_to_all | solution.py:52
  216.5 12.5 %collective-permute-start.17 = (bf16[96,2048]{1,0:T(8,128)(2,1)S(1)}, bf16[96,2048]{1,0:T(8,128)(2,1)}, u32[]{:S(2)}, u32[]{:S(2)}) collective-permute-start(bf16[96,2048]{1,0:T(8,128)(2,1)S(1)} %get-tuple-element.132), channel_id=1, source_target_pairs={{0,1},{1,16},{16,17},{17,32},{32,33},{33,48},{48,49},{49,0},{2,3},... | collective-permute-start | bytes 1179656 | tf_op jit(solution)/shard_map/ppermute | solution.py:36
  216.5 17.5 %collective-permute-start.15 = (bf16[96,2048]{1,0:T(8,128)(2,1)}, bf16[96,2048]{1,0:T(8,128)(2,1)}, u32[]{:S(2)}, u32[]{:S(2)}) collective-permute-start(bf16[96,2048]{1,0:T(8,128)(2,1)} %get-tuple-element.127), channel_id=1, source_target_pairs={{0,49},{1,0},{16,1},{17,16},{32,17},{33,32},{48,33},{49,48},{2,51}... | collective-permute-start | bytes 1179656 | tf_op jit(solution)/shard_map/ppermute | solution.py:36
  229.0 24.5 %all-to-all-start.7 = ((bf16[8,48,2048]{2,1,0:T(8,128)(2,1)}), bf16[8,48,2048]{2,1,0:T(8,128)(2,1)S(1)}, u32[]{:S(2)}, u32[]{:S(2)}) async-start(bf16[8,48,2048]{2,1,0:T(8,128)(2,1)} %bitcast.38), calls=%async_computation.7 | async-start | bytes 3145728 | tf_op jit(solution)/shard_map/all_to_all | solution.py:52
  235.1 11.2 %collective-permute-start.16 = (bf16[96,2048]{1,0:T(8,128)(2,1)S(1)}, bf16[96,2048]{1,0:T(8,128)(2,1)S(1)}, u32[]{:S(2)}, u32[]{:S(2)}) collective-permute-start(bf16[96,2048]{1,0:T(8,128)(2,1)S(1)} %add_convert_fusion.5), channel_id=1, source_target_pairs={{0,49},{1,0},{16,1},{17,16},{32,17},{33,32},{48,33},{49,48},{2,51}... | collective-permute-start | bytes 1179656 | tf_op jit(solution)/shard_map/ppermute | solution.py:36
  239.6 15.3 %collective-permute-start.20 = (bf16[96,2048]{1,0:T(8,128)(2,1)}, bf16[96,2048]{1,0:T(8,128)(2,1)}, u32[]{:S(2)}, u32[]{:S(2)}) collective-permute-start(bf16[96,2048]{1,0:T(8,128)(2,1)} %add_convert_fusion.2), channel_id=1, source_target_pairs={{0,1},{1,16},{16,17},{17,32},{32,33},{33,48},{48,49},{49,0},{2,3},... | collective-permute-start | bytes 1179656 | tf_op jit(solution)/shard_map/ppermute | solution.py:36
  247.2 10.8 %collective-permute-start.18 = (bf16[96,2048]{1,0:T(8,128)(2,1)}, bf16[96,2048]{1,0:T(8,128)(2,1)}, u32[]{:S(2)}, u32[]{:S(2)}) collective-permute-start(bf16[96,2048]{1,0:T(8,128)(2,1)} %add_convert_fusion.4), channel_id=1, source_target_pairs={{0,49},{1,0},{16,1},{17,16},{32,17},{33,32},{48,33},{49,48},{2,51}... | collective-permute-start | bytes 1179656 | tf_op jit(solution)/shard_map/ppermute | solution.py:36
  256.7 12.2 %collective-permute-start.21 = (bf16[96,2048]{1,0:T(8,128)(2,1)}, bf16[96,2048]{1,0:T(8,128)(2,1)}, u32[]{:S(2)}, u32[]{:S(2)}) collective-permute-start(bf16[96,2048]{1,0:T(8,128)(2,1)} %add_convert_fusion.1), channel_id=1, source_target_pairs={{0,1},{1,16},{16,17},{17,32},{32,33},{33,48},{48,49},{49,0},{2,3},... | collective-permute-start | bytes 1179656 | tf_op jit(solution)/shard_map/ppermute | solution.py:36
  259.8 10.6 %collective-permute-start.19 = (bf16[96,2048]{1,0:T(8,128)(2,1)}, bf16[96,2048]{1,0:T(8,128)(2,1)}, u32[]{:S(2)}, u32[]{:S(2)}) collective-permute-start(bf16[96,2048]{1,0:T(8,128)(2,1)} %add_convert_fusion.3), channel_id=1, source_target_pairs={{0,49},{1,0},{16,1},{17,16},{32,17},{33,32},{48,33},{49,48},{2,51}... | collective-permute-start | bytes 1179656 | tf_op jit(solution)/shard_map/ppermute | solution.py:36
  (25 other events, 76.0 us)
Sparse Core Ops, SparseCore 0:
  12.9 57.0 all-gather.4
  83.8 52.8 all-gather.6

commit v7 on v6

--- a/solution.py
+++ b/solution.py
@@ -377,25 +377,22 @@
     r0 = in_plane(d0)
     p2, m2, swapped = fence(p2, m2, swapped)
     p3, m3 = along_z(p2, 1), along_z(m2, -1)
-    d1, w1 = dispatch(place, (p2, m2))
-    d1, r0, p3, m3, swapped = fence(d1, r0, p3, m3, swapped)
-    swap_full = lax.all_gather(swapped, "y", axis=0, tiled=False)
-    r1 = in_plane(d1)
-    far = along_z(p3, 1)
-    far, first = fence(far, first)
     cut = call(
         cut_kernel, [shape(PIECE, SIDE)] * NZH, [SMEM, HBM], [HBM] * NZH, "cut",
         scratch=[pltpu.SemaphoreType.DMA((NZH,))],
     )(place, first)
+    d1, w1 = dispatch(place, (p2, m2))
+    d1, r0, p3, m3, swapped, *cut = fence(d1, r0, p3, m3, swapped, *cut)
+    swap_full = lax.all_gather(swapped, "y", axis=0, tiled=False)
+    r1 = in_plane(d1)
+    far = along_z(p3, 1)
     held = [cut[0]] + [shift(cut[k], "zh", NZH, k) for k in range(1, NZH)]
     d2, w2 = dispatch(place, (p3, m3, far))
-    d2, r1 = fence(d2, r1)
+    d2, r1, *held = fence(d2, r1, *held)
     r2 = in_plane(d2)
-    r0, r1, r2, first, hx, *held = fence(r0, r1, r2, first, hx, *held)
     x_turn = jnp.arange(NX, dtype=jnp.int32)
     x_from = jnp.take(pair_list, (x_turn * NZH + zh_me) * NC + c_me, mode="clip") >> 3
-    hx = across(jnp.take(hx, x_from, axis=0, mode="clip"), "x").reshape(PACK, SIDE)
-
+    hx = jnp.take(hx, x_from, axis=0, mode="clip")
     turn = (zh_me + jnp.arange(NZH, dtype=jnp.int32)) & (NZH - 1)
     matched = jnp.take(pair_list, (x_me * NZH + turn) * NC + c_me, mode="clip")
     chosen = (zh_me - (matched >> 1)) & (NZH - 1)
@@ -404,9 +401,10 @@
         scratch=[pltpu.SemaphoreType.DMA((NZH,))],
     )(chosen.astype(jnp.int32), *held)
     held = [picked[0]] + [shift(picked[k], "zh", NZH, k) for k in range(1, NZH)]
-
+    r0, r1, r2, hx, *held = fence(r0, r1, r2, hx, *held)
+    hx = across(hx, "x").reshape(PACK, SIDE)
     (s2,) = ffn(place, own_full, swap_full, (r2,), 384)
-    s2, r1, r0, hx, *held = fence(s2, r1, r0, hx, *held)
+    s2, r1, r0, hx = fence(s2, r1, r0, hx)
     b2 = in_plane(s2)
     s1, s0 = ffn(place, own_full, swap_full, (r1, r0), 320)
     b2, s1, s0 = fence(b2, s1, s0)
@@ -414,7 +412,7 @@
     down, rise = along_z(c_4, -1), along_z(c_p3, 1)
     b1 = in_plane(s1)
     down = along_z(joined(down, c_m3), -1)
-    b1, s0, rise, *held = fence(b1, s0, rise, *held)
+    b1, s0, rise = fence(b1, s0, rise)
     b0 = in_plane(s0)
     c_m2, c_p2 = combine(w1, b1, (F32, F32))
     down = along_z(joined(down, c_m2), -1)

time: 282 us -> 291 us (1.032)
  starting transfers between devices: 76.3 us -> 83.4 us
  local copies, waits for them, and re-layouts: 18.8 us -> 24.1 us
    ppermute x20, starting transfers between devices: 36.2 us -> 42.5 us  [shift(): lax.ppermute(value, axes, [(i, (i + step) % count) for i in range(count)])]
    unnamed x50 -> x68, local copies, waits for them, and re-layouts: 14.5 us -> 19.9 us
  transfers between devices with their start and end apart: 32 -> 32, of which waited for: 17 -> 17; matrix products, arithmetic and copies ran while one was open for 4% -> 4% of each run, Pallas kernels for 14% -> 13%
where the time goes in v7:
time: 291 us; the launch traced here: 289 us
  waiting for transfers between devices  115 us (40%)
  starting transfers between devices  83.4 us (29%)
  Pallas kernels  42.5 us (15%)
  local copies, waits for them, and re-layouts  24.1 us (8%)
  between operations  14.3 us (5%)
  other arithmetic  10.2 us (4%)
    ppermute x20, waiting for transfers between devices, shift(): lax.ppermute(value, axes, [(i, (i + step) % count) for i in range(count)])  106 us
    ppermute x20, starting transfers between devices, shift(): lax.ppermute(value, axes, [(i, (i + step) % count) for i in range(count)])  42.5 us
    all_to_all x8, starting transfers between devices, across(): return lax.all_to_all(value, axis, split_axis=0, concat_axis=0, tiled=True)  40.8 us
    pallas_call x2, Pallas kernels, ffn(): call(functools.partial(ffn_kernel, splits, block), [pltpu.HBM((r, WIDTH),...  22.5 us
    unnamed x68, local copies, waits for them, and re-layouts  19.9 us
    all_to_all x8, waiting for transfers between devices, across(): return lax.all_to_all(value, axis, split_axis=0, concat_axis=0, tiled=True)  8.98 us
    convert_element_type x5, other arithmetic, joined(): return (got.astype(F32) + mine).astype(BF)  7.4 us
    pallas_call x3, Pallas kernels, dispatch(): call(functools.partial(dispatch_kernel, n), [shape(PLACES * n * MOST, WID...  6.64 us
  transfers between devices with their start and end apart: 32, of which 17 were waited for; matrix products, arithmetic and copies ran while one was open for 4% of the time, Pallas kernels for 13%

profile of v7, /device:TPU:22, one launch (start us, length us, event | category | flops | bytes accessed | tf_op | source)
XLA Modules:
  0.0 289.2 jit_solution(13784170033392106620)
XLA Ops:
  7.3 4.4 %prep.1 = (bf16[104,2048]{1,0:T(8,128)(2,1)S(1)}, bf16[384,1536]{1,0:T(8,128)(2,1)}, bf16[384,1536]{1,0:T(8,128)(2,1)S(1)}, bf16[384,1536]{1,0:T(8,128)(2,1)}) custom-call(s32[4]{0:T(128)S(1)} %pad_add_fusion.place_ref, bf16[96,2048]{1,0:T(8,128)(2,1)} %tokens_ref.1, f32[1,2048]{1,0:T(1,128)} %bitcast.41, s32[8,96]{1,0:T(8,128)} %bitcast.42, ...), custom_call_target="tpu_custom_call" | custom-call | tf_op jit(solution)/shard_map/prep/pallas_call | solution.py:343
  12.9 4.8 %all-to-all-start = ((bf16[4,96,1536]{2,1,0:T(8,128)(2,1)}), bf16[4,96,1536]{2,1,0:T(8,128)(2,1)}, u32[]{:S(2)}, u32[]{:S(2)}) async-start(bf16[4,96,1536]{2,1,0:T(8,128)(2,1)} %bitcast.7), calls=%async_computation | async-start | bytes 2359296 | tf_op jit(solution)/shard_map/all_to_all | solution.py:52
  19.7 3.9 %collective-permute-start.1 = (bf16[104,2048]{1,0:T(8,128)(2,1)S(1)}, bf16[104,2048]{1,0:T(8,128)(2,1)S(1)}, u32[]{:S(2)}, u32[]{:S(2)}) collective-permute-start(bf16[104,2048]{1,0:T(8,128)(2,1)S(1)} %get-tuple-element.77.refs_0_), channel_id=1, source_target_pairs={{0,49},{1,0},{16,1},{17,16},{32,17},{33,32},{48,33},{49,48},{2,51}... | collective-permute-start | bytes 1277960 | tf_op jit(solution)/shard_map/ppermute | solution.py:36
  23.6 10.1 %collective-permute-done.refs_1_ = bf16[104,2048]{1,0:T(8,128)(2,1)S(1)} collective-permute-done((bf16[104,2048]{1,0:T(8,128)(2,1)S(1)}, bf16[104,2048]{1,0:T(8,128)(2,1)S(1)}, u32[]{:S(2)}, u32[]{:S(2)}) %collective-permute-start) | collective-permute-done | bytes 426016 | tf_op jit(solution)/shard_map/ppermute | solution.py:36
  38.1 4.8 %all-to-all-start.1 = ((bf16[8,48,2048]{2,1,0:T(8,128)(2,1)}), bf16[8,48,2048]{2,1,0:T(8,128)(2,1)S(1)}, u32[]{:S(2)}, u32[]{:S(2)}) async-start(bf16[8,48,2048]{2,1,0:T(8,128)(2,1)} %bitcast.8), calls=%async_computation.1 | async-start | bytes 3145728 | tf_op jit(solution)/shard_map/all_to_all | solution.py:52
  46.4 21.9 %collective-permute-done.2.refs_0_ = bf16[104,2048]{1,0:T(8,128)(2,1)S(1)} collective-permute-done((bf16[104,2048]{1,0:T(8,128)(2,1)S(1)}, bf16[104,2048]{1,0:T(8,128)(2,1)S(1)}, u32[]{:S(2)}, u32[]{:S(2)}) %collective-permute-start.2) | collective-permute-done | bytes 426016 | tf_op jit(solution)/shard_map/ppermute | solution.py:36
  79.0 3.3 %collective-permute-done.6.refs_0_ = bf16[104,2048]{1,0:T(8,128)(2,1)S(1)} collective-permute-done((bf16[104,2048]{1,0:T(8,128)(2,1)S(1)}, bf16[104,2048]{1,0:T(8,128)(2,1)S(1)}, u32[]{:S(2)}, u32[]{:S(2)}) %collective-permute-start.6) | collective-permute-done | bytes 426016 | tf_op jit(solution)/shard_map/ppermute | solution.py:36
  83.5 4.8 %all-to-all-start.2 = ((bf16[8,32,2048]{2,1,0:T(8,128)(2,1)}), bf16[8,32,2048]{2,1,0:T(8,128)(2,1)S(1)}, u32[]{:S(2)}, u32[]{:S(2)}) async-start(bf16[8,32,2048]{2,1,0:T(8,128)(2,1)} %bitcast.37), calls=%async_computation.2 | async-start | bytes 2097152 | tf_op jit(solution)/shard_map/all_to_all | solution.py:52
  92.0 4.4 %collective-permute-start.11 = (bf16[96,1536]{1,0:T(8,128)(2,1)}, bf16[96,1536]{1,0:T(8,128)(2,1)S(1)}, u32[]{:S(2)}, u32[]{:S(2)}) collective-permute-start(bf16[96,1536]{1,0:T(8,128)(2,1)} %copy-done.31), channel_id=1, source_target_pairs={{0,48},{16,0},{32,16},{48,32},{1,49},{17,1},{33,17},{49,33},{2,50}... | collective-permute-start | bytes 884744 | tf_op jit(solution)/shard_map/ppermute | solution.py:36
  96.4 6.3 %collective-permute-done.8.refs_2_ = bf16[104,2048]{1,0:T(8,128)(2,1)S(1)} collective-permute-done((bf16[104,2048]{1,0:T(8,128)(2,1)S(1)}, bf16[104,2048]{1,0:T(8,128)(2,1)S(1)}, u32[]{:S(2)}, u32[]{:S(2)}) %collective-permute-start.8) | collective-permute-done | bytes 426016 | tf_op jit(solution)/shard_map/ppermute | solution.py:36
  106.0 4.9 %collective-permute-done.10.refs_2_ = bf16[96,1536]{1,0:T(8,128)(2,1)S(1)} collective-permute-done((bf16[96,1536]{1,0:T(8,128)(2,1)}, bf16[96,1536]{1,0:T(8,128)(2,1)S(1)}, u32[]{:S(2)}, u32[]{:S(2)}) %collective-permute-start.10) | collective-permute-done | bytes 294944 | tf_op jit(solution)/shard_map/ppermute | solution.py:36
  111.6 9.2 %collective-permute-done.11.refs_3_ = bf16[96,1536]{1,0:T(8,128)(2,1)S(1)} collective-permute-done((bf16[96,1536]{1,0:T(8,128)(2,1)}, bf16[96,1536]{1,0:T(8,128)(2,1)S(1)}, u32[]{:S(2)}, u32[]{:S(2)}) %collective-permute-start.11) | collective-permute-done | bytes 294944 | tf_op jit(solution)/shard_map/ppermute | solution.py:36
  121.5 6.3 %collective-permute-done.9.refs_1_ = bf16[96,1536]{1,0:T(8,128)(2,1)S(1)} collective-permute-done((bf16[96,1536]{1,0:T(8,128)(2,1)}, bf16[96,1536]{1,0:T(8,128)(2,1)S(1)}, u32[]{:S(2)}, u32[]{:S(2)}) %collective-permute-start.9) | collective-permute-done | bytes 294944 | tf_op jit(solution)/shard_map/ppermute | solution.py:36
  129.5 4.8 %all-to-all-start.3 = ((bf16[8,48,2048]{2,1,0:T(8,128)(2,1)}), bf16[8,48,2048]{2,1,0:T(8,128)(2,1)S(1)}, u32[]{:S(2)}, u32[]{:S(2)}) async-start(bf16[8,48,2048]{2,1,0:T(8,128)(2,1)} %bitcast.14), calls=%async_computation.3 | async-start | bytes 3145728 | tf_op jit(solution)/shard_map/all_to_all | solution.py:52
  137.8 3.7 %collective-permute-start.13 = (bf16[96,1536]{1,0:T(8,128)(2,1)S(1)}, bf16[96,1536]{1,0:T(8,128)(2,1)S(1)}, u32[]{:S(2)}, u32[]{:S(2)}) collective-permute-start(bf16[96,1536]{1,0:T(8,128)(2,1)S(1)} %get-tuple-element.114), channel_id=1, source_target_pairs={{0,32},{16,48},{32,0},{48,16},{1,33},{17,49},{33,1},{49,17},{2,34}... | collective-permute-start | bytes 884744 | tf_op jit(solution)/shard_map/ppermute | solution.py:36
  141.5 4.1 %collective-permute-start.14 = (bf16[96,1536]{1,0:T(8,128)(2,1)S(1)}, bf16[96,1536]{1,0:T(8,128)(2,1)S(1)}, u32[]{:S(2)}, u32[]{:S(2)}) collective-permute-start(bf16[96,1536]{1,0:T(8,128)(2,1)S(1)} %get-tuple-element.115), channel_id=1, source_target_pairs={{0,48},{16,0},{32,16},{48,32},{1,49},{17,1},{33,17},{49,33},{2,50}... | collective-permute-start | bytes 884744 | tf_op jit(solution)/shard_map/ppermute | solution.py:36
  150.7 12.2 %collective-permute-done.13.refs_5_ = bf16[96,1536]{1,0:T(8,128)(2,1)S(1)} collective-permute-done((bf16[96,1536]{1,0:T(8,128)(2,1)S(1)}, bf16[96,1536]{1,0:T(8,128)(2,1)S(1)}, u32[]{:S(2)}, u32[]{:S(2)}) %collective-permute-start.13) | collective-permute-done | bytes 294944 | tf_op jit(solution)/shard_map/ppermute | solution.py:36
  165.8 4.8 %all-to-all-start.4 = ((bf16[4,96,1536]{2,1,0:T(8,128)(2,1)}), bf16[4,96,1536]{2,1,0:T(8,128)(2,1)S(1)}, u32[]{:S(2)}, u32[]{:S(2)}) async-start(bf16[4,96,1536]{2,1,0:T(8,128)(2,1)} %gather_fusion.1), calls=%async_computation.4 | async-start | bytes 2359296 | tf_op jit(solution)/shard_map/all_to_all | solution.py:52
  170.6 9.8 %expert_ffn.2 = bf16[384,2048]{1,0:T(8,128)(2,1)} custom-call(s32[4]{0:T(128)S(1)} %pad_add_fusion.place_ref, bf16[4,384,1536]{2,1,0:T(8,128)(2,1)} %bitcast.44, bf16[4,384,1536]{2,1,0:T(8,128)(2,1)} %bitcast.46, bf16[384,2048]{1,0:T(8,128)(2,1)S(1)} %bitcast.35), custom_call_target="tpu_custom_call" | custom-call | flops 3623878656 | bytes 15728640 | tf_op jit(solution)/shard_map/expert_ffn/pallas_call | solution.py:274
  180.4 4.8 %all-to-all-done.4 = bf16[4,96,1536]{2,1,0:T(8,128)(2,1)S(1)} async-done(((bf16[4,96,1536]{2,1,0:T(8,128)(2,1)}), bf16[4,96,1536]{2,1,0:T(8,128)(2,1)S(1)}, u32[]{:S(2)}, u32[]{:S(2)}) %all-to-all-start.4) | async-done | bytes 1179680 | tf_op jit(solution)/shard_map/all_to_all | solution.py:52
  185.2 5.6 %all-to-all-start.5 = ((bf16[8,48,2048]{2,1,0:T(8,128)(2,1)}), bf16[8,48,2048]{2,1,0:T(8,128)(2,1)S(1)}, u32[]{:S(2)}, u32[]{:S(2)}) async-start(bf16[8,48,2048]{2,1,0:T(8,128)(2,1)} %bitcast.39), calls=%async_computation.5 | async-start | bytes 3145728 | tf_op jit(solution)/shard_map/all_to_all | solution.py:52
  193.4 12.7 %expert_ffn.3 = (bf16[256,2048]{1,0:T(8,128)(2,1)}, bf16[384,2048]{1,0:T(8,128)(2,1)}) custom-call(s32[4]{0:T(128)S(1)} %pad_add_fusion.place_ref, bf16[4,384,1536]{2,1,0:T(8,128)(2,1)} %bitcast.45, bf16[4,384,1536]{2,1,0:T(8,128)(2,1)} %bitcast.47, bf16[256,2048]{1,0:T(8,128)(2,1)S(1)} %bitcast.36, bf16[384,2048]{1,0:T(8,128)(2,1)S(1)} %bitcast.34), custom_call_target="tpu_custom_call" | custom-call | flops 6039797760 | bytes 15728640 | tf_op jit(solution)/shard_map/expert_ffn/pallas_call | solution.py:274
  206.2 4.1 %all-to-all-done.5 = bf16[8,48,2048]{2,1,0:T(8,128)(2,1)S(1)} async-done(((bf16[8,48,2048]{2,1,0:T(8,128)(2,1)}), bf16[8,48,2048]{2,1,0:T(8,128)(2,1)S(1)}, u32[]{:S(2)}, u32[]{:S(2)}) %all-to-all-start.5) | async-done | bytes 1572896 | tf_op jit(solution)/shard_map/all_to_all | solution.py:52
  210.3 6.3 %all-to-all-start.6 = ((bf16[8,32,2048]{2,1,0:T(8,128)(2,1)}), bf16[8,32,2048]{2,1,0:T(8,128)(2,1)}, u32[]{:S(2)}, u32[]{:S(2)}) async-start(bf16[8,32,2048]{2,1,0:T(8,128)(2,1)} %bitcast.40), calls=%async_computation.6 | async-start | bytes 2097152 | tf_op jit(solution)/shard_map/all_to_all | solution.py:52
  221.9 9.2 %collective-permute-done.17 = bf16[96,2048]{1,0:T(8,128)(2,1)} collective-permute-done((bf16[96,2048]{1,0:T(8,128)(2,1)S(1)}, bf16[96,2048]{1,0:T(8,128)(2,1)}, u32[]{:S(2)}, u32[]{:S(2)}) %collective-permute-start.17) | collective-permute-done | bytes 393248 | tf_op jit(solution)/shard_map/ppermute | solution.py:36
  231.1 5.0 %all-to-all-start.7 = ((bf16[8,48,2048]{2,1,0:T(8,128)(2,1)}), bf16[8,48,2048]{2,1,0:T(8,128)(2,1)S(1)}, u32[]{:S(2)}, u32[]{:S(2)}) async-start(bf16[8,48,2048]{2,1,0:T(8,128)(2,1)} %bitcast.38), calls=%async_computation.7 | async-start | bytes 3145728 | tf_op jit(solution)/shard_map/all_to_all | solution.py:52
  237.2 3.7 %collective-permute-start.16 = (bf16[96,2048]{1,0:T(8,128)(2,1)S(1)}, bf16[96,2048]{1,0:T(8,128)(2,1)S(1)}, u32[]{:S(2)}, u32[]{:S(2)}) collective-permute-start(bf16[96,2048]{1,0:T(8,128)(2,1)S(1)} %add_convert_fusion.5), channel_id=1, source_target_pairs={{0,49},{1,0},{16,1},{17,16},{32,17},{33,32},{48,33},{49,48},{2,51}... | collective-permute-start | bytes 1179656 | tf_op jit(solution)/shard_map/ppermute | solution.py:36
  242.6 7.1 %collective-permute-done.16 = bf16[96,2048]{1,0:T(8,128)(2,1)S(1)} collective-permute-done((bf16[96,2048]{1,0:T(8,128)(2,1)S(1)}, bf16[96,2048]{1,0:T(8,128)(2,1)S(1)}, u32[]{:S(2)}, u32[]{:S(2)}) %collective-permute-start.16) | collective-permute-done | bytes 393248 | tf_op jit(solution)/shard_map/ppermute | solution.py:36
  250.5 3.7 %collective-permute-start.18 = (bf16[96,2048]{1,0:T(8,128)(2,1)}, bf16[96,2048]{1,0:T(8,128)(2,1)}, u32[]{:S(2)}, u32[]{:S(2)}) collective-permute-start(bf16[96,2048]{1,0:T(8,128)(2,1)} %add_convert_fusion.4), channel_id=1, source_target_pairs={{0,49},{1,0},{16,1},{17,16},{32,17},{33,32},{48,33},{49,48},{2,51}... | collective-permute-start | bytes 1179656 | tf_op jit(solution)/shard_map/ppermute | solution.py:36
  257.4 5.5 %collective-permute-done.18 = bf16[96,2048]{1,0:T(8,128)(2,1)} collective-permute-done((bf16[96,2048]{1,0:T(8,128)(2,1)}, bf16[96,2048]{1,0:T(8,128)(2,1)}, u32[]{:S(2)}, u32[]{:S(2)}) %collective-permute-start.18) | collective-permute-done | bytes 393248 | tf_op jit(solution)/shard_map/ppermute | solution.py:36
  264.7 3.2 %collective-permute-start.19 = (bf16[96,2048]{1,0:T(8,128)(2,1)}, bf16[96,2048]{1,0:T(8,128)(2,1)}, u32[]{:S(2)}, u32[]{:S(2)}) collective-permute-start(bf16[96,2048]{1,0:T(8,128)(2,1)} %add_convert_fusion.3), channel_id=1, source_target_pairs={{0,49},{1,0},{16,1},{17,16},{32,17},{33,32},{48,33},{49,48},{2,51}... | collective-permute-start | bytes 1179656 | tf_op jit(solution)/shard_map/ppermute | solution.py:36
  275.9 4.5 %collective-permute-done.21 = bf16[96,2048]{1,0:T(8,128)(2,1)} collective-permute-done((bf16[96,2048]{1,0:T(8,128)(2,1)}, bf16[96,2048]{1,0:T(8,128)(2,1)}, u32[]{:S(2)}, u32[]{:S(2)}) %collective-permute-start.21) | collective-permute-done | bytes 393248 | tf_op jit(solution)/shard_map/ppermute | solution.py:36
  (131 shorter events, 71.0 us)
Async XLA Ops:
  7.2 163.4 %all-gather.5.cloned.1.call-start = ((), (), s32[]{:S(2)}) async-start(), calls=%async_computation.8 | async-start | bytes 5898240 | tf_op jit(solution)/shard_map/all_gather | solution.py:367
  12.8 24.2 %collective-permute-start.5 = (bf16[384,1536]{1,0:T(8,128)(2,1)}, bf16[384,1536]{1,0:T(8,128)(2,1)S(1)}, u32[]{:S(2)}, u32[]{:S(2)}) collective-permute-start(bf16[384,1536]{1,0:T(8,128)(2,1)} %get-tuple-element.86.first_ref.refs_0_), channel_id=1, source_target_pairs={{0,8},{8,0},{1,9},{9,1},{2,10},{10,2},{3,11},{11,3},{4,12},{12,4},... | collective-permute-start | bytes 3538952 | tf_op jit(solution)/shard_map/ppermute | solution.py:329
  12.9 24.1 %all-to-all-start = ((bf16[4,96,1536]{2,1,0:T(8,128)(2,1)}), bf16[4,96,1536]{2,1,0:T(8,128)(2,1)}, u32[]{:S(2)}, u32[]{:S(2)}) async-start(bf16[4,96,1536]{2,1,0:T(8,128)(2,1)} %bitcast.7), calls=%async_computation | async-start | bytes 2359296 | tf_op jit(solution)/shard_map/all_to_all | solution.py:52
  17.7 16.0 %collective-permute-start = (bf16[104,2048]{1,0:T(8,128)(2,1)S(1)}, bf16[104,2048]{1,0:T(8,128)(2,1)S(1)}, u32[]{:S(2)}, u32[]{:S(2)}) collective-permute-start(bf16[104,2048]{1,0:T(8,128)(2,1)S(1)} %get-tuple-element.77.refs_0_), channel_id=1, source_target_pairs={{0,1},{1,16},{16,17},{17,32},{32,33},{33,48},{48,49},{49,0},{2,3},... | collective-permute-start | bytes 1277960 | tf_op jit(solution)/shard_map/ppermute | solution.py:36
  19.7 14.1 %collective-permute-start.1 = (bf16[104,2048]{1,0:T(8,128)(2,1)S(1)}, bf16[104,2048]{1,0:T(8,128)(2,1)S(1)}, u32[]{:S(2)}, u32[]{:S(2)}) collective-permute-start(bf16[104,2048]{1,0:T(8,128)(2,1)S(1)} %get-tuple-element.77.refs_0_), channel_id=1, source_target_pairs={{0,49},{1,0},{16,1},{17,16},{32,17},{33,32},{48,33},{49,48},{2,51}... | collective-permute-start | bytes 1277960 | tf_op jit(solution)/shard_map/ppermute | solution.py:36
  33.7 36.9 %collective-permute-start.4 = (bf16[384,1536]{1,0:T(8,128)(2,1)}, bf16[384,1536]{1,0:T(8,128)(2,1)}, u32[]{:S(2)}, u32[]{:S(2)}) collective-permute-start(bf16[384,1536]{1,0:T(8,128)(2,1)} %copy-done.29), channel_id=1, source_target_pairs={{0,1},{1,0},{2,3},{3,2},{4,5},{5,4},{6,7},{7,6},{8,9},{9,8},{10,11... | collective-permute-start | bytes 3538952 | tf_op jit(solution)/shard_map/ppermute | solution.py:329
  38.1 44.3 %all-to-all-start.1 = ((bf16[8,48,2048]{2,1,0:T(8,128)(2,1)}), bf16[8,48,2048]{2,1,0:T(8,128)(2,1)S(1)}, u32[]{:S(2)}, u32[]{:S(2)}) async-start(bf16[8,48,2048]{2,1,0:T(8,128)(2,1)} %bitcast.8), calls=%async_computation.1 | async-start | bytes 3145728 | tf_op jit(solution)/shard_map/all_to_all | solution.py:52
  42.9 127.7 %all-gather.7.cloned.1.call-start = ((), (), s32[]{:S(2)}) async-start(), calls=%async_computation.9 | async-start | bytes 5898240 | tf_op jit(solution)/shard_map/all_gather | solution.py:386
  42.9 25.5 %collective-permute-start.2 = (bf16[104,2048]{1,0:T(8,128)(2,1)S(1)}, bf16[104,2048]{1,0:T(8,128)(2,1)S(1)}, u32[]{:S(2)}, u32[]{:S(2)}) collective-permute-start(bf16[104,2048]{1,0:T(8,128)(2,1)S(1)} %collective-permute-done.refs_1_), channel_id=1, source_target_pairs={{0,1},{1,16},{16,17},{17,32},{32,33},{33,48},{48,49},{49,0},{2,3},... | collective-permute-start | bytes 1277960 | tf_op jit(solution)/shard_map/ppermute | solution.py:36
  44.9 25.7 %collective-permute-start.3 = (bf16[104,2048]{1,0:T(8,128)(2,1)S(1)}, bf16[104,2048]{1,0:T(8,128)(2,1)S(1)}, u32[]{:S(2)}, u32[]{:S(2)}) collective-permute-start(bf16[104,2048]{1,0:T(8,128)(2,1)S(1)} %collective-permute-done.1.refs_2_), channel_id=1, source_target_pairs={{0,49},{1,0},{16,1},{17,16},{32,17},{33,32},{48,33},{49,48},{2,51}... | collective-permute-start | bytes 1277960 | tf_op jit(solution)/shard_map/ppermute | solution.py:36
  70.6 11.8 %collective-permute-start.6 = (bf16[104,2048]{1,0:T(8,128)(2,1)S(1)}, bf16[104,2048]{1,0:T(8,128)(2,1)S(1)}, u32[]{:S(2)}, u32[]{:S(2)}) collective-permute-start(bf16[104,2048]{1,0:T(8,128)(2,1)S(1)} %collective-permute-done.2.refs_0_), channel_id=1, source_target_pairs={{0,1},{1,16},{16,17},{17,32},{32,33},{33,48},{48,49},{49,0},{2,3},... | collective-permute-start | bytes 1277960 | tf_op jit(solution)/shard_map/ppermute | solution.py:36
  70.9 11.5 %collective-permute-start.7 = (bf16[104,2048]{1,0:T(8,128)(2,1)S(1)}, bf16[104,2048]{1,0:T(8,128)(2,1)S(1)}, u32[]{:S(2)}, u32[]{:S(2)}) collective-permute-start(bf16[104,2048]{1,0:T(8,128)(2,1)S(1)} %collective-permute-done.3.refs_1_), channel_id=1, source_target_pairs={{0,49},{1,0},{16,1},{17,16},{32,17},{33,32},{48,33},{49,48},{2,51}... | collective-permute-start | bytes 1277960 | tf_op jit(solution)/shard_map/ppermute | solution.py:36
  83.5 45.0 %all-to-all-start.2 = ((bf16[8,32,2048]{2,1,0:T(8,128)(2,1)}), bf16[8,32,2048]{2,1,0:T(8,128)(2,1)S(1)}, u32[]{:S(2)}, u32[]{:S(2)}) async-start(bf16[8,32,2048]{2,1,0:T(8,128)(2,1)} %bitcast.37), calls=%async_computation.2 | async-start | bytes 2097152 | tf_op jit(solution)/shard_map/all_to_all | solution.py:52
  88.3 14.4 %collective-permute-start.8 = (bf16[104,2048]{1,0:T(8,128)(2,1)S(1)}, bf16[104,2048]{1,0:T(8,128)(2,1)S(1)}, u32[]{:S(2)}, u32[]{:S(2)}) collective-permute-start(bf16[104,2048]{1,0:T(8,128)(2,1)S(1)} %collective-permute-done.6.refs_0_), channel_id=1, source_target_pairs={{0,1},{1,16},{16,17},{17,32},{32,33},{33,48},{48,49},{49,0},{2,3},... | collective-permute-start | bytes 1277960 | tf_op jit(solution)/shard_map/ppermute | solution.py:36
  89.7 21.2 %collective-permute-start.10 = (bf16[96,1536]{1,0:T(8,128)(2,1)}, bf16[96,1536]{1,0:T(8,128)(2,1)S(1)}, u32[]{:S(2)}, u32[]{:S(2)}) collective-permute-start(bf16[96,1536]{1,0:T(8,128)(2,1)} %copy-done.32), channel_id=1, source_target_pairs={{0,32},{16,48},{32,0},{48,16},{1,33},{17,49},{33,1},{49,17},{2,34}... | collective-permute-start | bytes 884744 | tf_op jit(solution)/shard_map/ppermute | solution.py:36
  92.0 28.8 %collective-permute-start.11 = (bf16[96,1536]{1,0:T(8,128)(2,1)}, bf16[96,1536]{1,0:T(8,128)(2,1)S(1)}, u32[]{:S(2)}, u32[]{:S(2)}) collective-permute-start(bf16[96,1536]{1,0:T(8,128)(2,1)} %copy-done.31), channel_id=1, source_target_pairs={{0,48},{16,0},{32,16},{48,32},{1,49},{17,1},{33,17},{49,33},{2,50}... | collective-permute-start | bytes 884744 | tf_op jit(solution)/shard_map/ppermute | solution.py:36
  96.4 31.4 %collective-permute-start.9 = (bf16[96,1536]{1,0:T(8,128)(2,1)}, bf16[96,1536]{1,0:T(8,128)(2,1)S(1)}, u32[]{:S(2)}, u32[]{:S(2)}) collective-permute-start(bf16[96,1536]{1,0:T(8,128)(2,1)} %copy-done.30), channel_id=1, source_target_pairs={{0,16},{16,32},{32,48},{48,0},{1,17},{17,33},{33,49},{49,1},{2,18}... | collective-permute-start | bytes 884744 | tf_op jit(solution)/shard_map/ppermute | solution.py:36
  129.5 36.3 %all-to-all-start.3 = ((bf16[8,48,2048]{2,1,0:T(8,128)(2,1)}), bf16[8,48,2048]{2,1,0:T(8,128)(2,1)S(1)}, u32[]{:S(2)}, u32[]{:S(2)}) async-start(bf16[8,48,2048]{2,1,0:T(8,128)(2,1)} %bitcast.14), calls=%async_computation.3 | async-start | bytes 3145728 | tf_op jit(solution)/shard_map/all_to_all | solution.py:52
  137.8 12.2 %collective-permute-start.12 = (bf16[96,1536]{1,0:T(8,128)(2,1)}, bf16[96,1536]{1,0:T(8,128)(2,1)S(1)}, u32[]{:S(2)}, u32[]{:S(2)}) collective-permute-start(bf16[96,1536]{1,0:T(8,128)(2,1)} %get-tuple-element.113), channel_id=1, source_target_pairs={{0,16},{16,32},{32,48},{48,0},{1,17},{17,33},{33,49},{49,1},{2,18}... | collective-permute-start | bytes 884744 | tf_op jit(solution)/shard_map/ppermute | solution.py:36
  137.8 25.1 %collective-permute-start.13 = (bf16[96,1536]{1,0:T(8,128)(2,1)S(1)}, bf16[96,1536]{1,0:T(8,128)(2,1)S(1)}, u32[]{:S(2)}, u32[]{:S(2)}) collective-permute-start(bf16[96,1536]{1,0:T(8,128)(2,1)S(1)} %get-tuple-element.114), channel_id=1, source_target_pairs={{0,32},{16,48},{32,0},{48,16},{1,33},{17,49},{33,1},{49,17},{2,34}... | collective-permute-start | bytes 884744 | tf_op jit(solution)/shard_map/ppermute | solution.py:36
  141.5 23.6 %collective-permute-start.14 = (bf16[96,1536]{1,0:T(8,128)(2,1)S(1)}, bf16[96,1536]{1,0:T(8,128)(2,1)S(1)}, u32[]{:S(2)}, u32[]{:S(2)}) collective-permute-start(bf16[96,1536]{1,0:T(8,128)(2,1)S(1)} %get-tuple-element.115), channel_id=1, source_target_pairs={{0,48},{16,0},{32,16},{48,32},{1,49},{17,1},{33,17},{49,33},{2,50}... | collective-permute-start | bytes 884744 | tf_op jit(solution)/shard_map/ppermute | solution.py:36
  165.8 19.4 %all-to-all-start.4 = ((bf16[4,96,1536]{2,1,0:T(8,128)(2,1)}), bf16[4,96,1536]{2,1,0:T(8,128)(2,1)S(1)}, u32[]{:S(2)}, u32[]{:S(2)}) async-start(bf16[4,96,1536]{2,1,0:T(8,128)(2,1)} %gather_fusion.1), calls=%async_computation.4 | async-start | bytes 2359296 | tf_op jit(solution)/shard_map/all_to_all | solution.py:52
  185.2 25.1 %all-to-all-start.5 = ((bf16[8,48,2048]{2,1,0:T(8,128)(2,1)}), bf16[8,48,2048]{2,1,0:T(8,128)(2,1)S(1)}, u32[]{:S(2)}, u32[]{:S(2)}) async-start(bf16[8,48,2048]{2,1,0:T(8,128)(2,1)} %bitcast.39), calls=%async_computation.5 | async-start | bytes 3145728 | tf_op jit(solution)/shard_map/all_to_all | solution.py:52
  210.3 20.8 %all-to-all-start.6 = ((bf16[8,32,2048]{2,1,0:T(8,128)(2,1)}), bf16[8,32,2048]{2,1,0:T(8,128)(2,1)}, u32[]{:S(2)}, u32[]{:S(2)}) async-start(bf16[8,32,2048]{2,1,0:T(8,128)(2,1)} %bitcast.40), calls=%async_computation.6 | async-start | bytes 2097152 | tf_op jit(solution)/shard_map/all_to_all | solution.py:52
  218.6 12.5 %collective-permute-start.17 = (bf16[96,2048]{1,0:T(8,128)(2,1)S(1)}, bf16[96,2048]{1,0:T(8,128)(2,1)}, u32[]{:S(2)}, u32[]{:S(2)}) collective-permute-start(bf16[96,2048]{1,0:T(8,128)(2,1)S(1)} %get-tuple-element.131), channel_id=1, source_target_pairs={{0,1},{1,16},{16,17},{17,32},{32,33},{33,48},{48,49},{49,0},{2,3},... | collective-permute-start | bytes 1179656 | tf_op jit(solution)/shard_map/ppermute | solution.py:36
  219.8 16.3 %collective-permute-start.15 = (bf16[96,2048]{1,0:T(8,128)(2,1)}, bf16[96,2048]{1,0:T(8,128)(2,1)}, u32[]{:S(2)}, u32[]{:S(2)}) collective-permute-start(bf16[96,2048]{1,0:T(8,128)(2,1)} %get-tuple-element.126), channel_id=1, source_target_pairs={{0,49},{1,0},{16,1},{17,16},{32,17},{33,32},{48,33},{49,48},{2,51}... | collective-permute-start | bytes 1179656 | tf_op jit(solution)/shard_map/ppermute | solution.py:36
  231.1 24.9 %all-to-all-start.7 = ((bf16[8,48,2048]{2,1,0:T(8,128)(2,1)}), bf16[8,48,2048]{2,1,0:T(8,128)(2,1)S(1)}, u32[]{:S(2)}, u32[]{:S(2)}) async-start(bf16[8,48,2048]{2,1,0:T(8,128)(2,1)} %bitcast.38), calls=%async_computation.7 | async-start | bytes 3145728 | tf_op jit(solution)/shard_map/all_to_all | solution.py:52
  237.2 12.4 %collective-permute-start.16 = (bf16[96,2048]{1,0:T(8,128)(2,1)S(1)}, bf16[96,2048]{1,0:T(8,128)(2,1)S(1)}, u32[]{:S(2)}, u32[]{:S(2)}) collective-permute-start(bf16[96,2048]{1,0:T(8,128)(2,1)S(1)} %add_convert_fusion.5), channel_id=1, source_target_pairs={{0,49},{1,0},{16,1},{17,16},{32,17},{33,32},{48,33},{49,48},{2,51}... | collective-permute-start | bytes 1179656 | tf_op jit(solution)/shard_map/ppermute | solution.py:36
  250.5 12.4 %collective-permute-start.18 = (bf16[96,2048]{1,0:T(8,128)(2,1)}, bf16[96,2048]{1,0:T(8,128)(2,1)}, u32[]{:S(2)}, u32[]{:S(2)}) collective-permute-start(bf16[96,2048]{1,0:T(8,128)(2,1)} %add_convert_fusion.4), channel_id=1, source_target_pairs={{0,49},{1,0},{16,1},{17,16},{32,17},{33,32},{48,33},{49,48},{2,51}... | collective-permute-start | bytes 1179656 | tf_op jit(solution)/shard_map/ppermute | solution.py:36
  256.0 11.9 %collective-permute-start.20 = (bf16[96,2048]{1,0:T(8,128)(2,1)}, bf16[96,2048]{1,0:T(8,128)(2,1)}, u32[]{:S(2)}, u32[]{:S(2)}) collective-permute-start(bf16[96,2048]{1,0:T(8,128)(2,1)} %add_convert_fusion.2), channel_id=1, source_target_pairs={{0,1},{1,16},{16,17},{17,32},{32,33},{33,48},{48,49},{49,0},{2,3},... | collective-permute-start | bytes 1179656 | tf_op jit(solution)/shard_map/ppermute | solution.py:36
  264.7 11.2 %collective-permute-start.19 = (bf16[96,2048]{1,0:T(8,128)(2,1)}, bf16[96,2048]{1,0:T(8,128)(2,1)}, u32[]{:S(2)}, u32[]{:S(2)}) collective-permute-start(bf16[96,2048]{1,0:T(8,128)(2,1)} %add_convert_fusion.3), channel_id=1, source_target_pairs={{0,49},{1,0},{16,1},{17,16},{32,17},{33,32},{48,33},{49,48},{2,51}... | collective-permute-start | bytes 1179656 | tf_op jit(solution)/shard_map/ppermute | solution.py:36
  269.7 10.7 %collective-permute-start.21 = (bf16[96,2048]{1,0:T(8,128)(2,1)}, bf16[96,2048]{1,0:T(8,128)(2,1)}, u32[]{:S(2)}, u32[]{:S(2)}) collective-permute-start(bf16[96,2048]{1,0:T(8,128)(2,1)} %add_convert_fusion.1), channel_id=1, source_target_pairs={{0,1},{1,16},{16,17},{17,32},{32,33},{33,48},{48,49},{49,0},{2,3},... | collective-permute-start | bytes 1179656 | tf_op jit(solution)/shard_map/ppermute | solution.py:36
  (34 other events, 64.6 us)
Sparse Core Ops, SparseCore 0:
  12.9 57.0 all-gather.4
  82.5 53.7 all-gather.6

commit v8 on v7

--- a/solution.py
+++ b/solution.py
@@ -382,17 +382,23 @@
         scratch=[pltpu.SemaphoreType.DMA((NZH,))],
     )(place, first)
     d1, w1 = dispatch(place, (p2, m2))
-    d1, r0, p3, m3, swapped, *cut = fence(d1, r0, p3, m3, swapped, *cut)
+    r0, hx, swapped = fence(r0, hx, swapped)
     swap_full = lax.all_gather(swapped, "y", axis=0, tiled=False)
+    x_turn = jnp.arange(NX, dtype=jnp.int32)
+    x_from = jnp.take(pair_list, (x_turn * NZH + zh_me) * NC + c_me, mode="clip") >> 3
+    hx = across(jnp.take(hx, x_from, axis=0, mode="clip"), "x").reshape(PACK, SIDE)
+    d1, r0, p3, m3, hx, *cut = fence(d1, r0, p3, m3, hx, *cut)
     r1 = in_plane(d1)
     far = along_z(p3, 1)
     held = [cut[0]] + [shift(cut[k], "zh", NZH, k) for k in range(1, NZH)]
     d2, w2 = dispatch(place, (p3, m3, far))
-    d2, r1, *held = fence(d2, r1, *held)
+    d2, r1, held[1] = fence(d2, r1, held[1])
     r2 = in_plane(d2)
-    x_turn = jnp.arange(NX, dtype=jnp.int32)
-    x_from = jnp.take(pair_list, (x_turn * NZH + zh_me) * NC + c_me, mode="clip") >> 3
-    hx = jnp.take(hx, x_from, axis=0, mode="clip")
+    r0, r1, r2, hx, *held = fence(r0, r1, r2, hx, *held)
+    (s2,) = ffn(place, own_full, swap_full, (r2,), 384)
+    s2, r1, r0, hx, *held = fence(s2, r1, r0, hx, *held)
+    b2 = in_plane(s2)
+    s1, s0 = ffn(place, own_full, swap_full, (r1, r0), 320)
     turn = (zh_me + jnp.arange(NZH, dtype=jnp.int32)) & (NZH - 1)
     matched = jnp.take(pair_list, (x_me * NZH + turn) * NC + c_me, mode="clip")
     chosen = (zh_me - (matched >> 1)) & (NZH - 1)
@@ -401,13 +407,7 @@
         scratch=[pltpu.SemaphoreType.DMA((NZH,))],
     )(chosen.astype(jnp.int32), *held)
     held = [picked[0]] + [shift(picked[k], "zh", NZH, k) for k in range(1, NZH)]
-    r0, r1, r2, hx, *held = fence(r0, r1, r2, hx, *held)
-    hx = across(hx, "x").reshape(PACK, SIDE)
-    (s2,) = ffn(place, own_full, swap_full, (r2,), 384)
-    s2, r1, r0, hx = fence(s2, r1, r0, hx)
-    b2 = in_plane(s2)
-    s1, s0 = ffn(place, own_full, swap_full, (r1, r0), 320)
-    b2, s1, s0 = fence(b2, s1, s0)
+    b2, s1, s0, *held = fence(b2, s1, s0, *held)
     c_m3, c_p3, c_4 = combine(w2, b2, (F32, BF, BF))
     down, rise = along_z(c_4, -1), along_z(c_p3, 1)
     b1 = in_plane(s1)

time: 291 us -> 299 us (1.027)
  waiting for transfers between devices: 115 us -> 121 us
    ppermute x20, waiting for transfers between devices: 106 us -> 115 us  [shift(): lax.ppermute(value, axes, [(i, (i + step) % count) for i in range(count)])]
    unnamed x68 -> x76, local copies, waits for them, and re-layouts: 19.9 us -> 20.1 us
  transfers between devices with their start and end apart: 32 -> 32, of which waited for: 17 -> 18; matrix products, arithmetic and copies ran while one was open for 4% -> 4% of each run, Pallas kernels for 13% -> 10%
where the time goes in v8:
time: 299 us; the launch traced here: 296 us
  waiting for transfers between devices  121 us (40%)
  starting transfers between devices  83.1 us (28%)
  Pallas kernels  43.4 us (15%)
  local copies, waits for them, and re-layouts  24.3 us (8%)
  between operations  14.3 us (5%)
  other arithmetic  10.1 us (3%)
    ppermute x20, waiting for transfers between devices, shift(): lax.ppermute(value, axes, [(i, (i + step) % count) for i in range(count)])  115 us
    ppermute x20, starting transfers between devices, shift(): lax.ppermute(value, axes, [(i, (i + step) % count) for i in range(count)])  42.5 us
    all_to_all x8, starting transfers between devices, across(): return lax.all_to_all(value, axis, split_axis=0, concat_axis=0, tiled=True)  40.4 us
    pallas_call x2, Pallas kernels, ffn(): call(functools.partial(ffn_kernel, splits, block), [pltpu.HBM((r, WIDTH),...  22.4 us
    unnamed x76, local copies, waits for them, and re-layouts  20.1 us
    pallas_call x3, Pallas kernels, dispatch(): call(functools.partial(dispatch_kernel, n), [shape(PLACES * n * MOST, WID...  8.08 us
    convert_element_type x5, other arithmetic, joined(): return (got.astype(F32) + mine).astype(BF)  7.4 us
    all_to_all x8, waiting for transfers between devices, across(): return lax.all_to_all(value, axis, split_axis=0, concat_axis=0, tiled=True)  6.21 us
  transfers between devices with their start and end apart: 32, of which 18 were waited for; matrix products, arithmetic and copies ran while one was open for 4% of the time, Pallas kernels for 10%

profile of v8, /device:TPU:22, one launch (start us, length us, event | category | flops | bytes accessed | tf_op | source)
XLA Modules:
  0.0 296.2 jit_solution(11328803762964605114)
XLA Ops:
  7.3 4.4 %prep.1 = (bf16[104,2048]{1,0:T(8,128)(2,1)S(1)}, bf16[384,1536]{1,0:T(8,128)(2,1)}, bf16[384,1536]{1,0:T(8,128)(2,1)S(1)}, bf16[384,1536]{1,0:T(8,128)(2,1)}) custom-call(s32[4]{0:T(128)S(1)} %pad_add_fusion.place_ref, bf16[96,2048]{1,0:T(8,128)(2,1)} %tokens_ref.1, f32[1,2048]{1,0:T(1,128)} %bitcast.40, s32[8,96]{1,0:T(8,128)} %bitcast.41, ...), custom_call_target="tpu_custom_call" | custom-call | tf_op jit(solution)/shard_map/prep/pallas_call | solution.py:343
  12.8 4.8 %all-to-all-start = ((bf16[4,96,1536]{2,1,0:T(8,128)(2,1)}), bf16[4,96,1536]{2,1,0:T(8,128)(2,1)S(1)}, u32[]{:S(2)}, u32[]{:S(2)}) async-start(bf16[4,96,1536]{2,1,0:T(8,128)(2,1)} %bitcast.7), calls=%async_computation | async-start | bytes 2359296 | tf_op jit(solution)/shard_map/all_to_all | solution.py:52
  17.5 5.9 %collective-permute-start.1 = (bf16[104,2048]{1,0:T(8,128)(2,1)S(1)}, bf16[104,2048]{1,0:T(8,128)(2,1)S(1)}, u32[]{:S(2)}, u32[]{:S(2)}) collective-permute-start(bf16[104,2048]{1,0:T(8,128)(2,1)S(1)} %get-tuple-element.85.refs_0_), channel_id=1, source_target_pairs={{0,49},{1,0},{16,1},{17,16},{32,17},{33,32},{48,33},{49,48},{2,51}... | collective-permute-start | bytes 1277960 | tf_op jit(solution)/shard_map/ppermute | solution.py:36
  23.5 9.2 %collective-permute-done.1.refs_2_ = bf16[104,2048]{1,0:T(8,128)(2,1)S(1)} collective-permute-done((bf16[104,2048]{1,0:T(8,128)(2,1)S(1)}, bf16[104,2048]{1,0:T(8,128)(2,1)S(1)}, u32[]{:S(2)}, u32[]{:S(2)}) %collective-permute-start.1) | collective-permute-done | bytes 426016 | tf_op jit(solution)/shard_map/ppermute | solution.py:36
  32.6 3.5 %collective-permute-done.refs_1_ = bf16[104,2048]{1,0:T(8,128)(2,1)} collective-permute-done((bf16[104,2048]{1,0:T(8,128)(2,1)S(1)}, bf16[104,2048]{1,0:T(8,128)(2,1)}, u32[]{:S(2)}, u32[]{:S(2)}) %collective-permute-start) | collective-permute-done | bytes 426016 | tf_op jit(solution)/shard_map/ppermute | solution.py:36
  36.2 3.1 %dispatch.4 = (bf16[384,2048]{1,0:T(8,128)(2,1)}, bf16[3,128,128]{2,1,0:T(8,128)(2,1)S(1)}) custom-call(s32[4]{0:T(128)S(1)} %pad_add_fusion.place_ref, bf16[104,2048]{1,0:T(8,128)(2,1)S(1)} %get-tuple-element.85.refs_0_, bf16[104,2048]{1,0:T(8,128)(2,1)} %collective-permute-done.refs_1_, bf16[104,2048]{1,0:T(8,128)(2,1)S(1)} %collective-permute-done.1.refs_2_), custom_call_target="tpu_custom_call" | custom-call | bytes 83886080 | tf_op jit(solution)/shard_map/dispatch/pallas_call | solution.py:207
  42.2 4.8 %all-to-all-start.1 = ((bf16[8,48,2048]{2,1,0:T(8,128)(2,1)}), bf16[8,48,2048]{2,1,0:T(8,128)(2,1)S(1)}, u32[]{:S(2)}, u32[]{:S(2)}) async-start(bf16[8,48,2048]{2,1,0:T(8,128)(2,1)} %bitcast.8), calls=%async_computation.1 | async-start | bytes 3145728 | tf_op jit(solution)/shard_map/all_to_all | solution.py:52
  50.4 31.9 %collective-permute-done.2.refs_0_ = bf16[104,2048]{1,0:T(8,128)(2,1)S(1)} collective-permute-done((bf16[104,2048]{1,0:T(8,128)(2,1)}, bf16[104,2048]{1,0:T(8,128)(2,1)S(1)}, u32[]{:S(2)}, u32[]{:S(2)}) %collective-permute-start.2) | collective-permute-done | bytes 426016 | tf_op jit(solution)/shard_map/ppermute | solution.py:36
  85.2 2.9 gather_fusion.1
  88.1 4.8 %all-to-all-start.2 = ((bf16[4,96,1536]{2,1,0:T(8,128)(2,1)}), bf16[4,96,1536]{2,1,0:T(8,128)(2,1)S(1)}, u32[]{:S(2)}, u32[]{:S(2)}) async-start(bf16[4,96,1536]{2,1,0:T(8,128)(2,1)} %gather_fusion.1), calls=%async_computation.2 | async-start | bytes 2359296 | tf_op jit(solution)/shard_map/all_to_all | solution.py:52
  93.2 2.9 collective-permute-start.7
  98.8 2.2 dispatch.3
  101.6 3.0 %collective-permute-done.6.refs_0_ = bf16[104,2048]{1,0:T(8,128)(2,1)S(1)} collective-permute-done((bf16[104,2048]{1,0:T(8,128)(2,1)S(1)}, bf16[104,2048]{1,0:T(8,128)(2,1)S(1)}, u32[]{:S(2)}, u32[]{:S(2)}) %collective-permute-start.6) | collective-permute-done | bytes 426016 | tf_op jit(solution)/shard_map/ppermute | solution.py:36
  106.8 5.7 %all-to-all-start.3 = ((bf16[8,32,2048]{2,1,0:T(8,128)(2,1)}), bf16[8,32,2048]{2,1,0:T(8,128)(2,1)S(1)}, u32[]{:S(2)}, u32[]{:S(2)}) async-start(bf16[8,32,2048]{2,1,0:T(8,128)(2,1)} %bitcast.14), calls=%async_computation.3 | async-start | bytes 2097152 | tf_op jit(solution)/shard_map/all_to_all | solution.py:52
  113.1 18.9 %collective-permute-done.8.refs_2_ = bf16[104,2048]{1,0:T(8,128)(2,1)S(1)} collective-permute-done((bf16[104,2048]{1,0:T(8,128)(2,1)S(1)}, bf16[104,2048]{1,0:T(8,128)(2,1)S(1)}, u32[]{:S(2)}, u32[]{:S(2)}) %collective-permute-start.8) | collective-permute-done | bytes 426016 | tf_op jit(solution)/shard_map/ppermute | solution.py:36
  132.1 2.7 dispatch.5
  139.2 4.8 %all-to-all-start.4 = ((bf16[8,48,2048]{2,1,0:T(8,128)(2,1)}), bf16[8,48,2048]{2,1,0:T(8,128)(2,1)S(1)}, u32[]{:S(2)}, u32[]{:S(2)}) async-start(bf16[8,48,2048]{2,1,0:T(8,128)(2,1)} %bitcast.16), calls=%async_computation.4 | async-start | bytes 3145728 | tf_op jit(solution)/shard_map/all_to_all | solution.py:52
  144.1 18.2 %collective-permute-done.10.refs_2_ = bf16[96,1536]{1,0:T(8,128)(2,1)S(1)} collective-permute-done((bf16[96,1536]{1,0:T(8,128)(2,1)}, bf16[96,1536]{1,0:T(8,128)(2,1)S(1)}, u32[]{:S(2)}, u32[]{:S(2)}) %collective-permute-start.10) | collective-permute-done | bytes 294944 | tf_op jit(solution)/shard_map/ppermute | solution.py:36
  163.6 9.7 %expert_ffn.2 = bf16[384,2048]{1,0:T(8,128)(2,1)} custom-call(s32[4]{0:T(128)S(1)} %pad_add_fusion.place_ref, bf16[4,384,1536]{2,1,0:T(8,128)(2,1)} %bitcast.43, bf16[4,384,1536]{2,1,0:T(8,128)(2,1)} %bitcast.45, bf16[384,2048]{1,0:T(8,128)(2,1)S(1)} %bitcast.35), custom_call_target="tpu_custom_call" | custom-call | flops 3623878656 | bytes 15728640 | tf_op jit(solution)/shard_map/expert_ffn/pallas_call | solution.py:274
  173.3 5.7 %all-to-all-start.5 = ((bf16[8,48,2048]{2,1,0:T(8,128)(2,1)}), bf16[8,48,2048]{2,1,0:T(8,128)(2,1)S(1)}, u32[]{:S(2)}, u32[]{:S(2)}) async-start(bf16[8,48,2048]{2,1,0:T(8,128)(2,1)} %bitcast.38), calls=%async_computation.5 | async-start | bytes 3145728 | tf_op jit(solution)/shard_map/all_to_all | solution.py:52
  183.4 13.1 %collective-permute-start.12 = (bf16[96,1536]{1,0:T(8,128)(2,1)S(1)}, bf16[96,1536]{1,0:T(8,128)(2,1)S(1)}, u32[]{:S(2)}, u32[]{:S(2)}) collective-permute-start(bf16[96,1536]{1,0:T(8,128)(2,1)S(1)} %get-tuple-element.138), channel_id=1, source_target_pairs={{0,16},{16,32},{32,48},{48,0},{1,17},{17,33},{33,49},{49,1},{2,18}... | collective-permute-start | bytes 884744 | tf_op jit(solution)/shard_map/ppermute | solution.py:36
  198.6 4.1 %collective-permute-start.14 = (bf16[96,1536]{1,0:T(8,128)(2,1)S(1)}, bf16[96,1536]{1,0:T(8,128)(2,1)S(1)}, u32[]{:S(2)}, u32[]{:S(2)}) collective-permute-start(bf16[96,1536]{1,0:T(8,128)(2,1)S(1)} %get-tuple-element.140), channel_id=1, source_target_pairs={{0,48},{16,0},{32,16},{48,32},{1,49},{17,1},{33,17},{49,33},{2,50}... | collective-permute-start | bytes 884744 | tf_op jit(solution)/shard_map/ppermute | solution.py:36
  204.1 12.7 %expert_ffn.3 = (bf16[256,2048]{1,0:T(8,128)(2,1)}, bf16[384,2048]{1,0:T(8,128)(2,1)}) custom-call(s32[4]{0:T(128)S(1)} %pad_add_fusion.place_ref, bf16[4,384,1536]{2,1,0:T(8,128)(2,1)} %bitcast.44, bf16[4,384,1536]{2,1,0:T(8,128)(2,1)} %bitcast.46, bf16[256,2048]{1,0:T(8,128)(2,1)S(1)} %bitcast.36, bf16[384,2048]{1,0:T(8,128)(2,1)S(1)} %bitcast.34), custom_call_target="tpu_custom_call" | custom-call | flops 6039797760 | bytes 15728640 | tf_op jit(solution)/shard_map/expert_ffn/pallas_call | solution.py:274
  217.5 7.4 %collective-permute-done.13.refs_5_ = bf16[96,1536]{1,0:T(8,128)(2,1)S(1)} collective-permute-done((bf16[96,1536]{1,0:T(8,128)(2,1)S(1)}, bf16[96,1536]{1,0:T(8,128)(2,1)S(1)}, u32[]{:S(2)}, u32[]{:S(2)}) %collective-permute-start.13) | collective-permute-done | bytes 294944 | tf_op jit(solution)/shard_map/ppermute | solution.py:36
  226.3 4.8 %all-to-all-start.6 = ((bf16[8,32,2048]{2,1,0:T(8,128)(2,1)}), bf16[8,32,2048]{2,1,0:T(8,128)(2,1)}, u32[]{:S(2)}, u32[]{:S(2)}) async-start(bf16[8,32,2048]{2,1,0:T(8,128)(2,1)} %bitcast.39), calls=%async_computation.6 | async-start | bytes 2097152 | tf_op jit(solution)/shard_map/all_to_all | solution.py:52
  233.2 3.2 %collective-permute-start.15 = (bf16[96,2048]{1,0:T(8,128)(2,1)}, bf16[96,2048]{1,0:T(8,128)(2,1)}, u32[]{:S(2)}, u32[]{:S(2)}) collective-permute-start(bf16[96,2048]{1,0:T(8,128)(2,1)} %get-tuple-element.142), channel_id=1, source_target_pairs={{0,49},{1,0},{16,1},{17,16},{32,17},{33,32},{48,33},{49,48},{2,51}... | collective-permute-start | bytes 1179656 | tf_op jit(solution)/shard_map/ppermute | solution.py:36
  236.5 9.2 %collective-permute-done.17 = bf16[96,2048]{1,0:T(8,128)(2,1)} collective-permute-done((bf16[96,2048]{1,0:T(8,128)(2,1)S(1)}, bf16[96,2048]{1,0:T(8,128)(2,1)}, u32[]{:S(2)}, u32[]{:S(2)}) %collective-permute-start.17) | collective-permute-done | bytes 393248 | tf_op jit(solution)/shard_map/ppermute | solution.py:36
  245.7 5.0 %all-to-all-start.7 = ((bf16[8,48,2048]{2,1,0:T(8,128)(2,1)}), bf16[8,48,2048]{2,1,0:T(8,128)(2,1)S(1)}, u32[]{:S(2)}, u32[]{:S(2)}) async-start(bf16[8,48,2048]{2,1,0:T(8,128)(2,1)} %bitcast.37), calls=%async_computation.7 | async-start | bytes 3145728 | tf_op jit(solution)/shard_map/all_to_all | solution.py:52
  257.4 5.7 %collective-permute-done.16 = bf16[96,2048]{1,0:T(8,128)(2,1)S(1)} collective-permute-done((bf16[96,2048]{1,0:T(8,128)(2,1)S(1)}, bf16[96,2048]{1,0:T(8,128)(2,1)S(1)}, u32[]{:S(2)}, u32[]{:S(2)}) %collective-permute-start.16) | collective-permute-done | bytes 393248 | tf_op jit(solution)/shard_map/ppermute | solution.py:36
  265.8 4.5 %all-to-all-done.7 = bf16[8,48,2048]{2,1,0:T(8,128)(2,1)S(1)} async-done(((bf16[8,48,2048]{2,1,0:T(8,128)(2,1)}), bf16[8,48,2048]{2,1,0:T(8,128)(2,1)S(1)}, u32[]{:S(2)}, u32[]{:S(2)}) %all-to-all-start.7) | async-done | bytes 1572896 | tf_op jit(solution)/shard_map/all_to_all | solution.py:52
  276.5 3.0 collective-permute-start.19
  283.0 2.4 unpack.1
  (139 shorter events, 57.4 us)
Async XLA Ops:
  7.2 156.4 %all-gather.5.cloned.1.call-start = ((), (), s32[]{:S(2)}) async-start(), calls=%async_computation.8 | async-start | bytes 5898240 | tf_op jit(solution)/shard_map/all_gather | solution.py:367
  12.8 27.9 %collective-permute-start.5 = (bf16[384,1536]{1,0:T(8,128)(2,1)}, bf16[384,1536]{1,0:T(8,128)(2,1)S(1)}, u32[]{:S(2)}, u32[]{:S(2)}) collective-permute-start(bf16[384,1536]{1,0:T(8,128)(2,1)} %get-tuple-element.94.first_ref.refs_0_), channel_id=1, source_target_pairs={{0,8},{8,0},{1,9},{9,1},{2,10},{10,2},{3,11},{11,3},{4,12},{12,4},... | collective-permute-start | bytes 3538952 | tf_op jit(solution)/shard_map/ppermute | solution.py:329
  12.8 27.9 %all-to-all-start = ((bf16[4,96,1536]{2,1,0:T(8,128)(2,1)}), bf16[4,96,1536]{2,1,0:T(8,128)(2,1)S(1)}, u32[]{:S(2)}, u32[]{:S(2)}) async-start(bf16[4,96,1536]{2,1,0:T(8,128)(2,1)} %bitcast.7), calls=%async_computation | async-start | bytes 2359296 | tf_op jit(solution)/shard_map/all_to_all | solution.py:52
  17.5 15.1 %collective-permute-start.1 = (bf16[104,2048]{1,0:T(8,128)(2,1)S(1)}, bf16[104,2048]{1,0:T(8,128)(2,1)S(1)}, u32[]{:S(2)}, u32[]{:S(2)}) collective-permute-start(bf16[104,2048]{1,0:T(8,128)(2,1)S(1)} %get-tuple-element.85.refs_0_), channel_id=1, source_target_pairs={{0,49},{1,0},{16,1},{17,16},{32,17},{33,32},{48,33},{49,48},{2,51}... | collective-permute-start | bytes 1277960 | tf_op jit(solution)/shard_map/ppermute | solution.py:36
  23.5 12.7 %collective-permute-start = (bf16[104,2048]{1,0:T(8,128)(2,1)S(1)}, bf16[104,2048]{1,0:T(8,128)(2,1)}, u32[]{:S(2)}, u32[]{:S(2)}) collective-permute-start(bf16[104,2048]{1,0:T(8,128)(2,1)S(1)} %get-tuple-element.85.refs_0_), channel_id=1, source_target_pairs={{0,1},{1,16},{16,17},{17,32},{32,33},{33,48},{48,49},{49,0},{2,3},... | collective-permute-start | bytes 1277960 | tf_op jit(solution)/shard_map/ppermute | solution.py:36
  42.2 42.3 %all-to-all-start.1 = ((bf16[8,48,2048]{2,1,0:T(8,128)(2,1)}), bf16[8,48,2048]{2,1,0:T(8,128)(2,1)S(1)}, u32[]{:S(2)}, u32[]{:S(2)}) async-start(bf16[8,48,2048]{2,1,0:T(8,128)(2,1)} %bitcast.8), calls=%async_computation.1 | async-start | bytes 3145728 | tf_op jit(solution)/shard_map/all_to_all | solution.py:52
  47.0 116.6 %all-gather.7.cloned.1.call-start = ((), (), s32[]{:S(2)}) async-start(), calls=%async_computation.9 | async-start | bytes 5898240 | tf_op jit(solution)/shard_map/all_gather | solution.py:386
  47.0 37.4 %collective-permute-start.4 = (bf16[384,1536]{1,0:T(8,128)(2,1)}, bf16[384,1536]{1,0:T(8,128)(2,1)}, u32[]{:S(2)}, u32[]{:S(2)}) collective-permute-start(bf16[384,1536]{1,0:T(8,128)(2,1)} %copy-done.32), channel_id=1, source_target_pairs={{0,1},{1,0},{2,3},{3,2},{4,5},{5,4},{6,7},{7,6},{8,9},{9,8},{10,11... | collective-permute-start | bytes 3538952 | tf_op jit(solution)/shard_map/ppermute | solution.py:329
  47.1 35.3 %collective-permute-start.2 = (bf16[104,2048]{1,0:T(8,128)(2,1)}, bf16[104,2048]{1,0:T(8,128)(2,1)S(1)}, u32[]{:S(2)}, u32[]{:S(2)}) collective-permute-start(bf16[104,2048]{1,0:T(8,128)(2,1)} %collective-permute-done.refs_1_), channel_id=1, source_target_pairs={{0,1},{1,16},{16,17},{17,32},{32,33},{33,48},{48,49},{49,0},{2,3},... | collective-permute-start | bytes 1277960 | tf_op jit(solution)/shard_map/ppermute | solution.py:36
  49.1 35.3 %collective-permute-start.3 = (bf16[104,2048]{1,0:T(8,128)(2,1)S(1)}, bf16[104,2048]{1,0:T(8,128)(2,1)S(1)}, u32[]{:S(2)}, u32[]{:S(2)}) collective-permute-start(bf16[104,2048]{1,0:T(8,128)(2,1)S(1)} %copy-done.9), channel_id=1, source_target_pairs={{0,49},{1,0},{16,1},{17,16},{32,17},{33,32},{48,33},{49,48},{2,51}... | collective-permute-start | bytes 1277960 | tf_op jit(solution)/shard_map/ppermute | solution.py:36
  88.1 18.7 %all-to-all-start.2 = ((bf16[4,96,1536]{2,1,0:T(8,128)(2,1)}), bf16[4,96,1536]{2,1,0:T(8,128)(2,1)S(1)}, u32[]{:S(2)}, u32[]{:S(2)}) async-start(bf16[4,96,1536]{2,1,0:T(8,128)(2,1)} %gather_fusion.1), calls=%async_computation.2 | async-start | bytes 2359296 | tf_op jit(solution)/shard_map/all_to_all | solution.py:52
  92.9 11.7 %collective-permute-start.6 = (bf16[104,2048]{1,0:T(8,128)(2,1)S(1)}, bf16[104,2048]{1,0:T(8,128)(2,1)S(1)}, u32[]{:S(2)}, u32[]{:S(2)}) collective-permute-start(bf16[104,2048]{1,0:T(8,128)(2,1)S(1)} %collective-permute-done.2.refs_0_), channel_id=1, source_target_pairs={{0,1},{1,16},{16,17},{17,32},{32,33},{33,48},{48,49},{49,0},{2,3},... | collective-permute-start | bytes 1277960 | tf_op jit(solution)/shard_map/ppermute | solution.py:36
  93.2 11.4 %collective-permute-start.7 = (bf16[104,2048]{1,0:T(8,128)(2,1)}, bf16[104,2048]{1,0:T(8,128)(2,1)S(1)}, u32[]{:S(2)}, u32[]{:S(2)}) collective-permute-start(bf16[104,2048]{1,0:T(8,128)(2,1)} %copy-done.6), channel_id=1, source_target_pairs={{0,49},{1,0},{16,1},{17,16},{32,17},{33,32},{48,33},{49,48},{2,51}... | collective-permute-start | bytes 1277960 | tf_op jit(solution)/shard_map/ppermute | solution.py:36
  106.8 31.4 %all-to-all-start.3 = ((bf16[8,32,2048]{2,1,0:T(8,128)(2,1)}), bf16[8,32,2048]{2,1,0:T(8,128)(2,1)S(1)}, u32[]{:S(2)}, u32[]{:S(2)}) async-start(bf16[8,32,2048]{2,1,0:T(8,128)(2,1)} %bitcast.14), calls=%async_computation.3 | async-start | bytes 2097152 | tf_op jit(solution)/shard_map/all_to_all | solution.py:52
  112.5 19.5 %collective-permute-start.8 = (bf16[104,2048]{1,0:T(8,128)(2,1)S(1)}, bf16[104,2048]{1,0:T(8,128)(2,1)S(1)}, u32[]{:S(2)}, u32[]{:S(2)}) collective-permute-start(bf16[104,2048]{1,0:T(8,128)(2,1)S(1)} %collective-permute-done.6.refs_0_), channel_id=1, source_target_pairs={{0,1},{1,16},{16,17},{17,32},{32,33},{33,48},{48,49},{49,0},{2,3},... | collective-permute-start | bytes 1277960 | tf_op jit(solution)/shard_map/ppermute | solution.py:36
  113.1 24.4 %collective-permute-start.9 = (bf16[96,1536]{1,0:T(8,128)(2,1)}, bf16[96,1536]{1,0:T(8,128)(2,1)S(1)}, u32[]{:S(2)}, u32[]{:S(2)}) collective-permute-start(bf16[96,1536]{1,0:T(8,128)(2,1)} %copy-done.35), channel_id=1, source_target_pairs={{0,16},{16,32},{32,48},{48,0},{1,17},{17,33},{33,49},{49,1},{2,18}... | collective-permute-start | bytes 884744 | tf_op jit(solution)/shard_map/ppermute | solution.py:36
  139.2 24.3 %all-to-all-start.4 = ((bf16[8,48,2048]{2,1,0:T(8,128)(2,1)}), bf16[8,48,2048]{2,1,0:T(8,128)(2,1)S(1)}, u32[]{:S(2)}, u32[]{:S(2)}) async-start(bf16[8,48,2048]{2,1,0:T(8,128)(2,1)} %bitcast.16), calls=%async_computation.4 | async-start | bytes 3145728 | tf_op jit(solution)/shard_map/all_to_all | solution.py:52
  144.0 18.2 %collective-permute-start.10 = (bf16[96,1536]{1,0:T(8,128)(2,1)}, bf16[96,1536]{1,0:T(8,128)(2,1)S(1)}, u32[]{:S(2)}, u32[]{:S(2)}) collective-permute-start(bf16[96,1536]{1,0:T(8,128)(2,1)} %copy-done.34), channel_id=1, source_target_pairs={{0,32},{16,48},{32,0},{48,16},{1,33},{17,49},{33,1},{49,17},{2,34}... | collective-permute-start | bytes 884744 | tf_op jit(solution)/shard_map/ppermute | solution.py:36
  144.1 18.5 %collective-permute-start.11 = (bf16[96,1536]{1,0:T(8,128)(2,1)}, bf16[96,1536]{1,0:T(8,128)(2,1)S(1)}, u32[]{:S(2)}, u32[]{:S(2)}) collective-permute-start(bf16[96,1536]{1,0:T(8,128)(2,1)} %copy-done.33), channel_id=1, source_target_pairs={{0,48},{16,0},{32,16},{48,32},{1,49},{17,1},{33,17},{49,33},{2,50}... | collective-permute-start | bytes 884744 | tf_op jit(solution)/shard_map/ppermute | solution.py:36
  173.3 53.0 %all-to-all-start.5 = ((bf16[8,48,2048]{2,1,0:T(8,128)(2,1)}), bf16[8,48,2048]{2,1,0:T(8,128)(2,1)S(1)}, u32[]{:S(2)}, u32[]{:S(2)}) async-start(bf16[8,48,2048]{2,1,0:T(8,128)(2,1)} %bitcast.38), calls=%async_computation.5 | async-start | bytes 3145728 | tf_op jit(solution)/shard_map/all_to_all | solution.py:52
  183.4 33.4 %collective-permute-start.12 = (bf16[96,1536]{1,0:T(8,128)(2,1)S(1)}, bf16[96,1536]{1,0:T(8,128)(2,1)S(1)}, u32[]{:S(2)}, u32[]{:S(2)}) collective-permute-start(bf16[96,1536]{1,0:T(8,128)(2,1)S(1)} %get-tuple-element.138), channel_id=1, source_target_pairs={{0,16},{16,32},{32,48},{48,0},{1,17},{17,33},{33,49},{49,1},{2,18}... | collective-permute-start | bytes 884744 | tf_op jit(solution)/shard_map/ppermute | solution.py:36
  196.5 28.4 %collective-permute-start.13 = (bf16[96,1536]{1,0:T(8,128)(2,1)S(1)}, bf16[96,1536]{1,0:T(8,128)(2,1)S(1)}, u32[]{:S(2)}, u32[]{:S(2)}) collective-permute-start(bf16[96,1536]{1,0:T(8,128)(2,1)S(1)} %get-tuple-element.139), channel_id=1, source_target_pairs={{0,32},{16,48},{32,0},{48,16},{1,33},{17,49},{33,1},{49,17},{2,34}... | collective-permute-start | bytes 884744 | tf_op jit(solution)/shard_map/ppermute | solution.py:36
  198.6 27.1 %collective-permute-start.14 = (bf16[96,1536]{1,0:T(8,128)(2,1)S(1)}, bf16[96,1536]{1,0:T(8,128)(2,1)S(1)}, u32[]{:S(2)}, u32[]{:S(2)}) collective-permute-start(bf16[96,1536]{1,0:T(8,128)(2,1)S(1)} %get-tuple-element.140), channel_id=1, source_target_pairs={{0,48},{16,0},{32,16},{48,32},{1,49},{17,1},{33,17},{49,33},{2,50}... | collective-permute-start | bytes 884744 | tf_op jit(solution)/shard_map/ppermute | solution.py:36
  226.3 19.4 %all-to-all-start.6 = ((bf16[8,32,2048]{2,1,0:T(8,128)(2,1)}), bf16[8,32,2048]{2,1,0:T(8,128)(2,1)}, u32[]{:S(2)}, u32[]{:S(2)}) async-start(bf16[8,32,2048]{2,1,0:T(8,128)(2,1)} %bitcast.39), calls=%async_computation.6 | async-start | bytes 2097152 | tf_op jit(solution)/shard_map/all_to_all | solution.py:52
  233.2 12.5 %collective-permute-start.17 = (bf16[96,2048]{1,0:T(8,128)(2,1)S(1)}, bf16[96,2048]{1,0:T(8,128)(2,1)}, u32[]{:S(2)}, u32[]{:S(2)}) collective-permute-start(bf16[96,2048]{1,0:T(8,128)(2,1)S(1)} %get-tuple-element.147), channel_id=1, source_target_pairs={{0,1},{1,16},{16,17},{17,32},{32,33},{33,48},{48,49},{49,0},{2,3},... | collective-permute-start | bytes 1179656 | tf_op jit(solution)/shard_map/ppermute | solution.py:36
  233.2 17.5 %collective-permute-start.15 = (bf16[96,2048]{1,0:T(8,128)(2,1)}, bf16[96,2048]{1,0:T(8,128)(2,1)}, u32[]{:S(2)}, u32[]{:S(2)}) collective-permute-start(bf16[96,2048]{1,0:T(8,128)(2,1)} %get-tuple-element.142), channel_id=1, source_target_pairs={{0,49},{1,0},{16,1},{17,16},{32,17},{33,32},{48,33},{49,48},{2,51}... | collective-permute-start | bytes 1179656 | tf_op jit(solution)/shard_map/ppermute | solution.py:36
  245.7 24.5 %all-to-all-start.7 = ((bf16[8,48,2048]{2,1,0:T(8,128)(2,1)}), bf16[8,48,2048]{2,1,0:T(8,128)(2,1)S(1)}, u32[]{:S(2)}, u32[]{:S(2)}) async-start(bf16[8,48,2048]{2,1,0:T(8,128)(2,1)} %bitcast.37), calls=%async_computation.7 | async-start | bytes 3145728 | tf_op jit(solution)/shard_map/all_to_all | solution.py:52
  251.8 11.2 %collective-permute-start.16 = (bf16[96,2048]{1,0:T(8,128)(2,1)S(1)}, bf16[96,2048]{1,0:T(8,128)(2,1)S(1)}, u32[]{:S(2)}, u32[]{:S(2)}) collective-permute-start(bf16[96,2048]{1,0:T(8,128)(2,1)S(1)} %add_convert_fusion.5), channel_id=1, source_target_pairs={{0,49},{1,0},{16,1},{17,16},{32,17},{33,32},{48,33},{49,48},{2,51}... | collective-permute-start | bytes 1179656 | tf_op jit(solution)/shard_map/ppermute | solution.py:36
  256.0 15.6 %collective-permute-start.20 = (bf16[96,2048]{1,0:T(8,128)(2,1)}, bf16[96,2048]{1,0:T(8,128)(2,1)}, u32[]{:S(2)}, u32[]{:S(2)}) collective-permute-start(bf16[96,2048]{1,0:T(8,128)(2,1)} %add_convert_fusion.2), channel_id=1, source_target_pairs={{0,1},{1,16},{16,17},{17,32},{32,33},{33,48},{48,49},{49,0},{2,3},... | collective-permute-start | bytes 1179656 | tf_op jit(solution)/shard_map/ppermute | solution.py:36
  263.9 10.8 %collective-permute-start.18 = (bf16[96,2048]{1,0:T(8,128)(2,1)}, bf16[96,2048]{1,0:T(8,128)(2,1)}, u32[]{:S(2)}, u32[]{:S(2)}) collective-permute-start(bf16[96,2048]{1,0:T(8,128)(2,1)} %add_convert_fusion.4), channel_id=1, source_target_pairs={{0,49},{1,0},{16,1},{17,16},{32,17},{33,32},{48,33},{49,48},{2,51}... | collective-permute-start | bytes 1179656 | tf_op jit(solution)/shard_map/ppermute | solution.py:36
  273.4 12.2 %collective-permute-start.21 = (bf16[96,2048]{1,0:T(8,128)(2,1)}, bf16[96,2048]{1,0:T(8,128)(2,1)}, u32[]{:S(2)}, u32[]{:S(2)}) collective-permute-start(bf16[96,2048]{1,0:T(8,128)(2,1)} %add_convert_fusion.1), channel_id=1, source_target_pairs={{0,1},{1,16},{16,17},{17,32},{32,33},{33,48},{48,49},{49,0},{2,3},... | collective-permute-start | bytes 1179656 | tf_op jit(solution)/shard_map/ppermute | solution.py:36
  276.5 10.9 %collective-permute-start.19 = (bf16[96,2048]{1,0:T(8,128)(2,1)}, bf16[96,2048]{1,0:T(8,128)(2,1)}, u32[]{:S(2)}, u32[]{:S(2)}) collective-permute-start(bf16[96,2048]{1,0:T(8,128)(2,1)} %add_convert_fusion.3), channel_id=1, source_target_pairs={{0,49},{1,0},{16,1},{17,16},{32,17},{33,32},{48,33},{49,48},{2,51}... | collective-permute-start | bytes 1179656 | tf_op jit(solution)/shard_map/ppermute | solution.py:36
  (38 other events, 171.7 us)
Sparse Core Ops, SparseCore 0:
  11.8 57.0 all-gather.4
  84.6 51.4 all-gather.6

commit v9 on v8

--- a/solution.py
+++ b/solution.py
@@ -382,19 +382,19 @@
         scratch=[pltpu.SemaphoreType.DMA((NZH,))],
     )(place, first)
     d1, w1 = dispatch(place, (p2, m2))
-    r0, hx, swapped = fence(r0, hx, swapped)
+    d1, r0, p3, m3, swapped, *cut = fence(d1, r0, p3, m3, swapped, *cut)
     swap_full = lax.all_gather(swapped, "y", axis=0, tiled=False)
-    x_turn = jnp.arange(NX, dtype=jnp.int32)
-    x_from = jnp.take(pair_list, (x_turn * NZH + zh_me) * NC + c_me, mode="clip") >> 3
-    hx = across(jnp.take(hx, x_from, axis=0, mode="clip"), "x").reshape(PACK, SIDE)
-    d1, r0, p3, m3, hx, *cut = fence(d1, r0, p3, m3, hx, *cut)
     r1 = in_plane(d1)
     far = along_z(p3, 1)
     held = [cut[0]] + [shift(cut[k], "zh", NZH, k) for k in range(1, NZH)]
     d2, w2 = dispatch(place, (p3, m3, far))
     d2, r1, held[1] = fence(d2, r1, held[1])
     r2 = in_plane(d2)
+    x_turn = jnp.arange(NX, dtype=jnp.int32)
+    x_from = jnp.take(pair_list, (x_turn * NZH + zh_me) * NC + c_me, mode="clip") >> 3
+    hx = jnp.take(hx, x_from, axis=0, mode="clip")
     r0, r1, r2, hx, *held = fence(r0, r1, r2, hx, *held)
+    hx = across(hx, "x").reshape(PACK, SIDE)
     (s2,) = ffn(place, own_full, swap_full, (r2,), 384)
     s2, r1, r0, hx, *held = fence(s2, r1, r0, hx, *held)
     b2 = in_plane(s2)

time: 299 us -> 281 us (0.940)
  starting transfers between devices: 83.1 us -> 72.6 us
  waiting for transfers between devices: 121 us -> 114 us
    ppermute x20, waiting for transfers between devices: 115 us -> 105 us  [shift(): lax.ppermute(value, axes, [(i, (i + step) % count) for i in range(count)])]
    ppermute x20, starting transfers between devices: 42.5 us -> 33 us  [shift(): lax.ppermute(value, axes, [(i, (i + step) % count) for i in range(count)])]
    all_to_all x8, waiting for transfers between devices: 6.21 us -> 9.66 us  [across(): return lax.all_to_all(value, axis, split_axis=0, concat_axis=0, tiled=True)]
    unnamed x76 -> x72, local copies, waits for them, and re-layouts: 20.1 us -> 20.7 us
  transfers between devices with their start and end apart: 32 -> 32, of which waited for: 18 -> 18; matrix products, arithmetic and copies ran while one was open for 4% -> 4% of each run, Pallas kernels for 10% -> 14%
where the time goes in v9:
time: 281 us; the launch traced here: 278 us
  waiting for transfers between devices  114 us (41%)
  starting transfers between devices  72.6 us (26%)
  Pallas kernels  41.9 us (15%)
  local copies, waits for them, and re-layouts  24.9 us (9%)
  between operations  14.3 us (5%)
  other arithmetic  10.1 us (4%)
    ppermute x20, waiting for transfers between devices, shift(): lax.ppermute(value, axes, [(i, (i + step) % count) for i in range(count)])  105 us
    all_to_all x8, starting transfers between devices, across(): return lax.all_to_all(value, axis, split_axis=0, concat_axis=0, tiled=True)  39.5 us
    ppermute x20, starting transfers between devices, shift(): lax.ppermute(value, axes, [(i, (i + step) % count) for i in range(count)])  33 us
    pallas_call x2, Pallas kernels, ffn(): call(functools.partial(ffn_kernel, splits, block), [pltpu.HBM((r, WIDTH),...  22.5 us
    unnamed x72, local copies, waits for them, and re-layouts  20.7 us
    all_to_all x8, waiting for transfers between devices, across(): return lax.all_to_all(value, axis, split_axis=0, concat_axis=0, tiled=True)  9.66 us
    convert_element_type x5, other arithmetic, joined(): return (got.astype(F32) + mine).astype(BF)  7.39 us
    pallas_call x3, Pallas kernels, dispatch(): call(functools.partial(dispatch_kernel, n), [shape(PLACES * n * MOST, WID...  6.65 us
  transfers between devices with their start and end apart: 32, of which 18 were waited for; matrix products, arithmetic and copies ran while one was open for 4% of the time, Pallas kernels for 14%

profile of v9, /device:TPU:22, one launch (start us, length us, event | category | flops | bytes accessed | tf_op | source)
XLA Modules:
  0.0 278.3 jit_solution(1617730819187354152)
XLA Ops:
  7.3 4.4 %prep.1 = (bf16[104,2048]{1,0:T(8,128)(2,1)S(1)}, bf16[384,1536]{1,0:T(8,128)(2,1)}, bf16[384,1536]{1,0:T(8,128)(2,1)S(1)}, bf16[384,1536]{1,0:T(8,128)(2,1)}) custom-call(s32[4]{0:T(128)S(1)} %pad_add_fusion.place_ref, bf16[96,2048]{1,0:T(8,128)(2,1)} %tokens_ref.1, f32[1,2048]{1,0:T(1,128)} %bitcast.41, s32[8,96]{1,0:T(8,128)} %bitcast.42, ...), custom_call_target="tpu_custom_call" | custom-call | tf_op jit(solution)/shard_map/prep/pallas_call | solution.py:343
  12.9 4.8 %all-to-all-start = ((bf16[4,96,1536]{2,1,0:T(8,128)(2,1)}), bf16[4,96,1536]{2,1,0:T(8,128)(2,1)}, u32[]{:S(2)}, u32[]{:S(2)}) async-start(bf16[4,96,1536]{2,1,0:T(8,128)(2,1)} %bitcast.7), calls=%async_computation | async-start | bytes 2359296 | tf_op jit(solution)/shard_map/all_to_all | solution.py:52
  17.7 5.9 %collective-permute-start.1 = (bf16[104,2048]{1,0:T(8,128)(2,1)S(1)}, bf16[104,2048]{1,0:T(8,128)(2,1)S(1)}, u32[]{:S(2)}, u32[]{:S(2)}) collective-permute-start(bf16[104,2048]{1,0:T(8,128)(2,1)S(1)} %get-tuple-element.82.refs_0_), channel_id=1, source_target_pairs={{0,49},{1,0},{16,1},{17,16},{32,17},{33,32},{48,33},{49,48},{2,51}... | collective-permute-start | bytes 1277960 | tf_op jit(solution)/shard_map/ppermute | solution.py:36
  23.6 9.4 %collective-permute-done.1.refs_2_ = bf16[104,2048]{1,0:T(8,128)(2,1)S(1)} collective-permute-done((bf16[104,2048]{1,0:T(8,128)(2,1)S(1)}, bf16[104,2048]{1,0:T(8,128)(2,1)S(1)}, u32[]{:S(2)}, u32[]{:S(2)}) %collective-permute-start.1) | collective-permute-done | bytes 426016 | tf_op jit(solution)/shard_map/ppermute | solution.py:36
  33.0 3.4 %collective-permute-done.refs_1_ = bf16[104,2048]{1,0:T(8,128)(2,1)S(1)} collective-permute-done((bf16[104,2048]{1,0:T(8,128)(2,1)S(1)}, bf16[104,2048]{1,0:T(8,128)(2,1)S(1)}, u32[]{:S(2)}, u32[]{:S(2)}) %collective-permute-start) | collective-permute-done | bytes 426016 | tf_op jit(solution)/shard_map/ppermute | solution.py:36
  36.4 2.7 dispatch.4
  40.8 4.8 %all-to-all-start.1 = ((bf16[8,48,2048]{2,1,0:T(8,128)(2,1)}), bf16[8,48,2048]{2,1,0:T(8,128)(2,1)S(1)}, u32[]{:S(2)}, u32[]{:S(2)}) async-start(bf16[8,48,2048]{2,1,0:T(8,128)(2,1)} %bitcast.8), calls=%async_computation.1 | async-start | bytes 3145728 | tf_op jit(solution)/shard_map/all_to_all | solution.py:52
  48.8 21.6 %collective-permute-done.2.refs_0_ = bf16[104,2048]{1,0:T(8,128)(2,1)S(1)} collective-permute-done((bf16[104,2048]{1,0:T(8,128)(2,1)S(1)}, bf16[104,2048]{1,0:T(8,128)(2,1)S(1)}, u32[]{:S(2)}, u32[]{:S(2)}) %collective-permute-start.2) | collective-permute-done | bytes 426016 | tf_op jit(solution)/shard_map/ppermute | solution.py:36
  72.9 3.0 %collective-permute-start.7 = (bf16[104,2048]{1,0:T(8,128)(2,1)S(1)}, bf16[104,2048]{1,0:T(8,128)(2,1)S(1)}, u32[]{:S(2)}, u32[]{:S(2)}) collective-permute-start(bf16[104,2048]{1,0:T(8,128)(2,1)S(1)} %collective-permute-done.3.refs_1_), channel_id=1, source_target_pairs={{0,49},{1,0},{16,1},{17,16},{32,17},{33,32},{48,33},{49,48},{2,51}... | collective-permute-start | bytes 1277960 | tf_op jit(solution)/shard_map/ppermute | solution.py:36
  84.8 4.8 %all-to-all-start.2 = ((bf16[8,32,2048]{2,1,0:T(8,128)(2,1)}), bf16[8,32,2048]{2,1,0:T(8,128)(2,1)S(1)}, u32[]{:S(2)}, u32[]{:S(2)}) async-start(bf16[8,32,2048]{2,1,0:T(8,128)(2,1)} %bitcast.37), calls=%async_computation.2 | async-start | bytes 2097152 | tf_op jit(solution)/shard_map/all_to_all | solution.py:52
  89.6 3.2 %collective-permute-start.9 = (bf16[96,1536]{1,0:T(8,128)(2,1)}, bf16[96,1536]{1,0:T(8,128)(2,1)S(1)}, u32[]{:S(2)}, u32[]{:S(2)}) collective-permute-start(bf16[96,1536]{1,0:T(8,128)(2,1)} %copy-done.34), channel_id=1, source_target_pairs={{0,16},{16,32},{32,48},{48,0},{1,17},{17,33},{33,49},{49,1},{2,18}... | collective-permute-start | bytes 884744 | tf_op jit(solution)/shard_map/ppermute | solution.py:36
  92.8 10.8 %collective-permute-done.8.refs_2_ = bf16[104,2048]{1,0:T(8,128)(2,1)S(1)} collective-permute-done((bf16[104,2048]{1,0:T(8,128)(2,1)S(1)}, bf16[104,2048]{1,0:T(8,128)(2,1)S(1)}, u32[]{:S(2)}, u32[]{:S(2)}) %collective-permute-start.8) | collective-permute-done | bytes 426016 | tf_op jit(solution)/shard_map/ppermute | solution.py:36
  103.6 2.7 dispatch.5
  107.0 9.5 %collective-permute-done.9.refs_1_ = bf16[96,1536]{1,0:T(8,128)(2,1)S(1)} collective-permute-done((bf16[96,1536]{1,0:T(8,128)(2,1)}, bf16[96,1536]{1,0:T(8,128)(2,1)S(1)}, u32[]{:S(2)}, u32[]{:S(2)}) %collective-permute-start.9) | collective-permute-done | bytes 294944 | tf_op jit(solution)/shard_map/ppermute | solution.py:36
  118.2 4.8 %all-to-all-start.3 = ((bf16[8,48,2048]{2,1,0:T(8,128)(2,1)}), bf16[8,48,2048]{2,1,0:T(8,128)(2,1)S(1)}, u32[]{:S(2)}, u32[]{:S(2)}) async-start(bf16[8,48,2048]{2,1,0:T(8,128)(2,1)} %bitcast.14), calls=%async_computation.3 | async-start | bytes 3145728 | tf_op jit(solution)/shard_map/all_to_all | solution.py:52
  126.1 2.9 %gather_fusion.1 = bf16[4,96,1536]{2,1,0:T(8,128)(2,1)} fusion(bf16[4,96,1536]{2,1,0:T(8,128)(2,1)} %all-to-all-done, s32[1024]{0:T(1024)S(1)} %pad_clamp_fusion.1), kind=kCustom, calls=%fused_computation.1 | custom fusion | bytes 2359312 | tf_op jit(solution)/shard_map/jit(_take)/gather | solution.py:395
  129.1 13.0 %collective-permute-done.10.refs_2_ = bf16[96,1536]{1,0:T(8,128)(2,1)S(1)} collective-permute-done((bf16[96,1536]{1,0:T(8,128)(2,1)S(1)}, bf16[96,1536]{1,0:T(8,128)(2,1)S(1)}, u32[]{:S(2)}, u32[]{:S(2)}) %collective-permute-start.10) | collective-permute-done | bytes 294944 | tf_op jit(solution)/shard_map/ppermute | solution.py:36
  142.8 9.3 %collective-permute-done.11.refs_3_ = bf16[96,1536]{1,0:T(8,128)(2,1)S(1)} collective-permute-done((bf16[96,1536]{1,0:T(8,128)(2,1)S(1)}, bf16[96,1536]{1,0:T(8,128)(2,1)S(1)}, u32[]{:S(2)}, u32[]{:S(2)}) %collective-permute-start.11) | collective-permute-done | bytes 294944 | tf_op jit(solution)/shard_map/ppermute | solution.py:36
  152.9 4.8 %all-to-all-start.4 = ((bf16[4,96,1536]{2,1,0:T(8,128)(2,1)}), bf16[4,96,1536]{2,1,0:T(8,128)(2,1)S(1)}, u32[]{:S(2)}, u32[]{:S(2)}) async-start(bf16[4,96,1536]{2,1,0:T(8,128)(2,1)} %gather_fusion.1), calls=%async_computation.4 | async-start | bytes 2359296 | tf_op jit(solution)/shard_map/all_to_all | solution.py:52
  157.7 9.8 %expert_ffn.2 = bf16[384,2048]{1,0:T(8,128)(2,1)} custom-call(s32[4]{0:T(128)S(1)} %pad_add_fusion.place_ref, bf16[4,384,1536]{2,1,0:T(8,128)(2,1)} %bitcast.44, bf16[4,384,1536]{2,1,0:T(8,128)(2,1)} %bitcast.46, bf16[384,2048]{1,0:T(8,128)(2,1)S(1)} %bitcast.35), custom_call_target="tpu_custom_call" | custom-call | flops 3623878656 | bytes 15728640 | tf_op jit(solution)/shard_map/expert_ffn/pallas_call | solution.py:274
  167.4 4.8 %all-to-all-done.4 = bf16[4,96,1536]{2,1,0:T(8,128)(2,1)S(1)} async-done(((bf16[4,96,1536]{2,1,0:T(8,128)(2,1)}), bf16[4,96,1536]{2,1,0:T(8,128)(2,1)S(1)}, u32[]{:S(2)}, u32[]{:S(2)}) %all-to-all-start.4) | async-done | bytes 1179680 | tf_op jit(solution)/shard_map/all_to_all | solution.py:52
  172.3 5.7 %all-to-all-start.5 = ((bf16[8,48,2048]{2,1,0:T(8,128)(2,1)}), bf16[8,48,2048]{2,1,0:T(8,128)(2,1)S(1)}, u32[]{:S(2)}, u32[]{:S(2)}) async-start(bf16[8,48,2048]{2,1,0:T(8,128)(2,1)} %bitcast.39), calls=%async_computation.5 | async-start | bytes 3145728 | tf_op jit(solution)/shard_map/all_to_all | solution.py:52
  183.0 2.6 collective-permute-start.13
  189.0 12.7 %expert_ffn.3 = (bf16[256,2048]{1,0:T(8,128)(2,1)}, bf16[384,2048]{1,0:T(8,128)(2,1)}) custom-call(s32[4]{0:T(128)S(1)} %pad_add_fusion.place_ref, bf16[4,384,1536]{2,1,0:T(8,128)(2,1)} %bitcast.45, bf16[4,384,1536]{2,1,0:T(8,128)(2,1)} %bitcast.47, bf16[256,2048]{1,0:T(8,128)(2,1)S(1)} %bitcast.36, bf16[384,2048]{1,0:T(8,128)(2,1)S(1)} %bitcast.34), custom_call_target="tpu_custom_call" | custom-call | flops 6039797760 | bytes 15728640 | tf_op jit(solution)/shard_map/expert_ffn/pallas_call | solution.py:274
  205.3 2.8 collective-permute-done.14.refs_6_
  208.8 4.8 %all-to-all-start.6 = ((bf16[8,32,2048]{2,1,0:T(8,128)(2,1)}), bf16[8,32,2048]{2,1,0:T(8,128)(2,1)}, u32[]{:S(2)}, u32[]{:S(2)}) async-start(bf16[8,32,2048]{2,1,0:T(8,128)(2,1)} %bitcast.40), calls=%async_computation.6 | async-start | bytes 2097152 | tf_op jit(solution)/shard_map/all_to_all | solution.py:52
  215.7 3.2 %collective-permute-start.15 = (bf16[96,2048]{1,0:T(8,128)(2,1)}, bf16[96,2048]{1,0:T(8,128)(2,1)}, u32[]{:S(2)}, u32[]{:S(2)}) collective-permute-start(bf16[96,2048]{1,0:T(8,128)(2,1)} %get-tuple-element.136), channel_id=1, source_target_pairs={{0,49},{1,0},{16,1},{17,16},{32,17},{33,32},{48,33},{49,48},{2,51}... | collective-permute-start | bytes 1179656 | tf_op jit(solution)/shard_map/ppermute | solution.py:36
  218.9 9.2 %collective-permute-done.17 = bf16[96,2048]{1,0:T(8,128)(2,1)} collective-permute-done((bf16[96,2048]{1,0:T(8,128)(2,1)S(1)}, bf16[96,2048]{1,0:T(8,128)(2,1)}, u32[]{:S(2)}, u32[]{:S(2)}) %collective-permute-start.17) | collective-permute-done | bytes 393248 | tf_op jit(solution)/shard_map/ppermute | solution.py:36
  228.2 5.0 %all-to-all-start.7 = ((bf16[8,48,2048]{2,1,0:T(8,128)(2,1)}), bf16[8,48,2048]{2,1,0:T(8,128)(2,1)S(1)}, u32[]{:S(2)}, u32[]{:S(2)}) async-start(bf16[8,48,2048]{2,1,0:T(8,128)(2,1)} %bitcast.38), calls=%async_computation.7 | async-start | bytes 3145728 | tf_op jit(solution)/shard_map/all_to_all | solution.py:52
  239.8 5.7 %collective-permute-done.16 = bf16[96,2048]{1,0:T(8,128)(2,1)S(1)} collective-permute-done((bf16[96,2048]{1,0:T(8,128)(2,1)S(1)}, bf16[96,2048]{1,0:T(8,128)(2,1)S(1)}, u32[]{:S(2)}, u32[]{:S(2)}) %collective-permute-start.16) | collective-permute-done | bytes 393248 | tf_op jit(solution)/shard_map/ppermute | solution.py:36
  247.9 4.8 %all-to-all-done.7 = bf16[8,48,2048]{2,1,0:T(8,128)(2,1)S(1)} async-done(((bf16[8,48,2048]{2,1,0:T(8,128)(2,1)}), bf16[8,48,2048]{2,1,0:T(8,128)(2,1)S(1)}, u32[]{:S(2)}, u32[]{:S(2)}) %all-to-all-start.7) | async-done | bytes 1572896 | tf_op jit(solution)/shard_map/all_to_all | solution.py:52
  259.0 2.9 %collective-permute-start.19 = (bf16[96,2048]{1,0:T(8,128)(2,1)}, bf16[96,2048]{1,0:T(8,128)(2,1)}, u32[]{:S(2)}, u32[]{:S(2)}) collective-permute-start(bf16[96,2048]{1,0:T(8,128)(2,1)} %add_convert_fusion.3), channel_id=1, source_target_pairs={{0,49},{1,0},{16,1},{17,16},{32,17},{33,32},{48,33},{49,48},{2,51}... | collective-permute-start | bytes 1179656 | tf_op jit(solution)/shard_map/ppermute | solution.py:36
  (135 shorter events, 64.0 us)
Async XLA Ops:
  7.2 150.5 %all-gather.5.cloned.1.call-start = ((), (), s32[]{:S(2)}) async-start(), calls=%async_computation.8 | async-start | bytes 5898240 | tf_op jit(solution)/shard_map/all_gather | solution.py:367
  12.8 26.9 %collective-permute-start.5 = (bf16[384,1536]{1,0:T(8,128)(2,1)}, bf16[384,1536]{1,0:T(8,128)(2,1)S(1)}, u32[]{:S(2)}, u32[]{:S(2)}) collective-permute-start(bf16[384,1536]{1,0:T(8,128)(2,1)} %get-tuple-element.91.first_ref.refs_0_), channel_id=1, source_target_pairs={{0,8},{8,0},{1,9},{9,1},{2,10},{10,2},{3,11},{11,3},{4,12},{12,4},... | collective-permute-start | bytes 3538952 | tf_op jit(solution)/shard_map/ppermute | solution.py:329
  12.9 26.8 %all-to-all-start = ((bf16[4,96,1536]{2,1,0:T(8,128)(2,1)}), bf16[4,96,1536]{2,1,0:T(8,128)(2,1)}, u32[]{:S(2)}, u32[]{:S(2)}) async-start(bf16[4,96,1536]{2,1,0:T(8,128)(2,1)} %bitcast.7), calls=%async_computation | async-start | bytes 2359296 | tf_op jit(solution)/shard_map/all_to_all | solution.py:52
  17.7 15.3 %collective-permute-start.1 = (bf16[104,2048]{1,0:T(8,128)(2,1)S(1)}, bf16[104,2048]{1,0:T(8,128)(2,1)S(1)}, u32[]{:S(2)}, u32[]{:S(2)}) collective-permute-start(bf16[104,2048]{1,0:T(8,128)(2,1)S(1)} %get-tuple-element.82.refs_0_), channel_id=1, source_target_pairs={{0,49},{1,0},{16,1},{17,16},{32,17},{33,32},{48,33},{49,48},{2,51}... | collective-permute-start | bytes 1277960 | tf_op jit(solution)/shard_map/ppermute | solution.py:36
  23.6 12.8 %collective-permute-start = (bf16[104,2048]{1,0:T(8,128)(2,1)S(1)}, bf16[104,2048]{1,0:T(8,128)(2,1)S(1)}, u32[]{:S(2)}, u32[]{:S(2)}) collective-permute-start(bf16[104,2048]{1,0:T(8,128)(2,1)S(1)} %get-tuple-element.82.refs_0_), channel_id=1, source_target_pairs={{0,1},{1,16},{16,17},{17,32},{32,33},{33,48},{48,49},{49,0},{2,3},... | collective-permute-start | bytes 1277960 | tf_op jit(solution)/shard_map/ppermute | solution.py:36
  36.4 36.2 %collective-permute-start.4 = (bf16[384,1536]{1,0:T(8,128)(2,1)}, bf16[384,1536]{1,0:T(8,128)(2,1)}, u32[]{:S(2)}, u32[]{:S(2)}) collective-permute-start(bf16[384,1536]{1,0:T(8,128)(2,1)} %copy-done.29), channel_id=1, source_target_pairs={{0,1},{1,0},{2,3},{3,2},{4,5},{5,4},{6,7},{7,6},{8,9},{9,8},{10,11... | collective-permute-start | bytes 3538952 | tf_op jit(solution)/shard_map/ppermute | solution.py:329
  40.8 42.9 %all-to-all-start.1 = ((bf16[8,48,2048]{2,1,0:T(8,128)(2,1)}), bf16[8,48,2048]{2,1,0:T(8,128)(2,1)S(1)}, u32[]{:S(2)}, u32[]{:S(2)}) async-start(bf16[8,48,2048]{2,1,0:T(8,128)(2,1)} %bitcast.8), calls=%async_computation.1 | async-start | bytes 3145728 | tf_op jit(solution)/shard_map/all_to_all | solution.py:52
  45.6 112.1 %all-gather.7.cloned.1.call-start = ((), (), s32[]{:S(2)}) async-start(), calls=%async_computation.9 | async-start | bytes 5898240 | tf_op jit(solution)/shard_map/all_gather | solution.py:386
  45.6 24.9 %collective-permute-start.2 = (bf16[104,2048]{1,0:T(8,128)(2,1)S(1)}, bf16[104,2048]{1,0:T(8,128)(2,1)S(1)}, u32[]{:S(2)}, u32[]{:S(2)}) collective-permute-start(bf16[104,2048]{1,0:T(8,128)(2,1)S(1)} %collective-permute-done.refs_1_), channel_id=1, source_target_pairs={{0,1},{1,16},{16,17},{17,32},{32,33},{33,48},{48,49},{49,0},{2,3},... | collective-permute-start | bytes 1277960 | tf_op jit(solution)/shard_map/ppermute | solution.py:36
  47.6 25.0 %collective-permute-start.3 = (bf16[104,2048]{1,0:T(8,128)(2,1)S(1)}, bf16[104,2048]{1,0:T(8,128)(2,1)S(1)}, u32[]{:S(2)}, u32[]{:S(2)}) collective-permute-start(bf16[104,2048]{1,0:T(8,128)(2,1)S(1)} %collective-permute-done.1.refs_2_), channel_id=1, source_target_pairs={{0,49},{1,0},{16,1},{17,16},{32,17},{33,32},{48,33},{49,48},{2,51}... | collective-permute-start | bytes 1277960 | tf_op jit(solution)/shard_map/ppermute | solution.py:36
  72.6 11.0 %collective-permute-start.6 = (bf16[104,2048]{1,0:T(8,128)(2,1)S(1)}, bf16[104,2048]{1,0:T(8,128)(2,1)S(1)}, u32[]{:S(2)}, u32[]{:S(2)}) collective-permute-start(bf16[104,2048]{1,0:T(8,128)(2,1)S(1)} %collective-permute-done.2.refs_0_), channel_id=1, source_target_pairs={{0,1},{1,16},{16,17},{17,32},{32,33},{33,48},{48,49},{49,0},{2,3},... | collective-permute-start | bytes 1277960 | tf_op jit(solution)/shard_map/ppermute | solution.py:36
  72.9 10.7 %collective-permute-start.7 = (bf16[104,2048]{1,0:T(8,128)(2,1)S(1)}, bf16[104,2048]{1,0:T(8,128)(2,1)S(1)}, u32[]{:S(2)}, u32[]{:S(2)}) collective-permute-start(bf16[104,2048]{1,0:T(8,128)(2,1)S(1)} %collective-permute-done.3.refs_1_), channel_id=1, source_target_pairs={{0,49},{1,0},{16,1},{17,16},{32,17},{33,32},{48,33},{49,48},{2,51}... | collective-permute-start | bytes 1277960 | tf_op jit(solution)/shard_map/ppermute | solution.py:36
  84.8 32.4 %all-to-all-start.2 = ((bf16[8,32,2048]{2,1,0:T(8,128)(2,1)}), bf16[8,32,2048]{2,1,0:T(8,128)(2,1)S(1)}, u32[]{:S(2)}, u32[]{:S(2)}) async-start(bf16[8,32,2048]{2,1,0:T(8,128)(2,1)} %bitcast.37), calls=%async_computation.2 | async-start | bytes 2097152 | tf_op jit(solution)/shard_map/all_to_all | solution.py:52
  89.6 14.0 %collective-permute-start.8 = (bf16[104,2048]{1,0:T(8,128)(2,1)S(1)}, bf16[104,2048]{1,0:T(8,128)(2,1)S(1)}, u32[]{:S(2)}, u32[]{:S(2)}) collective-permute-start(bf16[104,2048]{1,0:T(8,128)(2,1)S(1)} %collective-permute-done.6.refs_0_), channel_id=1, source_target_pairs={{0,1},{1,16},{16,17},{17,32},{32,33},{33,48},{48,49},{49,0},{2,3},... | collective-permute-start | bytes 1277960 | tf_op jit(solution)/shard_map/ppermute | solution.py:36
  89.6 26.9 %collective-permute-start.9 = (bf16[96,1536]{1,0:T(8,128)(2,1)}, bf16[96,1536]{1,0:T(8,128)(2,1)S(1)}, u32[]{:S(2)}, u32[]{:S(2)}) collective-permute-start(bf16[96,1536]{1,0:T(8,128)(2,1)} %copy-done.34), channel_id=1, source_target_pairs={{0,16},{16,32},{32,48},{48,0},{1,17},{17,33},{33,49},{49,1},{2,18}... | collective-permute-start | bytes 884744 | tf_op jit(solution)/shard_map/ppermute | solution.py:36
  118.2 34.7 %all-to-all-start.3 = ((bf16[8,48,2048]{2,1,0:T(8,128)(2,1)}), bf16[8,48,2048]{2,1,0:T(8,128)(2,1)S(1)}, u32[]{:S(2)}, u32[]{:S(2)}) async-start(bf16[8,48,2048]{2,1,0:T(8,128)(2,1)} %bitcast.14), calls=%async_computation.3 | async-start | bytes 3145728 | tf_op jit(solution)/shard_map/all_to_all | solution.py:52
  123.7 18.4 %collective-permute-start.10 = (bf16[96,1536]{1,0:T(8,128)(2,1)S(1)}, bf16[96,1536]{1,0:T(8,128)(2,1)S(1)}, u32[]{:S(2)}, u32[]{:S(2)}) collective-permute-start(bf16[96,1536]{1,0:T(8,128)(2,1)S(1)} %copy-done.33), channel_id=1, source_target_pairs={{0,32},{16,48},{32,0},{48,16},{1,33},{17,49},{33,1},{49,17},{2,34}... | collective-permute-start | bytes 884744 | tf_op jit(solution)/shard_map/ppermute | solution.py:36
  126.1 26.1 %collective-permute-start.11 = (bf16[96,1536]{1,0:T(8,128)(2,1)S(1)}, bf16[96,1536]{1,0:T(8,128)(2,1)S(1)}, u32[]{:S(2)}, u32[]{:S(2)}) collective-permute-start(bf16[96,1536]{1,0:T(8,128)(2,1)S(1)} %copy-done.31), channel_id=1, source_target_pairs={{0,48},{16,0},{32,16},{48,32},{1,49},{17,1},{33,17},{49,33},{2,50}... | collective-permute-start | bytes 884744 | tf_op jit(solution)/shard_map/ppermute | solution.py:36
  152.9 19.4 %all-to-all-start.4 = ((bf16[4,96,1536]{2,1,0:T(8,128)(2,1)}), bf16[4,96,1536]{2,1,0:T(8,128)(2,1)S(1)}, u32[]{:S(2)}, u32[]{:S(2)}) async-start(bf16[4,96,1536]{2,1,0:T(8,128)(2,1)} %gather_fusion.1), calls=%async_computation.4 | async-start | bytes 2359296 | tf_op jit(solution)/shard_map/all_to_all | solution.py:52
  172.3 36.5 %all-to-all-start.5 = ((bf16[8,48,2048]{2,1,0:T(8,128)(2,1)}), bf16[8,48,2048]{2,1,0:T(8,128)(2,1)S(1)}, u32[]{:S(2)}, u32[]{:S(2)}) async-start(bf16[8,48,2048]{2,1,0:T(8,128)(2,1)} %bitcast.39), calls=%async_computation.5 | async-start | bytes 3145728 | tf_op jit(solution)/shard_map/all_to_all | solution.py:52
  182.3 19.4 %collective-permute-start.12 = (bf16[96,1536]{1,0:T(8,128)(2,1)S(1)}, bf16[96,1536]{1,0:T(8,128)(2,1)S(1)}, u32[]{:S(2)}, u32[]{:S(2)}) collective-permute-start(bf16[96,1536]{1,0:T(8,128)(2,1)S(1)} %get-tuple-element.132), channel_id=1, source_target_pairs={{0,16},{16,32},{32,48},{48,0},{1,17},{17,33},{33,49},{49,1},{2,18}... | collective-permute-start | bytes 884744 | tf_op jit(solution)/shard_map/ppermute | solution.py:36
  183.0 21.6 %collective-permute-start.13 = (bf16[96,1536]{1,0:T(8,128)(2,1)S(1)}, bf16[96,1536]{1,0:T(8,128)(2,1)S(1)}, u32[]{:S(2)}, u32[]{:S(2)}) collective-permute-start(bf16[96,1536]{1,0:T(8,128)(2,1)S(1)} %get-tuple-element.133), channel_id=1, source_target_pairs={{0,32},{16,48},{32,0},{48,16},{1,33},{17,49},{33,1},{49,17},{2,34}... | collective-permute-start | bytes 884744 | tf_op jit(solution)/shard_map/ppermute | solution.py:36
  185.6 22.5 %collective-permute-start.14 = (bf16[96,1536]{1,0:T(8,128)(2,1)S(1)}, bf16[96,1536]{1,0:T(8,128)(2,1)S(1)}, u32[]{:S(2)}, u32[]{:S(2)}) collective-permute-start(bf16[96,1536]{1,0:T(8,128)(2,1)S(1)} %get-tuple-element.134), channel_id=1, source_target_pairs={{0,48},{16,0},{32,16},{48,32},{1,49},{17,1},{33,17},{49,33},{2,50}... | collective-permute-start | bytes 884744 | tf_op jit(solution)/shard_map/ppermute | solution.py:36
  208.8 19.4 %all-to-all-start.6 = ((bf16[8,32,2048]{2,1,0:T(8,128)(2,1)}), bf16[8,32,2048]{2,1,0:T(8,128)(2,1)}, u32[]{:S(2)}, u32[]{:S(2)}) async-start(bf16[8,32,2048]{2,1,0:T(8,128)(2,1)} %bitcast.40), calls=%async_computation.6 | async-start | bytes 2097152 | tf_op jit(solution)/shard_map/all_to_all | solution.py:52
  215.7 12.5 %collective-permute-start.17 = (bf16[96,2048]{1,0:T(8,128)(2,1)S(1)}, bf16[96,2048]{1,0:T(8,128)(2,1)}, u32[]{:S(2)}, u32[]{:S(2)}) collective-permute-start(bf16[96,2048]{1,0:T(8,128)(2,1)S(1)} %get-tuple-element.141), channel_id=1, source_target_pairs={{0,1},{1,16},{16,17},{17,32},{32,33},{33,48},{48,49},{49,0},{2,3},... | collective-permute-start | bytes 1179656 | tf_op jit(solution)/shard_map/ppermute | solution.py:36
  215.7 17.5 %collective-permute-start.15 = (bf16[96,2048]{1,0:T(8,128)(2,1)}, bf16[96,2048]{1,0:T(8,128)(2,1)}, u32[]{:S(2)}, u32[]{:S(2)}) collective-permute-start(bf16[96,2048]{1,0:T(8,128)(2,1)} %get-tuple-element.136), channel_id=1, source_target_pairs={{0,49},{1,0},{16,1},{17,16},{32,17},{33,32},{48,33},{49,48},{2,51}... | collective-permute-start | bytes 1179656 | tf_op jit(solution)/shard_map/ppermute | solution.py:36
  228.2 24.5 %all-to-all-start.7 = ((bf16[8,48,2048]{2,1,0:T(8,128)(2,1)}), bf16[8,48,2048]{2,1,0:T(8,128)(2,1)S(1)}, u32[]{:S(2)}, u32[]{:S(2)}) async-start(bf16[8,48,2048]{2,1,0:T(8,128)(2,1)} %bitcast.38), calls=%async_computation.7 | async-start | bytes 3145728 | tf_op jit(solution)/shard_map/all_to_all | solution.py:52
  234.3 11.2 %collective-permute-start.16 = (bf16[96,2048]{1,0:T(8,128)(2,1)S(1)}, bf16[96,2048]{1,0:T(8,128)(2,1)S(1)}, u32[]{:S(2)}, u32[]{:S(2)}) collective-permute-start(bf16[96,2048]{1,0:T(8,128)(2,1)S(1)} %add_convert_fusion.5), channel_id=1, source_target_pairs={{0,49},{1,0},{16,1},{17,16},{32,17},{33,32},{48,33},{49,48},{2,51}... | collective-permute-start | bytes 1179656 | tf_op jit(solution)/shard_map/ppermute | solution.py:36
  237.8 16.2 %collective-permute-start.20 = (bf16[96,2048]{1,0:T(8,128)(2,1)}, bf16[96,2048]{1,0:T(8,128)(2,1)}, u32[]{:S(2)}, u32[]{:S(2)}) collective-permute-start(bf16[96,2048]{1,0:T(8,128)(2,1)} %add_convert_fusion.2), channel_id=1, source_target_pairs={{0,1},{1,16},{16,17},{17,32},{32,33},{33,48},{48,49},{49,0},{2,3},... | collective-permute-start | bytes 1179656 | tf_op jit(solution)/shard_map/ppermute | solution.py:36
  246.4 10.8 %collective-permute-start.18 = (bf16[96,2048]{1,0:T(8,128)(2,1)}, bf16[96,2048]{1,0:T(8,128)(2,1)}, u32[]{:S(2)}, u32[]{:S(2)}) collective-permute-start(bf16[96,2048]{1,0:T(8,128)(2,1)} %add_convert_fusion.4), channel_id=1, source_target_pairs={{0,49},{1,0},{16,1},{17,16},{32,17},{33,32},{48,33},{49,48},{2,51}... | collective-permute-start | bytes 1179656 | tf_op jit(solution)/shard_map/ppermute | solution.py:36
  255.9 12.2 %collective-permute-start.21 = (bf16[96,2048]{1,0:T(8,128)(2,1)}, bf16[96,2048]{1,0:T(8,128)(2,1)}, u32[]{:S(2)}, u32[]{:S(2)}) collective-permute-start(bf16[96,2048]{1,0:T(8,128)(2,1)} %add_convert_fusion.1), channel_id=1, source_target_pairs={{0,1},{1,16},{16,17},{17,32},{32,33},{33,48},{48,49},{49,0},{2,3},... | collective-permute-start | bytes 1179656 | tf_op jit(solution)/shard_map/ppermute | solution.py:36
  259.0 10.5 %collective-permute-start.19 = (bf16[96,2048]{1,0:T(8,128)(2,1)}, bf16[96,2048]{1,0:T(8,128)(2,1)}, u32[]{:S(2)}, u32[]{:S(2)}) collective-permute-start(bf16[96,2048]{1,0:T(8,128)(2,1)} %add_convert_fusion.3), channel_id=1, source_target_pairs={{0,49},{1,0},{16,1},{17,16},{32,17},{33,32},{48,33},{49,48},{2,51}... | collective-permute-start | bytes 1179656 | tf_op jit(solution)/shard_map/ppermute | solution.py:36
  (36 other events, 87.1 us)
Sparse Core Ops, SparseCore 0:
  12.9 57.0 all-gather.4
  83.8 52.8 all-gather.6

commit v10 on v6

--- a/solution.py
+++ b/solution.py
@@ -391,30 +391,29 @@
     d2, w2 = dispatch(place, (p3, m3, far))
     d2, r1 = fence(d2, r1)
     r2 = in_plane(d2)
-    r0, r1, r2, first, hx, *held = fence(r0, r1, r2, first, hx, *held)
     x_turn = jnp.arange(NX, dtype=jnp.int32)
     x_from = jnp.take(pair_list, (x_turn * NZH + zh_me) * NC + c_me, mode="clip") >> 3
-    hx = across(jnp.take(hx, x_from, axis=0, mode="clip"), "x").reshape(PACK, SIDE)
-
+    hx = jnp.take(hx, x_from, axis=0, mode="clip")
     turn = (zh_me + jnp.arange(NZH, dtype=jnp.int32)) & (NZH - 1)
     matched = jnp.take(pair_list, (x_me * NZH + turn) * NC + c_me, mode="clip")
-    chosen = (zh_me - (matched >> 1)) & (NZH - 1)
-    picked = call(
-        pick_kernel, [shape(PIECE, SIDE)] * NZH, [SMEM] + [HBM] * NZH, [HBM] * NZH, "pick",
-        scratch=[pltpu.SemaphoreType.DMA((NZH,))],
-    )(chosen.astype(jnp.int32), *held)
-    held = [picked[0]] + [shift(picked[k], "zh", NZH, k) for k in range(1, NZH)]
-
+    chosen = ((zh_me - (matched >> 1)) & (NZH - 1)).astype(jnp.int32)
+    r0, r1, r2, first, hx, chosen, *held = fence(r0, r1, r2, first, hx, chosen, *held)
+    hx = across(hx, "x").reshape(PACK, SIDE)
     (s2,) = ffn(place, own_full, swap_full, (r2,), 384)
     s2, r1, r0, hx, *held = fence(s2, r1, r0, hx, *held)
     b2 = in_plane(s2)
     s1, s0 = ffn(place, own_full, swap_full, (r1, r0), 320)
-    b2, s1, s0 = fence(b2, s1, s0)
+    picked = call(
+        pick_kernel, [shape(PIECE, SIDE)] * NZH, [SMEM] + [HBM] * NZH, [HBM] * NZH, "pick",
+        scratch=[pltpu.SemaphoreType.DMA((NZH,))],
+    )(chosen, *held)
+    held = [picked[0]] + [shift(picked[k], "zh", NZH, k) for k in range(1, NZH)]
+    b2, s1, s0, *held = fence(b2, s1, s0, *held)
     c_m3, c_p3, c_4 = combine(w2, b2, (F32, BF, BF))
     down, rise = along_z(c_4, -1), along_z(c_p3, 1)
     b1 = in_plane(s1)
     down = along_z(joined(down, c_m3), -1)
-    b1, s0, rise, *held = fence(b1, s0, rise, *held)
+    b1, s0, rise = fence(b1, s0, rise)
     b0 = in_plane(s0)
     c_m2, c_p2 = combine(w1, b1, (F32, F32))
     down = along_z(joined(down, c_m2), -1)

time: 282 us -> 283 us (level)
  waiting for transfers between devices: 117 us -> 107 us
  Pallas kernels: 42.7 us -> 50.8 us
  local copies, waits for them, and re-layouts: 18.8 us -> 22 us
    ppermute x20, waiting for transfers between devices: 109 us -> 98.4 us  [shift(): lax.ppermute(value, axes, [(i, (i + step) % count) for i in range(count)])]
    pallas_call x1, Pallas kernels: 1.82 us -> 10.6 us  [body(): call(cut_kernel, [shape(PIECE, SIDE)] * NZH, [SMEM, HBM], [HBM] * NZH, 'c...]
    unnamed x50 -> x54, local copies, waits for them, and re-layouts: 14.5 us -> 17.8 us
  transfers between devices with their start and end apart: 32 -> 32, of which waited for: 17 -> 16; matrix products, arithmetic and copies ran while one was open for 4% -> 4% of each run, Pallas kernels for 14% -> 17%
where the time goes in v10:
time: 283 us; the launch traced here: 280 us
  waiting for transfers between devices  107 us (38%)
  starting transfers between devices  75.7 us (27%)
  Pallas kernels  50.8 us (18%)
  local copies, waits for them, and re-layouts  22 us (8%)
  between operations  14.3 us (5%)
  other arithmetic  10.2 us (4%)
    ppermute x20, waiting for transfers between devices, shift(): lax.ppermute(value, axes, [(i, (i + step) % count) for i in range(count)])  98.4 us
    all_to_all x8, starting transfers between devices, across(): return lax.all_to_all(value, axis, split_axis=0, concat_axis=0, tiled=True)  39.3 us
    ppermute x20, starting transfers between devices, shift(): lax.ppermute(value, axes, [(i, (i + step) % count) for i in range(count)])  36.2 us
    pallas_call x2, Pallas kernels, ffn(): call(functools.partial(ffn_kernel, splits, block), [pltpu.HBM((r, WIDTH),...  22.5 us
    unnamed x54, local copies, waits for them, and re-layouts  17.8 us
    pallas_call x1, Pallas kernels, body(): call(cut_kernel, [shape(PIECE, SIDE)] * NZH, [SMEM, HBM], [HBM] * NZH, 'c...  10.6 us
    all_to_all x8, waiting for transfers between devices, across(): return lax.all_to_all(value, axis, split_axis=0, concat_axis=0, tiled=True)  9.02 us
    convert_element_type x5, other arithmetic, joined(): return (got.astype(F32) + mine).astype(BF)  7.39 us
  transfers between devices with their start and end apart: 32, of which 16 were waited for; matrix products, arithmetic and copies ran while one was open for 4% of the time, Pallas kernels for 17%

profile of v10, /device:TPU:22, one launch (start us, length us, event | category | flops | bytes accessed | tf_op | source)
XLA Modules:
  0.0 280.4 jit_solution(4265859598331543003)
XLA Ops:
  7.3 4.4 %prep.1 = (bf16[104,2048]{1,0:T(8,128)(2,1)S(1)}, bf16[384,1536]{1,0:T(8,128)(2,1)}, bf16[384,1536]{1,0:T(8,128)(2,1)S(1)}, bf16[384,1536]{1,0:T(8,128)(2,1)}) custom-call(s32[4]{0:T(128)S(1)} %pad_add_fusion.place_ref, bf16[96,2048]{1,0:T(8,128)(2,1)} %tokens_ref.1, f32[1,2048]{1,0:T(1,128)} %bitcast.41, s32[8,96]{1,0:T(8,128)} %bitcast.42, ...), custom_call_target="tpu_custom_call" | custom-call | tf_op jit(solution)/shard_map/prep/pallas_call | solution.py:343
  12.9 4.8 %all-to-all-start = ((bf16[4,96,1536]{2,1,0:T(8,128)(2,1)}), bf16[4,96,1536]{2,1,0:T(8,128)(2,1)}, u32[]{:S(2)}, u32[]{:S(2)}) async-start(bf16[4,96,1536]{2,1,0:T(8,128)(2,1)} %bitcast.7), calls=%async_computation | async-start | bytes 2359296 | tf_op jit(solution)/shard_map/all_to_all | solution.py:52
  17.7 5.9 %collective-permute-start.1 = (bf16[104,2048]{1,0:T(8,128)(2,1)S(1)}, bf16[104,2048]{1,0:T(8,128)(2,1)S(1)}, u32[]{:S(2)}, u32[]{:S(2)}) collective-permute-start(bf16[104,2048]{1,0:T(8,128)(2,1)S(1)} %get-tuple-element.81.refs_0_), channel_id=1, source_target_pairs={{0,49},{1,0},{16,1},{17,16},{32,17},{33,32},{48,33},{49,48},{2,51}... | collective-permute-start | bytes 1277960 | tf_op jit(solution)/shard_map/ppermute | solution.py:36
  23.6 9.4 %collective-permute-done.1.refs_2_ = bf16[104,2048]{1,0:T(8,128)(2,1)S(1)} collective-permute-done((bf16[104,2048]{1,0:T(8,128)(2,1)S(1)}, bf16[104,2048]{1,0:T(8,128)(2,1)S(1)}, u32[]{:S(2)}, u32[]{:S(2)}) %collective-permute-start.1) | collective-permute-done | bytes 426016 | tf_op jit(solution)/shard_map/ppermute | solution.py:36
  33.0 3.4 %collective-permute-done.refs_1_ = bf16[104,2048]{1,0:T(8,128)(2,1)S(1)} collective-permute-done((bf16[104,2048]{1,0:T(8,128)(2,1)S(1)}, bf16[104,2048]{1,0:T(8,128)(2,1)S(1)}, u32[]{:S(2)}, u32[]{:S(2)}) %collective-permute-start) | collective-permute-done | bytes 426016 | tf_op jit(solution)/shard_map/ppermute | solution.py:36
  40.8 4.8 %all-to-all-start.1 = ((bf16[8,48,2048]{2,1,0:T(8,128)(2,1)}), bf16[8,48,2048]{2,1,0:T(8,128)(2,1)S(1)}, u32[]{:S(2)}, u32[]{:S(2)}) async-start(bf16[8,48,2048]{2,1,0:T(8,128)(2,1)} %bitcast.8), calls=%async_computation.1 | async-start | bytes 3145728 | tf_op jit(solution)/shard_map/all_to_all | solution.py:52
  48.8 21.6 %collective-permute-done.2.refs_0_ = bf16[104,2048]{1,0:T(8,128)(2,1)S(1)} collective-permute-done((bf16[104,2048]{1,0:T(8,128)(2,1)S(1)}, bf16[104,2048]{1,0:T(8,128)(2,1)S(1)}, u32[]{:S(2)}, u32[]{:S(2)}) %collective-permute-start.2) | collective-permute-done | bytes 426016 | tf_op jit(solution)/shard_map/ppermute | solution.py:36
  72.9 3.0 %collective-permute-start.7 = (bf16[104,2048]{1,0:T(8,128)(2,1)S(1)}, bf16[104,2048]{1,0:T(8,128)(2,1)S(1)}, u32[]{:S(2)}, u32[]{:S(2)}) collective-permute-start(bf16[104,2048]{1,0:T(8,128)(2,1)S(1)} %collective-permute-done.3.refs_1_), channel_id=1, source_target_pairs={{0,49},{1,0},{16,1},{17,16},{32,17},{33,32},{48,33},{49,48},{2,51}... | collective-permute-start | bytes 1277960 | tf_op jit(solution)/shard_map/ppermute | solution.py:36
  77.1 6.5 %collective-permute-done.6.refs_0_ = bf16[104,2048]{1,0:T(8,128)(2,1)S(1)} collective-permute-done((bf16[104,2048]{1,0:T(8,128)(2,1)S(1)}, bf16[104,2048]{1,0:T(8,128)(2,1)S(1)}, u32[]{:S(2)}, u32[]{:S(2)}) %collective-permute-start.6) | collective-permute-done | bytes 426016 | tf_op jit(solution)/shard_map/ppermute | solution.py:36
  84.8 4.8 %all-to-all-start.2 = ((bf16[8,32,2048]{2,1,0:T(8,128)(2,1)}), bf16[8,32,2048]{2,1,0:T(8,128)(2,1)S(1)}, u32[]{:S(2)}, u32[]{:S(2)}) async-start(bf16[8,32,2048]{2,1,0:T(8,128)(2,1)} %bitcast.37), calls=%async_computation.2 | async-start | bytes 2097152 | tf_op jit(solution)/shard_map/all_to_all | solution.py:52
  89.6 13.1 %collective-permute-done.8.refs_2_ = bf16[104,2048]{1,0:T(8,128)(2,1)S(1)} collective-permute-done((bf16[104,2048]{1,0:T(8,128)(2,1)S(1)}, bf16[104,2048]{1,0:T(8,128)(2,1)S(1)}, u32[]{:S(2)}, u32[]{:S(2)}) %collective-permute-start.8) | collective-permute-done | bytes 426016 | tf_op jit(solution)/shard_map/ppermute | solution.py:36
  107.0 4.8 %all-to-all-start.3 = ((bf16[8,48,2048]{2,1,0:T(8,128)(2,1)}), bf16[8,48,2048]{2,1,0:T(8,128)(2,1)S(1)}, u32[]{:S(2)}, u32[]{:S(2)}) async-start(bf16[8,48,2048]{2,1,0:T(8,128)(2,1)} %bitcast.14), calls=%async_computation.3 | async-start | bytes 3145728 | tf_op jit(solution)/shard_map/all_to_all | solution.py:52
  113.2 10.6 %cut.1 = (bf16[96,1536]{1,0:T(8,128)(2,1)S(1)}, bf16[96,1536]{1,0:T(8,128)(2,1)}, bf16[96,1536]{1,0:T(8,128)(2,1)S(1)}, bf16[96,1536]{1,0:T(8,128)(2,1)S(1)}) custom-call(s32[4]{0:T(128)S(1)} %pad_add_fusion.place_ref, bf16[384,1536]{1,0:T(8,128)(2,1)} %get-tuple-element.148.first_ref.refs_0_), custom_call_target="tpu_custom_call" | custom-call | tf_op jit(solution)/shard_map/cut/pallas_call | solution.py:386
  123.9 3.1 %collective-permute-start.10 = (bf16[96,1536]{1,0:T(8,128)(2,1)S(1)}, bf16[96,1536]{1,0:T(8,128)(2,1)S(1)}, u32[]{:S(2)}, u32[]{:S(2)}) collective-permute-start(bf16[96,1536]{1,0:T(8,128)(2,1)S(1)} %get-tuple-element.108), channel_id=1, source_target_pairs={{0,32},{16,48},{32,0},{48,16},{1,33},{17,49},{33,1},{49,17},{2,34}... | collective-permute-start | bytes 884744 | tf_op jit(solution)/shard_map/ppermute | solution.py:36
  126.9 3.4 %collective-permute-start.11 = (bf16[96,1536]{1,0:T(8,128)(2,1)S(1)}, bf16[96,1536]{1,0:T(8,128)(2,1)S(1)}, u32[]{:S(2)}, u32[]{:S(2)}) collective-permute-start(bf16[96,1536]{1,0:T(8,128)(2,1)S(1)} %get-tuple-element.109), channel_id=1, source_target_pairs={{0,48},{16,0},{32,16},{48,32},{1,49},{17,1},{33,17},{49,33},{2,50}... | collective-permute-start | bytes 884744 | tf_op jit(solution)/shard_map/ppermute | solution.py:36
  130.4 2.9 %gather_fusion.1 = bf16[4,96,1536]{2,1,0:T(8,128)(2,1)} fusion(bf16[4,96,1536]{2,1,0:T(8,128)(2,1)} %all-to-all-done, s32[1024]{0:T(1024)S(1)} %pad_clamp_fusion.1), kind=kCustom, calls=%fused_computation.1 | custom fusion | bytes 2359312 | tf_op jit(solution)/shard_map/jit(_take)/gather | solution.py:396
  133.3 14.7 %collective-permute-done.9.refs_1_ = bf16[96,1536]{1,0:T(8,128)(2,1)S(1)} collective-permute-done((bf16[96,1536]{1,0:T(8,128)(2,1)}, bf16[96,1536]{1,0:T(8,128)(2,1)S(1)}, u32[]{:S(2)}, u32[]{:S(2)}) %collective-permute-start.9) | collective-permute-done | bytes 294944 | tf_op jit(solution)/shard_map/ppermute | solution.py:36
  148.7 6.3 %collective-permute-done.11.refs_3_ = bf16[96,1536]{1,0:T(8,128)(2,1)S(1)} collective-permute-done((bf16[96,1536]{1,0:T(8,128)(2,1)S(1)}, bf16[96,1536]{1,0:T(8,128)(2,1)S(1)}, u32[]{:S(2)}, u32[]{:S(2)}) %collective-permute-start.11) | collective-permute-done | bytes 294944 | tf_op jit(solution)/shard_map/ppermute | solution.py:36
  155.7 4.8 %all-to-all-start.4 = ((bf16[4,96,1536]{2,1,0:T(8,128)(2,1)}), bf16[4,96,1536]{2,1,0:T(8,128)(2,1)S(1)}, u32[]{:S(2)}, u32[]{:S(2)}) async-start(bf16[4,96,1536]{2,1,0:T(8,128)(2,1)} %gather_fusion.1), calls=%async_computation.4 | async-start | bytes 2359296 | tf_op jit(solution)/shard_map/all_to_all | solution.py:52
  160.5 9.7 %expert_ffn.2 = bf16[384,2048]{1,0:T(8,128)(2,1)} custom-call(s32[4]{0:T(128)S(1)} %pad_add_fusion.place_ref, bf16[4,384,1536]{2,1,0:T(8,128)(2,1)} %bitcast.44, bf16[4,384,1536]{2,1,0:T(8,128)(2,1)} %bitcast.46, bf16[384,2048]{1,0:T(8,128)(2,1)S(1)} %bitcast.35), custom_call_target="tpu_custom_call" | custom-call | flops 3623878656 | bytes 15728640 | tf_op jit(solution)/shard_map/expert_ffn/pallas_call | solution.py:274
  170.3 4.9 %all-to-all-done.4 = bf16[4,96,1536]{2,1,0:T(8,128)(2,1)S(1)} async-done(((bf16[4,96,1536]{2,1,0:T(8,128)(2,1)}), bf16[4,96,1536]{2,1,0:T(8,128)(2,1)S(1)}, u32[]{:S(2)}, u32[]{:S(2)}) %all-to-all-start.4) | async-done | bytes 1179680 | tf_op jit(solution)/shard_map/all_to_all | solution.py:52
  175.1 5.6 %all-to-all-start.5 = ((bf16[8,48,2048]{2,1,0:T(8,128)(2,1)}), bf16[8,48,2048]{2,1,0:T(8,128)(2,1)S(1)}, u32[]{:S(2)}, u32[]{:S(2)}) async-start(bf16[8,48,2048]{2,1,0:T(8,128)(2,1)} %bitcast.39), calls=%async_computation.5 | async-start | bytes 3145728 | tf_op jit(solution)/shard_map/all_to_all | solution.py:52
  186.7 3.5 %collective-permute-start.13 = (bf16[96,1536]{1,0:T(8,128)(2,1)S(1)}, bf16[96,1536]{1,0:T(8,128)(2,1)S(1)}, u32[]{:S(2)}, u32[]{:S(2)}) collective-permute-start(bf16[96,1536]{1,0:T(8,128)(2,1)S(1)} %get-tuple-element.130), channel_id=1, source_target_pairs={{0,32},{16,48},{32,0},{48,16},{1,33},{17,49},{33,1},{49,17},{2,34}... | collective-permute-start | bytes 884744 | tf_op jit(solution)/shard_map/ppermute | solution.py:36
  192.2 12.7 %expert_ffn.3 = (bf16[256,2048]{1,0:T(8,128)(2,1)}, bf16[384,2048]{1,0:T(8,128)(2,1)}) custom-call(s32[4]{0:T(128)S(1)} %pad_add_fusion.place_ref, bf16[4,384,1536]{2,1,0:T(8,128)(2,1)} %bitcast.45, bf16[4,384,1536]{2,1,0:T(8,128)(2,1)} %bitcast.47, bf16[256,2048]{1,0:T(8,128)(2,1)S(1)} %bitcast.36, bf16[384,2048]{1,0:T(8,128)(2,1)S(1)} %bitcast.34), custom_call_target="tpu_custom_call" | custom-call | flops 6039797760 | bytes 15728640 | tf_op jit(solution)/shard_map/expert_ffn/pallas_call | solution.py:274
  207.1 3.0 %collective-permute-done.14.refs_6_ = bf16[96,1536]{1,0:T(8,128)(2,1)S(1)} collective-permute-done((bf16[96,1536]{1,0:T(8,128)(2,1)S(1)}, bf16[96,1536]{1,0:T(8,128)(2,1)S(1)}, u32[]{:S(2)}, u32[]{:S(2)}) %collective-permute-start.14) | collective-permute-done | bytes 294944 | tf_op jit(solution)/shard_map/ppermute | solution.py:36
  210.8 4.8 %all-to-all-start.6 = ((bf16[8,32,2048]{2,1,0:T(8,128)(2,1)}), bf16[8,32,2048]{2,1,0:T(8,128)(2,1)}, u32[]{:S(2)}, u32[]{:S(2)}) async-start(bf16[8,32,2048]{2,1,0:T(8,128)(2,1)} %bitcast.40), calls=%async_computation.6 | async-start | bytes 2097152 | tf_op jit(solution)/shard_map/all_to_all | solution.py:52
  217.7 3.2 %collective-permute-start.15 = (bf16[96,2048]{1,0:T(8,128)(2,1)}, bf16[96,2048]{1,0:T(8,128)(2,1)}, u32[]{:S(2)}, u32[]{:S(2)}) collective-permute-start(bf16[96,2048]{1,0:T(8,128)(2,1)} %get-tuple-element.133), channel_id=1, source_target_pairs={{0,49},{1,0},{16,1},{17,16},{32,17},{33,32},{48,33},{49,48},{2,51}... | collective-permute-start | bytes 1179656 | tf_op jit(solution)/shard_map/ppermute | solution.py:36
  220.9 9.2 %collective-permute-done.17 = bf16[96,2048]{1,0:T(8,128)(2,1)} collective-permute-done((bf16[96,2048]{1,0:T(8,128)(2,1)S(1)}, bf16[96,2048]{1,0:T(8,128)(2,1)}, u32[]{:S(2)}, u32[]{:S(2)}) %collective-permute-start.17) | collective-permute-done | bytes 393248 | tf_op jit(solution)/shard_map/ppermute | solution.py:36
  230.2 5.0 %all-to-all-start.7 = ((bf16[8,48,2048]{2,1,0:T(8,128)(2,1)}), bf16[8,48,2048]{2,1,0:T(8,128)(2,1)S(1)}, u32[]{:S(2)}, u32[]{:S(2)}) async-start(bf16[8,48,2048]{2,1,0:T(8,128)(2,1)} %bitcast.38), calls=%async_computation.7 | async-start | bytes 3145728 | tf_op jit(solution)/shard_map/all_to_all | solution.py:52
  241.8 5.7 %collective-permute-done.16 = bf16[96,2048]{1,0:T(8,128)(2,1)S(1)} collective-permute-done((bf16[96,2048]{1,0:T(8,128)(2,1)S(1)}, bf16[96,2048]{1,0:T(8,128)(2,1)S(1)}, u32[]{:S(2)}, u32[]{:S(2)}) %collective-permute-start.16) | collective-permute-done | bytes 393248 | tf_op jit(solution)/shard_map/ppermute | solution.py:36
  250.5 4.1 %all-to-all-done.7 = bf16[8,48,2048]{2,1,0:T(8,128)(2,1)S(1)} async-done(((bf16[8,48,2048]{2,1,0:T(8,128)(2,1)}), bf16[8,48,2048]{2,1,0:T(8,128)(2,1)S(1)}, u32[]{:S(2)}, u32[]{:S(2)}) %all-to-all-start.7) | async-done | bytes 1572896 | tf_op jit(solution)/shard_map/all_to_all | solution.py:52
  261.0 3.3 %collective-permute-start.19 = (bf16[96,2048]{1,0:T(8,128)(2,1)}, bf16[96,2048]{1,0:T(8,128)(2,1)}, u32[]{:S(2)}, u32[]{:S(2)}) collective-permute-start(bf16[96,2048]{1,0:T(8,128)(2,1)} %add_convert_fusion.3), channel_id=1, source_target_pairs={{0,49},{1,0},{16,1},{17,16},{32,17},{33,32},{48,33},{49,48},{2,51}... | collective-permute-start | bytes 1179656 | tf_op jit(solution)/shard_map/ppermute | solution.py:36
  (117 shorter events, 59.0 us)
Async XLA Ops:
  7.2 153.4 %all-gather.5.cloned.1.call-start = ((), (), s32[]{:S(2)}) async-start(), calls=%async_computation.8 | async-start | bytes 5898240 | tf_op jit(solution)/shard_map/all_gather | solution.py:367
  12.8 26.9 %collective-permute-start.5 = (bf16[384,1536]{1,0:T(8,128)(2,1)}, bf16[384,1536]{1,0:T(8,128)(2,1)S(1)}, u32[]{:S(2)}, u32[]{:S(2)}) collective-permute-start(bf16[384,1536]{1,0:T(8,128)(2,1)} %get-tuple-element.148.first_ref.refs_0_), channel_id=1, source_target_pairs={{0,8},{8,0},{1,9},{9,1},{2,10},{10,2},{3,11},{11,3},{4,12},{12,4},... | collective-permute-start | bytes 3538952 | tf_op jit(solution)/shard_map/ppermute | solution.py:329
  12.9 26.8 %all-to-all-start = ((bf16[4,96,1536]{2,1,0:T(8,128)(2,1)}), bf16[4,96,1536]{2,1,0:T(8,128)(2,1)}, u32[]{:S(2)}, u32[]{:S(2)}) async-start(bf16[4,96,1536]{2,1,0:T(8,128)(2,1)} %bitcast.7), calls=%async_computation | async-start | bytes 2359296 | tf_op jit(solution)/shard_map/all_to_all | solution.py:52
  17.7 15.3 %collective-permute-start.1 = (bf16[104,2048]{1,0:T(8,128)(2,1)S(1)}, bf16[104,2048]{1,0:T(8,128)(2,1)S(1)}, u32[]{:S(2)}, u32[]{:S(2)}) collective-permute-start(bf16[104,2048]{1,0:T(8,128)(2,1)S(1)} %get-tuple-element.81.refs_0_), channel_id=1, source_target_pairs={{0,49},{1,0},{16,1},{17,16},{32,17},{33,32},{48,33},{49,48},{2,51}... | collective-permute-start | bytes 1277960 | tf_op jit(solution)/shard_map/ppermute | solution.py:36
  23.6 12.8 %collective-permute-start = (bf16[104,2048]{1,0:T(8,128)(2,1)S(1)}, bf16[104,2048]{1,0:T(8,128)(2,1)S(1)}, u32[]{:S(2)}, u32[]{:S(2)}) collective-permute-start(bf16[104,2048]{1,0:T(8,128)(2,1)S(1)} %get-tuple-element.81.refs_0_), channel_id=1, source_target_pairs={{0,1},{1,16},{16,17},{17,32},{32,33},{33,48},{48,49},{49,0},{2,3},... | collective-permute-start | bytes 1277960 | tf_op jit(solution)/shard_map/ppermute | solution.py:36
  36.4 36.2 %collective-permute-start.4 = (bf16[384,1536]{1,0:T(8,128)(2,1)}, bf16[384,1536]{1,0:T(8,128)(2,1)}, u32[]{:S(2)}, u32[]{:S(2)}) collective-permute-start(bf16[384,1536]{1,0:T(8,128)(2,1)} %copy-done.25), channel_id=1, source_target_pairs={{0,1},{1,0},{2,3},{3,2},{4,5},{5,4},{6,7},{7,6},{8,9},{9,8},{10,11... | collective-permute-start | bytes 3538952 | tf_op jit(solution)/shard_map/ppermute | solution.py:329
  40.8 42.9 %all-to-all-start.1 = ((bf16[8,48,2048]{2,1,0:T(8,128)(2,1)}), bf16[8,48,2048]{2,1,0:T(8,128)(2,1)S(1)}, u32[]{:S(2)}, u32[]{:S(2)}) async-start(bf16[8,48,2048]{2,1,0:T(8,128)(2,1)} %bitcast.8), calls=%async_computation.1 | async-start | bytes 3145728 | tf_op jit(solution)/shard_map/all_to_all | solution.py:52
  45.6 115.0 %all-gather.7.cloned.1.call-start = ((), (), s32[]{:S(2)}) async-start(), calls=%async_computation.9 | async-start | bytes 5898240 | tf_op jit(solution)/shard_map/all_gather | solution.py:382
  45.6 24.8 %collective-permute-start.2 = (bf16[104,2048]{1,0:T(8,128)(2,1)S(1)}, bf16[104,2048]{1,0:T(8,128)(2,1)S(1)}, u32[]{:S(2)}, u32[]{:S(2)}) collective-permute-start(bf16[104,2048]{1,0:T(8,128)(2,1)S(1)} %collective-permute-done.refs_1_), channel_id=1, source_target_pairs={{0,1},{1,16},{16,17},{17,32},{32,33},{33,48},{48,49},{49,0},{2,3},... | collective-permute-start | bytes 1277960 | tf_op jit(solution)/shard_map/ppermute | solution.py:36
  47.6 25.0 %collective-permute-start.3 = (bf16[104,2048]{1,0:T(8,128)(2,1)S(1)}, bf16[104,2048]{1,0:T(8,128)(2,1)S(1)}, u32[]{:S(2)}, u32[]{:S(2)}) collective-permute-start(bf16[104,2048]{1,0:T(8,128)(2,1)S(1)} %collective-permute-done.1.refs_2_), channel_id=1, source_target_pairs={{0,49},{1,0},{16,1},{17,16},{32,17},{33,32},{48,33},{49,48},{2,51}... | collective-permute-start | bytes 1277960 | tf_op jit(solution)/shard_map/ppermute | solution.py:36
  72.6 11.0 %collective-permute-start.6 = (bf16[104,2048]{1,0:T(8,128)(2,1)S(1)}, bf16[104,2048]{1,0:T(8,128)(2,1)S(1)}, u32[]{:S(2)}, u32[]{:S(2)}) collective-permute-start(bf16[104,2048]{1,0:T(8,128)(2,1)S(1)} %collective-permute-done.2.refs_0_), channel_id=1, source_target_pairs={{0,1},{1,16},{16,17},{17,32},{32,33},{33,48},{48,49},{49,0},{2,3},... | collective-permute-start | bytes 1277960 | tf_op jit(solution)/shard_map/ppermute | solution.py:36
  72.9 10.7 %collective-permute-start.7 = (bf16[104,2048]{1,0:T(8,128)(2,1)S(1)}, bf16[104,2048]{1,0:T(8,128)(2,1)S(1)}, u32[]{:S(2)}, u32[]{:S(2)}) collective-permute-start(bf16[104,2048]{1,0:T(8,128)(2,1)S(1)} %collective-permute-done.3.refs_1_), channel_id=1, source_target_pairs={{0,49},{1,0},{16,1},{17,16},{32,17},{33,32},{48,33},{49,48},{2,51}... | collective-permute-start | bytes 1277960 | tf_op jit(solution)/shard_map/ppermute | solution.py:36
  84.8 21.3 %all-to-all-start.2 = ((bf16[8,32,2048]{2,1,0:T(8,128)(2,1)}), bf16[8,32,2048]{2,1,0:T(8,128)(2,1)S(1)}, u32[]{:S(2)}, u32[]{:S(2)}) async-start(bf16[8,32,2048]{2,1,0:T(8,128)(2,1)} %bitcast.37), calls=%async_computation.2 | async-start | bytes 2097152 | tf_op jit(solution)/shard_map/all_to_all | solution.py:52
  89.6 13.1 %collective-permute-start.8 = (bf16[104,2048]{1,0:T(8,128)(2,1)S(1)}, bf16[104,2048]{1,0:T(8,128)(2,1)S(1)}, u32[]{:S(2)}, u32[]{:S(2)}) collective-permute-start(bf16[104,2048]{1,0:T(8,128)(2,1)S(1)} %collective-permute-done.6.refs_0_), channel_id=1, source_target_pairs={{0,1},{1,16},{16,17},{17,32},{32,33},{33,48},{48,49},{49,0},{2,3},... | collective-permute-start | bytes 1277960 | tf_op jit(solution)/shard_map/ppermute | solution.py:36
  107.0 48.7 %all-to-all-start.3 = ((bf16[8,48,2048]{2,1,0:T(8,128)(2,1)}), bf16[8,48,2048]{2,1,0:T(8,128)(2,1)S(1)}, u32[]{:S(2)}, u32[]{:S(2)}) async-start(bf16[8,48,2048]{2,1,0:T(8,128)(2,1)} %bitcast.14), calls=%async_computation.3 | async-start | bytes 3145728 | tf_op jit(solution)/shard_map/all_to_all | solution.py:52
  123.8 24.2 %collective-permute-start.9 = (bf16[96,1536]{1,0:T(8,128)(2,1)}, bf16[96,1536]{1,0:T(8,128)(2,1)S(1)}, u32[]{:S(2)}, u32[]{:S(2)}) collective-permute-start(bf16[96,1536]{1,0:T(8,128)(2,1)} %get-tuple-element.107), channel_id=1, source_target_pairs={{0,16},{16,32},{32,48},{48,0},{1,17},{17,33},{33,49},{49,1},{2,18}... | collective-permute-start | bytes 884744 | tf_op jit(solution)/shard_map/ppermute | solution.py:36
  123.9 24.1 %collective-permute-start.10 = (bf16[96,1536]{1,0:T(8,128)(2,1)S(1)}, bf16[96,1536]{1,0:T(8,128)(2,1)S(1)}, u32[]{:S(2)}, u32[]{:S(2)}) collective-permute-start(bf16[96,1536]{1,0:T(8,128)(2,1)S(1)} %get-tuple-element.108), channel_id=1, source_target_pairs={{0,32},{16,48},{32,0},{48,16},{1,33},{17,49},{33,1},{49,17},{2,34}... | collective-permute-start | bytes 884744 | tf_op jit(solution)/shard_map/ppermute | solution.py:36
  126.9 28.1 %collective-permute-start.11 = (bf16[96,1536]{1,0:T(8,128)(2,1)S(1)}, bf16[96,1536]{1,0:T(8,128)(2,1)S(1)}, u32[]{:S(2)}, u32[]{:S(2)}) collective-permute-start(bf16[96,1536]{1,0:T(8,128)(2,1)S(1)} %get-tuple-element.109), channel_id=1, source_target_pairs={{0,48},{16,0},{32,16},{48,32},{1,49},{17,1},{33,17},{49,33},{2,50}... | collective-permute-start | bytes 884744 | tf_op jit(solution)/shard_map/ppermute | solution.py:36
  155.7 19.4 %all-to-all-start.4 = ((bf16[4,96,1536]{2,1,0:T(8,128)(2,1)}), bf16[4,96,1536]{2,1,0:T(8,128)(2,1)S(1)}, u32[]{:S(2)}, u32[]{:S(2)}) async-start(bf16[4,96,1536]{2,1,0:T(8,128)(2,1)} %gather_fusion.1), calls=%async_computation.4 | async-start | bytes 2359296 | tf_op jit(solution)/shard_map/all_to_all | solution.py:52
  175.1 35.7 %all-to-all-start.5 = ((bf16[8,48,2048]{2,1,0:T(8,128)(2,1)}), bf16[8,48,2048]{2,1,0:T(8,128)(2,1)S(1)}, u32[]{:S(2)}, u32[]{:S(2)}) async-start(bf16[8,48,2048]{2,1,0:T(8,128)(2,1)} %bitcast.39), calls=%async_computation.5 | async-start | bytes 3145728 | tf_op jit(solution)/shard_map/all_to_all | solution.py:52
  184.3 20.6 %collective-permute-start.12 = (bf16[96,1536]{1,0:T(8,128)(2,1)S(1)}, bf16[96,1536]{1,0:T(8,128)(2,1)S(1)}, u32[]{:S(2)}, u32[]{:S(2)}) collective-permute-start(bf16[96,1536]{1,0:T(8,128)(2,1)S(1)} %get-tuple-element.129), channel_id=1, source_target_pairs={{0,16},{16,32},{32,48},{48,0},{1,17},{17,33},{33,49},{49,1},{2,18}... | collective-permute-start | bytes 884744 | tf_op jit(solution)/shard_map/ppermute | solution.py:36
  186.7 19.6 %collective-permute-start.13 = (bf16[96,1536]{1,0:T(8,128)(2,1)S(1)}, bf16[96,1536]{1,0:T(8,128)(2,1)S(1)}, u32[]{:S(2)}, u32[]{:S(2)}) collective-permute-start(bf16[96,1536]{1,0:T(8,128)(2,1)S(1)} %get-tuple-element.130), channel_id=1, source_target_pairs={{0,32},{16,48},{32,0},{48,16},{1,33},{17,49},{33,1},{49,17},{2,34}... | collective-permute-start | bytes 884744 | tf_op jit(solution)/shard_map/ppermute | solution.py:36
  190.2 19.9 %collective-permute-start.14 = (bf16[96,1536]{1,0:T(8,128)(2,1)S(1)}, bf16[96,1536]{1,0:T(8,128)(2,1)S(1)}, u32[]{:S(2)}, u32[]{:S(2)}) collective-permute-start(bf16[96,1536]{1,0:T(8,128)(2,1)S(1)} %get-tuple-element.131), channel_id=1, source_target_pairs={{0,48},{16,0},{32,16},{48,32},{1,49},{17,1},{33,17},{49,33},{2,50}... | collective-permute-start | bytes 884744 | tf_op jit(solution)/shard_map/ppermute | solution.py:36
  210.8 19.4 %all-to-all-start.6 = ((bf16[8,32,2048]{2,1,0:T(8,128)(2,1)}), bf16[8,32,2048]{2,1,0:T(8,128)(2,1)}, u32[]{:S(2)}, u32[]{:S(2)}) async-start(bf16[8,32,2048]{2,1,0:T(8,128)(2,1)} %bitcast.40), calls=%async_computation.6 | async-start | bytes 2097152 | tf_op jit(solution)/shard_map/all_to_all | solution.py:52
  217.7 12.5 %collective-permute-start.17 = (bf16[96,2048]{1,0:T(8,128)(2,1)S(1)}, bf16[96,2048]{1,0:T(8,128)(2,1)}, u32[]{:S(2)}, u32[]{:S(2)}) collective-permute-start(bf16[96,2048]{1,0:T(8,128)(2,1)S(1)} %get-tuple-element.138), channel_id=1, source_target_pairs={{0,1},{1,16},{16,17},{17,32},{32,33},{33,48},{48,49},{49,0},{2,3},... | collective-permute-start | bytes 1179656 | tf_op jit(solution)/shard_map/ppermute | solution.py:36
  217.7 17.5 %collective-permute-start.15 = (bf16[96,2048]{1,0:T(8,128)(2,1)}, bf16[96,2048]{1,0:T(8,128)(2,1)}, u32[]{:S(2)}, u32[]{:S(2)}) collective-permute-start(bf16[96,2048]{1,0:T(8,128)(2,1)} %get-tuple-element.133), channel_id=1, source_target_pairs={{0,49},{1,0},{16,1},{17,16},{32,17},{33,32},{48,33},{49,48},{2,51}... | collective-permute-start | bytes 1179656 | tf_op jit(solution)/shard_map/ppermute | solution.py:36
  230.2 24.5 %all-to-all-start.7 = ((bf16[8,48,2048]{2,1,0:T(8,128)(2,1)}), bf16[8,48,2048]{2,1,0:T(8,128)(2,1)S(1)}, u32[]{:S(2)}, u32[]{:S(2)}) async-start(bf16[8,48,2048]{2,1,0:T(8,128)(2,1)} %bitcast.38), calls=%async_computation.7 | async-start | bytes 3145728 | tf_op jit(solution)/shard_map/all_to_all | solution.py:52
  236.3 11.2 %collective-permute-start.16 = (bf16[96,2048]{1,0:T(8,128)(2,1)S(1)}, bf16[96,2048]{1,0:T(8,128)(2,1)S(1)}, u32[]{:S(2)}, u32[]{:S(2)}) collective-permute-start(bf16[96,2048]{1,0:T(8,128)(2,1)S(1)} %add_convert_fusion.5), channel_id=1, source_target_pairs={{0,49},{1,0},{16,1},{17,16},{32,17},{33,32},{48,33},{49,48},{2,51}... | collective-permute-start | bytes 1179656 | tf_op jit(solution)/shard_map/ppermute | solution.py:36
  240.8 15.3 %collective-permute-start.20 = (bf16[96,2048]{1,0:T(8,128)(2,1)}, bf16[96,2048]{1,0:T(8,128)(2,1)}, u32[]{:S(2)}, u32[]{:S(2)}) collective-permute-start(bf16[96,2048]{1,0:T(8,128)(2,1)} %add_convert_fusion.2), channel_id=1, source_target_pairs={{0,1},{1,16},{16,17},{17,32},{32,33},{33,48},{48,49},{49,0},{2,3},... | collective-permute-start | bytes 1179656 | tf_op jit(solution)/shard_map/ppermute | solution.py:36
  248.4 10.8 %collective-permute-start.18 = (bf16[96,2048]{1,0:T(8,128)(2,1)}, bf16[96,2048]{1,0:T(8,128)(2,1)}, u32[]{:S(2)}, u32[]{:S(2)}) collective-permute-start(bf16[96,2048]{1,0:T(8,128)(2,1)} %add_convert_fusion.4), channel_id=1, source_target_pairs={{0,49},{1,0},{16,1},{17,16},{32,17},{33,32},{48,33},{49,48},{2,51}... | collective-permute-start | bytes 1179656 | tf_op jit(solution)/shard_map/ppermute | solution.py:36
  257.9 12.4 %collective-permute-start.21 = (bf16[96,2048]{1,0:T(8,128)(2,1)}, bf16[96,2048]{1,0:T(8,128)(2,1)}, u32[]{:S(2)}, u32[]{:S(2)}) collective-permute-start(bf16[96,2048]{1,0:T(8,128)(2,1)} %add_convert_fusion.1), channel_id=1, source_target_pairs={{0,1},{1,16},{16,17},{17,32},{32,33},{33,48},{48,49},{49,0},{2,3},... | collective-permute-start | bytes 1179656 | tf_op jit(solution)/shard_map/ppermute | solution.py:36
  261.0 10.6 %collective-permute-start.19 = (bf16[96,2048]{1,0:T(8,128)(2,1)}, bf16[96,2048]{1,0:T(8,128)(2,1)}, u32[]{:S(2)}, u32[]{:S(2)}) collective-permute-start(bf16[96,2048]{1,0:T(8,128)(2,1)} %add_convert_fusion.3), channel_id=1, source_target_pairs={{0,49},{1,0},{16,1},{17,16},{32,17},{33,32},{48,33},{49,48},{2,51}... | collective-permute-start | bytes 1179656 | tf_op jit(solution)/shard_map/ppermute | solution.py:36
  (27 other events, 61.2 us)
Sparse Core Ops, SparseCore 0:
  12.9 57.0 all-gather.4
  83.8 52.8 all-gather.6

commit v11 on v10

--- a/solution.py
+++ b/solution.py
@@ -377,16 +377,16 @@
     r0 = in_plane(d0)
     p2, m2, swapped = fence(p2, m2, swapped)
     p3, m3 = along_z(p2, 1), along_z(m2, -1)
+    cut = call(
+        cut_kernel, [shape(PIECE, SIDE)] * NZH, [SMEM, HBM], [VMEM] * NZH, "cut",
+        scratch=[pltpu.SemaphoreType.DMA((NZH,))],
+    )(place, first)
     d1, w1 = dispatch(place, (p2, m2))
-    d1, r0, p3, m3, swapped = fence(d1, r0, p3, m3, swapped)
+    d1, r0, p3, m3, swapped, *cut = fence(d1, r0, p3, m3, swapped, *cut)
     swap_full = lax.all_gather(swapped, "y", axis=0, tiled=False)
     r1 = in_plane(d1)
     far = along_z(p3, 1)
-    far, first = fence(far, first)
-    cut = call(
-        cut_kernel, [shape(PIECE, SIDE)] * NZH, [SMEM, HBM], [HBM] * NZH, "cut",
-        scratch=[pltpu.SemaphoreType.DMA((NZH,))],
-    )(place, first)
+    far, first, *cut = fence(far, first, *cut)
     held = [cut[0]] + [shift(cut[k], "zh", NZH, k) for k in range(1, NZH)]
     d2, w2 = dispatch(place, (p3, m3, far))
     d2, r1 = fence(d2, r1)
@@ -404,7 +404,7 @@
     b2 = in_plane(s2)
     s1, s0 = ffn(place, own_full, swap_full, (r1, r0), 320)
     picked = call(
-        pick_kernel, [shape(PIECE, SIDE)] * NZH, [SMEM] + [HBM] * NZH, [HBM] * NZH, "pick",
+        pick_kernel, [shape(PIECE, SIDE)] * NZH, [SMEM] + [HBM] * NZH, [VMEM] * NZH, "pick",
         scratch=[pltpu.SemaphoreType.DMA((NZH,))],
     )(chosen, *held)
     held = [picked[0]] + [shift(picked[k], "zh", NZH, k) for k in range(1, NZH)]

time: 283 us -> 273 us (0.965)
  Pallas kernels: 50.8 us -> 43.1 us
  waiting for transfers between devices: 107 us -> 102 us
    pallas_call x2, Pallas kernels: 11.6 us -> 2.75 us  [the longest x1 1.81 us: body(): call(cut_kernel, [shape(PIECE, SIDE)] * NZH, [SMEM, HBM], [VMEM] * NZH, '...]
    ppermute x20, waiting for transfers between devices: 98.4 us -> 93.4 us  [shift(): lax.ppermute(value, axes, [(i, (i + step) % count) for i in range(count)])]
    unnamed x54 -> x66, local copies, waits for them, and re-layouts: 17.8 us -> 19.9 us
  transfers between devices with their start and end apart: 32 -> 32, of which waited for: 16 -> 16; matrix products, arithmetic and copies ran while one was open for 4% -> 5% of each run, Pallas kernels for 17% -> 14%
where the time goes in v11:
time: 273 us; the launch traced here: 270 us
  waiting for transfers between devices  102 us (37%)
  starting transfers between devices  75.8 us (28%)
  Pallas kernels  43.1 us (16%)
  local copies, waits for them, and re-layouts  24.1 us (9%)
  between operations  14.3 us (5%)
  other arithmetic  10.2 us (4%)
    ppermute x20, waiting for transfers between devices, shift(): lax.ppermute(value, axes, [(i, (i + step) % count) for i in range(count)])  93.4 us
    all_to_all x8, starting transfers between devices, across(): return lax.all_to_all(value, axis, split_axis=0, concat_axis=0, tiled=True)  39.5 us
    ppermute x20, starting transfers between devices, shift(): lax.ppermute(value, axes, [(i, (i + step) % count) for i in range(count)])  36.2 us
    pallas_call x2, Pallas kernels, ffn(): call(functools.partial(ffn_kernel, splits, block), [pltpu.HBM((r, WIDTH),...  22.5 us
    unnamed x66, local copies, waits for them, and re-layouts  19.9 us
    all_to_all x8, waiting for transfers between devices, across(): return lax.all_to_all(value, axis, split_axis=0, concat_axis=0, tiled=True)  9 us
    convert_element_type x5, other arithmetic, joined(): return (got.astype(F32) + mine).astype(BF)  7.39 us
    pallas_call x3, Pallas kernels, dispatch(): call(functools.partial(dispatch_kernel, n), [shape(PLACES * n * MOST, WID...  6.66 us
  transfers between devices with their start and end apart: 32, of which 16 were waited for; matrix products, arithmetic and copies ran while one was open for 5% of the time, Pallas kernels for 14%

profile of v11, /device:TPU:22, one launch (start us, length us, event | category | flops | bytes accessed | tf_op | source)
XLA Modules:
  0.0 270.0 jit_solution(3662973412801549106)
XLA Ops:
  7.3 4.3 %prep.1 = (bf16[104,2048]{1,0:T(8,128)(2,1)S(1)}, bf16[384,1536]{1,0:T(8,128)(2,1)}, bf16[384,1536]{1,0:T(8,128)(2,1)S(1)}, bf16[384,1536]{1,0:T(8,128)(2,1)}) custom-call(s32[4]{0:T(128)S(1)} %pad_add_fusion.place_ref, bf16[96,2048]{1,0:T(8,128)(2,1)} %tokens_ref.1, f32[1,2048]{1,0:T(1,128)} %bitcast.41, s32[8,96]{1,0:T(8,128)} %bitcast.42, ...), custom_call_target="tpu_custom_call" | custom-call | tf_op jit(solution)/shard_map/prep/pallas_call | solution.py:343
  12.9 4.8 %all-to-all-start = ((bf16[4,96,1536]{2,1,0:T(8,128)(2,1)}), bf16[4,96,1536]{2,1,0:T(8,128)(2,1)}, u32[]{:S(2)}, u32[]{:S(2)}) async-start(bf16[4,96,1536]{2,1,0:T(8,128)(2,1)} %bitcast.7), calls=%async_computation | async-start | bytes 2359296 | tf_op jit(solution)/shard_map/all_to_all | solution.py:52
  17.7 5.9 %collective-permute-start.1 = (bf16[104,2048]{1,0:T(8,128)(2,1)S(1)}, bf16[104,2048]{1,0:T(8,128)(2,1)S(1)}, u32[]{:S(2)}, u32[]{:S(2)}) collective-permute-start(bf16[104,2048]{1,0:T(8,128)(2,1)S(1)} %get-tuple-element.89.refs_0_), channel_id=1, source_target_pairs={{0,49},{1,0},{16,1},{17,16},{32,17},{33,32},{48,33},{49,48},{2,51}... | collective-permute-start | bytes 1277960 | tf_op jit(solution)/shard_map/ppermute | solution.py:36
  23.6 9.4 %collective-permute-done.1.refs_2_ = bf16[104,2048]{1,0:T(8,128)(2,1)S(1)} collective-permute-done((bf16[104,2048]{1,0:T(8,128)(2,1)S(1)}, bf16[104,2048]{1,0:T(8,128)(2,1)S(1)}, u32[]{:S(2)}, u32[]{:S(2)}) %collective-permute-start.1) | collective-permute-done | bytes 426016 | tf_op jit(solution)/shard_map/ppermute | solution.py:36
  33.0 3.4 %collective-permute-done.refs_1_ = bf16[104,2048]{1,0:T(8,128)(2,1)S(1)} collective-permute-done((bf16[104,2048]{1,0:T(8,128)(2,1)S(1)}, bf16[104,2048]{1,0:T(8,128)(2,1)S(1)}, u32[]{:S(2)}, u32[]{:S(2)}) %collective-permute-start) | collective-permute-done | bytes 426016 | tf_op jit(solution)/shard_map/ppermute | solution.py:36
  40.8 4.8 %all-to-all-start.1 = ((bf16[8,48,2048]{2,1,0:T(8,128)(2,1)}), bf16[8,48,2048]{2,1,0:T(8,128)(2,1)S(1)}, u32[]{:S(2)}, u32[]{:S(2)}) async-start(bf16[8,48,2048]{2,1,0:T(8,128)(2,1)} %bitcast.8), calls=%async_computation.1 | async-start | bytes 3145728 | tf_op jit(solution)/shard_map/all_to_all | solution.py:52
  48.8 21.6 %collective-permute-done.2.refs_0_ = bf16[104,2048]{1,0:T(8,128)(2,1)S(1)} collective-permute-done((bf16[104,2048]{1,0:T(8,128)(2,1)S(1)}, bf16[104,2048]{1,0:T(8,128)(2,1)S(1)}, u32[]{:S(2)}, u32[]{:S(2)}) %collective-permute-start.2) | collective-permute-done | bytes 426016 | tf_op jit(solution)/shard_map/ppermute | solution.py:36
  72.9 3.0 %collective-permute-start.7 = (bf16[104,2048]{1,0:T(8,128)(2,1)S(1)}, bf16[104,2048]{1,0:T(8,128)(2,1)S(1)}, u32[]{:S(2)}, u32[]{:S(2)}) collective-permute-start(bf16[104,2048]{1,0:T(8,128)(2,1)S(1)} %collective-permute-done.3.refs_1_), channel_id=1, source_target_pairs={{0,49},{1,0},{16,1},{17,16},{32,17},{33,32},{48,33},{49,48},{2,51}... | collective-permute-start | bytes 1277960 | tf_op jit(solution)/shard_map/ppermute | solution.py:36
  84.8 4.8 %all-to-all-start.2 = ((bf16[8,32,2048]{2,1,0:T(8,128)(2,1)}), bf16[8,32,2048]{2,1,0:T(8,128)(2,1)S(1)}, u32[]{:S(2)}, u32[]{:S(2)}) async-start(bf16[8,32,2048]{2,1,0:T(8,128)(2,1)} %bitcast.37), calls=%async_computation.2 | async-start | bytes 2097152 | tf_op jit(solution)/shard_map/all_to_all | solution.py:52
  89.6 13.1 %collective-permute-done.8.refs_2_ = bf16[104,2048]{1,0:T(8,128)(2,1)S(1)} collective-permute-done((bf16[104,2048]{1,0:T(8,128)(2,1)S(1)}, bf16[104,2048]{1,0:T(8,128)(2,1)S(1)}, u32[]{:S(2)}, u32[]{:S(2)}) %collective-permute-start.8) | collective-permute-done | bytes 426016 | tf_op jit(solution)/shard_map/ppermute | solution.py:36
  102.7 2.7 %dispatch.5 = (bf16[384,2048]{1,0:T(8,128)(2,1)}, bf16[3,128,128]{2,1,0:T(8,128)(2,1)S(1)}) custom-call(s32[4]{0:T(128)S(1)} %pad_add_fusion.place_ref, bf16[104,2048]{1,0:T(8,128)(2,1)S(1)} %collective-permute-done.6.refs_0_, bf16[104,2048]{1,0:T(8,128)(2,1)S(1)} %collective-permute-done.7.refs_1_, bf16[104,2048]{1,0:T(8,128)(2,1)S(1)} %collective-permute-done.8.refs_2_), custom_call_target="tpu_custom_call" | custom-call | bytes 83886080 | tf_op jit(solution)/shard_map/dispatch/pallas_call | solution.py:207
  107.0 4.8 %all-to-all-start.3 = ((bf16[8,48,2048]{2,1,0:T(8,128)(2,1)}), bf16[8,48,2048]{2,1,0:T(8,128)(2,1)S(1)}, u32[]{:S(2)}, u32[]{:S(2)}) async-start(bf16[8,48,2048]{2,1,0:T(8,128)(2,1)} %bitcast.14), calls=%async_computation.3 | async-start | bytes 3145728 | tf_op jit(solution)/shard_map/all_to_all | solution.py:52
  113.2 3.1 %collective-permute-start.10 = (bf16[96,1536]{1,0:T(8,128)(2,1)}, bf16[96,1536]{1,0:T(8,128)(2,1)S(1)}, u32[]{:S(2)}, u32[]{:S(2)}) collective-permute-start(bf16[96,1536]{1,0:T(8,128)(2,1)} %copy-done.30), channel_id=1, source_target_pairs={{0,32},{16,48},{32,0},{48,16},{1,33},{17,49},{33,1},{49,17},{2,34}... | collective-permute-start | bytes 884744 | tf_op jit(solution)/shard_map/ppermute | solution.py:36
  116.3 3.4 %collective-permute-start.11 = (bf16[96,1536]{1,0:T(8,128)(2,1)S(1)}, bf16[96,1536]{1,0:T(8,128)(2,1)S(1)}, u32[]{:S(2)}, u32[]{:S(2)}) collective-permute-start(bf16[96,1536]{1,0:T(8,128)(2,1)S(1)} %copy-done.29), channel_id=1, source_target_pairs={{0,48},{16,0},{32,16},{48,32},{1,49},{17,1},{33,17},{49,33},{2,50}... | collective-permute-start | bytes 884744 | tf_op jit(solution)/shard_map/ppermute | solution.py:36
  119.7 2.9 %gather_fusion.1 = bf16[4,96,1536]{2,1,0:T(8,128)(2,1)} fusion(bf16[4,96,1536]{2,1,0:T(8,128)(2,1)} %all-to-all-done, s32[1024]{0:T(1024)S(1)} %pad_clamp_fusion.1), kind=kCustom, calls=%fused_computation.1 | custom fusion | bytes 2359312 | tf_op jit(solution)/shard_map/jit(_take)/gather | solution.py:396
  122.6 14.6 %collective-permute-done.9.refs_1_ = bf16[96,1536]{1,0:T(8,128)(2,1)S(1)} collective-permute-done((bf16[96,1536]{1,0:T(8,128)(2,1)}, bf16[96,1536]{1,0:T(8,128)(2,1)S(1)}, u32[]{:S(2)}, u32[]{:S(2)}) %collective-permute-start.9) | collective-permute-done | bytes 294944 | tf_op jit(solution)/shard_map/ppermute | solution.py:36
  138.0 6.5 %collective-permute-done.11.refs_3_ = bf16[96,1536]{1,0:T(8,128)(2,1)S(1)} collective-permute-done((bf16[96,1536]{1,0:T(8,128)(2,1)S(1)}, bf16[96,1536]{1,0:T(8,128)(2,1)S(1)}, u32[]{:S(2)}, u32[]{:S(2)}) %collective-permute-start.11) | collective-permute-done | bytes 294944 | tf_op jit(solution)/shard_map/ppermute | solution.py:36
  145.2 4.8 %all-to-all-start.4 = ((bf16[4,96,1536]{2,1,0:T(8,128)(2,1)}), bf16[4,96,1536]{2,1,0:T(8,128)(2,1)S(1)}, u32[]{:S(2)}, u32[]{:S(2)}) async-start(bf16[4,96,1536]{2,1,0:T(8,128)(2,1)} %gather_fusion.1), calls=%async_computation.4 | async-start | bytes 2359296 | tf_op jit(solution)/shard_map/all_to_all | solution.py:52
  150.0 9.8 %expert_ffn.2 = bf16[384,2048]{1,0:T(8,128)(2,1)} custom-call(s32[4]{0:T(128)S(1)} %pad_add_fusion.place_ref, bf16[4,384,1536]{2,1,0:T(8,128)(2,1)} %bitcast.44, bf16[4,384,1536]{2,1,0:T(8,128)(2,1)} %bitcast.46, bf16[384,2048]{1,0:T(8,128)(2,1)S(1)} %bitcast.35), custom_call_target="tpu_custom_call" | custom-call | flops 3623878656 | bytes 15728640 | tf_op jit(solution)/shard_map/expert_ffn/pallas_call | solution.py:274
  159.8 4.8 %all-to-all-done.4 = bf16[4,96,1536]{2,1,0:T(8,128)(2,1)S(1)} async-done(((bf16[4,96,1536]{2,1,0:T(8,128)(2,1)}), bf16[4,96,1536]{2,1,0:T(8,128)(2,1)S(1)}, u32[]{:S(2)}, u32[]{:S(2)}) %all-to-all-start.4) | async-done | bytes 1179680 | tf_op jit(solution)/shard_map/all_to_all | solution.py:52
  164.7 5.7 %all-to-all-start.5 = ((bf16[8,48,2048]{2,1,0:T(8,128)(2,1)}), bf16[8,48,2048]{2,1,0:T(8,128)(2,1)S(1)}, u32[]{:S(2)}, u32[]{:S(2)}) async-start(bf16[8,48,2048]{2,1,0:T(8,128)(2,1)} %bitcast.39), calls=%async_computation.5 | async-start | bytes 3145728 | tf_op jit(solution)/shard_map/all_to_all | solution.py:52
  176.4 3.5 %collective-permute-start.13 = (bf16[96,1536]{1,0:T(8,128)(2,1)S(1)}, bf16[96,1536]{1,0:T(8,128)(2,1)S(1)}, u32[]{:S(2)}, u32[]{:S(2)}) collective-permute-start(bf16[96,1536]{1,0:T(8,128)(2,1)S(1)} %get-tuple-element.146), channel_id=1, source_target_pairs={{0,32},{16,48},{32,0},{48,16},{1,33},{17,49},{33,1},{49,17},{2,34}... | collective-permute-start | bytes 884744 | tf_op jit(solution)/shard_map/ppermute | solution.py:36
  181.9 12.8 %expert_ffn.3 = (bf16[256,2048]{1,0:T(8,128)(2,1)}, bf16[384,2048]{1,0:T(8,128)(2,1)}) custom-call(s32[4]{0:T(128)S(1)} %pad_add_fusion.place_ref, bf16[4,384,1536]{2,1,0:T(8,128)(2,1)} %bitcast.45, bf16[4,384,1536]{2,1,0:T(8,128)(2,1)} %bitcast.47, bf16[256,2048]{1,0:T(8,128)(2,1)S(1)} %bitcast.36, bf16[384,2048]{1,0:T(8,128)(2,1)S(1)} %bitcast.34), custom_call_target="tpu_custom_call" | custom-call | flops 6039797760 | bytes 15728640 | tf_op jit(solution)/shard_map/expert_ffn/pallas_call | solution.py:274
  196.7 3.0 %collective-permute-done.14.refs_6_ = bf16[96,1536]{1,0:T(8,128)(2,1)S(1)} collective-permute-done((bf16[96,1536]{1,0:T(8,128)(2,1)S(1)}, bf16[96,1536]{1,0:T(8,128)(2,1)S(1)}, u32[]{:S(2)}, u32[]{:S(2)}) %collective-permute-start.14) | collective-permute-done | bytes 294944 | tf_op jit(solution)/shard_map/ppermute | solution.py:36
  200.4 4.8 %all-to-all-start.6 = ((bf16[8,32,2048]{2,1,0:T(8,128)(2,1)}), bf16[8,32,2048]{2,1,0:T(8,128)(2,1)}, u32[]{:S(2)}, u32[]{:S(2)}) async-start(bf16[8,32,2048]{2,1,0:T(8,128)(2,1)} %bitcast.40), calls=%async_computation.6 | async-start | bytes 2097152 | tf_op jit(solution)/shard_map/all_to_all | solution.py:52
  207.3 3.2 %collective-permute-start.15 = (bf16[96,2048]{1,0:T(8,128)(2,1)}, bf16[96,2048]{1,0:T(8,128)(2,1)}, u32[]{:S(2)}, u32[]{:S(2)}) collective-permute-start(bf16[96,2048]{1,0:T(8,128)(2,1)} %get-tuple-element.149), channel_id=1, source_target_pairs={{0,49},{1,0},{16,1},{17,16},{32,17},{33,32},{48,33},{49,48},{2,51}... | collective-permute-start | bytes 1179656 | tf_op jit(solution)/shard_map/ppermute | solution.py:36
  210.6 9.2 %collective-permute-done.17 = bf16[96,2048]{1,0:T(8,128)(2,1)} collective-permute-done((bf16[96,2048]{1,0:T(8,128)(2,1)S(1)}, bf16[96,2048]{1,0:T(8,128)(2,1)}, u32[]{:S(2)}, u32[]{:S(2)}) %collective-permute-start.17) | collective-permute-done | bytes 393248 | tf_op jit(solution)/shard_map/ppermute | solution.py:36
  219.8 5.0 %all-to-all-start.7 = ((bf16[8,48,2048]{2,1,0:T(8,128)(2,1)}), bf16[8,48,2048]{2,1,0:T(8,128)(2,1)S(1)}, u32[]{:S(2)}, u32[]{:S(2)}) async-start(bf16[8,48,2048]{2,1,0:T(8,128)(2,1)} %bitcast.38), calls=%async_computation.7 | async-start | bytes 3145728 | tf_op jit(solution)/shard_map/all_to_all | solution.py:52
  231.5 5.7 %collective-permute-done.16 = bf16[96,2048]{1,0:T(8,128)(2,1)S(1)} collective-permute-done((bf16[96,2048]{1,0:T(8,128)(2,1)S(1)}, bf16[96,2048]{1,0:T(8,128)(2,1)S(1)}, u32[]{:S(2)}, u32[]{:S(2)}) %collective-permute-start.16) | collective-permute-done | bytes 393248 | tf_op jit(solution)/shard_map/ppermute | solution.py:36
  240.2 4.1 %all-to-all-done.7 = bf16[8,48,2048]{2,1,0:T(8,128)(2,1)S(1)} async-done(((bf16[8,48,2048]{2,1,0:T(8,128)(2,1)}), bf16[8,48,2048]{2,1,0:T(8,128)(2,1)S(1)}, u32[]{:S(2)}, u32[]{:S(2)}) %all-to-all-start.7) | async-done | bytes 1572896 | tf_op jit(solution)/shard_map/all_to_all | solution.py:52
  250.6 3.3 %collective-permute-start.19 = (bf16[96,2048]{1,0:T(8,128)(2,1)}, bf16[96,2048]{1,0:T(8,128)(2,1)}, u32[]{:S(2)}, u32[]{:S(2)}) collective-permute-start(bf16[96,2048]{1,0:T(8,128)(2,1)} %add_convert_fusion.3), channel_id=1, source_target_pairs={{0,49},{1,0},{16,1},{17,16},{32,17},{33,32},{48,33},{49,48},{2,51}... | collective-permute-start | bytes 1179656 | tf_op jit(solution)/shard_map/ppermute | solution.py:36
  257.5 3.6 %unpack.1 = (bf16[256,768]{1,0:T(8,128)(2,1)}, bf16[256,768]{1,0:T(8,128)(2,1)}, bf16[96,2048]{1,0:T(8,128)(2,1)}) custom-call(s32[1]{0:T(128)} %bitcast.25.kind_ref, s32[4]{0:T(128)S(1)} %pad_add_fusion.place_ref, bf16[384,1536]{1,0:T(8,128)(2,1)} %get-tuple-element.164.first_ref.refs_0_, bf16[384,1536]{1,0:T(8,128)(2,1)S(1)} %copy-done.3, ...), custom_call_target="tpu_custom_call" | custom-call | tf_op jit(solution)/shard_map/unpack/pallas_call | solution.py:424
  (129 shorter events, 59.2 us)
Async XLA Ops:
  7.2 142.9 %all-gather.5.cloned.1.call-start = ((), (), s32[]{:S(2)}) async-start(), calls=%async_computation.8 | async-start | bytes 5898240 | tf_op jit(solution)/shard_map/all_gather | solution.py:367
  12.8 26.9 %collective-permute-start.5 = (bf16[384,1536]{1,0:T(8,128)(2,1)}, bf16[384,1536]{1,0:T(8,128)(2,1)S(1)}, u32[]{:S(2)}, u32[]{:S(2)}) collective-permute-start(bf16[384,1536]{1,0:T(8,128)(2,1)} %get-tuple-element.164.first_ref.refs_0_), channel_id=1, source_target_pairs={{0,8},{8,0},{1,9},{9,1},{2,10},{10,2},{3,11},{11,3},{4,12},{12,4},... | collective-permute-start | bytes 3538952 | tf_op jit(solution)/shard_map/ppermute | solution.py:329
  12.9 26.8 %all-to-all-start = ((bf16[4,96,1536]{2,1,0:T(8,128)(2,1)}), bf16[4,96,1536]{2,1,0:T(8,128)(2,1)}, u32[]{:S(2)}, u32[]{:S(2)}) async-start(bf16[4,96,1536]{2,1,0:T(8,128)(2,1)} %bitcast.7), calls=%async_computation | async-start | bytes 2359296 | tf_op jit(solution)/shard_map/all_to_all | solution.py:52
  17.7 15.3 %collective-permute-start.1 = (bf16[104,2048]{1,0:T(8,128)(2,1)S(1)}, bf16[104,2048]{1,0:T(8,128)(2,1)S(1)}, u32[]{:S(2)}, u32[]{:S(2)}) collective-permute-start(bf16[104,2048]{1,0:T(8,128)(2,1)S(1)} %get-tuple-element.89.refs_0_), channel_id=1, source_target_pairs={{0,49},{1,0},{16,1},{17,16},{32,17},{33,32},{48,33},{49,48},{2,51}... | collective-permute-start | bytes 1277960 | tf_op jit(solution)/shard_map/ppermute | solution.py:36
  23.6 12.8 %collective-permute-start = (bf16[104,2048]{1,0:T(8,128)(2,1)S(1)}, bf16[104,2048]{1,0:T(8,128)(2,1)S(1)}, u32[]{:S(2)}, u32[]{:S(2)}) collective-permute-start(bf16[104,2048]{1,0:T(8,128)(2,1)S(1)} %get-tuple-element.89.refs_0_), channel_id=1, source_target_pairs={{0,1},{1,16},{16,17},{17,32},{32,33},{33,48},{48,49},{49,0},{2,3},... | collective-permute-start | bytes 1277960 | tf_op jit(solution)/shard_map/ppermute | solution.py:36
  36.4 36.2 %collective-permute-start.4 = (bf16[384,1536]{1,0:T(8,128)(2,1)}, bf16[384,1536]{1,0:T(8,128)(2,1)}, u32[]{:S(2)}, u32[]{:S(2)}) collective-permute-start(bf16[384,1536]{1,0:T(8,128)(2,1)} %copy-done.27), channel_id=1, source_target_pairs={{0,1},{1,0},{2,3},{3,2},{4,5},{5,4},{6,7},{7,6},{8,9},{9,8},{10,11... | collective-permute-start | bytes 3538952 | tf_op jit(solution)/shard_map/ppermute | solution.py:329
  40.8 42.9 %all-to-all-start.1 = ((bf16[8,48,2048]{2,1,0:T(8,128)(2,1)}), bf16[8,48,2048]{2,1,0:T(8,128)(2,1)S(1)}, u32[]{:S(2)}, u32[]{:S(2)}) async-start(bf16[8,48,2048]{2,1,0:T(8,128)(2,1)} %bitcast.8), calls=%async_computation.1 | async-start | bytes 3145728 | tf_op jit(solution)/shard_map/all_to_all | solution.py:52
  45.6 104.5 %all-gather.7.cloned.1.call-start = ((), (), s32[]{:S(2)}) async-start(), calls=%async_computation.9 | async-start | bytes 5898240 | tf_op jit(solution)/shard_map/all_gather | solution.py:386
  45.6 24.8 %collective-permute-start.2 = (bf16[104,2048]{1,0:T(8,128)(2,1)S(1)}, bf16[104,2048]{1,0:T(8,128)(2,1)S(1)}, u32[]{:S(2)}, u32[]{:S(2)}) collective-permute-start(bf16[104,2048]{1,0:T(8,128)(2,1)S(1)} %collective-permute-done.refs_1_), channel_id=1, source_target_pairs={{0,1},{1,16},{16,17},{17,32},{32,33},{33,48},{48,49},{49,0},{2,3},... | collective-permute-start | bytes 1277960 | tf_op jit(solution)/shard_map/ppermute | solution.py:36
  47.6 25.0 %collective-permute-start.3 = (bf16[104,2048]{1,0:T(8,128)(2,1)S(1)}, bf16[104,2048]{1,0:T(8,128)(2,1)S(1)}, u32[]{:S(2)}, u32[]{:S(2)}) collective-permute-start(bf16[104,2048]{1,0:T(8,128)(2,1)S(1)} %collective-permute-done.1.refs_2_), channel_id=1, source_target_pairs={{0,49},{1,0},{16,1},{17,16},{32,17},{33,32},{48,33},{49,48},{2,51}... | collective-permute-start | bytes 1277960 | tf_op jit(solution)/shard_map/ppermute | solution.py:36
  72.6 11.0 %collective-permute-start.6 = (bf16[104,2048]{1,0:T(8,128)(2,1)S(1)}, bf16[104,2048]{1,0:T(8,128)(2,1)S(1)}, u32[]{:S(2)}, u32[]{:S(2)}) collective-permute-start(bf16[104,2048]{1,0:T(8,128)(2,1)S(1)} %collective-permute-done.2.refs_0_), channel_id=1, source_target_pairs={{0,1},{1,16},{16,17},{17,32},{32,33},{33,48},{48,49},{49,0},{2,3},... | collective-permute-start | bytes 1277960 | tf_op jit(solution)/shard_map/ppermute | solution.py:36
  72.9 10.7 %collective-permute-start.7 = (bf16[104,2048]{1,0:T(8,128)(2,1)S(1)}, bf16[104,2048]{1,0:T(8,128)(2,1)S(1)}, u32[]{:S(2)}, u32[]{:S(2)}) collective-permute-start(bf16[104,2048]{1,0:T(8,128)(2,1)S(1)} %collective-permute-done.3.refs_1_), channel_id=1, source_target_pairs={{0,49},{1,0},{16,1},{17,16},{32,17},{33,32},{48,33},{49,48},{2,51}... | collective-permute-start | bytes 1277960 | tf_op jit(solution)/shard_map/ppermute | solution.py:36
  84.8 21.3 %all-to-all-start.2 = ((bf16[8,32,2048]{2,1,0:T(8,128)(2,1)}), bf16[8,32,2048]{2,1,0:T(8,128)(2,1)S(1)}, u32[]{:S(2)}, u32[]{:S(2)}) async-start(bf16[8,32,2048]{2,1,0:T(8,128)(2,1)} %bitcast.37), calls=%async_computation.2 | async-start | bytes 2097152 | tf_op jit(solution)/shard_map/all_to_all | solution.py:52
  89.6 13.1 %collective-permute-start.8 = (bf16[104,2048]{1,0:T(8,128)(2,1)S(1)}, bf16[104,2048]{1,0:T(8,128)(2,1)S(1)}, u32[]{:S(2)}, u32[]{:S(2)}) collective-permute-start(bf16[104,2048]{1,0:T(8,128)(2,1)S(1)} %collective-permute-done.6.refs_0_), channel_id=1, source_target_pairs={{0,1},{1,16},{16,17},{17,32},{32,33},{33,48},{48,49},{49,0},{2,3},... | collective-permute-start | bytes 1277960 | tf_op jit(solution)/shard_map/ppermute | solution.py:36
  107.0 38.2 %all-to-all-start.3 = ((bf16[8,48,2048]{2,1,0:T(8,128)(2,1)}), bf16[8,48,2048]{2,1,0:T(8,128)(2,1)S(1)}, u32[]{:S(2)}, u32[]{:S(2)}) async-start(bf16[8,48,2048]{2,1,0:T(8,128)(2,1)} %bitcast.14), calls=%async_computation.3 | async-start | bytes 3145728 | tf_op jit(solution)/shard_map/all_to_all | solution.py:52
  113.2 24.1 %collective-permute-start.9 = (bf16[96,1536]{1,0:T(8,128)(2,1)}, bf16[96,1536]{1,0:T(8,128)(2,1)S(1)}, u32[]{:S(2)}, u32[]{:S(2)}) collective-permute-start(bf16[96,1536]{1,0:T(8,128)(2,1)} %copy-done.31), channel_id=1, source_target_pairs={{0,16},{16,32},{32,48},{48,0},{1,17},{17,33},{33,49},{49,1},{2,18}... | collective-permute-start | bytes 884744 | tf_op jit(solution)/shard_map/ppermute | solution.py:36
  113.2 24.1 %collective-permute-start.10 = (bf16[96,1536]{1,0:T(8,128)(2,1)}, bf16[96,1536]{1,0:T(8,128)(2,1)S(1)}, u32[]{:S(2)}, u32[]{:S(2)}) collective-permute-start(bf16[96,1536]{1,0:T(8,128)(2,1)} %copy-done.30), channel_id=1, source_target_pairs={{0,32},{16,48},{32,0},{48,16},{1,33},{17,49},{33,1},{49,17},{2,34}... | collective-permute-start | bytes 884744 | tf_op jit(solution)/shard_map/ppermute | solution.py:36
  116.3 28.3 %collective-permute-start.11 = (bf16[96,1536]{1,0:T(8,128)(2,1)S(1)}, bf16[96,1536]{1,0:T(8,128)(2,1)S(1)}, u32[]{:S(2)}, u32[]{:S(2)}) collective-permute-start(bf16[96,1536]{1,0:T(8,128)(2,1)S(1)} %copy-done.29), channel_id=1, source_target_pairs={{0,48},{16,0},{32,16},{48,32},{1,49},{17,1},{33,17},{49,33},{2,50}... | collective-permute-start | bytes 884744 | tf_op jit(solution)/shard_map/ppermute | solution.py:36
  145.2 19.4 %all-to-all-start.4 = ((bf16[4,96,1536]{2,1,0:T(8,128)(2,1)}), bf16[4,96,1536]{2,1,0:T(8,128)(2,1)S(1)}, u32[]{:S(2)}, u32[]{:S(2)}) async-start(bf16[4,96,1536]{2,1,0:T(8,128)(2,1)} %gather_fusion.1), calls=%async_computation.4 | async-start | bytes 2359296 | tf_op jit(solution)/shard_map/all_to_all | solution.py:52
  164.7 35.8 %all-to-all-start.5 = ((bf16[8,48,2048]{2,1,0:T(8,128)(2,1)}), bf16[8,48,2048]{2,1,0:T(8,128)(2,1)S(1)}, u32[]{:S(2)}, u32[]{:S(2)}) async-start(bf16[8,48,2048]{2,1,0:T(8,128)(2,1)} %bitcast.39), calls=%async_computation.5 | async-start | bytes 3145728 | tf_op jit(solution)/shard_map/all_to_all | solution.py:52
  174.0 20.7 %collective-permute-start.12 = (bf16[96,1536]{1,0:T(8,128)(2,1)S(1)}, bf16[96,1536]{1,0:T(8,128)(2,1)S(1)}, u32[]{:S(2)}, u32[]{:S(2)}) collective-permute-start(bf16[96,1536]{1,0:T(8,128)(2,1)S(1)} %get-tuple-element.145), channel_id=1, source_target_pairs={{0,16},{16,32},{32,48},{48,0},{1,17},{17,33},{33,49},{49,1},{2,18}... | collective-permute-start | bytes 884744 | tf_op jit(solution)/shard_map/ppermute | solution.py:36
  176.4 19.6 %collective-permute-start.13 = (bf16[96,1536]{1,0:T(8,128)(2,1)S(1)}, bf16[96,1536]{1,0:T(8,128)(2,1)S(1)}, u32[]{:S(2)}, u32[]{:S(2)}) collective-permute-start(bf16[96,1536]{1,0:T(8,128)(2,1)S(1)} %get-tuple-element.146), channel_id=1, source_target_pairs={{0,32},{16,48},{32,0},{48,16},{1,33},{17,49},{33,1},{49,17},{2,34}... | collective-permute-start | bytes 884744 | tf_op jit(solution)/shard_map/ppermute | solution.py:36
  179.9 19.8 %collective-permute-start.14 = (bf16[96,1536]{1,0:T(8,128)(2,1)S(1)}, bf16[96,1536]{1,0:T(8,128)(2,1)S(1)}, u32[]{:S(2)}, u32[]{:S(2)}) collective-permute-start(bf16[96,1536]{1,0:T(8,128)(2,1)S(1)} %get-tuple-element.147), channel_id=1, source_target_pairs={{0,48},{16,0},{32,16},{48,32},{1,49},{17,1},{33,17},{49,33},{2,50}... | collective-permute-start | bytes 884744 | tf_op jit(solution)/shard_map/ppermute | solution.py:36
  200.4 19.4 %all-to-all-start.6 = ((bf16[8,32,2048]{2,1,0:T(8,128)(2,1)}), bf16[8,32,2048]{2,1,0:T(8,128)(2,1)}, u32[]{:S(2)}, u32[]{:S(2)}) async-start(bf16[8,32,2048]{2,1,0:T(8,128)(2,1)} %bitcast.40), calls=%async_computation.6 | async-start | bytes 2097152 | tf_op jit(solution)/shard_map/all_to_all | solution.py:52
  207.3 12.5 %collective-permute-start.17 = (bf16[96,2048]{1,0:T(8,128)(2,1)S(1)}, bf16[96,2048]{1,0:T(8,128)(2,1)}, u32[]{:S(2)}, u32[]{:S(2)}) collective-permute-start(bf16[96,2048]{1,0:T(8,128)(2,1)S(1)} %get-tuple-element.154), channel_id=1, source_target_pairs={{0,1},{1,16},{16,17},{17,32},{32,33},{33,48},{48,49},{49,0},{2,3},... | collective-permute-start | bytes 1179656 | tf_op jit(solution)/shard_map/ppermute | solution.py:36
  207.3 17.5 %collective-permute-start.15 = (bf16[96,2048]{1,0:T(8,128)(2,1)}, bf16[96,2048]{1,0:T(8,128)(2,1)}, u32[]{:S(2)}, u32[]{:S(2)}) collective-permute-start(bf16[96,2048]{1,0:T(8,128)(2,1)} %get-tuple-element.149), channel_id=1, source_target_pairs={{0,49},{1,0},{16,1},{17,16},{32,17},{33,32},{48,33},{49,48},{2,51}... | collective-permute-start | bytes 1179656 | tf_op jit(solution)/shard_map/ppermute | solution.py:36
  219.8 24.5 %all-to-all-start.7 = ((bf16[8,48,2048]{2,1,0:T(8,128)(2,1)}), bf16[8,48,2048]{2,1,0:T(8,128)(2,1)S(1)}, u32[]{:S(2)}, u32[]{:S(2)}) async-start(bf16[8,48,2048]{2,1,0:T(8,128)(2,1)} %bitcast.38), calls=%async_computation.7 | async-start | bytes 3145728 | tf_op jit(solution)/shard_map/all_to_all | solution.py:52
  225.9 11.2 %collective-permute-start.16 = (bf16[96,2048]{1,0:T(8,128)(2,1)S(1)}, bf16[96,2048]{1,0:T(8,128)(2,1)S(1)}, u32[]{:S(2)}, u32[]{:S(2)}) collective-permute-start(bf16[96,2048]{1,0:T(8,128)(2,1)S(1)} %add_convert_fusion.5), channel_id=1, source_target_pairs={{0,49},{1,0},{16,1},{17,16},{32,17},{33,32},{48,33},{49,48},{2,51}... | collective-permute-start | bytes 1179656 | tf_op jit(solution)/shard_map/ppermute | solution.py:36
  230.4 15.3 %collective-permute-start.20 = (bf16[96,2048]{1,0:T(8,128)(2,1)}, bf16[96,2048]{1,0:T(8,128)(2,1)}, u32[]{:S(2)}, u32[]{:S(2)}) collective-permute-start(bf16[96,2048]{1,0:T(8,128)(2,1)} %add_convert_fusion.2), channel_id=1, source_target_pairs={{0,1},{1,16},{16,17},{17,32},{32,33},{33,48},{48,49},{49,0},{2,3},... | collective-permute-start | bytes 1179656 | tf_op jit(solution)/shard_map/ppermute | solution.py:36
  238.0 10.8 %collective-permute-start.18 = (bf16[96,2048]{1,0:T(8,128)(2,1)}, bf16[96,2048]{1,0:T(8,128)(2,1)}, u32[]{:S(2)}, u32[]{:S(2)}) collective-permute-start(bf16[96,2048]{1,0:T(8,128)(2,1)} %add_convert_fusion.4), channel_id=1, source_target_pairs={{0,49},{1,0},{16,1},{17,16},{32,17},{33,32},{48,33},{49,48},{2,51}... | collective-permute-start | bytes 1179656 | tf_op jit(solution)/shard_map/ppermute | solution.py:36
  247.5 13.5 %collective-permute-start.21 = (bf16[96,2048]{1,0:T(8,128)(2,1)}, bf16[96,2048]{1,0:T(8,128)(2,1)}, u32[]{:S(2)}, u32[]{:S(2)}) collective-permute-start(bf16[96,2048]{1,0:T(8,128)(2,1)} %add_convert_fusion.1), channel_id=1, source_target_pairs={{0,1},{1,16},{16,17},{17,32},{32,33},{33,48},{48,49},{49,0},{2,3},... | collective-permute-start | bytes 1179656 | tf_op jit(solution)/shard_map/ppermute | solution.py:36
  250.6 10.6 %collective-permute-start.19 = (bf16[96,2048]{1,0:T(8,128)(2,1)}, bf16[96,2048]{1,0:T(8,128)(2,1)}, u32[]{:S(2)}, u32[]{:S(2)}) collective-permute-start(bf16[96,2048]{1,0:T(8,128)(2,1)} %add_convert_fusion.3), channel_id=1, source_target_pairs={{0,49},{1,0},{16,1},{17,16},{32,17},{33,32},{48,33},{49,48},{2,51}... | collective-permute-start | bytes 1179656 | tf_op jit(solution)/shard_map/ppermute | solution.py:36
  (33 other events, 75.2 us)
Sparse Core Ops, SparseCore 0:
  12.9 57.0 all-gather.4
  83.8 52.8 all-gather.6
